TPU v7x, 32 devices: a whole 2x2x4 slice. The times are simulated.
32 devices in a mesh: dp: 4 (over x, core), fsdp: 2 (over y), tensor: 4 (over z).
Axes of the slice: x: 2, y: 2, z: 4, core: 2. Of those that a mesh axis runs over, the one named last changes fastest.
Arguments:
- layer_input: bfloat16 [4096, 2048], P(('dp', 'fsdp', 'tensor')), may hold values from -6 to 6
- first_gain: bfloat16 [2048], P('fsdp'), may hold values from 0.5 to 1.5
- w_query: bfloat16 [2048, 2048], P('fsdp', 'tensor'), may hold values from -0.125 to 0.125
- w_key: bfloat16 [2048, 2048], P('fsdp', 'tensor'), may hold values from -0.125 to 0.125
- w_value: bfloat16 [2048, 2048], P('fsdp', 'tensor'), may hold values from -0.125 to 0.125
- w_gating: bfloat16 [2048, 2048], P('fsdp', 'tensor'), may hold values from -0.125 to 0.125
- w_beta: bfloat16 [2048, 16], P('fsdp', 'tensor'), may hold values from -0.125 to 0.125
- conv_query: bfloat16 [4, 2048], P(None, 'tensor'), may hold values from -3 to 3
- conv_key: bfloat16 [4, 2048], P(None, 'tensor'), may hold values from -3 to 3
- conv_value: bfloat16 [4, 2048], P(None, 'tensor'), may hold values from -3 to 3
- head_gain: bfloat16 [128], replicated, may hold values from 0.5 to 1.5
- w_project: bfloat16 [2048, 2048], P('tensor', 'fsdp'), may hold values from -0.1875 to 0.1875
- second_gain: bfloat16 [2048], P('fsdp'), may hold values from 0.5 to 1.5
- w_gate: bfloat16 [2048, 5632], P('fsdp', 'tensor'), may hold values from -0.125 to 0.125
- w_up: bfloat16 [2048, 5632], P('fsdp', 'tensor'), may hold values from -0.125 to 0.125
- w_down: bfloat16 [5632, 2048], P('tensor', 'fsdp'), may hold values from -0.109375 to 0.109375
- doc_starts: int32 [8, 4], P(('dp', 'fsdp')), may hold values from 1 to 508, as said below
- seq_lengths: int32 [8], P(('dp', 'fsdp')), may hold values from 256 to 512, as said below
- output_grad: bfloat16 [4096, 2048], P(('dp', 'fsdp', 'tensor')), may hold values from -6 to 6
Outputs:
- result: bfloat16 [4096, 2048], P(('dp', 'fsdp', 'tensor'))
- input_grad: float32 [4096, 2048], P(('dp', 'fsdp', 'tensor'))
- grad_first: float32 [2048], P(('dp', 'fsdp'))
- grad_query: float32 [2048, 2048], P(('dp', 'fsdp'), 'tensor')
- grad_key: float32 [2048, 2048], P(('dp', 'fsdp'), 'tensor')
- grad_value: float32 [2048, 2048], P(('dp', 'fsdp'), 'tensor')
- grad_gating: float32 [2048, 2048], P(('dp', 'fsdp'), 'tensor')
- grad_beta: float32 [2048, 16], P(('dp', 'fsdp'), 'tensor')
- convgrad_query: float32 [4, 2048], P(None, 'tensor')
- convgrad_key: float32 [4, 2048], P(None, 'tensor')
- convgrad_value: float32 [4, 2048], P(None, 'tensor')
- grad_head: float32 [128], replicated
- grad_project: float32 [2048, 2048], P('tensor', ('dp', 'fsdp'))
- grad_second: float32 [2048], P(('dp', 'fsdp'))
- grad_gate: float32 [2048, 5632], P(('dp', 'fsdp'), 'tensor')
- grad_up: float32 [2048, 5632], P(('dp', 'fsdp'), 'tensor')
- grad_down: float32 [5632, 2048], P('tensor', ('dp', 'fsdp'))
Inputs may be any that keep to these rules, and one draw needn't show every extreme that they name: `doc_starts`: each row rises strictly; position 0 begins the first document of a sequence and each entry begins the next. `seq_lengths`: rows at positions at or past a sequence's length are padding.
All inputs are finite; a program needn't handle non-finite values.
Results may differ from a plain program's by a relative error of at most 0.015.
Values may be sent and summed in bfloat16 or wider, within the bound.
A program may use at most 256 MiB of HBM per device.

v0:
```python
import jax
import jax.numpy as jnp
from jax import lax
from jax.sharding import PartitionSpec as P

KERNEL = 4
BLOCK = 64


def rms_scale(values):
    return lax.rsqrt(jnp.mean(values * values, axis=-1, keepdims=True) + 1e-05)


def rms_back(values, scale_rows, gain, grad):
    scaled_grad = grad * gain
    inner = jnp.mean(scaled_grad * values, axis=-1, keepdims=True)
    return scale_rows * (scaled_grad - values * scale_rows * scale_rows * inner)


def short_conv(raw_rows, weights, doc_ids):
    row_count = raw_rows.shape[0]
    total = jnp.zeros_like(raw_rows)
    for tap_index in range(KERNEL):
        delay_rows = KERNEL - 1 - tap_index
        moved = jnp.pad(raw_rows, ((delay_rows, 0), (0, 0)))[:row_count]
        moved_doc = jnp.pad(doc_ids, (delay_rows, 0), constant_values=-1)[:row_count]
        keep_mask = (moved_doc == doc_ids).astype(raw_rows.dtype)
        total = total + weights[tap_index] * moved * keep_mask[:, None]
    return total


def delta_rule(query, keyed, valued, rate, doc_ids):
    row_count, head_count, head_width = query.shape
    blocks = row_count // BLOCK
    float_type = query.dtype

    def to_blocks(array):
        return array.reshape(blocks, BLOCK, head_count, head_width).transpose(0, 2, 1, 3)

    query_blk = to_blocks(query)
    key_blk = to_blocks(keyed)
    value_blk = to_blocks(valued)
    rate_blk = rate.reshape(blocks, BLOCK, head_count).transpose(0, 2, 1)
    doc_blk = doc_ids.reshape(blocks, BLOCK)
    prior_doc = jnp.concatenate([jnp.full((1,), -1, jnp.int32), doc_blk[:-1, -1]])
    carry_in = (doc_blk == prior_doc[:, None]).astype(float_type)
    same_doc = doc_blk[:, :, None] == doc_blk[:, None, :]
    positions = jnp.arange(BLOCK)
    strict = positions[:, None] > positions[None, :]
    inclusive = positions[:, None] >= positions[None, :]
    key_key = jnp.einsum("nhtd,nhsd->nhts", key_blk, key_blk, precision=lax.Precision.HIGHEST)
    mixing = key_key * rate_blk[..., None] * (same_doc & strict)[:, None].astype(float_type)
    system = mixing + jnp.eye(BLOCK, dtype=float_type)
    scaled_values = value_blk * rate_blk[..., None]
    scaled_keys = key_blk * (rate_blk * carry_in[:, None, :])[..., None]
    solved_values = jax.scipy.linalg.solve_triangular(
        system, scaled_values, lower=True, unit_diagonal=True
    )
    solved_keys = jax.scipy.linalg.solve_triangular(
        system, scaled_keys, lower=True, unit_diagonal=True
    )
    scores = jnp.einsum("nhtd,nhsd->nhts", query_blk, key_blk, precision=lax.Precision.HIGHEST)
    scores = scores * (same_doc & inclusive)[:, None].astype(float_type)
    last_same = (doc_blk == doc_blk[:, -1:]).astype(float_type)
    carry_end = carry_in[:, -1]

    def advance(memory, inputs):
        solved_v, solved_k, score_n, query_n, key_n, carry_n, last_n, end_n = inputs
        update = solved_v - jnp.einsum(
            "htk,hvk->htv", solved_k, memory, precision=lax.Precision.HIGHEST
        )
        output = carry_n[None, :, None] * jnp.einsum(
            "hvk,htk->htv", memory, query_n, precision=lax.Precision.HIGHEST
        )
        output = output + jnp.einsum(
            "hts,hsv->htv", score_n, update, precision=lax.Precision.HIGHEST
        )
        memory = end_n * memory + jnp.einsum(
            "htv,htk->hvk", update * last_n[None, :, None], key_n, precision=lax.Precision.HIGHEST
        )
        return (memory, output)

    initial = jnp.zeros((head_count, head_width, head_width), float_type)
    _, outputs = lax.scan(
        advance,
        initial,
        (solved_values, solved_keys, scores, query_blk, key_blk, carry_in, last_same, carry_end),
    )
    return outputs.transpose(0, 2, 1, 3).reshape(row_count, head_count, head_width)


def mixer(
    query_raw,
    key_raw,
    value_raw,
    gating_raw,
    beta_raw,
    conv_q,
    conv_k,
    conv_v,
    gain_head,
    doc_ids,
    live,
):
    head_width = gain_head.shape[0]
    row_count = query_raw.shape[0]
    query_unit = jax.nn.silu(short_conv(query_raw, conv_q, doc_ids)).reshape(
        row_count, -1, head_width
    )
    query_unit = query_unit * lax.rsqrt(
        jnp.sum(query_unit * query_unit, axis=-1, keepdims=True) + 1e-06
    )
    key_unit = jax.nn.silu(short_conv(key_raw, conv_k, doc_ids)).reshape(row_count, -1, head_width)
    key_unit = key_unit * lax.rsqrt(jnp.sum(key_unit * key_unit, axis=-1, keepdims=True) + 1e-06)
    value_rows = jax.nn.silu(short_conv(value_raw, conv_v, doc_ids)).reshape(
        row_count, -1, head_width
    )
    beta_rate = jax.nn.sigmoid(beta_raw) * live[:, None]
    mixed = delta_rule(query_unit, key_unit, value_rows, beta_rate, doc_ids)
    norm_scale = lax.rsqrt(jnp.mean(mixed * mixed, axis=-1, keepdims=True) + 1e-05)
    gated = (
        mixed * norm_scale * gain_head * jax.nn.silu(gating_raw.reshape(row_count, -1, head_width))
    )
    gated = gated * live[:, None, None]
    return gated.reshape(row_count, -1)


def matmul(left, right):
    return jnp.dot(left, right, preferred_element_type=jnp.float32)


def matmul_nt(left, right):
    return lax.dot_general(
        left, right, (((1,), (1,)), ((), ())), preferred_element_type=jnp.float32
    )


def matmul_tn(left, right):
    return lax.dot_general(
        left, right, (((0,), (0,)), ((), ())), preferred_element_type=jnp.float32
    )


def gather_rows(rows):
    return lax.all_gather(rows, "tensor", axis=0, tiled=True)


def scatter_rows(partial_rows):
    return lax.psum_scatter(partial_rows, "tensor", scatter_dimension=0, tiled=True)


def fetch_mixer(first_gain, w_query, w_key, w_value, w_gating, w_beta, w_project):
    return (
        lax.all_gather(first_gain, "fsdp", axis=0, tiled=True),
        lax.all_gather(w_query, "fsdp", axis=0, tiled=True),
        lax.all_gather(w_key, "fsdp", axis=0, tiled=True),
        lax.all_gather(w_value, "fsdp", axis=0, tiled=True),
        lax.all_gather(w_gating, "fsdp", axis=0, tiled=True),
        lax.all_gather(w_beta, "fsdp", axis=0, tiled=True),
        lax.all_gather(w_project, "fsdp", axis=1, tiled=True),
    )


def fetch_ffn(second_gain, w_gate, w_up, w_down):
    return (
        lax.all_gather(second_gain, "fsdp", axis=0, tiled=True),
        lax.all_gather(w_gate, "fsdp", axis=0, tiled=True),
        lax.all_gather(w_up, "fsdp", axis=0, tiled=True),
        lax.all_gather(w_down, "fsdp", axis=1, tiled=True),
    )


def body(
    layer_input,
    first_gain,
    w_query,
    w_key,
    w_value,
    w_gating,
    w_beta,
    conv_query,
    conv_key,
    conv_value,
    head_gain,
    w_project,
    second_gain,
    w_gate,
    w_up,
    w_down,
    doc_starts,
    seq_lengths,
    output_grad,
):
    input_float = layer_input.astype(jnp.float32)
    seq_rows = layer_input.shape[0] * lax.axis_size("tensor")
    positions = jnp.arange(seq_rows, dtype=jnp.int32)
    doc_ids = jnp.sum((doc_starts[0][None, :] <= positions[:, None]).astype(jnp.int32), axis=1)
    live = (positions < seq_lengths[0]).astype(jnp.float32)
    conv_q = conv_query.astype(jnp.float32)
    conv_k = conv_key.astype(jnp.float32)
    conv_v = conv_value.astype(jnp.float32)
    gain_head = head_gain.astype(jnp.float32)
    gain_one, query_full, key_full, value_full, gating_full, beta_full, project_full = fetch_mixer(
        first_gain, w_query, w_key, w_value, w_gating, w_beta, w_project
    )
    scale_one = rms_scale(input_float)
    normed1 = (input_float * scale_one * gain_one.astype(jnp.float32)).astype(jnp.bfloat16)
    rows_one = gather_rows(normed1)
    query_raw = matmul(rows_one, query_full)
    key_raw = matmul(rows_one, key_full)
    value_raw = matmul(rows_one, value_full)
    gating_raw = matmul(rows_one, gating_full)
    beta_raw = matmul(rows_one, beta_full)

    def mixer_local(
        query_in, key_in, value_in, gating_in, beta_in, conv_qin, conv_kin, conv_vin, gain_in
    ):
        return mixer(
            query_in,
            key_in,
            value_in,
            gating_in,
            beta_in,
            conv_qin,
            conv_kin,
            conv_vin,
            gain_in,
            doc_ids,
            live,
        )

    mixer_inputs = (
        query_raw,
        key_raw,
        value_raw,
        gating_raw,
        beta_raw,
        conv_q,
        conv_k,
        conv_v,
        gain_head,
    )
    gated_float, pullback = jax.vjp(mixer_local, *mixer_inputs)
    gated = gated_float.astype(jnp.bfloat16)
    attn_out = scatter_rows(matmul(gated, project_full))
    resid = input_float + attn_out
    gain_two, gate_full, up_full, down_full = fetch_ffn(second_gain, w_gate, w_up, w_down)
    scale_two = rms_scale(resid)
    normed2 = (resid * scale_two * gain_two.astype(jnp.float32)).astype(jnp.bfloat16)
    rows_two = gather_rows(normed2)
    gate_val = matmul(rows_two, gate_full)
    up_val = matmul(rows_two, up_full)
    gate_sig = jax.nn.sigmoid(gate_val)
    silu_gate = gate_val * gate_sig
    hidden = (silu_gate * up_val).astype(jnp.bfloat16)
    ffn_out = scatter_rows(matmul(hidden, down_full))
    result = (resid + ffn_out).astype(jnp.bfloat16)
    gain_two, gate_full, up_full, down_full = fetch_ffn(second_gain, w_gate, w_up, w_down)
    grad_rows = gather_rows(output_grad)
    d_hidden = matmul_nt(grad_rows, down_full)
    grad_down = matmul_tn(hidden, grad_rows)
    d_gate = (d_hidden * up_val * gate_sig * (1.0 + gate_val * (1.0 - gate_sig))).astype(
        jnp.bfloat16
    )
    d_up = (d_hidden * silu_gate).astype(jnp.bfloat16)
    grad_gate = matmul_tn(rows_two, d_gate)
    grad_up = matmul_tn(rows_two, d_up)
    d_normed2 = scatter_rows(matmul_nt(d_gate, gate_full) + matmul_nt(d_up, up_full))
    grad_second = jnp.sum(d_normed2 * resid * scale_two, axis=0)
    d_resid = output_grad.astype(jnp.float32) + rms_back(
        resid, scale_two, gain_two.astype(jnp.float32), d_normed2
    )
    gain_one, query_full, key_full, value_full, gating_full, beta_full, project_full = fetch_mixer(
        first_gain, w_query, w_key, w_value, w_gating, w_beta, w_project
    )
    d_attn = gather_rows(d_resid.astype(jnp.bfloat16))
    d_gated = matmul_nt(d_attn, project_full)
    grad_project = matmul_tn(gated, d_attn)
    cotangents = pullback(d_gated)
    d_query = cotangents[0].astype(jnp.bfloat16)
    d_key = cotangents[1].astype(jnp.bfloat16)
    d_value = cotangents[2].astype(jnp.bfloat16)
    d_gating = cotangents[3].astype(jnp.bfloat16)
    d_beta = cotangents[4].astype(jnp.bfloat16)
    grad_query = matmul_tn(rows_one, d_query)
    grad_key = matmul_tn(rows_one, d_key)
    grad_value = matmul_tn(rows_one, d_value)
    grad_gating = matmul_tn(rows_one, d_gating)
    grad_beta = matmul_tn(rows_one, d_beta)
    d_norm_one = (
        matmul_nt(d_query, query_full) + matmul_nt(d_key, key_full) + matmul_nt(d_value, value_full)
    )
    d_norm_one = d_norm_one + matmul_nt(d_gating, gating_full) + matmul_nt(d_beta, beta_full)
    d_normed1 = scatter_rows(d_norm_one)
    grad_first = jnp.sum(d_normed1 * input_float * scale_one, axis=0)
    input_grad = d_resid + rms_back(input_float, scale_one, gain_one.astype(jnp.float32), d_normed1)
    gain_totals = lax.psum((grad_first, grad_second, cotangents[8]), "tensor")
    conv_totals = lax.psum(
        (cotangents[5], cotangents[6], cotangents[7], gain_totals[2]), ("dp", "fsdp")
    )
    shards = (
        lax.psum_scatter(
            gain_totals[0].astype(jnp.bfloat16), ("dp", "fsdp"), scatter_dimension=0, tiled=True
        ).astype(jnp.float32),
        lax.psum_scatter(
            grad_query.astype(jnp.bfloat16), ("dp", "fsdp"), scatter_dimension=0, tiled=True
        ).astype(jnp.float32),
        lax.psum_scatter(
            grad_key.astype(jnp.bfloat16), ("dp", "fsdp"), scatter_dimension=0, tiled=True
        ).astype(jnp.float32),
        lax.psum_scatter(
            grad_value.astype(jnp.bfloat16), ("dp", "fsdp"), scatter_dimension=0, tiled=True
        ).astype(jnp.float32),
        lax.psum_scatter(
            grad_gating.astype(jnp.bfloat16), ("dp", "fsdp"), scatter_dimension=0, tiled=True
        ).astype(jnp.float32),
        lax.psum_scatter(
            grad_beta.astype(jnp.bfloat16), ("dp", "fsdp"), scatter_dimension=0, tiled=True
        ).astype(jnp.float32),
        lax.psum_scatter(
            grad_project.astype(jnp.bfloat16), ("dp", "fsdp"), scatter_dimension=1, tiled=True
        ).astype(jnp.float32),
        lax.psum_scatter(
            gain_totals[1].astype(jnp.bfloat16), ("dp", "fsdp"), scatter_dimension=0, tiled=True
        ).astype(jnp.float32),
        lax.psum_scatter(
            grad_gate.astype(jnp.bfloat16), ("dp", "fsdp"), scatter_dimension=0, tiled=True
        ).astype(jnp.float32),
        lax.psum_scatter(
            grad_up.astype(jnp.bfloat16), ("dp", "fsdp"), scatter_dimension=0, tiled=True
        ).astype(jnp.float32),
        lax.psum_scatter(
            grad_down.astype(jnp.bfloat16), ("dp", "fsdp"), scatter_dimension=1, tiled=True
        ).astype(jnp.float32),
    )
    return (
        result,
        input_grad,
        shards[0],
        shards[1],
        shards[2],
        shards[3],
        shards[4],
        shards[5],
        conv_totals[0],
        conv_totals[1],
        conv_totals[2],
        conv_totals[3],
        shards[6],
        shards[7],
        shards[8],
        shards[9],
        shards[10],
    )


def solution(mesh):
    placed = (
        P(("dp", "fsdp", "tensor"), None),
        P("fsdp"),
        P("fsdp", "tensor"),
        P("fsdp", "tensor"),
        P("fsdp", "tensor"),
        P("fsdp", "tensor"),
        P("fsdp", "tensor"),
        P(None, "tensor"),
        P(None, "tensor"),
        P(None, "tensor"),
        P(),
        P("tensor", "fsdp"),
        P("fsdp"),
        P("fsdp", "tensor"),
        P("fsdp", "tensor"),
        P("tensor", "fsdp"),
        P(("dp", "fsdp"), None),
        P(("dp", "fsdp")),
        P(("dp", "fsdp", "tensor"), None),
    )
    return jax.shard_map(
        body,
        mesh=mesh,
        in_specs=placed,
        out_specs=(
            P(("dp", "fsdp", "tensor"), None),
            P(("dp", "fsdp", "tensor"), None),
            P(("dp", "fsdp")),
            P(("dp", "fsdp"), "tensor"),
            P(("dp", "fsdp"), "tensor"),
            P(("dp", "fsdp"), "tensor"),
            P(("dp", "fsdp"), "tensor"),
            P(("dp", "fsdp"), "tensor"),
            P(None, "tensor"),
            P(None, "tensor"),
            P(None, "tensor"),
            P(),
            P("tensor", ("dp", "fsdp")),
            P(("dp", "fsdp")),
            P(("dp", "fsdp"), "tensor"),
            P(("dp", "fsdp"), "tensor"),
            P("tensor", ("dp", "fsdp")),
        ),
        check_vma=False,
    )
```

profile of v0, /device:TPU:0, one launch (start us, length us, event | category | flops | bytes accessed | tf_op | source)
XLA Modules:
  0.0 1605.7 jit_solution(16888827830021161958)
XLA Ops:
  8.0 5.5 all_gather.56
  21.7 4.5 all_gather.59
  26.4 19.2 %all-gather.19.cloned.1.call-done = bf16[2048,512]{1,0:T(8,128)(2,1)} async-done(((bf16[1024,512]{1,0:T(8,128)(2,1)}), bf16[2048,512]{1,0:T(8,128)(2,1)}) %all-gather.19.cloned.1.call-update) | async-done | bytes 2097168 | tf_op jit(solution)/shard_map/all_gather | solution.py:155
  45.6 48.2 %all-gather.13.cloned.1.call-done = bf16[512,2048]{1,0:T(8,128)(2,1)} async-done(((bf16[128,2048]{1,0:T(8,128)(2,1)}), bf16[512,2048]{1,0:T(8,128)(2,1)}) %all-gather.13.cloned.1.call-update) | async-done | bytes 2097168 | tf_op jit(solution)/shard_map/all_gather | solution.py:145
  93.8 4.6 fusion.184
  98.4 28.8 %all-gather.17.cloned.1.call-done = bf16[2048,512]{1,0:T(8,128)(2,1)} async-done(((bf16[1024,512]{1,0:T(8,128)(2,1)}), bf16[2048,512]{1,0:T(8,128)(2,1)}) %all-gather.17.cloned.1.call-update) | async-done | bytes 2097168 | tf_op jit(solution)/shard_map/all_gather | solution.py:157
  136.1 25.6 %all-gather.15.cloned.1.call-done = bf16[2048,512]{1,0:T(8,128)(2,1)} async-done(((bf16[1024,512]{1,0:T(8,128)(2,1)}), bf16[2048,512]{1,0:T(8,128)(2,1)}) %all-gather.15.cloned.1.call-update) | async-done | bytes 2097168 | tf_op jit(solution)/shard_map/all_gather | solution.py:156
  161.7 3.5 fusion.181
  182.0 158.2 %custom-call.12 = f32[8,4,1,64,64]{3,4,2,1,0:T(8,128)S(1)} custom-call(f32[8,4,1,64,64]{4,3,2,1,0:T(8,128)} %add_bitcast_fusion), custom_call_target="InvertDiagBlocksLowerTriangular" | custom-call | tf_op jit(solution)/shard_map/jvp(jit(_solve_triangular))/vmap(vmap())/triangular_solve | solution.py:56
  342.7 4.4 fusion.125
  356.3 70.5 %while.48 = (s32[]{:T(128)}, f32[4,128,128]{2,1,0:T(8,128)S(1)}, f32[8,4,64,128]{3,2,1,0:T(8,128)}, f32[8,4,128,128]{3,2,1,0:T(8,128)}, f32[8,1,64,1]{2,3,1,0:T(...) while((s32[]{:T(128)}, f32[4,128,128]{2,1,0:T(8,128)S(1)}, ...), condition=%wide.region_5.7_spmd.clone, body=%wide.region_4.6_spmd.clone.sunk | while | flops 176717824 | bytes 3283676 | solution.py:84
  430.9 5.4 multiply_convert_fusion.4
  436.3 5.0 fusion.185
  442.2 4.8 all_gather.64
  447.0 71.4 %reduce-scatter.16.cloned.1.call-done = f32[128,2048]{1,0:T(8,128)} async-done(((f32[512,2048]{1,0:T(8,128)}), f32[128,2048]{1,0:T(8,128)}) %reduce-scatter.16.cloned.1.call-update) | async-done | bytes 1048592 | tf_op jit(solution)/shard_map/reduce_scatter | solution.py:149
  522.9 72.1 %all-gather.27.cloned.1.call-done = bf16[2048,1408]{1,0:T(8,128)(2,1)} async-done(((bf16[1024,1408]{1,0:T(8,128)(2,1)}), bf16[2048,1408]{1,0:T(8,128)(2,1)}) %all-gather.27.cloned.1.call-update) | async-done | bytes 5767184 | tf_op jit(solution)/shard_map/all_gather | solution.py:167
  595.0 48.2 %all-gather.25.cloned.1.call-done = bf16[512,2048]{1,0:T(8,128)(2,1)} async-done(((bf16[128,2048]{1,0:T(8,128)(2,1)}), bf16[512,2048]{1,0:T(8,128)(2,1)}) %all-gather.25.cloned.1.call-update) | async-done | bytes 2097168 | tf_op jit(solution)/shard_map/all_gather | solution.py:145
  643.2 8.2 fusion.186
  651.4 66.4 %all-gather.29.cloned.1.call-done = bf16[2048,1408]{1,0:T(8,128)(2,1)} async-done(((bf16[1024,1408]{1,0:T(8,128)(2,1)}), bf16[2048,1408]{1,0:T(8,128)(2,1)}) %all-gather.29.cloned.1.call-update) | async-done | bytes 5767184 | tf_op jit(solution)/shard_map/all_gather | solution.py:168
  717.9 8.3 fusion.187
  726.2 39.3 %all-gather.33.cloned.1.call-done = bf16[512,2048]{1,0:T(8,128)(2,1)} async-done(((bf16[128,2048]{1,0:T(8,128)(2,1)}), bf16[512,2048]{1,0:T(8,128)(2,1)}) %all-gather.33.cloned.1.call-update) | async-done | bytes 2097168 | tf_op jit(solution)/shard_map/all_gather | solution.py:145
  765.5 74.7 %all-gather.31.cloned.1.call-done = bf16[1408,2048]{1,0:T(8,128)(2,1)} async-done(((bf16[1408,1024]{1,0:T(8,128)(2,1)}), bf16[1408,2048]{1,0:T(8,128)(2,1)}) %all-gather.31.cloned.1.call-update) | async-done | bytes 5767184 | tf_op jit(solution)/shard_map/all_gather | solution.py:169
  840.2 10.4 multiply_convert_fusion
  850.6 6.6 fusion.189
  857.2 5.0 convolution_add_fusion.3
  862.3 76.9 %reduce-scatter.20.cloned.1.call-done = f32[128,2048]{1,0:T(8,128)} async-done(((f32[512,2048]{1,0:T(8,128)}), f32[128,2048]{1,0:T(8,128)}) %reduce-scatter.20.cloned.1.call-update) | async-done | bytes 1048592 | tf_op jit(solution)/shard_map/reduce_scatter | solution.py:149
  942.3 7.9 convolution_convert_fusion.2
  950.3 8.1 convolution_convert_fusion.1
  963.3 7.7 convolution_convert_fusion
  971.1 17.5 %all-gather.35.cloned.1.call-done = bf16[512,2048]{1,0:T(8,128)(2,1)} async-done(((bf16[128,2048]{1,0:T(8,128)(2,1)}), bf16[512,2048]{1,0:T(8,128)(2,1)}) %all-gather.35.cloned.1.call-update) | async-done | bytes 2097168 | tf_op jit(solution)/shard_map/all_gather | solution.py:145
  988.7 5.7 fusion.117
  997.0 3.7 multiply_reduce_fusion.1
  1007.6 126.0 %while.49 = (s32[]{:T(128)}, f32[4,128,128]{2,1,0:T(8,128)S(1)}, f32[8,4,64,128]{3,2,1,0:T(8,128)}, f32[8,4,64,128]{3,2,1,0:T(8,128)}, f32[8,4,64,64]{3,2,1,0:T(...) while((s32[]{:T(128)}, f32[4,128,128]{2,1,0:T(8,128)S(1)}, ...), condition=%wide.region_14.16_spmd.clone, body=%wide.region_13.15_spmd.clone.sunk | while | flops 352911360 | bytes 4731118 | solution.py:84
  1133.7 3.4 fusion.192
  1172.7 3.7 multiply_multiply_fusion
  1195.9 3.7 convolution_convert_fusion.4
  1200.6 4.2 convolution_convert_fusion.3
  1218.3 7.5 fusion.188
  1236.4 21.0 %reduce-scatter.24.cloned.1.call-done = bf16[256,512]{1,0:T(8,128)(2,1)} async-done(((bf16[2048,512]{1,0:T(8,128)(2,1)}), bf16[256,512]{1,0:T(8,128)(2,1)}) %reduce-scatter.24.cloned.1.call-update) | async-done | bytes 262160 | tf_op jit(solution)/shard_map/reduce_scatter | solution.py:305
  1259.2 43.0 %reduce-scatter.26.cloned.1.call-done = bf16[256,512]{1,0:T(8,128)(2,1)} async-done(((bf16[2048,512]{1,0:T(8,128)(2,1)}), bf16[256,512]{1,0:T(8,128)(2,1)}) %reduce-scatter.26.cloned.1.call-update) | async-done | bytes 262160 | tf_op jit(solution)/shard_map/reduce_scatter | solution.py:308
  1304.0 42.7 %reduce-scatter.28.cloned.1.call-done = bf16[256,512]{1,0:T(8,128)(2,1)} async-done(((bf16[2048,512]{1,0:T(8,128)(2,1)}), bf16[256,512]{1,0:T(8,128)(2,1)}) %reduce-scatter.28.cloned.1.call-update) | async-done | bytes 262160 | tf_op jit(solution)/shard_map/reduce_scatter | solution.py:311
  1348.5 43.1 %reduce-scatter.30.cloned.1.call-done = bf16[256,512]{1,0:T(8,128)(2,1)} async-done(((bf16[2048,512]{1,0:T(8,128)(2,1)}), bf16[256,512]{1,0:T(8,128)(2,1)}) %reduce-scatter.30.cloned.1.call-update) | async-done | bytes 262160 | tf_op jit(solution)/shard_map/reduce_scatter | solution.py:314
  1393.4 42.8 %reduce-scatter.32.cloned.1.call-done = bf16[512,256]{1,0:T(8,128)(2,1)} async-done(((bf16[512,2048]{1,0:T(8,128)(2,1)}), bf16[512,256]{1,0:T(8,128)(2,1)}) %reduce-scatter.32.cloned.1.call-update) | async-done | bytes 262160 | tf_op jit(solution)/shard_map/reduce_scatter | solution.py:320
  1438.0 77.3 %reduce-scatter.22.cloned.1.call-done = f32[128,2048]{1,0:T(8,128)} async-done(((f32[512,2048]{1,0:T(8,128)}), f32[128,2048]{1,0:T(8,128)}) %reduce-scatter.22.cloned.1.call-update) | async-done | bytes 1048592 | tf_op jit(solution)/shard_map/reduce_scatter | solution.py:149
  1516.7 18.8 %all-reduce.36 = (bf16[2048]{0:T(1024)(128)(2,1)S(1)}, f32[128]{0:T(128)S(1)}, bf16[2048]{0:T(1024)(128)(2,1)S(1)}) all-reduce(f32[2048]{0:T(1024)S(1)} %get-tuple-element.717, f32[128]{0:T(128)S(1)} %copy-done.107, f32[2048]{0:T(1024)S(1)} %get-tuple-element.701), channel_id=1, replica_groups=mesh['dp'=4,'fsdp'=2,'tensor'=4] {'tensor'}, use_global_device_ids=true, to_apply=%region_23.26 | all-reduce | flops 4224 | bytes 25600 | tf_op jit(solution)/shard_map/psum | solution.py:297
  1535.6 14.6 all-reduce.37
  1550.2 24.6 %all-reduce.35 = (f32[4,512]{1,0:T(4,128)}, f32[4,512]{1,0:T(4,128)}, f32[4,512]{1,0:T(4,128)}, f32[128]{0:T(128)}) all-reduce(f32[4,512]{1,0:T(4,128)S(1)} %pad_add_fusion.2, f32[4,512]{1,0:T(4,128)S(1)} %pad_add_fusion.1, f32[4,512]{1,0:T(4,128)S(1)} %pad_add_fusion, ...), channel_id=1, replica_groups=mesh['dp'=4,'fsdp'=2,'tensor'=4] {'dp','fsdp'}, use_global_device_ids=true, to_apply=%region_34.37 | all-reduce | flops 6272 | bytes 50176 | tf_op jit(solution)/shard_map/psum | solution.py:298
  1576.1 19.3 %reduce-scatter.18.cloned.1.call-done = f32[128,2048]{1,0:T(8,128)} async-done(((f32[512,2048]{1,0:T(8,128)}), f32[128,2048]{1,0:T(8,128)}) %reduce-scatter.18.cloned.1.call-update) | async-done | bytes 1048592 | tf_op jit(solution)/shard_map/reduce_scatter | solution.py:149
  (580 shorter events, 362.0 us)
Async XLA Ops:
  7.2 38.4 %all-gather.19.cloned.1.call-start = ((), (), s32[]{:S(2)}) async-start(), calls=%async_computation.16 | async-start | bytes 3145728 | tf_op jit(solution)/shard_map/all_gather | solution.py:155
  7.9 85.8 %all-gather.13.cloned.1.call-start = ((), (), s32[]{:S(2)}) async-start(), calls=%async_computation.13 | async-start | bytes 2621440 | tf_op jit(solution)/shard_map/all_gather | solution.py:145
  16.8 110.4 %all-gather.17.cloned.1.call-start = ((), (), s32[]{:S(2)}) async-start(), calls=%async_computation.15 | async-start | bytes 3145728 | tf_op jit(solution)/shard_map/all_gather | solution.py:157
  17.5 144.2 %all-gather.15.cloned.1.call-start = ((), (), s32[]{:S(2)}) async-start(), calls=%async_computation.14 | async-start | bytes 3145728 | tf_op jit(solution)/shard_map/all_gather | solution.py:156
  18.1 412.2 %all-gather.21.cloned.1.call-start = ((), (), s32[]{:S(2)}) async-start(), calls=%async_computation.17 | async-start | bytes 3145728 | tf_op jit(solution)/shard_map/all_gather | solution.py:158
  18.7 417.6 %all-gather.23.cloned.1.call-start = ((), (), s32[]{:S(2)}) async-start(), calls=%async_computation.18 | async-start | bytes 3145728 | tf_op jit(solution)/shard_map/all_gather | solution.py:160
  19.3 499.0 %reduce-scatter.16.cloned.1.call-start = ((), (), s32[]{:S(2)}) async-start(), calls=%async_computation.19 | async-start | bytes 5242880 | tf_op jit(solution)/shard_map/reduce_scatter | solution.py:149
  20.7 410.2 %copy-start.69 = (f32[512]{0:T(512)}, f32[512]{0:T(512)S(1)}, u32[]{:S(2)}) copy-start(f32[512]{0:T(512)S(1)} %fusion.165) | copy-start | bytes 6148
  20.8 410.1 %copy-start.105 = (f32[512]{0:T(512)}, f32[512]{0:T(512)S(1)}, u32[]{:S(2)}) copy-start(f32[512]{0:T(512)S(1)} %broadcast_bitcast_fusion) | copy-start | bytes 6148
  21.5 108.6 %copy-start.67 = (f32[1,512]{1,0:T(1,128)}, f32[1,512]{1,0:T(1,128)S(1)}, u32[]{:S(2)}) copy-start(f32[1,512]{1,0:T(1,128)S(1)} %get-tuple-element.853) | copy-start | bytes 6148
  21.5 108.6 %copy-start.74 = (f32[1,512]{1,0:T(1,128)}, f32[1,512]{1,0:T(1,128)S(1)}, u32[]{:S(2)}) copy-start(f32[1,512]{1,0:T(1,128)S(1)} %get-tuple-element.850) | copy-start | bytes 6148
  21.5 108.6 %copy-start.76 = (f32[1,512]{1,0:T(1,128)}, f32[1,512]{1,0:T(1,128)S(1)}, u32[]{:S(2)}) copy-start(f32[1,512]{1,0:T(1,128)S(1)} %get-tuple-element.851) | copy-start | bytes 6148
  21.5 108.6 %copy-start.78 = (f32[1,512]{1,0:T(1,128)}, f32[1,512]{1,0:T(1,128)S(1)}, u32[]{:S(2)}) copy-start(f32[1,512]{1,0:T(1,128)S(1)} %get-tuple-element.852) | copy-start | bytes 6148
  21.5 108.6 %copy-start.65 = (f32[1,512]{1,0:T(1,128)}, f32[1,512]{1,0:T(1,128)S(1)}, u32[]{:S(2)}) copy-start(f32[1,512]{1,0:T(1,128)S(1)} %get-tuple-element.859) | copy-start | bytes 6148
  21.6 143.6 %copy-start.72 = (f32[1,512]{1,0:T(1,128)}, f32[1,512]{1,0:T(1,128)S(1)}, u32[]{:S(2)}) copy-start(f32[1,512]{1,0:T(1,128)S(1)} %get-tuple-element.863) | copy-start | bytes 6148
  21.6 143.6 %copy-start.86 = (f32[1,512]{1,0:T(1,128)}, f32[1,512]{1,0:T(1,128)S(1)}, u32[]{:S(2)}) copy-start(f32[1,512]{1,0:T(1,128)S(1)} %get-tuple-element.860) | copy-start | bytes 6148
  21.6 143.6 %copy-start.88 = (f32[1,512]{1,0:T(1,128)}, f32[1,512]{1,0:T(1,128)S(1)}, u32[]{:S(2)}) copy-start(f32[1,512]{1,0:T(1,128)S(1)} %get-tuple-element.861) | copy-start | bytes 6148
  21.6 143.6 %copy-start.90 = (f32[1,512]{1,0:T(1,128)}, f32[1,512]{1,0:T(1,128)S(1)}, u32[]{:S(2)}) copy-start(f32[1,512]{1,0:T(1,128)S(1)} %get-tuple-element.862) | copy-start | bytes 6148
  26.2 144.7 %copy-start.61 = (bf16[2048,4]{0,1:T(4,128)(2,1)}, bf16[2048,4]{0,1:T(4,128)(2,1)S(1)}, u32[]{:S(2)}) copy-start(bf16[2048,4]{0,1:T(4,128)(2,1)S(1)} %all_gather.59) | copy-start | bytes 49156
  26.4 153.3 %copy-start.50 = (f32[8,64,64]{2,1,0:T(8,128)}, f32[8,64,64]{2,1,0:T(8,128)S(1)}, u32[]{:S(2)}) copy-start(f32[8,64,64]{2,1,0:T(8,128)S(1)} %get-tuple-element.849) | copy-start | bytes 393220
  26.4 323.8 %copy-start.42 = (f32[8,64,64]{2,1,0:T(8,128)}, f32[8,64,64]{2,1,0:T(8,128)S(1)}, u32[]{:S(2)}) copy-start(f32[8,64,64]{2,1,0:T(8,128)S(1)} %get-tuple-element.848) | copy-start | bytes 393220
  441.4 153.6 %all-gather.27.cloned.1.call-start = ((), (), s32[]{:S(2)}) async-start(), calls=%async_computation.21 | async-start | bytes 8650752 | tf_op jit(solution)/shard_map/all_gather | solution.py:167
  442.1 201.1 %all-gather.25.cloned.1.call-start = ((), (), s32[]{:S(2)}) async-start(), calls=%async_computation.20 | async-start | bytes 2621440 | tf_op jit(solution)/shard_map/all_gather | solution.py:145
  519.9 420.9 %copy-start.96 = (f32[128]{0:T(128)}, f32[128]{0:T(128)S(1)}, u32[]{:S(2)}) copy-start(f32[128]{0:T(128)S(1)} %add_rsqrt_fusion.2) | copy-start | bytes 1540
  520.9 196.9 %all-gather.29.cloned.1.call-start = ((), (), s32[]{:S(2)}) async-start(), calls=%async_computation.22 | async-start | bytes 8650752 | tf_op jit(solution)/shard_map/all_gather | solution.py:168
  521.5 244.0 %all-gather.33.cloned.1.call-start = ((), (), s32[]{:S(2)}) async-start(), calls=%async_computation.25 | async-start | bytes 2621440 | tf_op jit(solution)/shard_map/all_gather | solution.py:145
  522.2 317.9 %all-gather.31.cloned.1.call-start = ((), (), s32[]{:S(2)}) async-start(), calls=%async_computation.23 | async-start | bytes 8650752 | tf_op jit(solution)/shard_map/all_gather | solution.py:169
  522.8 416.4 %reduce-scatter.20.cloned.1.call-start = ((), (), s32[]{:S(2)}) async-start(), calls=%async_computation.26 | async-start | bytes 5242880 | tf_op jit(solution)/shard_map/reduce_scatter | solution.py:149
  862.3 126.4 %all-gather.35.cloned.1.call-start = ((), (), s32[]{:S(2)}) async-start(), calls=%async_computation.27 | async-start | bytes 2621440 | tf_op jit(solution)/shard_map/all_gather | solution.py:145
  942.1 285.7 %reduce-scatter.34.cloned.1.call-start = ((), (), s32[]{:S(2)}) async-start(), calls=%async_computation.34 | async-start | bytes 6488064 | tf_op jit(solution)/shard_map/reduce_scatter | solution.py:326
  950.2 279.9 %reduce-scatter.36.cloned.1.call-start = ((), (), s32[]{:S(2)}) async-start(), calls=%async_computation.35 | async-start | bytes 6488064 | tf_op jit(solution)/shard_map/reduce_scatter | solution.py:329
  958.4 274.0 %reduce-scatter.38.cloned.1.call-start = ((), (), s32[]{:S(2)}) async-start(), calls=%async_computation.36 | async-start | bytes 6488064 | tf_op jit(solution)/shard_map/reduce_scatter | solution.py:332
  971.1 263.7 %reduce-scatter.40.cloned.1.call-start = ((), (), s32[]{:S(2)}) async-start(), calls=%async_computation.37 | async-start | bytes 589824
  1164.3 93.1 %reduce-scatter.24.cloned.1.call-start = ((), (), s32[]{:S(2)}) async-start(), calls=%async_computation.29 | async-start | bytes 2359296 | tf_op jit(solution)/shard_map/reduce_scatter | solution.py:305
  1180.8 121.4 %reduce-scatter.26.cloned.1.call-start = ((), (), s32[]{:S(2)}) async-start(), calls=%async_computation.30 | async-start | bytes 2359296 | tf_op jit(solution)/shard_map/reduce_scatter | solution.py:308
  1187.4 159.3 %reduce-scatter.28.cloned.1.call-start = ((), (), s32[]{:S(2)}) async-start(), calls=%async_computation.31 | async-start | bytes 2359296 | tf_op jit(solution)/shard_map/reduce_scatter | solution.py:311
  1194.3 197.3 %reduce-scatter.30.cloned.1.call-start = ((), (), s32[]{:S(2)}) async-start(), calls=%async_computation.32 | async-start | bytes 2359296 | tf_op jit(solution)/shard_map/reduce_scatter | solution.py:314
  1199.6 236.6 %reduce-scatter.32.cloned.1.call-start = ((), (), s32[]{:S(2)}) async-start(), calls=%async_computation.33 | async-start | bytes 2359296 | tf_op jit(solution)/shard_map/reduce_scatter | solution.py:320
  1204.8 310.4 %reduce-scatter.22.cloned.1.call-start = ((), (), s32[]{:S(2)}) async-start(), calls=%async_computation.28 | async-start | bytes 5242880 | tf_op jit(solution)/shard_map/reduce_scatter | solution.py:149
  1217.0 378.5 %reduce-scatter.18.cloned.1.call-start = ((), (), s32[]{:S(2)}) async-start(), calls=%async_computation.24 | async-start | bytes 5242880 | tf_op jit(solution)/shard_map/reduce_scatter | solution.py:149
  1234.7 280.5 %copy-start.4 = (bf16[128,2048]{1,0:T(8,128)(2,1)S(1)}, bf16[128,2048]{1,0:T(8,128)(2,1)}, u32[]{:S(2)}) copy-start(bf16[128,2048]{1,0:T(8,128)(2,1)} %param.29) | copy-start | bytes 1572868
  1234.7 280.5 %copy-start.64 = (f32[2048]{0:T(1024)S(1)}, f32[2048]{0:T(1024)}, u32[]{:S(2)}) copy-start(f32[2048]{0:T(1024)} %copy-done.63) | copy-start | bytes 24580
  1234.7 280.5 %copy-start.99 = (f32[128]{0:T(128)S(1)}, f32[128]{0:T(128)}, u32[]{:S(2)}) copy-start(f32[128]{0:T(128)} %copy-done.98) | copy-start | bytes 1540
  1304.0 212.8 %copy-start.107 = (f32[128]{0:T(128)S(1)}, f32[128]{0:T(128)}, u32[]{:S(2)}) copy-start(f32[128]{0:T(128)} %get-tuple-element.703) | copy-start | bytes 1540
  1304.0 291.5 %copy-start.9 = (f32[128,2048]{1,0:T(8,128)S(1)}, f32[128,2048]{1,0:T(8,128)}, u32[]{:S(2)}) copy-start(f32[128,2048]{1,0:T(8,128)} %reduce-scatter.20.cloned.1.call-done) | copy-start | bytes 3145732
  1304.0 291.5 %copy-start.24 = (bf16[128,2048]{1,0:T(8,128)(2,1)S(1)}, bf16[128,2048]{1,0:T(8,128)(2,1)}, u32[]{:S(2)}) copy-start(bf16[128,2048]{1,0:T(8,128)(2,1)} %param.47) | copy-start | bytes 1572868
  1304.0 291.5 %copy-start.97 = (f32[128]{0:T(128)S(1)}, f32[128]{0:T(128)}, u32[]{:S(2)}) copy-start(f32[128]{0:T(128)} %copy-done.96) | copy-start | bytes 1540
  1304.0 291.5 %copy-start.103 = (f32[128]{0:T(128)S(1)}, f32[128]{0:T(128)}, u32[]{:S(2)}) copy-start(f32[128]{0:T(128)} %copy-done.102) | copy-start | bytes 1540
  (94 other events, 629.4 us)
Sparse Core Ops, SparseCore 0:
  9.6 35.9 all-gather.18
  47.7 45.9 all-gather.12
  95.3 31.8 all-gather.16
  128.6 33.1 all-gather.14
  163.1 33.1 all-gather.20
  197.7 33.2 all-gather.22
  441.5 76.8 reduce-scatter.15
  520.0 74.9 all-gather.26
  597.2 45.9 all-gather.24
  644.6 73.1 all-gather.28
  719.5 45.9 all-gather.32
  767.0 73.1 all-gather.30
  862.4 76.7 reduce-scatter.19
  942.2 46.4 all-gather.34
  992.0 57.7 reduce-scatter.33
  1053.4 59.0 reduce-scatter.35
  1115.8 59.0 reduce-scatter.37
  1178.7 34.0 reduce-scatter.39
  1216.1 41.2 reduce-scatter.23
  1260.9 41.2 reduce-scatter.25
  1305.5 41.2 reduce-scatter.27
  1350.4 41.2 reduce-scatter.29
  1394.9 41.2 reduce-scatter.31
  1438.4 76.7 reduce-scatter.21
  1517.5 77.8 reduce-scatter.17
where the time goes:
time: 1620 us; the launch traced here: 1610 us
  waiting for transfers between devices  883 us (55%)
  matrix products  329 us (20%)
  other arithmetic  228 us (14%)
  local copies, waits for them, and re-layouts  73.6 us (5%)
  blocking collectives  72.9 us (5%)
  between operations  17.5 us (1%)
    reduce_scatter x4, waiting for transfers between devices, scatter_rows(): lax.psum_scatter(partial_rows, 'tensor', scatter_dimension=0, tiled=True)  245 us
    another operation x5, other arithmetic, delta_rule(): jax.scipy.linalg.solve_triangular(system, scaled_values, lower=True, unit...  160 us
    all_gather x4, waiting for transfers between devices, gather_rows(): return lax.all_gather(rows, 'tensor', axis=0, tiled=True)  153 us
    all_gather x1, waiting for transfers between devices, fetch_ffn(): lax.all_gather(w_down, 'fsdp', axis=1, tiled=True)  74.7 us
    all_gather x1, waiting for transfers between devices, fetch_ffn(): lax.all_gather(w_gate, 'fsdp', axis=0, tiled=True)  72.1 us
    all_gather x1, waiting for transfers between devices, fetch_ffn(): lax.all_gather(w_up, 'fsdp', axis=0, tiled=True)  66.4 us
    dot_general x24, matrix products, advance(): jnp.einsum('hvk,htk->htv', memory, query_n, precision=lax.Precision.HIGHEST)  52.5 us
    dot_general x9, matrix products, matmul(): return jnp.dot(left, right, preferred_element_type=jnp.float32)  47.9 us
  transfers between devices with their start and end apart: 25, of which 19 were waited for; matrix products, arithmetic and copies ran while one was open for 36% of the time, Pallas kernels for 0%

commit v1 on v0

v1 whole, which is shorter than its diff:
```python
import jax, jax.numpy as jnp
from jax import lax
from jax.experimental import pallas as pl
from jax.experimental.pallas import tpu as pltpu
from jax.sharding import PartitionSpec as P

KERNEL = 4
CHUNK = 256
G, Q, K, V = range(4)
F32 = jnp.float32
BF16 = jnp.bfloat16


def dot(left, right):
    return jnp.dot(left, right, preferred_element_type=F32)


def dot_nt(left, right):
    return lax.dot_general(left, right, (((1,), (1,)), ((), ())), preferred_element_type=F32)


def dot_tn(left, right):
    return lax.dot_general(left, right, (((0,), (0,)), ((), ())), preferred_element_type=F32)


def lane_sum(values):
    return jnp.sum(values, axis=-1, keepdims=True)


def document_of(starts_ref, positions):
    total = jnp.zeros_like(positions)
    for entry in range(starts_ref.shape[1]):
        total = total + (positions >= starts_ref[0, entry]).astype(jnp.int32)
    return total


def fill_masks(starts_ref, length_ref, keep_ref, live_ref, carry_ref):
    rows, lanes = live_ref.shape
    place = lax.broadcasted_iota(jnp.int32, (rows, lanes), 0)
    docs = document_of(starts_ref, place)
    for delay in range(1, KERNEL):
        prior = document_of(starts_ref, place - delay)
        keep_ref[delay - 1] = jnp.where((prior == docs) & (place >= delay), 1.0, 0.0)
    live_ref[...] = jnp.where(place < length_ref[0], 1.0, 0.0)
    for edge in range(rows // CHUNK - 1):
        seam = jnp.int32((edge + 1) * CHUNK - 1)
        carry_ref[edge] = jnp.where(docs == document_of(starts_ref, seam), 1.0, 0.0)


def pair_mask(starts_ref, chunk):
    row = lax.broadcasted_iota(jnp.int32, (CHUNK, CHUNK), 0)
    col = lax.broadcasted_iota(jnp.int32, (CHUNK, CHUNK), 1)
    first = chunk * CHUNK
    same = document_of(starts_ref, row + first) == document_of(starts_ref, col + first)
    return same & (row > col), same & (row >= col)


def convolve(raw, taps, keep_ref):
    parts = [raw]
    for delay in range(1, KERNEL):
        parts.append(pltpu.roll(raw, delay, 0) * keep_ref[delay - 1])
    total = parts[0] * taps[KERNEL - 1 : KERNEL]
    for delay in range(1, KERNEL):
        total = total + parts[delay] * taps[KERNEL - 1 - delay : KERNEL - delay]
    return total, parts


def sigmoid(values):
    return 0.5 * jnp.tanh(0.5 * values) + 0.5


def column(values, index):
    lane = lax.broadcasted_iota(jnp.int32, values.shape, 1)
    return lane_sum(jnp.where(lane == index, values, 0.0))


def invert(system):
    size = system[0].shape[0]
    row = lax.broadcasted_iota(jnp.int32, (size, size), 0)
    col = lax.broadcasted_iota(jnp.int32, (size, size), 1)
    apart = row ^ col
    eye = jnp.where(row == col, 1.0, 0.0)
    low = [matrix.astype(BF16) for matrix in system]
    solved = [eye - jnp.where(apart == 1, matrix, 0.0) for matrix in system]
    step = 2
    while step < size:
        level = (apart >= step) & (apart < 2 * step)
        for index, matrix in enumerate(low):
            part = jnp.where(level, matrix, 0.0)
            held = solved[index].astype(BF16)
            solved[index] = solved[index] - dot(dot(held, part).astype(BF16), held)
        step *= 2
    refined = []
    for matrix, high, inverse in zip(system, low, solved):
        rest = (matrix - high.astype(F32)).astype(BF16)
        head = inverse.astype(BF16)
        tail = (inverse - head.astype(F32)).astype(BF16)
        product = dot(high, head) + dot(rest, head) + dot(high, tail)
        residue = eye - inverse - product
        refined.append(inverse + dot(head, residue.astype(BF16)))
    return refined


def unit_rows(conv):
    gate = sigmoid(conv)
    act = conv * gate
    scale = lax.rsqrt(lane_sum(act * act) + 1e-06)
    return gate, act, scale


def forward_kernel(
    starts_ref, length_ref, raw_ref, conv_q_ref, conv_k_ref, conv_v_ref, gain_ref,
    gated_ref, mixed_ref, solve_ref, update_ref, state_ref,
    keep_ref, live_ref, carry_ref, strict_ref, incl_ref,
):
    rows, head_width = live_ref.shape
    width = gated_ref.shape[1]
    chunks = rows // CHUNK
    fill_masks(starts_ref, length_ref, keep_ref, live_ref, carry_ref)
    for chunk in range(chunks):
        strict, incl = pair_mask(starts_ref, chunk)
        strict_ref[chunk] = jnp.where(strict, 1.0, 0.0)
        incl_ref[chunk] = jnp.where(incl, 1.0, 0.0)

    @pl.loop(0, width // head_width)
    def _(head):
        start = pl.multiple_of(head * head_width, head_width)

        def stream(index):
            return raw_ref[:, pl.ds(pl.multiple_of(index * width + start, head_width), head_width)]

        cols = pl.ds(start, head_width)
        conv, _ = convolve(stream(Q), conv_q_ref[:, cols], keep_ref)
        _, act, scale = unit_rows(conv)
        query = (act * scale).astype(BF16)
        conv, _ = convolve(stream(K), conv_k_ref[:, cols], keep_ref)
        _, act, scale = unit_rows(conv)
        keyed = act * scale
        key_low = keyed.astype(BF16)
        conv, _ = convolve(stream(V), conv_v_ref[:, cols], keep_ref)
        valued = conv * sigmoid(conv)
        rate = sigmoid(column(raw_ref[:, 4 * width :], head)) * live_ref[...]
        scaled_value = (valued * rate).astype(BF16)
        scaled_key = keyed * rate
        system = []
        for chunk in range(chunks):
            span = slice(chunk * CHUNK, (chunk + 1) * CHUNK)
            pair = dot_nt(key_low[span], key_low[span])
            wide = jnp.concatenate([rate[span]] * (CHUNK // head_width), axis=1)
            system.append(pair * wide * strict_ref[chunk])
        memory = None
        for chunk, solved in enumerate(invert(system)):
            span = slice(chunk * CHUNK, (chunk + 1) * CHUNK)
            solve_low = solved.astype(BF16)
            solve_ref[head * chunks + chunk] = solve_low
            score = dot_nt(query[span], key_low[span]) * incl_ref[chunk]
            if chunk == 0:
                update = dot(solve_low, scaled_value[span])
                update_low = update.astype(BF16)
                mixed = dot(score.astype(BF16), update_low)
            else:
                carry = carry_ref[chunk - 1][span]
                right = jnp.concatenate(
                    [scaled_value[span], (scaled_key[span] * carry).astype(BF16)], axis=1
                )
                both = dot(solve_low, right)
                memory_low = memory.astype(BF16)
                state_ref[head * (chunks - 1) + chunk - 1] = memory_low
                update = both[:, :head_width] - dot(both[:, head_width:].astype(BF16), memory_low)
                update_low = update.astype(BF16)
                mixed = carry * dot(query[span], memory_low) + dot(score.astype(BF16), update_low)
            update_ref[span, cols] = update_low
            mixed_ref[span, cols] = mixed
            if chunk + 1 < chunks:
                last = (keyed[span] * carry_ref[chunk][span]).astype(BF16)
                fresh = dot_tn(last, update_low)
                if memory is None:
                    memory = fresh
                else:
                    memory = memory * carry_ref[chunk - 1][span][CHUNK - 1 :] + fresh
        mixed = mixed_ref[:, cols]
        norm = lax.rsqrt(lane_sum(mixed * mixed) * (1.0 / head_width) + 1e-05)
        gating = stream(G)
        gated = mixed * norm * gain_ref[...] * (gating * sigmoid(gating)) * live_ref[...]
        gated_ref[:, cols] = gated.astype(BF16)


def delta_forward(starts, length, raw, conv_q, conv_k, conv_v, gain):
    rows = raw.shape[0]
    head_width = gain.shape[-1]
    width = conv_q.shape[1]
    heads, chunks = width // head_width, rows // CHUNK
    vmem = pl.BlockSpec(memory_space=pltpu.VMEM)
    smem = pl.BlockSpec(memory_space=pltpu.SMEM)
    return pl.pallas_call(
        forward_kernel,
        out_shape=(
            jax.ShapeDtypeStruct((rows, width), BF16),
            jax.ShapeDtypeStruct((rows, width), F32),
            jax.ShapeDtypeStruct((heads * chunks, CHUNK, CHUNK), BF16),
            jax.ShapeDtypeStruct((rows, width), BF16),
            jax.ShapeDtypeStruct((heads * (chunks - 1), head_width, head_width), BF16),
        ),
        in_specs=[smem, smem] + [vmem] * 5,
        out_specs=[vmem] * 5,
        scratch_shapes=[
            pltpu.VMEM((KERNEL - 1, rows, head_width), F32),
            pltpu.VMEM((rows, head_width), F32),
            pltpu.VMEM((chunks - 1, rows, head_width), F32),
            pltpu.VMEM((chunks, CHUNK, CHUNK), F32),
            pltpu.VMEM((chunks, CHUNK, CHUNK), F32),
        ],
        compiler_params=pltpu.CompilerParams(vmem_limit_bytes=40 * 1024 * 1024),
        cost_estimate=pl.CostEstimate(
            flops=2 * 24 * heads * chunks * CHUNK**3, bytes_accessed=12 * 2**20, transcendentals=0
        ),
        name="delta_forward",
    )(starts, length, raw, conv_q, conv_k, conv_v, gain)


def backward_kernel(
    starts_ref, length_ref, raw_ref, conv_q_ref, conv_k_ref, conv_v_ref, gain_ref,
    mixed_ref, solve_ref, update_ref, state_ref, grad_ref,
    d_raw_ref, d_conv_ref, d_gain_ref,
    keep_ref, live_ref, carry_ref, strict_ref, incl_ref, d_query_ref, d_key_ref, d_value_ref, d_rate_ref,
):
    rows, head_width = live_ref.shape
    width = mixed_ref.shape[1]
    chunks = rows // CHUNK
    fill_masks(starts_ref, length_ref, keep_ref, live_ref, carry_ref)
    for chunk in range(chunks):
        strict, incl = pair_mask(starts_ref, chunk)
        strict_ref[chunk] = jnp.where(strict, 1.0, 0.0)
        incl_ref[chunk] = jnp.where(incl, 1.0, 0.0)
    d_gain_ref[...] = jnp.zeros_like(d_gain_ref)
    d_raw_ref[:, 4 * width :] = jnp.zeros((rows, head_width), BF16)

    @pl.loop(0, width // head_width)
    def _(head):
        start = pl.multiple_of(head * head_width, head_width)

        def place(index):
            return pl.ds(pl.multiple_of(index * width + start, head_width), head_width)

        cols = pl.ds(start, head_width)
        live = live_ref[...]
        mixed = mixed_ref[:, cols]
        norm = lax.rsqrt(lane_sum(mixed * mixed) * (1.0 / head_width) + 1e-05)
        gating = raw_ref[:, place(G)]
        gate = sigmoid(gating)
        normal = mixed * norm
        grad = grad_ref[:, cols].astype(F32) * live
        grad_gain = grad * gain_ref[...]
        swish = gating * gate
        d_raw_ref[:, place(G)] = (grad_gain * normal * gate * (1.0 + gating - swish)).astype(BF16)
        d_gain_ref[...] += jnp.sum(grad * normal * swish, axis=0, keepdims=True)
        d_normal = grad_gain * swish
        d_mixed = norm * (d_normal - normal * (lane_sum(d_normal * normal) * (1.0 / head_width)))
        d_mixed_low = d_mixed.astype(BF16)

        conv_q, parts_q = convolve(raw_ref[:, place(Q)], conv_q_ref[:, cols], keep_ref)
        gate_q, act_q, scale_q = unit_rows(conv_q)
        unit_q = act_q * scale_q
        query = unit_q.astype(BF16)
        conv_k, parts_k = convolve(raw_ref[:, place(K)], conv_k_ref[:, cols], keep_ref)
        gate_k, act_k, scale_k = unit_rows(conv_k)
        keyed = act_k * scale_k
        key_low = keyed.astype(BF16)
        conv_v, parts_v = convolve(raw_ref[:, place(V)], conv_v_ref[:, cols], keep_ref)
        gate_v = sigmoid(conv_v)
        valued = conv_v * gate_v
        sig = sigmoid(column(raw_ref[:, 4 * width :], head))
        rate = sig * live
        scaled_value = (valued * rate).astype(BF16)
        scaled_key = keyed * rate

        d_memory = None
        for chunk in range(chunks - 1, -1, -1):
            span = slice(chunk * CHUNK, (chunk + 1) * CHUNK)
            key_c, query_c, d_mixed_c = key_low[span], query[span], d_mixed_low[span]
            solve = solve_ref[head * chunks + chunk]
            update = update_ref[span, cols]
            incl, strict = incl_ref[chunk], strict_ref[chunk]
            score = (dot_nt(query_c, key_c) * incl).astype(BF16)
            d_update = dot_tn(score, d_mixed_c)
            d_key = None
            if d_memory is not None:
                last = carry_ref[chunk][span]
                d_memory_low = d_memory.astype(BF16)
                d_update = d_update + dot((keyed[span] * last).astype(BF16), d_memory_low)
                d_key = last * dot_nt(update, d_memory_low)
            d_update_low = d_update.astype(BF16)
            d_score = (dot_nt(d_mixed_c, update) * incl).astype(BF16)
            d_query = dot(d_score, key_c)
            d_key_score = dot_tn(d_score, query_c)
            d_key = d_key_score if d_key is None else d_key + d_key_score
            if chunk == 0:
                right = scaled_value[span]
                solved = dot(solve, right)
                d_right = dot_tn(solve, d_update_low)
                d_value_in = d_right
                d_rate = lane_sum(d_value_in * valued[span])
            else:
                carry = carry_ref[chunk - 1][span]
                state = state_ref[head * (chunks - 1) + chunk - 1]
                right = jnp.concatenate([scaled_value[span], (scaled_key[span] * carry).astype(BF16)], axis=1)
                solved = dot(solve, right)
                d_solved_key = -dot_nt(d_update_low, state)
                d_right = dot_tn(solve, jnp.concatenate([d_update_low, d_solved_key.astype(BF16)], axis=1))
                d_value_in = d_right[:, :head_width]
                d_key_in = d_right[:, head_width:] * carry
                carried = (carry * d_mixed[span]).astype(BF16)
                d_query = d_query + dot_nt(carried, state)
                d_key = d_key + rate[span] * d_key_in
                d_rate = lane_sum(d_value_in * valued[span] + d_key_in * keyed[span])
                fresh = dot_tn(query_c, carried) - dot_tn(solved[:, head_width:].astype(BF16), d_update_low)
                if d_memory is None:
                    d_memory = fresh
                else:
                    d_memory = d_memory * carry[CHUNK - 1 :] + fresh
            d_system = dot_nt(d_right.astype(BF16), solved.astype(BF16)) * -strict
            pair = dot_nt(key_c, key_c)
            d_rate = d_rate + lane_sum(d_system * pair)
            wide = jnp.concatenate([rate[span]] * (CHUNK // head_width), axis=1)
            d_pair = (d_system * wide).astype(BF16)
            d_key = d_key + dot(d_pair, key_c) + dot_tn(d_pair, key_c)
            d_query_ref[span] = d_query
            d_key_ref[span] = d_key
            d_value_ref[span] = rate[span] * d_value_in
            d_rate_ref[span] = jnp.broadcast_to(d_rate, (CHUNK, head_width))

        lane = lax.broadcasted_iota(jnp.int32, (rows, head_width), 1)
        d_beta = d_rate_ref[...] * rate * (1.0 - sig)
        tail = d_raw_ref[:, 4 * width :]
        d_raw_ref[:, 4 * width :] = jnp.where(lane == head, d_beta.astype(BF16), tail)

        def conv_back(index, d_conv, parts, taps):
            sums = [jnp.sum(d_conv * part, axis=0, keepdims=True) for part in parts]
            for delay in range(KERNEL):
                tap = KERNEL - 1 - delay
                d_conv_ref[tap : tap + 1, place(index - 1)] = sums[delay]
            total = d_conv * taps[KERNEL - 1 : KERNEL]
            for delay in range(1, KERNEL):
                tap = KERNEL - 1 - delay
                back = pltpu.roll(d_conv * keep_ref[delay - 1], rows - delay, 0)
                total = total + back * taps[tap : tap + 1]
            d_raw_ref[:, place(index)] = total.astype(BF16)

        def unit_back(d_unit, unit, scale, conv, act, gate):
            d_act = scale * (d_unit - unit * lane_sum(d_unit * unit))
            return d_act * gate * (1.0 + conv - act)

        conv_back(Q, unit_back(d_query_ref[...], unit_q, scale_q, conv_q, act_q, gate_q), parts_q, conv_q_ref[:, cols])
        conv_back(K, unit_back(d_key_ref[...], keyed, scale_k, conv_k, act_k, gate_k), parts_k, conv_k_ref[:, cols])
        d_conv_v = d_value_ref[...] * gate_v * (1.0 + conv_v - valued)
        conv_back(V, d_conv_v, parts_v, conv_v_ref[:, cols])


def delta_backward(starts, length, raw, conv_q, conv_k, conv_v, gain, mixed, solve, update, state, grad):
    rows = raw.shape[0]
    head_width = gain.shape[-1]
    width = conv_q.shape[1]
    heads, chunks = width // head_width, rows // CHUNK
    vmem = pl.BlockSpec(memory_space=pltpu.VMEM)
    smem = pl.BlockSpec(memory_space=pltpu.SMEM)
    return pl.pallas_call(
        backward_kernel,
        out_shape=(
            jax.ShapeDtypeStruct((rows, 4 * width + head_width), BF16),
            jax.ShapeDtypeStruct((KERNEL, 3 * width), F32),
            jax.ShapeDtypeStruct((1, head_width), F32),
        ),
        in_specs=[smem, smem] + [vmem] * 10,
        out_specs=[vmem] * 3,
        scratch_shapes=[
            pltpu.VMEM((KERNEL - 1, rows, head_width), F32),
            pltpu.VMEM((rows, head_width), F32),
            pltpu.VMEM((chunks - 1, rows, head_width), F32),
            pltpu.VMEM((chunks, CHUNK, CHUNK), F32),
            pltpu.VMEM((chunks, CHUNK, CHUNK), F32),
        ]
        + [pltpu.VMEM((rows, head_width), F32)] * 4,
        compiler_params=pltpu.CompilerParams(vmem_limit_bytes=48 * 1024 * 1024),
        cost_estimate=pl.CostEstimate(
            flops=2 * 12 * heads * chunks * CHUNK**3, bytes_accessed=16 * 2**20, transcendentals=0
        ),
        name="delta_backward",
    )(starts, length, raw, conv_q, conv_k, conv_v, gain, mixed, solve, update, state, grad)


def rms_scale(values):
    return lax.rsqrt(jnp.mean(values * values, axis=-1, keepdims=True) + 1e-05)


def rms_back(values, scale_rows, gain, grad):
    scaled_grad = grad * gain
    inner = jnp.mean(scaled_grad * values, axis=-1, keepdims=True)
    return scale_rows * (scaled_grad - values * scale_rows * scale_rows * inner)


def shifted(count, shift):
    return [(index, (index + shift) % count) for index in range(count)]


def gather_rows(rows):
    count = lax.axis_size("tensor")
    mine = lax.axis_index("tensor")
    height = rows.shape[0]
    whole = jnp.zeros((count * height, rows.shape[1]), rows.dtype)
    whole = lax.dynamic_update_slice_in_dim(whole, rows, mine * height, 0)
    for shift in range(1, count):
        came = lax.ppermute(rows, "tensor", shifted(count, shift))
        source = lax.rem(mine + count - shift, count)
        whole = lax.dynamic_update_slice_in_dim(whole, came, source * height, 0)
    return whole


def scatter_rows(partial_rows):
    count = lax.axis_size("tensor")
    mine = lax.axis_index("tensor")
    height = partial_rows.shape[0] // count
    total = lax.dynamic_slice_in_dim(partial_rows, mine * height, height, 0).astype(F32)
    for shift in range(1, count):
        target = lax.rem(mine + shift, count)
        piece = lax.dynamic_slice_in_dim(partial_rows, target * height, height, 0)
        total = total + lax.ppermute(piece, "tensor", shifted(count, shift)).astype(F32)
    return total


def gather_weights(pieces):
    return lax.all_gather(jnp.concatenate(pieces, axis=1), ("fsdp", "dp"), axis=0, tiled=True)


def scatter_grads(grads):
    return lax.psum_scatter(grads, ("dp", "fsdp"), scatter_dimension=0, tiled=True).astype(F32)


def body(
    layer_input,
    first_gain,
    w_query,
    w_key,
    w_value,
    w_gating,
    w_beta,
    conv_query,
    conv_key,
    conv_value,
    head_gain,
    w_project,
    second_gain,
    w_gate,
    w_up,
    w_down,
    doc_starts,
    seq_lengths,
    output_grad,
):
    replicas = lax.axis_size("dp")
    replica = lax.axis_index("dp")
    width = w_query.shape[1]
    units = w_gate.shape[1]
    heads = w_beta.shape[1]
    head_width = head_gain.shape[0]

    def piece(weight, axis):
        size = weight.shape[axis] // replicas
        return lax.dynamic_slice_in_dim(weight, replica * size, size, axis)

    input_float = layer_input.astype(F32)
    conv_q = conv_query.astype(F32)
    conv_k = conv_key.astype(F32)
    conv_v = conv_value.astype(F32)
    gain_head = head_gain.astype(F32)[None, :]
    gains = lax.all_gather(jnp.stack([first_gain, second_gain]), "fsdp", axis=1, tiled=True).astype(F32)
    gain_one, gain_two = gains[0], gains[1]
    beta_piece = jnp.pad(piece(w_beta, 0), ((0, 0), (0, head_width - heads)))
    mix_full = gather_weights(
        [piece(w_gating, 0), piece(w_query, 0), piece(w_key, 0), piece(w_value, 0), beta_piece]
    )
    ffn_full = gather_weights(
        [piece(w_project, 1).T, piece(w_gate, 0), piece(w_up, 0), piece(w_down, 1).T]
    )
    project_t = ffn_full[:, :width]
    gate_up = ffn_full[:, width : width + 2 * units]
    down_t = ffn_full[:, width + 2 * units :]

    scale_one = rms_scale(input_float)
    normed1 = (input_float * scale_one * gain_one).astype(BF16)
    rows_one = gather_rows(normed1)
    raw = dot(rows_one, mix_full)
    gated, mixed, solve, update, state = delta_forward(
        doc_starts, seq_lengths, raw, conv_q, conv_k, conv_v, gain_head
    )
    attn_out = scatter_rows(dot_nt(gated, project_t).astype(BF16))
    resid = input_float + attn_out
    scale_two = rms_scale(resid)
    normed2 = (resid * scale_two * gain_two).astype(BF16)
    rows_two = gather_rows(normed2)
    grad_rows = gather_rows(output_grad)
    d_hidden = dot(grad_rows, down_t)
    both = dot(rows_two, gate_up)
    gate_val, up_val = both[:, :units], both[:, units:]
    gate_sig = jax.nn.sigmoid(gate_val)
    silu_gate = gate_val * gate_sig
    hidden = (silu_gate * up_val).astype(BF16)
    d_gate = (d_hidden * up_val * gate_sig * (1.0 + gate_val * (1.0 - gate_sig))).astype(BF16)
    d_up = (d_hidden * silu_gate).astype(BF16)
    d_both = jnp.concatenate([d_gate, d_up], axis=1)
    d_normed2 = scatter_rows(dot_nt(d_both, gate_up).astype(BF16))
    down_shard = scatter_grads(dot_tn(grad_rows, hidden).astype(BF16))
    ffn_out = scatter_rows(dot_nt(hidden, down_t).astype(BF16))
    result = (resid + ffn_out).astype(BF16)
    both_shard = scatter_grads(dot_tn(rows_two, d_both).astype(BF16))
    grad_second = jnp.sum(d_normed2 * resid * scale_two, axis=0)
    d_resid = output_grad.astype(F32) + rms_back(resid, scale_two, gain_two, d_normed2)
    d_attn = gather_rows(d_resid.astype(BF16))
    d_gated = dot(d_attn, project_t)
    project_shard = scatter_grads(dot_tn(d_attn, gated).astype(BF16))
    d_raw, d_conv, d_head = delta_backward(
        doc_starts, seq_lengths, raw, conv_q, conv_k, conv_v, gain_head, mixed, solve, update, state, d_gated
    )
    d_normed1 = scatter_rows(dot_nt(d_raw, mix_full).astype(BF16))
    mix_shard = scatter_grads(dot_tn(rows_one, d_raw).astype(BF16))
    grad_first = jnp.sum(d_normed1 * input_float * scale_one, axis=0)
    input_grad = d_resid + rms_back(input_float, scale_one, gain_one, d_normed1)
    conv_totals = lax.psum(d_conv, ("dp", "fsdp"))
    group = lax.axis_index("dp") * lax.axis_size("fsdp") + lax.axis_index("fsdp")
    gain_size = grad_first.shape[0] // (replicas * lax.axis_size("fsdp"))
    gain_totals = lax.psum(
        jnp.concatenate([grad_first, grad_second, d_head[0]]), ("dp", "fsdp", "tensor")
    )
    features = grad_first.shape[0]

    def gain_shard(first):
        return lax.dynamic_slice_in_dim(gain_totals, first + group * gain_size, gain_size, 0)

    return (
        result,
        input_grad,
        gain_shard(0),
        mix_shard[:, width : 2 * width],
        mix_shard[:, 2 * width : 3 * width],
        mix_shard[:, 3 * width : 4 * width],
        mix_shard[:, :width],
        mix_shard[:, 4 * width : 4 * width + heads],
        conv_totals[:, :width],
        conv_totals[:, width : 2 * width],
        conv_totals[:, 2 * width :],
        gain_totals[2 * features :],
        project_shard.T,
        gain_shard(features),
        both_shard[:, :units],
        both_shard[:, units:],
        down_shard.T,
    )


def solution(mesh):
    placed = (
        P(("dp", "fsdp", "tensor"), None),
        P("fsdp"),
        P("fsdp", "tensor"),
        P("fsdp", "tensor"),
        P("fsdp", "tensor"),
        P("fsdp", "tensor"),
        P("fsdp", "tensor"),
        P(None, "tensor"),
        P(None, "tensor"),
        P(None, "tensor"),
        P(),
        P("tensor", "fsdp"),
        P("fsdp"),
        P("fsdp", "tensor"),
        P("fsdp", "tensor"),
        P("tensor", "fsdp"),
        P(("dp", "fsdp"), None),
        P(("dp", "fsdp")),
        P(("dp", "fsdp", "tensor"), None),
    )
    return jax.shard_map(
        body,
        mesh=mesh,
        in_specs=placed,
        out_specs=(
            P(("dp", "fsdp", "tensor"), None),
            P(("dp", "fsdp", "tensor"), None),
            P(("dp", "fsdp")),
            P(("dp", "fsdp"), "tensor"),
            P(("dp", "fsdp"), "tensor"),
            P(("dp", "fsdp"), "tensor"),
            P(("dp", "fsdp"), "tensor"),
            P(("dp", "fsdp"), "tensor"),
            P(None, "tensor"),
            P(None, "tensor"),
            P(None, "tensor"),
            P(),
            P("tensor", ("dp", "fsdp")),
            P(("dp", "fsdp")),
            P(("dp", "fsdp"), "tensor"),
            P(("dp", "fsdp"), "tensor"),
            P("tensor", ("dp", "fsdp")),
        ),
        check_vma=False,
    )
```

time: 1620 us -> 747 us (0.46)
  waiting for transfers between devices: 883 us -> 379 us
  matrix products: 329 us -> 86.8 us
  other arithmetic: 228 us -> 14.2 us
  starting transfers between devices: 1.44 us -> 84.6 us
  Pallas kernels: 0 us -> 32.7 us
  local copies, waits for them, and re-layouts: 73.6 us -> 44.6 us
    all_gather x12 -> x2, waiting for transfers between devices: 440 us -> 82.1 us  [gather_weights(): lax.all_gather(jnp.concatenate(pieces, axis=1), ('fsdp', 'dp'), axis=0, t...]
    reduce_scatter x12 -> x4, waiting for transfers between devices: 437 us -> 86.8 us  [scatter_grads(): lax.psum_scatter(grads, ('dp', 'fsdp'), scatter_dimension=0, tiled=True)]
    dot_general x131 -> x12, matrix products: 313 us -> 86.8 us  [the longest x4 31.7 us: dot(): return jnp.dot(left, right, preferred_element_type=F32)]
    ppermute x0 -> x24, waiting for transfers between devices: none -> 210 us  [the longest x12 118 us: gather_rows(): came = lax.ppermute(rows, 'tensor', shifted(count, shift))]
    another operation x7 -> x1, other arithmetic: 160 us -> 0.02 us  [body(): jnp.stack([first_gain, second_gain])]
    ppermute x0 -> x24, starting transfers between devices: none -> 83.9 us  [the longest x12 59 us: gather_rows(): came = lax.ppermute(rows, 'tensor', shifted(count, shift))]
    pallas_call x0 -> x2, Pallas kernels: none -> 32.7 us  [the longest x1 17.1 us: delta_forward(): pl.pallas_call(forward_kernel, out_shape=(jax.ShapeDtypeStruct((rows, wid...]
    psum x2, blocking collectives: 43.5 us -> 74.3 us  [the longest x1 50.4 us: body(): lax.psum(jnp.concatenate([grad_first, grad_second, d_head[0]]), ('dp', 'f...]
  transfers between devices with their start and end apart: 25 -> 30, of which waited for: 19 -> 17; matrix products, arithmetic and copies ran while one was open for 36% -> 12% of each run, Pallas kernels for 0% -> 4%
where the time goes in v1:
time: 747 us; the launch traced here: 737 us
  waiting for transfers between devices  379 us (51%)
  matrix products  86.8 us (12%)
  starting transfers between devices  84.6 us (11%)
  blocking collectives  79.8 us (11%)
  local copies, waits for them, and re-layouts  44.6 us (6%)
  Pallas kernels  32.7 us (4%)
  between operations  15.9 us (2%)
  other arithmetic  14.2 us (2%)
    ppermute x12, waiting for transfers between devices, gather_rows(): came = lax.ppermute(rows, 'tensor', shifted(count, shift))  118 us
    ppermute x12, waiting for transfers between devices, scatter_rows(): lax.ppermute(piece, 'tensor', shifted(count, shift)).astype(F32)  91.8 us
    reduce_scatter x4, waiting for transfers between devices, scatter_grads(): lax.psum_scatter(grads, ('dp', 'fsdp'), scatter_dimension=0, tiled=True)  86.8 us
    all_gather x2, waiting for transfers between devices, gather_weights(): lax.all_gather(jnp.concatenate(pieces, axis=1), ('fsdp', 'dp'), axis=0, t...  82.1 us
    ppermute x12, starting transfers between devices, gather_rows(): came = lax.ppermute(rows, 'tensor', shifted(count, shift))  59 us
    psum x1, blocking collectives, body(): lax.psum(jnp.concatenate([grad_first, grad_second, d_head[0]]), ('dp', 'f...  50.4 us
    dot_general x4, matrix products, dot(): return jnp.dot(left, right, preferred_element_type=F32)  31.7 us
    dot_general x4, matrix products, dot_tn(): lax.dot_general(left, right, (((0,), (0,)), ((), ())), preferred_element_...  27.9 us
  transfers between devices with their start and end apart: 30, of which 17 were waited for; matrix products, arithmetic and copies ran while one was open for 12% of the time, Pallas kernels for 4%

profile of v1, /device:TPU:0, one launch (start us, length us, event | category | flops | bytes accessed | tf_op | source)
XLA Modules:
  0.0 737.5 jit_solution(7468878677711262474)
XLA Ops:
  15.6 2.5 constant_dynamic-slice_fusion.12
  18.2 2.2 copy.43
  26.4 5.5 all_gather.9
  35.5 2.6 collective-permute-start.1
  40.2 10.6 %collective-permute-done = bf16[128,2048]{1,0:T(8,128)(2,1)} collective-permute-done((bf16[128,2048]{1,0:T(8,128)(2,1)}, bf16[128,2048]{1,0:T(8,128)(2,1)}, u32[]{:S(2)}, u32[]{:S(2)}) %collective-permute-start) | collective-permute-done | bytes 524320 | tf_op jit(solution)/shard_map/ppermute | solution.py:412
  51.9 19.5 %collective-permute-done.1 = bf16[128,2048]{1,0:T(8,128)(2,1)} collective-permute-done((bf16[128,2048]{1,0:T(8,128)(2,1)}, bf16[128,2048]{1,0:T(8,128)(2,1)}, u32[]{:S(2)}, u32[]{:S(2)}) %collective-permute-start.1) | collective-permute-done | bytes 524320 | tf_op jit(solution)/shard_map/ppermute | solution.py:412
  72.6 2.5 all-gather.3.cloned.1.call-done
  75.1 7.8 %fusion.39.raw_ref = f32[512,2176]{1,0:T(8,128)S(1)} fusion(bf16[512,2048]{1,0:T(8,128)(2,1)S(1)} %constant_dynamic-update-slice_fusion.12, bf16[2048,2176]{1,0:T(8,128)(2,1)} %all-gather.3.cloned.1.call-done), kind=kOutput, calls=%fused_computation.105 | convolution fusion | flops 4563402752 | bytes 15466496 | tf_op jit(solution)/shard_map/dot_general | solution.py:15
  82.9 17.1 %delta_forward.1 = (bf16[512,512]{1,0:T(8,128)(2,1)S(1)}, f32[512,512]{1,0:T(8,128)S(1)}, bf16[8,256,256]{2,1,0:T(8,128)(2,1)S(1)}, bf16[512,512]{1,0:T(8,128)(2,1)S(1)}, bf16[4,128,128]{2,1,0:T(8,128)(2,1)S(1)}) custom-call(s32[1,4]{1,0:T(1,128)S(1)} %copy-done.2, s32[1]{0:T(128)S(6)} %copy.65.length_ref, f32[512,2176]{1,0:T(8,128)S(1)} %fusion.39.raw_ref, ...), custom_call_target="tpu_custom_call" | custom-call | flops 6442450944 | bytes 12582912 | tf_op jit(solution)/shard_map/delta_forward/pallas_call | solution.py:195
  102.2 79.6 %all-gather.5.cloned.1.call-done = bf16[2048,4736]{0,1:T(8,128)(2,1)} async-done(((bf16[256,4736]{0,1:T(8,128)(2,1)}), bf16[2048,4736]{0,1:T(8,128)(2,1)}) %all-gather.5.cloned.1.call-update) | async-done | bytes 19398672 | tf_op jit(solution)/shard_map/all_gather | solution.py:431
  181.8 2.9 convolution_convert_fusion.4
  186.4 2.3 collective-permute-start.5
  190.9 2.3 collective-permute-start.14
  193.5 8.0 %collective-permute-done.3 = bf16[128,2048]{1,0:T(8,128)(2,1)S(1)} collective-permute-done((bf16[128,2048]{1,0:T(8,128)(2,1)S(1)}, bf16[128,2048]{1,0:T(8,128)(2,1)S(1)}, u32[]{:S(2)}, u32[]{:S(2)}) %collective-permute-start.3) | collective-permute-done | bytes 524320 | tf_op jit(solution)/shard_map/ppermute | solution.py:426
  201.5 23.0 %collective-permute-start.13 = (bf16[128,2048]{1,0:T(8,128)(2,1)S(1)}, bf16[128,2048]{1,0:T(8,128)(2,1)S(1)}, u32[]{:S(2)}, u32[]{:S(2)}) collective-permute-start(bf16[128,2048]{1,0:T(8,128)(2,1)S(1)} %copy-done.15), channel_id=1, source_target_pairs={{0,2},{1,3},{2,0},{3,1},{4,6},{5,7},{6,4},{7,5},{8,10},{9,11},{10,... | collective-permute-start | bytes 1572872 | tf_op jit(solution)/shard_map/ppermute | solution.py:412
  224.6 22.0 %collective-permute-done.4 = bf16[128,2048]{1,0:T(8,128)(2,1)S(1)} collective-permute-done((bf16[128,2048]{1,0:T(8,128)(2,1)S(1)}, bf16[128,2048]{1,0:T(8,128)(2,1)S(1)}, u32[]{:S(2)}, u32[]{:S(2)}) %collective-permute-start.4) | collective-permute-done | bytes 524320 | tf_op jit(solution)/shard_map/ppermute | solution.py:426
  247.5 9.3 %collective-permute-start.6 = (bf16[128,2048]{1,0:T(8,128)(2,1)S(1)}, bf16[128,2048]{1,0:T(8,128)(2,1)S(1)}, u32[]{:S(2)}, u32[]{:S(2)}) collective-permute-start(bf16[128,2048]{1,0:T(8,128)(2,1)S(1)} %get-tuple-element.59), channel_id=1, source_target_pairs={{0,1},{1,2},{2,3},{3,0},{4,5},{5,6},{6,7},{7,4},{8,9},{9,10},{10,1... | collective-permute-start | bytes 1572872 | tf_op jit(solution)/shard_map/ppermute | solution.py:412
  256.9 12.7 %collective-permute-start.7 = (bf16[128,2048]{1,0:T(8,128)(2,1)S(1)}, bf16[128,2048]{1,0:T(8,128)(2,1)S(1)}, u32[]{:S(2)}, u32[]{:S(2)}) collective-permute-start(bf16[128,2048]{1,0:T(8,128)(2,1)S(1)} %get-tuple-element.59), channel_id=1, source_target_pairs={{0,2},{1,3},{2,0},{3,1},{4,6},{5,7},{6,4},{7,5},{8,10},{9,11},{10,... | collective-permute-start | bytes 1572872 | tf_op jit(solution)/shard_map/ppermute | solution.py:412
  269.6 32.4 %collective-permute-done.13 = bf16[128,2048]{1,0:T(8,128)(2,1)S(1)} collective-permute-done((bf16[128,2048]{1,0:T(8,128)(2,1)S(1)}, bf16[128,2048]{1,0:T(8,128)(2,1)S(1)}, u32[]{:S(2)}, u32[]{:S(2)}) %collective-permute-start.13) | collective-permute-done | bytes 524320 | tf_op jit(solution)/shard_map/ppermute | solution.py:412
  302.5 10.8 %collective-permute-done.7 = bf16[128,2048]{1,0:T(8,128)(2,1)S(1)} collective-permute-done((bf16[128,2048]{1,0:T(8,128)(2,1)S(1)}, bf16[128,2048]{1,0:T(8,128)(2,1)S(1)}, u32[]{:S(2)}, u32[]{:S(2)}) %collective-permute-start.7) | collective-permute-done | bytes 524320 | tf_op jit(solution)/shard_map/ppermute | solution.py:412
  313.4 11.0 %collective-permute-done.8 = bf16[128,2048]{1,0:T(8,128)(2,1)S(1)} collective-permute-done((bf16[128,2048]{1,0:T(8,128)(2,1)S(1)}, bf16[128,2048]{1,0:T(8,128)(2,1)S(1)}, u32[]{:S(2)}, u32[]{:S(2)}) %collective-permute-start.8) | collective-permute-done | bytes 524320 | tf_op jit(solution)/shard_map/ppermute | solution.py:412
  324.5 12.0 %fusion.2 = f32[512,2816]{1,0:T(8,128)} fusion(bf16[512,2048]{1,0:T(8,128)(2,1)S(1)} %constant_dynamic-update-slice_fusion.8, bf16[2048,4736]{0,1:T(8,128)(2,1)} %all-gather.5.cloned.1.call-done), kind=kOutput, calls=%fused_computation.4 | convolution fusion | flops 5905580032 | bytes 19398656 | tf_op jit(solution)/shard_map/dot_general | solution.py:15
  336.5 8.9 %multiply_convert_fusion.1 = (bf16[512,1408]{1,0:T(8,128)(2,1)S(1)}, bf16[512,1408]{1,0:T(8,128)(2,1)S(1)}, bf16[512,1408]{1,0:T(8,128)(2,1)}) fusion(f32[512,2816]{1,0:T(8,128)} %fusion.2, bf16[512,2048]{1,0:T(8,128)(2,1)S(1)} %constant_dynamic-update-slice_fusion.4, bf16[2048,4736]{0,1:T(8,128)(2,1)} %all-gather.5.cloned.1.call-done), kind=kOutput, calls=%fused_computation.18 | convolution fusion | flops 2963603456 | bytes 17956864 | tf_op jit(solution)/shard_map/dot_general | solution.py:15
  346.5 8.9 %fusion.8 = bf16[512,2048]{1,0:T(8,128)(2,1)S(1)} fusion(bf16[2048,4736]{0,1:T(8,128)(2,1)} %all-gather.5.cloned.1.call-done, bf16[512,1408]{1,0:T(8,128)(2,1)S(1)} %get-tuple-element.65, bf16[512,1408]{1,0:T(8,128)(2,1)S(1)} %get-tuple-element.64), kind=kOutput, calls=%fused_computation.11 | convolution fusion | flops 5912395776 | bytes 16515072 | tf_op jit(solution)/shard_map/dot_general | solution.py:19
  356.3 3.2 collective-permute-start.17
  359.6 12.8 %collective-permute-done.15 = bf16[128,2048]{1,0:T(8,128)(2,1)S(1)} collective-permute-done((bf16[128,2048]{1,0:T(8,128)(2,1)S(1)}, bf16[128,2048]{1,0:T(8,128)(2,1)S(1)}, u32[]{:S(2)}, u32[]{:S(2)}) %collective-permute-start.15) | collective-permute-done | bytes 524320 | tf_op jit(solution)/shard_map/ppermute | solution.py:426
  372.4 9.8 %collective-permute-done.17 = bf16[128,2048]{1,0:T(8,128)(2,1)S(1)} collective-permute-done((bf16[128,2048]{1,0:T(8,128)(2,1)S(1)}, bf16[128,2048]{1,0:T(8,128)(2,1)S(1)}, u32[]{:S(2)}, u32[]{:S(2)}) %collective-permute-start.17) | collective-permute-done | bytes 524320 | tf_op jit(solution)/shard_map/ppermute | solution.py:426
  382.2 21.2 %collective-permute-done.16 = bf16[128,2048]{1,0:T(8,128)(2,1)S(1)} collective-permute-done((bf16[128,2048]{1,0:T(8,128)(2,1)S(1)}, bf16[128,2048]{1,0:T(8,128)(2,1)S(1)}, u32[]{:S(2)}, u32[]{:S(2)}) %collective-permute-start.16) | collective-permute-done | bytes 524320 | tf_op jit(solution)/shard_map/ppermute | solution.py:426
  408.8 12.9 %collective-permute-done.18 = bf16[128,2048]{1,0:T(8,128)(2,1)S(1)} collective-permute-done((bf16[128,2048]{1,0:T(8,128)(2,1)S(1)}, bf16[128,2048]{1,0:T(8,128)(2,1)S(1)}, u32[]{:S(2)}, u32[]{:S(2)}) %collective-permute-start.18) | collective-permute-done | bytes 524320 | tf_op jit(solution)/shard_map/ppermute | solution.py:412
  421.8 20.6 %collective-permute-done.19 = bf16[128,2048]{1,0:T(8,128)(2,1)S(1)} collective-permute-done((bf16[128,2048]{1,0:T(8,128)(2,1)S(1)}, bf16[128,2048]{1,0:T(8,128)(2,1)S(1)}, u32[]{:S(2)}, u32[]{:S(2)}) %collective-permute-start.19) | collective-permute-done | bytes 524320 | tf_op jit(solution)/shard_map/ppermute | solution.py:412
  444.0 2.6 convolution_convert_fusion.3
  448.2 6.7 convolution_convert_fusion.2
  456.5 3.0 fusion.15.grad_ref
  459.6 15.6 %delta_backward.1 = (bf16[512,2176]{1,0:T(8,128)(2,1)S(1)}, f32[4,1536]{1,0:T(4,128)S(1)}, f32[1,128]{1,0:T(1,128)S(1)}) custom-call(s32[1,4]{1,0:T(1,128)S(1)} %copy-done.2, s32[1]{0:T(128)S(6)} %copy.65.length_ref, f32[512,2176]{1,0:T(8,128)} %copy-done.3, f32[4,512]{1,0:T(4,128)S(1)} %convert_element_type.125.conv_q_ref, ...), custom_call_target="tpu_custom_call" | custom-call | flops 3221225472 | bytes 16777216 | tf_op jit(solution)/shard_map/delta_backward/pallas_call | solution.py:366
  475.2 7.4 %convolution_convert_fusion.1 = bf16[2048,2176]{1,0:T(8,128)(2,1)} fusion(bf16[512,2048]{1,0:T(8,128)(2,1)S(1)} %copy-done.23, bf16[512,2176]{1,0:T(8,128)(2,1)S(1)} %get-tuple-element.30), kind=kOutput, calls=%fused_computation.1 | convolution fusion | flops 4567859200 | bytes 13238272 | tf_op jit(solution)/shard_map/dot_general | solution.py:23
  483.0 11.2 %convolution_convert_fusion = bf16[2048,2816]{1,0:T(8,128)(2,1)} fusion(bf16[512,2048]{1,0:T(8,128)(2,1)} %copy-done.24, bf16[512,1408]{1,0:T(8,128)(2,1)} %copy-done.36, bf16[512,1408]{1,0:T(8,128)(2,1)} %copy-done.35), kind=kOutput, calls=%fused_computation | convolution fusion | flops 5917114368 | bytes 16515072 | tf_op jit(solution)/shard_map/dot_general | solution.py:23
  494.2 8.9 %convolution_convert_fusion.5 = bf16[512,2048]{1,0:T(8,128)(2,1)S(1)} fusion(bf16[512,2176]{1,0:T(8,128)(2,1)S(1)} %get-tuple-element.30, bf16[2048,2176]{1,0:T(8,128)(2,1)} %all-gather.3.cloned.1.call-done), kind=kOutput, calls=%fused_computation.15 | convolution fusion | flops 4564451328 | bytes 13238272 | tf_op jit(solution)/shard_map/dot_general | solution.py:19
  504.3 11.3 %collective-permute-start.21 = (bf16[128,2048]{1,0:T(8,128)(2,1)}, bf16[128,2048]{1,0:T(8,128)(2,1)}, u32[]{:S(2)}, u32[]{:S(2)}) collective-permute-start(bf16[128,2048]{1,0:T(8,128)(2,1)} %get-tuple-element.67), channel_id=1, source_target_pairs={{0,1},{1,2},{2,3},{3,0},{4,5},{5,6},{6,7},{7,4},{8,9},{9,10},{10,1... | collective-permute-start | bytes 1572872 | tf_op jit(solution)/shard_map/ppermute | solution.py:426
  517.0 6.4 fusion.11
  526.5 3.2 collective-permute-start.11
  529.8 23.9 %psum.15 = f32[4,1536]{1,0:T(4,128)S(1)} all-reduce(f32[4,1536]{1,0:T(4,128)S(1)} %get-tuple-element.32), channel_id=1, replica_groups=mesh['dp'=4,'fsdp'=2,'tensor'=4] {'dp','fsdp'}, use_global_device_ids=true, to_apply=%region_8.9 | all-reduce | flops 6144 | bytes 49152 | tf_op jit(solution)/shard_map/psum | solution.py:527
  554.3 17.9 %collective-permute-done.22 = bf16[128,2048]{1,0:T(8,128)(2,1)} collective-permute-done((bf16[128,2048]{1,0:T(8,128)(2,1)}, bf16[128,2048]{1,0:T(8,128)(2,1)}, u32[]{:S(2)}, u32[]{:S(2)}) %collective-permute-start.22) | collective-permute-done | bytes 524320 | tf_op jit(solution)/shard_map/ppermute | solution.py:426
  572.2 3.3 fusion.28
  575.5 50.4 %psum.14 = f32[4224]{0:T(1024)S(1)} all-reduce(f32[4224]{0:T(1024)S(1)} %pad_maximum_fusion.4), channel_id=1, replica_groups=mesh['dp'=4,'fsdp'=2,'tensor'=4] {'dp','fsdp','tensor'}, use_global_device_ids=true, to_apply=%region_6.7 | all-reduce | flops 4224 | bytes 33792 | tf_op jit(solution)/shard_map/psum | solution.py:530
  627.1 4.1 fusion.24
  638.8 2.8 fusion.35
  641.6 85.6 %reduce-scatter.9.cloned.1.call-done = bf16[256,2816]{1,0:T(8,128)(2,1)} async-done(((bf16[2048,2816]{1,0:T(8,128)(2,1)}), bf16[256,2816]{1,0:T(8,128)(2,1)}) %reduce-scatter.9.cloned.1.call-update) | async-done | bytes 1441808 | tf_op jit(solution)/shard_map/reduce_scatter | solution.py:435
  727.1 3.1 fusion.34
  (175 shorter events, 56.7 us)
Async XLA Ops:
  7.2 16.6 %copy-start = (bf16[1408,1024]{1,0:T(8,128)(2,1)S(1)}, bf16[1408,1024]{1,0:T(8,128)(2,1)}, u32[]{:S(2)}) copy-start(bf16[1408,1024]{1,0:T(8,128)(2,1)} %param.34) | copy-start | bytes 8650756
  7.2 67.9 %all-gather.3.cloned.1.call-start = ((), (), s32[]{:S(2)}) async-start(), calls=%async_computation.4 | async-start | bytes 10027008 | tf_op jit(solution)/shard_map/all_gather | solution.py:431
  15.6 166.2 %all-gather.5.cloned.1.call-start = ((), (), s32[]{:S(2)}) async-start(), calls=%async_computation.5 | async-start | bytes 21823488 | tf_op jit(solution)/shard_map/all_gather | solution.py:431
  25.7 605.6 %reduce-scatter.7.cloned.1.call-start = ((), (), s32[]{:S(2)}) async-start(), calls=%async_computation.7 | async-start | bytes 2359296 | tf_op jit(solution)/shard_map/reduce_scatter | solution.py:435
  31.9 8.3 %copy-start.30 = (bf16[4,512]{1,0:T(4,128)(2,1)S(1)}, bf16[4,512]{1,0:T(4,128)(2,1)}, u32[]{:S(2)}) copy-start(bf16[4,512]{1,0:T(4,128)(2,1)} %param.28) | copy-start | bytes 12292
  33.4 17.5 %collective-permute-start = (bf16[128,2048]{1,0:T(8,128)(2,1)}, bf16[128,2048]{1,0:T(8,128)(2,1)}, u32[]{:S(2)}, u32[]{:S(2)}) collective-permute-start(bf16[128,2048]{1,0:T(8,128)(2,1)} %get-tuple-element.63), channel_id=1, source_target_pairs={{0,1},{1,2},{2,3},{3,0},{4,5},{5,6},{6,7},{7,4},{8,9},{9,10},{10,1... | collective-permute-start | bytes 1572872 | tf_op jit(solution)/shard_map/ppermute | solution.py:412
  35.5 35.9 %collective-permute-start.1 = (bf16[128,2048]{1,0:T(8,128)(2,1)}, bf16[128,2048]{1,0:T(8,128)(2,1)}, u32[]{:S(2)}, u32[]{:S(2)}) collective-permute-start(bf16[128,2048]{1,0:T(8,128)(2,1)} %get-tuple-element.63), channel_id=1, source_target_pairs={{0,2},{1,3},{2,0},{3,1},{4,6},{5,7},{6,4},{7,5},{8,10},{9,11},{10,... | collective-permute-start | bytes 1572872 | tf_op jit(solution)/shard_map/ppermute | solution.py:412
  38.1 34.4 %collective-permute-start.2 = (bf16[128,2048]{1,0:T(8,128)(2,1)}, bf16[128,2048]{1,0:T(8,128)(2,1)S(1)}, u32[]{:S(2)}, u32[]{:S(2)}) collective-permute-start(bf16[128,2048]{1,0:T(8,128)(2,1)} %get-tuple-element.63), channel_id=1, source_target_pairs={{0,3},{1,0},{2,1},{3,2},{4,7},{5,4},{6,5},{7,6},{8,11},{9,8},{10,9... | collective-permute-start | bytes 1572872 | tf_op jit(solution)/shard_map/ppermute | solution.py:412
  72.6 10.3 %copy-start.2 = (s32[1,4]{1,0:T(1,128)S(1)}, s32[1,4]{1,0:T(1,128)}, u32[]{:S(2)}) copy-start(s32[1,4]{1,0:T(1,128)} %starts_ref.3) | copy-start | bytes 52
  102.2 82.5 %copy-start.4 = (bf16[8,256,256]{2,1,0:T(8,128)(2,1)}, bf16[8,256,256]{2,1,0:T(8,128)(2,1)S(1)}, u32[]{:S(2)}) copy-start(bf16[8,256,256]{2,1,0:T(8,128)(2,1)S(1)} %get-tuple-element.27.solve_ref) | copy-start | bytes 3145732
  102.2 82.5 %copy-start.6 = (bf16[512,512]{1,0:T(8,128)(2,1)}, bf16[512,512]{1,0:T(8,128)(2,1)S(1)}, u32[]{:S(2)}) copy-start(bf16[512,512]{1,0:T(8,128)(2,1)S(1)} %get-tuple-element.28.update_ref) | copy-start | bytes 1572868
  184.9 61.7 %copy-start.11 = (bf16[128,2048]{1,0:T(8,128)(2,1)S(1)}, bf16[128,2048]{1,0:T(8,128)(2,1)}, u32[]{:S(2)}) copy-start(bf16[128,2048]{1,0:T(8,128)(2,1)} %param.19) | copy-start | bytes 1572868
  184.9 16.6 %collective-permute-start.3 = (bf16[128,2048]{1,0:T(8,128)(2,1)S(1)}, bf16[128,2048]{1,0:T(8,128)(2,1)S(1)}, u32[]{:S(2)}, u32[]{:S(2)}) collective-permute-start(bf16[128,2048]{1,0:T(8,128)(2,1)S(1)} %get-tuple-element.76), channel_id=1, source_target_pairs={{0,1},{1,2},{2,3},{3,0},{4,5},{5,6},{6,7},{7,4},{8,9},{9,10},{10,1... | collective-permute-start | bytes 1572872 | tf_op jit(solution)/shard_map/ppermute | solution.py:426
  186.4 38.1 %collective-permute-start.5 = (bf16[128,2048]{1,0:T(8,128)(2,1)S(1)}, bf16[128,2048]{1,0:T(8,128)(2,1)S(1)}, u32[]{:S(2)}, u32[]{:S(2)}) collective-permute-start(bf16[128,2048]{1,0:T(8,128)(2,1)S(1)} %get-tuple-element.77), channel_id=1, source_target_pairs={{0,3},{1,0},{2,1},{3,2},{4,7},{5,4},{6,5},{7,6},{8,11},{9,8},{10,9... | collective-permute-start | bytes 1572872 | tf_op jit(solution)/shard_map/ppermute | solution.py:426
  188.8 57.8 %collective-permute-start.4 = (bf16[128,2048]{1,0:T(8,128)(2,1)S(1)}, bf16[128,2048]{1,0:T(8,128)(2,1)S(1)}, u32[]{:S(2)}, u32[]{:S(2)}) collective-permute-start(bf16[128,2048]{1,0:T(8,128)(2,1)S(1)} %get-tuple-element.78), channel_id=1, source_target_pairs={{0,2},{1,3},{2,0},{3,1},{4,6},{5,7},{6,4},{7,5},{8,10},{9,11},{10,... | collective-permute-start | bytes 1572872 | tf_op jit(solution)/shard_map/ppermute | solution.py:426
  189.4 67.5 %collective-permute-start.12 = (bf16[128,2048]{1,0:T(8,128)(2,1)S(1)}, bf16[128,2048]{1,0:T(8,128)(2,1)S(1)}, u32[]{:S(2)}, u32[]{:S(2)}) collective-permute-start(bf16[128,2048]{1,0:T(8,128)(2,1)S(1)} %copy-done.15), channel_id=1, source_target_pairs={{0,1},{1,2},{2,3},{3,0},{4,5},{5,6},{6,7},{7,4},{8,9},{9,10},{10,1... | collective-permute-start | bytes 1572872 | tf_op jit(solution)/shard_map/ppermute | solution.py:412
  190.9 111.5 %collective-permute-start.14 = (bf16[128,2048]{1,0:T(8,128)(2,1)S(1)}, bf16[128,2048]{1,0:T(8,128)(2,1)S(1)}, u32[]{:S(2)}, u32[]{:S(2)}) collective-permute-start(bf16[128,2048]{1,0:T(8,128)(2,1)S(1)} %copy-done.15), channel_id=1, source_target_pairs={{0,3},{1,0},{2,1},{3,2},{4,7},{5,4},{6,5},{7,6},{8,11},{9,8},{10,9... | collective-permute-start | bytes 1572872 | tf_op jit(solution)/shard_map/ppermute | solution.py:412
  201.5 100.5 %collective-permute-start.13 = (bf16[128,2048]{1,0:T(8,128)(2,1)S(1)}, bf16[128,2048]{1,0:T(8,128)(2,1)S(1)}, u32[]{:S(2)}, u32[]{:S(2)}) collective-permute-start(bf16[128,2048]{1,0:T(8,128)(2,1)S(1)} %copy-done.15), channel_id=1, source_target_pairs={{0,2},{1,3},{2,0},{3,1},{4,6},{5,7},{6,4},{7,5},{8,10},{9,11},{10,... | collective-permute-start | bytes 1572872 | tf_op jit(solution)/shard_map/ppermute | solution.py:412
  247.1 157.2 %copy-start.8 = (f32[128,2048]{1,0:T(8,128)}, f32[128,2048]{1,0:T(8,128)S(1)}, u32[]{:S(2)}) copy-start(f32[128,2048]{1,0:T(8,128)S(1)} %get-tuple-element.61) | copy-start | bytes 3145732
  247.5 54.9 %collective-permute-start.6 = (bf16[128,2048]{1,0:T(8,128)(2,1)S(1)}, bf16[128,2048]{1,0:T(8,128)(2,1)S(1)}, u32[]{:S(2)}, u32[]{:S(2)}) collective-permute-start(bf16[128,2048]{1,0:T(8,128)(2,1)S(1)} %get-tuple-element.59), channel_id=1, source_target_pairs={{0,1},{1,2},{2,3},{3,0},{4,5},{5,6},{6,7},{7,4},{8,9},{9,10},{10,1... | collective-permute-start | bytes 1572872 | tf_op jit(solution)/shard_map/ppermute | solution.py:412
  256.9 56.4 %collective-permute-start.7 = (bf16[128,2048]{1,0:T(8,128)(2,1)S(1)}, bf16[128,2048]{1,0:T(8,128)(2,1)S(1)}, u32[]{:S(2)}, u32[]{:S(2)}) collective-permute-start(bf16[128,2048]{1,0:T(8,128)(2,1)S(1)} %get-tuple-element.59), channel_id=1, source_target_pairs={{0,2},{1,3},{2,0},{3,1},{4,6},{5,7},{6,4},{7,5},{8,10},{9,11},{10,... | collective-permute-start | bytes 1572872 | tf_op jit(solution)/shard_map/ppermute | solution.py:412
  302.1 22.3 %collective-permute-start.8 = (bf16[128,2048]{1,0:T(8,128)(2,1)S(1)}, bf16[128,2048]{1,0:T(8,128)(2,1)S(1)}, u32[]{:S(2)}, u32[]{:S(2)}) collective-permute-start(bf16[128,2048]{1,0:T(8,128)(2,1)S(1)} %get-tuple-element.59), channel_id=1, source_target_pairs={{0,3},{1,0},{2,1},{3,2},{4,7},{5,4},{6,5},{7,6},{8,11},{9,8},{10,9... | collective-permute-start | bytes 1572872 | tf_op jit(solution)/shard_map/ppermute | solution.py:412
  302.4 34.1 %copy-start.25 = (bf16[512,2048]{1,0:T(8,128)(2,1)}, bf16[512,2048]{1,0:T(8,128)(2,1)S(1)}, u32[]{:S(2)}) copy-start(bf16[512,2048]{1,0:T(8,128)(2,1)S(1)} %constant_dynamic-update-slice_fusion.4) | copy-start | bytes 6291460
  324.5 12.0 %copy-start.24 = (bf16[512,2048]{1,0:T(8,128)(2,1)}, bf16[512,2048]{1,0:T(8,128)(2,1)S(1)}, u32[]{:S(2)}) copy-start(bf16[512,2048]{1,0:T(8,128)(2,1)S(1)} %constant_dynamic-update-slice_fusion.8) | copy-start | bytes 6291460
  345.4 10.1 %copy-start.36 = (bf16[512,1408]{1,0:T(8,128)(2,1)}, bf16[512,1408]{1,0:T(8,128)(2,1)S(1)}, u32[]{:S(2)}) copy-start(bf16[512,1408]{1,0:T(8,128)(2,1)S(1)} %get-tuple-element.65) | copy-start | bytes 4325380
  355.7 16.7 %collective-permute-start.15 = (bf16[128,2048]{1,0:T(8,128)(2,1)S(1)}, bf16[128,2048]{1,0:T(8,128)(2,1)S(1)}, u32[]{:S(2)}, u32[]{:S(2)}) collective-permute-start(bf16[128,2048]{1,0:T(8,128)(2,1)S(1)} %get-tuple-element.70), channel_id=1, source_target_pairs={{0,1},{1,2},{2,3},{3,0},{4,5},{5,6},{6,7},{7,4},{8,9},{9,10},{10,1... | collective-permute-start | bytes 1572872 | tf_op jit(solution)/shard_map/ppermute | solution.py:426
  356.3 25.8 %collective-permute-start.17 = (bf16[128,2048]{1,0:T(8,128)(2,1)S(1)}, bf16[128,2048]{1,0:T(8,128)(2,1)S(1)}, u32[]{:S(2)}, u32[]{:S(2)}) collective-permute-start(bf16[128,2048]{1,0:T(8,128)(2,1)S(1)} %get-tuple-element.71), channel_id=1, source_target_pairs={{0,3},{1,0},{2,1},{3,2},{4,7},{5,4},{6,5},{7,6},{8,11},{9,8},{10,9... | collective-permute-start | bytes 1572872 | tf_op jit(solution)/shard_map/ppermute | solution.py:426
  359.6 43.8 %collective-permute-start.16 = (bf16[128,2048]{1,0:T(8,128)(2,1)S(1)}, bf16[128,2048]{1,0:T(8,128)(2,1)S(1)}, u32[]{:S(2)}, u32[]{:S(2)}) collective-permute-start(bf16[128,2048]{1,0:T(8,128)(2,1)S(1)} %get-tuple-element.72), channel_id=1, source_target_pairs={{0,2},{1,3},{2,0},{3,1},{4,6},{5,7},{6,4},{7,5},{8,10},{9,11},{10,... | collective-permute-start | bytes 1572872 | tf_op jit(solution)/shard_map/ppermute | solution.py:426
  405.0 16.8 %collective-permute-start.18 = (bf16[128,2048]{1,0:T(8,128)(2,1)S(1)}, bf16[128,2048]{1,0:T(8,128)(2,1)S(1)}, u32[]{:S(2)}, u32[]{:S(2)}) collective-permute-start(bf16[128,2048]{1,0:T(8,128)(2,1)S(1)} %get-tuple-element.56), channel_id=1, source_target_pairs={{0,1},{1,2},{2,3},{3,0},{4,5},{5,6},{6,7},{7,4},{8,9},{9,10},{10,1... | collective-permute-start | bytes 1572872 | tf_op jit(solution)/shard_map/ppermute | solution.py:412
  405.0 37.5 %collective-permute-start.19 = (bf16[128,2048]{1,0:T(8,128)(2,1)S(1)}, bf16[128,2048]{1,0:T(8,128)(2,1)S(1)}, u32[]{:S(2)}, u32[]{:S(2)}) collective-permute-start(bf16[128,2048]{1,0:T(8,128)(2,1)S(1)} %get-tuple-element.56), channel_id=1, source_target_pairs={{0,2},{1,3},{2,0},{3,1},{4,6},{5,7},{6,4},{7,5},{8,10},{9,11},{10,... | collective-permute-start | bytes 1572872 | tf_op jit(solution)/shard_map/ppermute | solution.py:412
  406.7 35.9 %collective-permute-start.20 = (bf16[128,2048]{1,0:T(8,128)(2,1)S(1)}, bf16[128,2048]{1,0:T(8,128)(2,1)S(1)}, u32[]{:S(2)}, u32[]{:S(2)}) collective-permute-start(bf16[128,2048]{1,0:T(8,128)(2,1)S(1)} %get-tuple-element.56), channel_id=1, source_target_pairs={{0,3},{1,0},{2,1},{3,2},{4,7},{5,4},{6,5},{7,6},{8,11},{9,8},{10,9... | collective-permute-start | bytes 1572872 | tf_op jit(solution)/shard_map/ppermute | solution.py:412
  446.7 186.6 %reduce-scatter.11.cloned.1.call-start = ((), (), s32[]{:S(2)}) async-start(), calls=%async_computation.9 | async-start | bytes 6488064 | tf_op jit(solution)/shard_map/reduce_scatter | solution.py:435
  455.0 182.3 %reduce-scatter.5.cloned.1.call-start = ((), (), s32[]{:S(2)}) async-start(), calls=%async_computation.6 | async-start | bytes 10027008 | tf_op jit(solution)/shard_map/reduce_scatter | solution.py:435
  459.6 15.7 %copy-start.23 = (bf16[512,2048]{1,0:T(8,128)(2,1)S(1)}, bf16[512,2048]{1,0:T(8,128)(2,1)}, u32[]{:S(2)}) copy-start(bf16[512,2048]{1,0:T(8,128)(2,1)} %copy-done.22) | copy-start | bytes 6291460
  482.7 244.4 %reduce-scatter.9.cloned.1.call-start = ((), (), s32[]{:S(2)}) async-start(), calls=%async_computation.8 | async-start | bytes 12976128 | tf_op jit(solution)/shard_map/reduce_scatter | solution.py:435
  503.1 20.4 %copy-start.27 = (bf16[512,2048]{1,0:T(8,128)(2,1)}, bf16[512,2048]{1,0:T(8,128)(2,1)S(1)}, u32[]{:S(2)}) copy-start(bf16[512,2048]{1,0:T(8,128)(2,1)S(1)} %convolution_convert_fusion.5) | copy-start | bytes 6291460
  503.1 13.9 %copy-start.34 = (bf16[512,1408]{1,0:T(8,128)(2,1)S(1)}, bf16[512,1408]{1,0:T(8,128)(2,1)}, u32[]{:S(2)}) copy-start(bf16[512,1408]{1,0:T(8,128)(2,1)} %get-tuple-element.66) | copy-start | bytes 4325380
  504.3 50.0 %collective-permute-start.21 = (bf16[128,2048]{1,0:T(8,128)(2,1)}, bf16[128,2048]{1,0:T(8,128)(2,1)}, u32[]{:S(2)}, u32[]{:S(2)}) collective-permute-start(bf16[128,2048]{1,0:T(8,128)(2,1)} %get-tuple-element.67), channel_id=1, source_target_pairs={{0,1},{1,2},{2,3},{3,0},{4,5},{5,6},{6,7},{7,4},{8,9},{9,10},{10,1... | collective-permute-start | bytes 1572872 | tf_op jit(solution)/shard_map/ppermute | solution.py:426
  515.6 38.8 %collective-permute-start.23 = (bf16[128,2048]{1,0:T(8,128)(2,1)}, bf16[128,2048]{1,0:T(8,128)(2,1)}, u32[]{:S(2)}, u32[]{:S(2)}) collective-permute-start(bf16[128,2048]{1,0:T(8,128)(2,1)} %get-tuple-element.68), channel_id=1, source_target_pairs={{0,3},{1,0},{2,1},{3,2},{4,7},{5,4},{6,5},{7,6},{8,11},{9,8},{10,9... | collective-permute-start | bytes 1572872 | tf_op jit(solution)/shard_map/ppermute | solution.py:426
  515.6 56.7 %collective-permute-start.22 = (bf16[128,2048]{1,0:T(8,128)(2,1)}, bf16[128,2048]{1,0:T(8,128)(2,1)}, u32[]{:S(2)}, u32[]{:S(2)}) collective-permute-start(bf16[128,2048]{1,0:T(8,128)(2,1)} %get-tuple-element.69), channel_id=1, source_target_pairs={{0,2},{1,3},{2,0},{3,1},{4,6},{5,7},{6,4},{7,5},{8,10},{9,11},{10,... | collective-permute-start | bytes 1572872 | tf_op jit(solution)/shard_map/ppermute | solution.py:426
  524.8 47.5 %copy-start.12 = (bf16[128,2048]{1,0:T(8,128)(2,1)S(1)}, bf16[128,2048]{1,0:T(8,128)(2,1)}, u32[]{:S(2)}) copy-start(bf16[128,2048]{1,0:T(8,128)(2,1)} %param.19) | copy-start | bytes 1572868
  525.9 101.2 %copy-start.9 = (f32[128,2048]{1,0:T(8,128)S(1)}, f32[128,2048]{1,0:T(8,128)}, u32[]{:S(2)}) copy-start(f32[128,2048]{1,0:T(8,128)} %copy-done.8) | copy-start | bytes 3145732
  525.9 101.2 %copy-start.14 = (f32[128,2048]{1,0:T(8,128)S(1)}, f32[128,2048]{1,0:T(8,128)}, u32[]{:S(2)}) copy-start(f32[128,2048]{1,0:T(8,128)} %copy-done.13) | copy-start | bytes 3145732
  526.0 101.2 %copy-start.16 = (bf16[128,2048]{1,0:T(8,128)(2,1)S(1)}, bf16[128,2048]{1,0:T(8,128)(2,1)}, u32[]{:S(2)}) copy-start(bf16[128,2048]{1,0:T(8,128)(2,1)} %param.37) | copy-start | bytes 1572868
  526.0 101.1 %collective-permute-start.9 = (bf16[128,2048]{1,0:T(8,128)(2,1)}, bf16[128,2048]{1,0:T(8,128)(2,1)}, u32[]{:S(2)}, u32[]{:S(2)}) collective-permute-start(bf16[128,2048]{1,0:T(8,128)(2,1)} %get-tuple-element.73), channel_id=1, source_target_pairs={{0,1},{1,2},{2,3},{3,0},{4,5},{5,6},{6,7},{7,4},{8,9},{9,10},{10,1... | collective-permute-start | bytes 1572872 | tf_op jit(solution)/shard_map/ppermute | solution.py:426
  526.5 100.6 %collective-permute-start.11 = (bf16[128,2048]{1,0:T(8,128)(2,1)}, bf16[128,2048]{1,0:T(8,128)(2,1)}, u32[]{:S(2)}, u32[]{:S(2)}) collective-permute-start(bf16[128,2048]{1,0:T(8,128)(2,1)} %get-tuple-element.74), channel_id=1, source_target_pairs={{0,3},{1,0},{2,1},{3,2},{4,7},{5,4},{6,5},{7,6},{8,11},{9,8},{10,9... | collective-permute-start | bytes 1572872 | tf_op jit(solution)/shard_map/ppermute | solution.py:426
  554.3 72.8 %collective-permute-start.10 = (bf16[128,2048]{1,0:T(8,128)(2,1)}, bf16[128,2048]{1,0:T(8,128)(2,1)}, u32[]{:S(2)}, u32[]{:S(2)}) collective-permute-start(bf16[128,2048]{1,0:T(8,128)(2,1)} %get-tuple-element.75), channel_id=1, source_target_pairs={{0,2},{1,3},{2,0},{3,1},{4,6},{5,7},{6,4},{7,5},{8,10},{9,11},{10,... | collective-permute-start | bytes 1572872 | tf_op jit(solution)/shard_map/ppermute | solution.py:426
  638.8 91.4 %copy-start.1 = (bf16[1408,1024]{1,0:T(8,128)(2,1)S(1)}, bf16[1408,1024]{1,0:T(8,128)(2,1)}, u32[]{:S(2)}) copy-start(bf16[1408,1024]{1,0:T(8,128)(2,1)} %param.34) | copy-start | bytes 8650756
  (19 other events, 57.6 us)
Sparse Core Ops, SparseCore 0:
  15.7 59.3 all-gather.2
  77.0 104.7 all-gather.4
  446.8 48.5 reduce-scatter.6
  499.1 59.6 reduce-scatter.10
  562.2 74.9 reduce-scatter.4
  640.6 86.4 reduce-scatter.8

commit v2 on v1

--- a/solution.py
+++ b/solution.py
@@ -1,3 +1,4 @@
+import functools
 import jax, jax.numpy as jnp
 from jax import lax
 from jax.experimental import pallas as pl
@@ -7,6 +8,7 @@
 KERNEL = 4
 CHUNK = 256
 G, Q, K, V = range(4)
+MESH = pl.DeviceIdType.MESH
 F32 = jnp.float32
 BF16 = jnp.bfloat16
 
@@ -388,6 +390,119 @@
     )(starts, length, raw, conv_q, conv_k, conv_v, gain, mixed, solve, update, state, grad)
 
 
+def reduce_kernel(
+    group_size, line_size, fsdp_size, gain_ref, head_ref, conv_ref, gain_out, head_out, conv_out,
+    line_gain, line_head, stage, group_gain, group_conv,
+    line_send, line_recv, group_send, group_recv,
+):
+    dp, fsdp, tensor = (lax.axis_index(name) for name in ("dp", "fsdp", "tensor"))
+    group = dp * fsdp_size + fsdp
+    size = gain_out.shape[1]
+
+    def line_peer(shift):
+        return (dp, fsdp, lax.rem(tensor + shift, line_size))
+
+    def group_peer(shift):
+        peer = lax.rem(group + shift, group_size)
+        return peer, (lax.div(peer, fsdp_size), lax.rem(peer, fsdp_size), tensor)
+
+    barrier = pltpu.get_barrier_semaphore()
+    for shift in range(1, line_size):
+        pl.semaphore_signal(barrier, inc=1, device_id=line_peer(shift), device_id_type=MESH)
+    for shift in range(1, group_size):
+        pl.semaphore_signal(barrier, inc=1, device_id=group_peer(shift)[1], device_id_type=MESH)
+    pl.semaphore_wait(barrier, line_size + group_size - 2)
+
+    copies = []
+    for shift in range(1, line_size):
+        for part, (source, target) in enumerate(((gain_ref, line_gain), (head_ref, line_head))):
+            copy = pltpu.make_async_remote_copy(
+                src_ref=source, dst_ref=target.at[shift - 1],
+                send_sem=line_send.at[shift - 1, part], recv_sem=line_recv.at[shift - 1, part],
+                device_id=line_peer(shift), device_id_type=MESH,
+            )
+            copy.start()
+            copies.append(copy)
+    conv_copies = []
+    for shift in range(1, group_size):
+        copy = pltpu.make_async_remote_copy(
+            src_ref=conv_ref, dst_ref=group_conv.at[shift - 1],
+            send_sem=group_send.at[shift - 1, 1], recv_sem=group_recv.at[shift - 1, 1],
+            device_id=group_peer(shift)[1], device_id_type=MESH,
+        )
+        copy.start()
+        conv_copies.append(copy)
+    for copy in copies:
+        copy.wait()
+    gain = gain_ref[...]
+    head = head_ref[...]
+    for shift in range(1, line_size):
+        gain = gain + line_gain[shift - 1]
+        head = head + line_head[shift - 1]
+    for peer in range(group_size):
+        stage[peer] = jnp.zeros(stage.shape[1:], F32)
+        stage[peer, :2, :size] = gain[:, peer * size : (peer + 1) * size]
+        stage[peer, 2:3, : head.shape[1]] = head
+    for copy in conv_copies:
+        copy.wait()
+    conv = conv_ref[...]
+    for shift in range(1, group_size):
+        conv = conv + group_conv[shift - 1]
+    conv_out[...] = conv
+    copies = []
+    for shift in range(1, group_size):
+        peer, where = group_peer(shift)
+        copy = pltpu.make_async_remote_copy(
+            src_ref=stage.at[peer], dst_ref=group_gain.at[shift - 1],
+            send_sem=group_send.at[shift - 1, 0], recv_sem=group_recv.at[shift - 1, 0],
+            device_id=where, device_id_type=MESH,
+        )
+        copy.start()
+        copies.append(copy)
+    for copy in copies:
+        copy.wait()
+    total = stage[group]
+    for shift in range(1, group_size):
+        total = total + group_gain[shift - 1]
+    gain_out[...] = total[:2, :size]
+    head_out[...] = total[2:3, : head.shape[1]]
+
+
+def reduce_small(gain, head, conv):
+    fsdp_size, line_size = lax.axis_size("fsdp"), lax.axis_size("tensor")
+    group_size = lax.axis_size("dp") * fsdp_size
+    size = gain.shape[1] // group_size
+    pad = max(size, head.shape[1])
+    vmem = pl.BlockSpec(memory_space=pltpu.VMEM)
+    dma = pltpu.SemaphoreType.DMA
+    return pl.pallas_call(
+        functools.partial(reduce_kernel, group_size, line_size, fsdp_size),
+        out_shape=(
+            jax.ShapeDtypeStruct((2, size), F32),
+            jax.ShapeDtypeStruct(head.shape, F32),
+            jax.ShapeDtypeStruct(conv.shape, F32),
+        ),
+        in_specs=[vmem] * 3,
+        out_specs=[vmem] * 3,
+        scratch_shapes=[
+            pltpu.VMEM((line_size - 1,) + gain.shape, F32),
+            pltpu.VMEM((line_size - 1,) + head.shape, F32),
+            pltpu.VMEM((group_size, 8, pad), F32),
+            pltpu.VMEM((group_size - 1, 8, pad), F32),
+            pltpu.VMEM((group_size - 1,) + conv.shape, F32),
+            dma((line_size - 1, 2)),
+            dma((line_size - 1, 2)),
+            dma((group_size - 1, 2)),
+            dma((group_size - 1, 2)),
+        ],
+        compiler_params=pltpu.CompilerParams(collective_id=1, has_side_effects=True, vmem_limit_bytes=16 * 2**20),
+        name="reduce_small",
+    )(gain, head, conv)
+
+
+PARTS = 4
+
+
 def rms_scale(values):
     return lax.rsqrt(jnp.mean(values * values, axis=-1, keepdims=True) + 1e-05)
 
@@ -396,6 +511,233 @@
     scaled_grad = grad * gain
     inner = jnp.mean(scaled_grad * values, axis=-1, keepdims=True)
     return scale_rows * (scaled_grad - values * scale_rows * scale_rows * inner)
+
+
+class Line:
+
+    def __init__(self, count, rows, sums, rows_out):
+        self.count = count
+        self.rows = rows
+        self.part = rows // PARTS
+        self.sums = sums
+        self.rows_out = rows_out
+        self.dp, self.fsdp, self.place = (lax.axis_index(name) for name in ("dp", "fsdp", "tensor"))
+
+    def device(self, step):
+        return (self.dp, self.fsdp, self.place + step)
+
+    def ahead(self, step):
+        return self.place < self.count - 1 if step > 0 else self.place > 0
+
+    def behind(self, step):
+        return self.ahead(-step)
+
+    def barrier(self):
+        barrier = pltpu.get_barrier_semaphore()
+        for step in (1, -1):
+            @pl.when(self.ahead(step))
+            def _():
+                pl.semaphore_signal(barrier, inc=1, device_id=self.device(step), device_id_type=MESH)
+        ends = (self.place == 0).astype(jnp.int32) + (self.place == self.count - 1).astype(jnp.int32)
+        pl.semaphore_wait(barrier, 2 - ends)
+
+    def span(self, owner, part):
+        return pl.ds(pl.multiple_of(owner * self.rows + part * self.part, self.part), self.part)
+
+    def sum_copy(self, source, step, slot, part):
+        recv, _, send_sem, recv_sem = self.sums[step]
+        return pltpu.make_async_remote_copy(
+            src_ref=source, dst_ref=recv.at[slot, part],
+            send_sem=send_sem.at[slot, part], recv_sem=recv_sem.at[slot, part],
+            device_id=self.device(step), device_id_type=MESH,
+        )
+
+    def owner_of(self, step, slot):
+        return self.count - 1 - slot if step > 0 else slot
+
+    def inject(self, partial_ref, part):
+        for step in (1, -1):
+            @pl.when(jnp.logical_not(self.behind(step)))
+            def _():
+                for slot in range(self.count - 1):
+                    owner = self.owner_of(step, slot)
+                    self.sum_copy(partial_ref.at[self.span(owner, part)], step, slot, part).start()
+
+    def passes(self, step, slot):
+        owner = self.owner_of(step, slot)
+        further = self.place < owner if step > 0 else self.place > owner
+        return jnp.logical_and(self.behind(step), further)
+
+    def forward(self, partial_ref, part):
+        for slot in range(self.count - 1):
+            for step in (1, -1):
+                recv, send, _, _ = self.sums[step]
+
+                @pl.when(self.passes(step, slot))
+                def _():
+                    self.sum_copy(send.at[slot, part], step, slot, part).wait_recv()
+                    mine = partial_ref[self.span(self.owner_of(step, slot), part), :].astype(F32)
+                    send[slot, part] = (mine + recv[slot, part].astype(F32)).astype(BF16)
+                    self.sum_copy(send.at[slot, part], step, slot, part).start()
+
+    def collect(self, partial_ref, total_ref, part):
+        total_ref[...] = partial_ref[self.span(self.place, part), :].astype(F32)
+        for step in (1, -1):
+            recv, send, _, _ = self.sums[step]
+            slot = self.count - 1 - self.place if step > 0 else self.place
+
+            @pl.when(self.behind(step))
+            def _():
+                self.sum_copy(send.at[0, part], step, slot, part).wait_recv()
+                total_ref[...] += recv[slot, part].astype(F32)
+
+    def drain_sums(self, partial_ref):
+        for part in range(PARTS):
+            for step in (1, -1):
+                _, send, _, _ = self.sums[step]
+                for slot in range(self.count - 1):
+                    owner = self.owner_of(step, slot)
+                    further = self.place < owner if step > 0 else self.place > owner
+
+                    @pl.when(further)
+                    def _():
+                        self.sum_copy(send.at[slot, part], step, slot, part).wait_send()
+
+    def row_copy(self, ref, step, owner, distance, part):
+        send_sem, recv_sem = self.rows_out[step]
+        where = ref.at[self.span(owner, part)]
+        return pltpu.make_async_remote_copy(
+            src_ref=where, dst_ref=where,
+            send_sem=send_sem.at[distance, part], recv_sem=recv_sem.at[distance, part],
+            device_id=self.device(step), device_id_type=MESH,
+        )
+
+    def spread(self, ref, part):
+        for step in (1, -1):
+            @pl.when(self.ahead(step))
+            def _():
+                self.row_copy(ref, step, self.place, 0, part).start()
+
+    def relay(self, ref, distance, part):
+        for step in (1, -1):
+            owner = self.place - step * distance
+            inside = owner >= 0 if step > 0 else owner < self.count
+
+            @pl.when(inside)
+            def _():
+                self.row_copy(ref, step, owner, distance - 1, part).wait_recv()
+
+                if distance < self.count - 1:
+                    @pl.when(self.ahead(step))
+                    def _():
+                        self.row_copy(ref, step, owner, distance, part).start()
+
+    def drain_rows(self, ref):
+        for part in range(PARTS):
+            for step in (1, -1):
+                for distance in range(self.count - 1):
+                    owner = self.place - step * distance
+                    inside = owner >= 0 if step > 0 else owner < self.count
+
+                    @pl.when(jnp.logical_and(inside, self.ahead(step)))
+                    def _():
+                        self.row_copy(ref, step, owner, distance, part).wait_send()
+
+
+def line_scratch(count, rows, features, spread):
+    dma = pltpu.SemaphoreType.DMA
+    slots = (count - 1, PARTS)
+    scratch = []
+    for _ in range(2):
+        scratch += [pltpu.VMEM(slots + (rows // PARTS, features), BF16)] * 2 + [dma(slots)] * 2
+    if spread:
+        scratch += [dma(slots)] * 4
+    return scratch + [pltpu.VMEM((rows // PARTS, features), F32)]
+
+
+def line_of(count, rows, scratch):
+    sums = {1: scratch[0:4], -1: scratch[4:8]}
+    rows_out = {1: scratch[8:10], -1: scratch[10:12]} if len(scratch) > 9 else None
+    return Line(count, rows, sums, rows_out), scratch[-1]
+
+
+def run_line(line, partial_ref, total_ref, finish, rows_ref):
+    line.barrier()
+    line.inject(partial_ref, 0)
+    line.inject(partial_ref, 1)
+    for turn in range(PARTS + (line.count - 1 if rows_ref is not None else 0)):
+        if turn < PARTS:
+            line.forward(partial_ref, turn)
+            line.collect(partial_ref, total_ref, turn)
+            finish(turn, pl.ds(turn * line.part, line.part), line.span(line.place, turn))
+            if rows_ref is not None:
+                line.spread(rows_ref, turn)
+            if turn + 2 < PARTS:
+                line.inject(partial_ref, turn + 2)
+        if rows_ref is not None:
+            for distance in range(1, line.count):
+                if 0 <= turn - distance < PARTS:
+                    line.relay(rows_ref, distance, turn - distance)
+    line.drain_sums(partial_ref)
+    if rows_ref is not None:
+        line.drain_rows(rows_ref)
+
+
+def middle_kernel(count, partial_ref, input_ref, gain_ref, rows_ref, resid_ref, *scratch):
+    line, total_ref = line_of(count, input_ref.shape[0], scratch)
+
+    def finish(part, local, place):
+        resid = input_ref[local, :].astype(F32) + total_ref[...]
+        resid_ref[local, :] = resid
+        rows_ref[place, :] = (resid * rms_scale(resid) * gain_ref[...]).astype(BF16)
+
+    run_line(line, partial_ref, total_ref, finish, rows_ref)
+
+
+def turn_kernel(count, partial_ref, resid_ref, grad_ref, gain_ref, rows_ref, d_resid_ref, d_gain_ref, *scratch):
+    line, total_ref = line_of(count, resid_ref.shape[0], scratch)
+
+    def finish(part, local, place):
+        resid, total = resid_ref[local, :], total_ref[...]
+        scale = rms_scale(resid)
+        sums = jnp.sum(total * resid * scale, axis=0, keepdims=True)
+        d_gain_ref[...] = sums if part == 0 else d_gain_ref[...] + sums
+        d_resid = grad_ref[local, :].astype(F32) + rms_back(resid, scale, gain_ref[...], total)
+        d_resid_ref[local, :] = d_resid
+        rows_ref[place, :] = d_resid.astype(BF16)
+
+    run_line(line, partial_ref, total_ref, finish, rows_ref)
+
+
+def last_kernel(count, partial_ref, input_ref, d_resid_ref, gain_ref, d_input_ref, d_gain_ref, *scratch):
+    line, total_ref = line_of(count, input_ref.shape[0], scratch)
+
+    def finish(part, local, place):
+        values, total = input_ref[local, :].astype(F32), total_ref[...]
+        scale = rms_scale(values)
+        sums = jnp.sum(total * values * scale, axis=0, keepdims=True)
+        d_gain_ref[...] = sums if part == 0 else d_gain_ref[...] + sums
+        d_input_ref[local, :] = d_resid_ref[local, :] + rms_back(values, scale, gain_ref[...], total)
+
+    run_line(line, partial_ref, total_ref, finish, None)
+
+
+def line_call(kernel, name, ident, spread, out_shape, operands):
+    count = lax.axis_size("tensor")
+    partial_rows, features = operands[0].shape
+    vmem = pl.BlockSpec(memory_space=pltpu.VMEM)
+    return pl.pallas_call(
+        functools.partial(kernel, count),
+        out_shape=out_shape,
+        in_specs=[vmem] * len(operands),
+        out_specs=[vmem] * len(out_shape),
+        scratch_shapes=line_scratch(count, partial_rows // count, features, spread),
+        compiler_params=pltpu.CompilerParams(
+            collective_id=ident, has_side_effects=True, vmem_limit_bytes=32 * 2**20
+        ),
+        cost_estimate=pl.CostEstimate(flops=10**9, bytes_accessed=60 * 2**20, transcendentals=0),
+        name=name,
+    )(*operands)
 
 
 def shifted(count, shift):
@@ -412,6 +754,23 @@
         came = lax.ppermute(rows, "tensor", shifted(count, shift))
         source = lax.rem(mine + count - shift, count)
         whole = lax.dynamic_update_slice_in_dim(whole, came, source * height, 0)
+    return whole
+
+
+def send_rows(rows):
+    count = lax.axis_size("tensor")
+    return [lax.ppermute(rows, "tensor", shifted(count, shift)) for shift in range(1, count)]
+
+
+def place_rows(rows, came):
+    count = lax.axis_size("tensor")
+    mine = lax.axis_index("tensor")
+    height = rows.shape[0]
+    whole = jnp.zeros((count * height, rows.shape[1]), rows.dtype)
+    whole = lax.dynamic_update_slice_in_dim(whole, rows, mine * height, 0)
+    for shift in range(1, count):
+        source = lax.rem(mine + count - shift, count)
+        whole = lax.dynamic_update_slice_in_dim(whole, came[shift - 1], source * height, 0)
     return whole
 
 
@@ -473,31 +832,37 @@
     conv_v = conv_value.astype(F32)
     gain_head = head_gain.astype(F32)[None, :]
     gains = lax.all_gather(jnp.stack([first_gain, second_gain]), "fsdp", axis=1, tiled=True).astype(F32)
-    gain_one, gain_two = gains[0], gains[1]
+    gain_one, gain_two = gains[:1], gains[1:]
     beta_piece = jnp.pad(piece(w_beta, 0), ((0, 0), (0, head_width - heads)))
     mix_full = gather_weights(
-        [piece(w_gating, 0), piece(w_query, 0), piece(w_key, 0), piece(w_value, 0), beta_piece]
+        [piece(w_gating, 0), piece(w_query, 0), piece(w_key, 0), piece(w_value, 0), beta_piece, piece(w_project, 1).T]
     )
     ffn_full = gather_weights(
-        [piece(w_project, 1).T, piece(w_gate, 0), piece(w_up, 0), piece(w_down, 1).T]
-    )
-    project_t = ffn_full[:, :width]
-    gate_up = ffn_full[:, width : width + 2 * units]
-    down_t = ffn_full[:, width + 2 * units :]
+        [piece(w_gate, 0), piece(w_up, 0), piece(w_down, 1).T]
+    )
+    project_t = mix_full[:, 4 * width + head_width :]
+    mix_full = mix_full[:, : 4 * width + head_width]
+    gate_up = ffn_full[:, : 2 * units]
+    down_t = ffn_full[:, 2 * units :]
 
     scale_one = rms_scale(input_float)
     normed1 = (input_float * scale_one * gain_one).astype(BF16)
     rows_one = gather_rows(normed1)
+    late_grad, rows_one = lax.optimization_barrier((output_grad, rows_one))
+    came = send_rows(late_grad)
     raw = dot(rows_one, mix_full)
     gated, mixed, solve, update, state = delta_forward(
         doc_starts, seq_lengths, raw, conv_q, conv_k, conv_v, gain_head
     )
-    attn_out = scatter_rows(dot_nt(gated, project_t).astype(BF16))
-    resid = input_float + attn_out
-    scale_two = rms_scale(resid)
-    normed2 = (resid * scale_two * gain_two).astype(BF16)
-    rows_two = gather_rows(normed2)
-    grad_rows = gather_rows(output_grad)
+    gated, came = lax.optimization_barrier((gated, came))
+    grad_rows = place_rows(output_grad, came)
+    attn_partial = dot_nt(gated, project_t).astype(BF16)
+    whole_rows = jax.ShapeDtypeStruct(rows_one.shape, BF16)
+    own_rows = jax.ShapeDtypeStruct(layer_input.shape, F32)
+    gain_sums = jax.ShapeDtypeStruct((1, layer_input.shape[1]), F32)
+    rows_two, resid = line_call(
+        middle_kernel, "middle", 2, True, (whole_rows, own_rows), (attn_partial, layer_input, gain_two)
+    )
     d_hidden = dot(grad_rows, down_t)
     both = dot(rows_two, gate_up)
     gate_val, up_val = both[:, :units], both[:, units:]
@@ -507,38 +872,41 @@
     d_gate = (d_hidden * up_val * gate_sig * (1.0 + gate_val * (1.0 - gate_sig))).astype(BF16)
     d_up = (d_hidden * silu_gate).astype(BF16)
     d_both = jnp.concatenate([d_gate, d_up], axis=1)
-    d_normed2 = scatter_rows(dot_nt(d_both, gate_up).astype(BF16))
-    down_shard = scatter_grads(dot_tn(grad_rows, hidden).astype(BF16))
-    ffn_out = scatter_rows(dot_nt(hidden, down_t).astype(BF16))
+    grad_down = dot_tn(grad_rows, hidden).astype(BF16)
+    down_shard = scatter_grads(grad_down)
+    grad_both = dot_tn(rows_two, d_both).astype(BF16)
+    both_shard = scatter_grads(grad_both)
+    d_partial, _, _ = lax.optimization_barrier(
+        (dot_nt(d_both, gate_up).astype(BF16), grad_down, grad_both)
+    )
+    d_attn, d_resid, grad_second = line_call(
+        turn_kernel, "turn", 3, True, (whole_rows, own_rows, gain_sums), (d_partial, resid, output_grad, gain_two)
+    )
+    ffn_partial, d_attn, down_shard = lax.optimization_barrier((dot_nt(hidden, down_t).astype(BF16), d_attn, down_shard))
+    ffn_out = scatter_rows(ffn_partial)
     result = (resid + ffn_out).astype(BF16)
-    both_shard = scatter_grads(dot_tn(rows_two, d_both).astype(BF16))
-    grad_second = jnp.sum(d_normed2 * resid * scale_two, axis=0)
-    d_resid = output_grad.astype(F32) + rms_back(resid, scale_two, gain_two, d_normed2)
-    d_attn = gather_rows(d_resid.astype(BF16))
     d_gated = dot(d_attn, project_t)
-    project_shard = scatter_grads(dot_tn(d_attn, gated).astype(BF16))
+    grad_project = dot_tn(d_attn, gated).astype(BF16)
     d_raw, d_conv, d_head = delta_backward(
         doc_starts, seq_lengths, raw, conv_q, conv_k, conv_v, gain_head, mixed, solve, update, state, d_gated
     )
-    d_normed1 = scatter_rows(dot_nt(d_raw, mix_full).astype(BF16))
-    mix_shard = scatter_grads(dot_tn(rows_one, d_raw).astype(BF16))
-    grad_first = jnp.sum(d_normed1 * input_float * scale_one, axis=0)
-    input_grad = d_resid + rms_back(input_float, scale_one, gain_one, d_normed1)
-    conv_totals = lax.psum(d_conv, ("dp", "fsdp"))
-    group = lax.axis_index("dp") * lax.axis_size("fsdp") + lax.axis_index("fsdp")
-    gain_size = grad_first.shape[0] // (replicas * lax.axis_size("fsdp"))
-    gain_totals = lax.psum(
-        jnp.concatenate([grad_first, grad_second, d_head[0]]), ("dp", "fsdp", "tensor")
-    )
-    features = grad_first.shape[0]
-
-    def gain_shard(first):
-        return lax.dynamic_slice_in_dim(gain_totals, first + group * gain_size, gain_size, 0)
-
+    grad_mix = dot_tn(rows_one, d_raw).astype(BF16)
+    mix_shard = scatter_grads(jnp.concatenate([grad_mix, grad_project], axis=1))
+    project_shard = mix_shard[:, 4 * width + head_width :]
+    mix_partial, result, both_shard = lax.optimization_barrier(
+        (dot_nt(d_raw, mix_full).astype(BF16), result, both_shard)
+    )
+    input_grad, grad_first = line_call(
+        last_kernel, "last", 4, False, (own_rows, gain_sums),
+        (mix_partial, layer_input, d_resid, gain_one),
+    )
+    gain_total, head_total, conv_totals = reduce_small(
+        jnp.concatenate([grad_first, grad_second], axis=0), d_head, d_conv
+    )
     return (
         result,
         input_grad,
-        gain_shard(0),
+        gain_total[0],
         mix_shard[:, width : 2 * width],
         mix_shard[:, 2 * width : 3 * width],
         mix_shard[:, 3 * width : 4 * width],
@@ -547,9 +915,9 @@
         conv_totals[:, :width],
         conv_totals[:, width : 2 * width],
         conv_totals[:, 2 * width :],
-        gain_totals[2 * features :],
+        head_total[0],
         project_shard.T,
-        gain_shard(features),
+        gain_total[1],
         both_shard[:, :units],
         both_shard[:, units:],
         down_shard.T,

time: 747 us -> 538 us (0.72)
  waiting for transfers between devices: 379 us -> 66.8 us
  Pallas kernels: 32.7 us -> 255 us
  blocking collectives: 79.8 us -> 5.43 us
  starting transfers between devices: 84.6 us -> 23.8 us
  local copies, waits for them, and re-layouts: 44.6 us -> 56.9 us
    pallas_call x0 -> x4, Pallas kernels: none -> 223 us  [the longest x3 214 us: line_call(): pl.pallas_call(functools.partial(kernel, count), out_shape=out_shape, in_...]
    ppermute x12 -> x3, waiting for transfers between devices: 118 us -> 27.7 us  [gather_rows(): came = lax.ppermute(rows, 'tensor', shifted(count, shift))]
    reduce_scatter x4 -> x3, waiting for transfers between devices: 86.8 us -> 0.01 us  [scatter_grads(): lax.psum_scatter(grads, ('dp', 'fsdp'), scatter_dimension=0, tiled=True)]
    all_gather x2, waiting for transfers between devices: 82.1 us -> 0.8 us  [gather_weights(): lax.all_gather(jnp.concatenate(pieces, axis=1), ('fsdp', 'dp'), axis=0, t...]
    psum x2 -> x0, blocking collectives: 74.3 us -> none  [the longest x1 50.4 us: body(): lax.psum(jnp.concatenate([grad_first, grad_second, d_head[0]]), ('dp', 'f...]
    ppermute x12 -> x3, waiting for transfers between devices: 91.8 us -> 19.9 us  [scatter_rows(): lax.ppermute(piece, 'tensor', shifted(count, shift)).astype(F32)]
    ppermute x12 -> x3, starting transfers between devices: 59 us -> 6.15 us  [gather_rows(): came = lax.ppermute(rows, 'tensor', shifted(count, shift))]
    ppermute x12 -> x3, starting transfers between devices: 24.9 us -> 4.06 us  [scatter_rows(): lax.ppermute(piece, 'tensor', shifted(count, shift)).astype(F32)]
  transfers between devices with their start and end apart: 30 -> 14, of which waited for: 17 -> 5; matrix products, arithmetic and copies ran while one was open for 12% -> 19% of each run, Pallas kernels for 4% -> 48%
where the time goes in v2:
time: 538 us; the launch traced here: 528 us
  Pallas kernels  255 us (47%)
  matrix products  87.5 us (16%)
  waiting for transfers between devices  66.8 us (12%)
  local copies, waits for them, and re-layouts  56.9 us (11%)
  starting transfers between devices  23.8 us (4%)
  other arithmetic  16.6 us (3%)
  between operations  15.4 us (3%)
  blocking collectives  5.43 us (1%)
    pallas_call x3, Pallas kernels, line_call(): pl.pallas_call(functools.partial(kernel, count), out_shape=out_shape, in_...  214 us
    dot_general x4, matrix products, dot_nt(): lax.dot_general(left, right, (((1,), (1,)), ((), ())), preferred_element_...  31.1 us
    dot_general x4, matrix products, dot(): return jnp.dot(left, right, preferred_element_type=F32)  30.9 us
    unnamed x80, local copies, waits for them, and re-layouts  28 us
    ppermute x3, waiting for transfers between devices, gather_rows(): came = lax.ppermute(rows, 'tensor', shifted(count, shift))  27.7 us
    dot_general x4, matrix products, dot_tn(): lax.dot_general(left, right, (((0,), (0,)), ((), ())), preferred_element_...  25.5 us
    ppermute x3, waiting for transfers between devices, scatter_rows(): lax.ppermute(piece, 'tensor', shifted(count, shift)).astype(F32)  19.9 us
    ppermute x3, waiting for transfers between devices, send_rows(): lax.ppermute(rows, 'tensor', shifted(count, shift))  18.3 us
  transfers between devices with their start and end apart: 14, of which 5 were waited for; matrix products, arithmetic and copies ran while one was open for 19% of the time, Pallas kernels for 48%

profile of v2, /device:TPU:0, one launch (start us, length us, event | category | flops | bytes accessed | tf_op | source)
XLA Modules:
  0.0 528.0 jit_solution(10891941239854154560)
XLA Ops:
  8.1 1.8 constant_dynamic-slice_fusion.8
  11.8 1.9 constant_dynamic-slice_fusion.6
  14.7 1.8 copy.49
  16.5 1.7 constant_dynamic-update-slice_fusion.3
  18.9 1.7 constant_dynamic-update-slice_fusion.1
  21.9 1.7 bitcast_dynamic-update-slice_fusion
  23.7 2.5 constant_dynamic-slice_fusion.3
  26.2 2.2 copy.52
  28.5 2.2 copy.51
  30.8 2.8 pad_maximum_fusion.2
  34.4 5.4 %all_gather.9 = bf16[2,2048]{1,0:T(2,128)(2,1)S(1)} all-gather(bf16[2,1024]{1,0:T(2,128)(2,1)S(1)} %pad_maximum_fusion.6), channel_id=1, replica_groups=mesh['dp'=4,'fsdp'=2,'tensor'=4] {'fsdp'}, dimensions={1}, use_global_device_ids=true | all-gather | bytes 12288 | tf_op jit(solution)/shard_map/all_gather | solution.py:834
  40.5 2.2 collective-permute-start
  42.8 2.6 collective-permute-start.1
  46.7 1.6 broadcast.25.clone.1
  49.9 7.9 %collective-permute-done = bf16[128,2048]{1,0:T(8,128)(2,1)S(1)} collective-permute-done((bf16[128,2048]{1,0:T(8,128)(2,1)S(1)}, bf16[128,2048]{1,0:T(8,128)(2,1)S(1)}, u32[]{:S(2)}, u32[]{:S(2)}) %collective-permute-start) | collective-permute-done | bytes 524320 | tf_op jit(solution)/shard_map/ppermute | solution.py:754
  58.6 19.8 %collective-permute-done.1 = bf16[128,2048]{1,0:T(8,128)(2,1)S(1)} collective-permute-done((bf16[128,2048]{1,0:T(8,128)(2,1)S(1)}, bf16[128,2048]{1,0:T(8,128)(2,1)S(1)}, u32[]{:S(2)}, u32[]{:S(2)}) %collective-permute-start.1) | collective-permute-done | bytes 524320 | tf_op jit(solution)/shard_map/ppermute | solution.py:754
  80.1 12.7 %collective-permute-start.5 = (bf16[128,2048]{1,0:T(8,128)(2,1)S(1)}, bf16[128,2048]{1,0:T(8,128)(2,1)}, u32[]{:S(2)}, u32[]{:S(2)}) collective-permute-start(bf16[128,2048]{1,0:T(8,128)(2,1)S(1)} %copy-done.5), channel_id=1, source_target_pairs={{0,3},{1,0},{2,1},{3,2},{4,7},{5,4},{6,5},{7,6},{8,11},{9,8},{10,9... | collective-permute-start | bytes 1572872 | tf_op jit(solution)/shard_map/ppermute | solution.py:762
  94.1 8.5 %fusion.6.raw_ref = f32[512,2176]{1,0:T(8,128)S(1)} fusion(bf16[512,2048]{1,0:T(8,128)(2,1)} %constant_dynamic-update-slice_fusion.8, bf16[2048,2688]{0,1:T(8,128)(2,1)} %all-gather.3.cloned.1.call-done), kind=kOutput, calls=%fused_computation.9 | convolution fusion | flops 4563402752 | bytes 15466496 | tf_op jit(solution)/shard_map/dot_general | solution.py:17
  102.7 17.1 %delta_forward.1 = (bf16[512,512]{1,0:T(8,128)(2,1)S(1)}, f32[512,512]{1,0:T(8,128)S(1)}, bf16[8,256,256]{2,1,0:T(8,128)(2,1)S(1)}, bf16[512,512]{1,0:T(8,128)(2,1)S(1)}, bf16[4,128,128]{2,1,0:T(8,128)(2,1)S(1)}) custom-call(s32[1,4]{1,0:T(1,128)S(1)} %copy-done.6, s32[1]{0:T(128)S(6)} %copy.68.length_ref, f32[512,2176]{1,0:T(8,128)S(1)} %fusion.6.raw_ref, ...), custom_call_target="tpu_custom_call" | custom-call | flops 6442450944 | bytes 12582912 | tf_op jit(solution)/shard_map/delta_forward/pallas_call | solution.py:197
  119.8 18.3 %collective-permute-done.4 = bf16[128,2048]{1,0:T(8,128)(2,1)} collective-permute-done((bf16[128,2048]{1,0:T(8,128)(2,1)S(1)}, bf16[128,2048]{1,0:T(8,128)(2,1)}, u32[]{:S(2)}, u32[]{:S(2)}) %collective-permute-start.4) | collective-permute-done | bytes 524320 | tf_op jit(solution)/shard_map/ppermute | solution.py:762
  138.1 2.9 convolution_convert_fusion.4.partial_ref
  141.1 77.5 %middle.1 = (bf16[512,2048]{1,0:T(8,128)(2,1)S(1)}, f32[128,2048]{1,0:T(8,128)S(1)}) custom-call(bf16[512,2048]{1,0:T(8,128)(2,1)S(1)} %convolution_convert_fusion.4.partial_ref, bf16[128,2048]{1,0:T(8,128)(2,1)S(1)} %copy-done.2, f32[1,2048]{1,0:T(1,128)S(1)} %get-tuple-element.113.gain_ref), custom_call_target="tpu_custom_call" | custom-call | flops 1000000000 | bytes 62914560 | tf_op jit(solution)/shard_map/middle/pallas_call | solution.py:729
  219.9 1.9 constant_dynamic-update-slice_fusion.6
  221.8 1.9 constant_dynamic-update-slice_fusion.5
  223.7 1.9 constant_dynamic-update-slice_fusion.4
  225.6 10.2 %fusion.2 = f32[512,2816]{1,0:T(8,128)S(1)} fusion(bf16[512,2048]{1,0:T(8,128)(2,1)} %copy-done.10, bf16[2048,4224]{0,1:T(8,128)(2,1)} %all-gather.5.cloned.1.call-done), kind=kOutput, calls=%fused_computation.5 | convolution fusion | flops 5905580032 | bytes 19398656 | tf_op jit(solution)/shard_map/dot_general | solution.py:17
  235.8 9.2 %multiply_convert_fusion.1 = (bf16[512,1408]{1,0:T(8,128)(2,1)}, bf16[512,1408]{1,0:T(8,128)(2,1)}, bf16[512,1408]{1,0:T(8,128)(2,1)S(1)}) fusion(f32[512,2816]{1,0:T(8,128)S(1)} %fusion.2, bf16[512,2048]{1,0:T(8,128)(2,1)} %constant_dynamic-update-slice_fusion.4, bf16[2048,4224]{0,1:T(8,128)(2,1)} %all-gather.5.cloned.1.call-done), kind=kOutput, calls=%fused_computation.23 | convolution fusion | flops 2963603456 | bytes 17956864 | tf_op jit(solution)/shard_map/dot_general | solution.py:17
  246.1 7.5 %convolution_convert_fusion.2 = bf16[2048,1408]{1,0:T(8,128)(2,1)} fusion(bf16[512,2048]{1,0:T(8,128)(2,1)} %constant_dynamic-update-slice_fusion.4, bf16[512,1408]{1,0:T(8,128)(2,1)S(1)} %get-tuple-element.100), kind=kOutput, calls=%fused_computation.11 | convolution fusion | flops 2955673600 | bytes 9306112 | tf_op jit(solution)/shard_map/dot_general | solution.py:25
  253.8 11.4 %convolution_convert_fusion.1 = bf16[2048,2816]{1,0:T(8,128)(2,1)} fusion(bf16[512,2048]{1,0:T(8,128)(2,1)} %copy-done.10, bf16[512,1408]{1,0:T(8,128)(2,1)} %get-tuple-element.99, bf16[512,1408]{1,0:T(8,128)(2,1)} %get-tuple-element.98), kind=kOutput, calls=%fused_computation.1 | convolution fusion | flops 5917114368 | bytes 16515072 | tf_op jit(solution)/shard_map/dot_general | solution.py:25
  265.3 10.4 %fusion.15.partial_ref = bf16[512,2048]{1,0:T(8,128)(2,1)S(1)} fusion(bf16[2048,4224]{0,1:T(8,128)(2,1)} %all-gather.5.cloned.1.call-done, bf16[512,1408]{1,0:T(8,128)(2,1)} %get-tuple-element.99, bf16[512,1408]{1,0:T(8,128)(2,1)} %get-tuple-element.98), kind=kOutput, calls=%fused_computation.17 | convolution fusion | flops 5912395776 | bytes 16515072 | tf_op jit(solution)/shard_map/dot_general | solution.py:21
  275.7 80.4 %turn.1 = (bf16[512,2048]{1,0:T(8,128)(2,1)S(1)}, f32[128,2048]{1,0:T(8,128)S(1)}, f32[1,2048]{1,0:T(1,128)S(1)}) custom-call(bf16[512,2048]{1,0:T(8,128)(2,1)S(1)} %fusion.15.partial_ref, f32[128,2048]{1,0:T(8,128)S(1)} %get-tuple-element.61.resid_ref, bf16[128,2048]{1,0:T(8,128)(2,1)S(1)} %copy-done.5, f32[1,2048]{1,0:T(1,128)S(1)} %get-tuple-element.113.gain_ref), custom_call_target="tpu_custom_call" | custom-call | flops 1000000000 | bytes 62914560 | tf_op jit(solution)/shard_map/turn/pallas_call | solution.py:729
  357.5 7.7 %fusion.18 = bf16[512,2048]{1,0:T(8,128)(2,1)} fusion(bf16[512,1408]{1,0:T(8,128)(2,1)S(1)} %copy-done.31, bf16[2048,4224]{0,1:T(8,128)(2,1)} %all-gather.5.cloned.1.call-done), kind=kOutput, calls=%fused_computation.20 | convolution fusion | flops 2953838592 | bytes 9306112 | tf_op jit(solution)/shard_map/dot_general | solution.py:21
  365.2 2.5 convert_element_type.92
  367.7 3.0 fusion.22.grad_ref
  370.7 15.3 %delta_backward.1 = (bf16[512,2176]{1,0:T(8,128)(2,1)S(1)}, f32[4,1536]{1,0:T(4,128)S(1)}, f32[1,128]{1,0:T(1,128)S(1)}) custom-call(s32[1,4]{1,0:T(1,128)S(1)} %copy-done.6, s32[1]{0:T(128)S(6)} %copy.68.length_ref, f32[512,2176]{1,0:T(8,128)} %copy-done.11, f32[4,512]{1,0:T(4,128)S(1)} %convert_element_type.81.conv_q_ref, ...), custom_call_target="tpu_custom_call" | custom-call | flops 3221225472 | bytes 16777216 | tf_op jit(solution)/shard_map/delta_backward/pallas_call | solution.py:368
  388.5 5.3 %convolution_convert_fusion = bf16[2048,2176]{1,0:T(8,128)(2,1)S(1)} fusion(bf16[512,2048]{1,0:T(8,128)(2,1)S(1)} %copy-done.23, bf16[512,2176]{1,0:T(8,128)(2,1)S(1)} %get-tuple-element.64), kind=kOutput, calls=%fused_computation | convolution fusion | flops 4567859200 | bytes 13238272 | tf_op jit(solution)/shard_map/dot_general | solution.py:25
  393.9 5.0 pad_maximum_fusion
  398.9 2.7 constant_dynamic-slice_fusion.2
  401.6 4.1 collective-permute-start.8
  405.7 10.0 %fusion.12.partial_ref = bf16[512,2048]{1,0:T(8,128)(2,1)} fusion(bf16[512,2176]{1,0:T(8,128)(2,1)S(1)} %copy-done.13, bf16[2048,2688]{0,1:T(8,128)(2,1)} %all-gather.3.cloned.1.call-done), kind=kOutput, calls=%fused_computation.16 | convolution fusion | flops 4564451328 | bytes 13238272 | tf_op jit(solution)/shard_map/dot_general | solution.py:21
  415.7 3.3 copy.45
  419.0 19.9 %collective-permute-done.7 = bf16[128,2048]{1,0:T(8,128)(2,1)} collective-permute-done((bf16[128,2048]{1,0:T(8,128)(2,1)}, bf16[128,2048]{1,0:T(8,128)(2,1)}, u32[]{:S(2)}, u32[]{:S(2)}) %collective-permute-start.7) | collective-permute-done | bytes 524320 | tf_op jit(solution)/shard_map/ppermute | solution.py:785
  438.8 2.7 add_convert_fusion
  441.5 1.7 convert_element_type.99
  443.5 56.2 %last.1 = (f32[128,2048]{1,0:T(8,128)S(1)}, f32[1,2048]{1,0:T(1,128)S(1)}) custom-call(bf16[512,2048]{1,0:T(8,128)(2,1)S(1)} %copy-done.7, bf16[128,2048]{1,0:T(8,128)(2,1)S(1)} %copy-done.2, f32[128,2048]{1,0:T(8,128)S(1)} %get-tuple-element.68.d_resid_ref, f32[1,2048]{1,0:T(1,128)S(1)} %get-tuple-element.114.gain_ref), custom_call_target="tpu_custom_call" | custom-call | flops 1000000000 | bytes 62914560 | tf_op jit(solution)/shard_map/last/pallas_call | solution.py:729
  500.8 9.0 %reduce_small.1 = (f32[2,256]{1,0:T(2,128)S(1)}, f32[1,128]{1,0:T(1,128)S(1)}, f32[4,1536]{1,0:T(4,128)S(1)}) custom-call(f32[2,2048]{1,0:T(2,128)S(1)} %pad_maximum_fusion.5.gain_ref, f32[1,128]{1,0:T(1,128)S(1)} %get-tuple-element.72.head_ref, f32[4,1536]{1,0:T(4,128)S(1)} %get-tuple-element.73.conv_ref), custom_call_target="tpu_custom_call" | custom-call | tf_op jit(solution)/shard_map/reduce_small/pallas_call | solution.py:478
  510.9 1.8 fusion.31
  516.8 2.8 fusion.32
  (124 shorter events, 28.2 us)
Async XLA Ops:
  7.2 23.5 %copy-start = (bf16[1408,1024]{1,0:T(8,128)(2,1)S(1)}, bf16[1408,1024]{1,0:T(8,128)(2,1)}, u32[]{:S(2)}) copy-start(bf16[1408,1024]{1,0:T(8,128)(2,1)} %param.34) | copy-start | bytes 8650756
  7.2 86.9 %all-gather.3.cloned.1.call-start = ((), (), s32[]{:S(2)}) async-start(), calls=%async_computation.3 | async-start | bytes 12386304 | tf_op jit(solution)/shard_map/all_gather | solution.py:790
  23.6 202.0 %all-gather.5.cloned.1.call-start = ((), (), s32[]{:S(2)}) async-start(), calls=%async_computation.4 | async-start | bytes 19464192 | tf_op jit(solution)/shard_map/all_gather | solution.py:790
  33.6 0.7 copy-start.27
  33.6 0.7 copy-start.28
  33.6 6.2 %copy-start.2 = (bf16[128,2048]{1,0:T(8,128)(2,1)S(1)}, bf16[128,2048]{1,0:T(8,128)(2,1)}, u32[]{:S(2)}) copy-start(bf16[128,2048]{1,0:T(8,128)(2,1)} %input_ref.3) | copy-start | bytes 1572868
  33.7 331.5 %reduce-scatter.4.cloned.1.call-start = ((), (), s32[]{:S(2)}) async-start(), calls=%async_computation.5 | async-start | bytes 6488064 | tf_op jit(solution)/shard_map/reduce_scatter | solution.py:794
  40.3 8.0 %copy-start.5 = (bf16[128,2048]{1,0:T(8,128)(2,1)S(1)}, bf16[128,2048]{1,0:T(8,128)(2,1)}, u32[]{:S(2)}) copy-start(bf16[128,2048]{1,0:T(8,128)(2,1)} %grad_ref.1) | copy-start | bytes 1572868
  40.3 8.8 %copy-start.29 = (bf16[128]{0:T(256)(128)(2,1)S(1)}, bf16[128]{0:T(256)(128)(2,1)}, u32[]{:S(2)}) copy-start(bf16[128]{0:T(256)(128)(2,1)} %param.29) | copy-start | bytes 772
  40.3 9.5 %copy-start.24 = (bf16[4,512]{1,0:T(4,128)(2,1)S(1)}, bf16[4,512]{1,0:T(4,128)(2,1)}, u32[]{:S(2)}) copy-start(bf16[4,512]{1,0:T(4,128)(2,1)} %param.26) | copy-start | bytes 12292
  40.3 9.5 %copy-start.25 = (bf16[4,512]{1,0:T(4,128)(2,1)S(1)}, bf16[4,512]{1,0:T(4,128)(2,1)}, u32[]{:S(2)}) copy-start(bf16[4,512]{1,0:T(4,128)(2,1)} %param.27) | copy-start | bytes 12292
  40.3 9.5 %copy-start.26 = (bf16[4,512]{1,0:T(4,128)(2,1)S(1)}, bf16[4,512]{1,0:T(4,128)(2,1)}, u32[]{:S(2)}) copy-start(bf16[4,512]{1,0:T(4,128)(2,1)} %param.28) | copy-start | bytes 12292
  40.5 7.7 %copy-start.22 = (bf16[512,2048]{1,0:T(8,128)(2,1)}, bf16[512,2048]{1,0:T(8,128)(2,1)S(1)}, u32[]{:S(2)}) copy-start(bf16[512,2048]{1,0:T(8,128)(2,1)S(1)} %get-tuple-element.96) | copy-start | bytes 6291460
  40.5 17.2 %collective-permute-start = (bf16[128,2048]{1,0:T(8,128)(2,1)S(1)}, bf16[128,2048]{1,0:T(8,128)(2,1)S(1)}, u32[]{:S(2)}, u32[]{:S(2)}) collective-permute-start(bf16[128,2048]{1,0:T(8,128)(2,1)S(1)} %get-tuple-element.97), channel_id=1, source_target_pairs={{0,1},{1,2},{2,3},{3,0},{4,5},{5,6},{6,7},{7,4},{8,9},{9,10},{10,1... | collective-permute-start | bytes 1572872 | tf_op jit(solution)/shard_map/ppermute | solution.py:754
  42.8 35.6 %collective-permute-start.1 = (bf16[128,2048]{1,0:T(8,128)(2,1)S(1)}, bf16[128,2048]{1,0:T(8,128)(2,1)S(1)}, u32[]{:S(2)}, u32[]{:S(2)}) collective-permute-start(bf16[128,2048]{1,0:T(8,128)(2,1)S(1)} %get-tuple-element.97), channel_id=1, source_target_pairs={{0,2},{1,3},{2,0},{3,1},{4,6},{5,7},{6,4},{7,5},{8,10},{9,11},{10,... | collective-permute-start | bytes 1572872 | tf_op jit(solution)/shard_map/ppermute | solution.py:754
  45.4 33.9 %collective-permute-start.2 = (bf16[128,2048]{1,0:T(8,128)(2,1)S(1)}, bf16[128,2048]{1,0:T(8,128)(2,1)S(1)}, u32[]{:S(2)}, u32[]{:S(2)}) collective-permute-start(bf16[128,2048]{1,0:T(8,128)(2,1)S(1)} %get-tuple-element.97), channel_id=1, source_target_pairs={{0,3},{1,0},{2,1},{3,2},{4,7},{5,4},{6,5},{7,6},{8,11},{9,8},{10,9... | collective-permute-start | bytes 1572872 | tf_op jit(solution)/shard_map/ppermute | solution.py:754
  80.1 22.5 %copy-start.6 = (s32[1,4]{1,0:T(1,128)S(1)}, s32[1,4]{1,0:T(1,128)}, u32[]{:S(2)}) copy-start(s32[1,4]{1,0:T(1,128)} %starts_ref.3) | copy-start | bytes 52
  80.1 39.7 %collective-permute-start.5 = (bf16[128,2048]{1,0:T(8,128)(2,1)S(1)}, bf16[128,2048]{1,0:T(8,128)(2,1)}, u32[]{:S(2)}, u32[]{:S(2)}) collective-permute-start(bf16[128,2048]{1,0:T(8,128)(2,1)S(1)} %copy-done.5), channel_id=1, source_target_pairs={{0,3},{1,0},{2,1},{3,2},{4,7},{5,4},{6,5},{7,6},{8,11},{9,8},{10,9... | collective-permute-start | bytes 1572872 | tf_op jit(solution)/shard_map/ppermute | solution.py:762
  92.8 45.4 %collective-permute-start.4 = (bf16[128,2048]{1,0:T(8,128)(2,1)S(1)}, bf16[128,2048]{1,0:T(8,128)(2,1)}, u32[]{:S(2)}, u32[]{:S(2)}) collective-permute-start(bf16[128,2048]{1,0:T(8,128)(2,1)S(1)} %copy-done.5), channel_id=1, source_target_pairs={{0,2},{1,3},{2,0},{3,1},{4,6},{5,7},{6,4},{7,5},{8,10},{9,11},{10,... | collective-permute-start | bytes 1572872 | tf_op jit(solution)/shard_map/ppermute | solution.py:762
  92.8 45.4 %collective-permute-start.3 = (bf16[128,2048]{1,0:T(8,128)(2,1)S(1)}, bf16[128,2048]{1,0:T(8,128)(2,1)}, u32[]{:S(2)}, u32[]{:S(2)}) collective-permute-start(bf16[128,2048]{1,0:T(8,128)(2,1)S(1)} %copy-done.5), channel_id=1, source_target_pairs={{0,1},{1,2},{2,3},{3,0},{4,5},{5,6},{6,7},{7,4},{8,9},{9,10},{10,1... | collective-permute-start | bytes 1572872 | tf_op jit(solution)/shard_map/ppermute | solution.py:762
  102.7 17.1 %copy-start.11 = (f32[512,2176]{1,0:T(8,128)}, f32[512,2176]{1,0:T(8,128)S(1)}, u32[]{:S(2)}) copy-start(f32[512,2176]{1,0:T(8,128)S(1)} %fusion.6.raw_ref) | copy-start | bytes 13369348
  119.8 21.3 %copy-start.14 = (bf16[512,512]{1,0:T(8,128)(2,1)}, bf16[512,512]{1,0:T(8,128)(2,1)S(1)}, u32[]{:S(2)}) copy-start(bf16[512,512]{1,0:T(8,128)(2,1)S(1)} %get-tuple-element.55) | copy-start | bytes 1572868
  119.8 21.3 %copy-start.16 = (f32[512,512]{1,0:T(8,128)}, f32[512,512]{1,0:T(8,128)S(1)}, u32[]{:S(2)}) copy-start(f32[512,512]{1,0:T(8,128)S(1)} %get-tuple-element.49.mixed_ref) | copy-start | bytes 3145732
  119.8 21.3 %copy-start.18 = (bf16[8,256,256]{2,1,0:T(8,128)(2,1)}, bf16[8,256,256]{2,1,0:T(8,128)(2,1)S(1)}, u32[]{:S(2)}) copy-start(bf16[8,256,256]{2,1,0:T(8,128)(2,1)S(1)} %get-tuple-element.50.solve_ref) | copy-start | bytes 3145732
  119.8 21.3 %copy-start.20 = (bf16[512,512]{1,0:T(8,128)(2,1)}, bf16[512,512]{1,0:T(8,128)(2,1)S(1)}, u32[]{:S(2)}) copy-start(bf16[512,512]{1,0:T(8,128)(2,1)S(1)} %get-tuple-element.51.update_ref) | copy-start | bytes 1572868
  218.6 1.3 copy-start.10
  245.0 1.1 copy-start.30
  253.6 187.9 %reduce-scatter.6.cloned.1.call-start = ((), (), s32[]{:S(2)}) async-start(), calls=%async_computation.6 | async-start | bytes 12976128 | tf_op jit(solution)/shard_map/reduce_scatter | solution.py:794
  265.3 247.4 %reduce-scatter.8.cloned.1.call-start = ((), (), s32[]{:S(2)}) async-start(), calls=%async_computation.7 | async-start | bytes 12386304 | tf_op jit(solution)/shard_map/reduce_scatter | solution.py:794
  275.7 81.8 %copy-start.31 = (bf16[512,1408]{1,0:T(8,128)(2,1)S(1)}, bf16[512,1408]{1,0:T(8,128)(2,1)}, u32[]{:S(2)}) copy-start(bf16[512,1408]{1,0:T(8,128)(2,1)} %copy-done.30) | copy-start | bytes 4325380
  356.1 1.3 copy-start.8
  365.2 2.5 copy-start.9
  367.7 3.0 copy-start.17
  367.7 3.1 copy-start.19
  367.7 3.1 copy-start.21
  370.7 15.4 %copy-start.15 = (bf16[512,512]{1,0:T(8,128)(2,1)S(1)}, bf16[512,512]{1,0:T(8,128)(2,1)}, u32[]{:S(2)}) copy-start(bf16[512,512]{1,0:T(8,128)(2,1)} %copy-done.14) | copy-start | bytes 1572868
  386.1 1.5 copy-start.12
  386.1 2.4 copy-start.23
  398.9 6.8 %copy-start.13 = (bf16[512,2176]{1,0:T(8,128)(2,1)S(1)}, bf16[512,2176]{1,0:T(8,128)(2,1)}, u32[]{:S(2)}) copy-start(bf16[512,2176]{1,0:T(8,128)(2,1)} %copy-done.12) | copy-start | bytes 6684676
  401.6 17.3 %collective-permute-start.6 = (bf16[128,2048]{1,0:T(8,128)(2,1)}, bf16[128,2048]{1,0:T(8,128)(2,1)}, u32[]{:S(2)}, u32[]{:S(2)}) collective-permute-start(bf16[128,2048]{1,0:T(8,128)(2,1)} %get-tuple-element.103), channel_id=1, source_target_pairs={{0,1},{1,2},{2,3},{3,0},{4,5},{5,6},{6,7},{7,4},{8,9},{9,10},{10,1... | collective-permute-start | bytes 1572872 | tf_op jit(solution)/shard_map/ppermute | solution.py:785
  401.6 17.3 %collective-permute-start.8 = (bf16[128,2048]{1,0:T(8,128)(2,1)}, bf16[128,2048]{1,0:T(8,128)(2,1)}, u32[]{:S(2)}, u32[]{:S(2)}) collective-permute-start(bf16[128,2048]{1,0:T(8,128)(2,1)} %get-tuple-element.104), channel_id=1, source_target_pairs={{0,3},{1,0},{2,1},{3,2},{4,7},{5,4},{6,5},{7,6},{8,11},{9,8},{10,9... | collective-permute-start | bytes 1572872 | tf_op jit(solution)/shard_map/ppermute | solution.py:785
  405.7 33.2 %collective-permute-start.7 = (bf16[128,2048]{1,0:T(8,128)(2,1)}, bf16[128,2048]{1,0:T(8,128)(2,1)}, u32[]{:S(2)}, u32[]{:S(2)}) collective-permute-start(bf16[128,2048]{1,0:T(8,128)(2,1)} %get-tuple-element.105), channel_id=1, source_target_pairs={{0,2},{1,3},{2,0},{3,1},{4,6},{5,7},{6,4},{7,5},{8,10},{9,11},{10,... | collective-permute-start | bytes 1572872 | tf_op jit(solution)/shard_map/ppermute | solution.py:785
  441.5 2.0 copy-start.7
  499.8 1.0 copy-start.3
  516.8 2.8 copy-start.4
  516.8 4.2 copy-start.1
Sparse Core Ops, SparseCore 0:
  23.7 70.3 all-gather.2
  96.0 95.4 all-gather.4
  253.7 58.2 reduce-scatter.3
  315.8 86.7 reduce-scatter.5
  406.5 83.9 reduce-scatter.7

commit v3 on v2

--- a/solution.py
+++ b/solution.py
@@ -3,6 +3,7 @@
 from jax import lax
 from jax.experimental import pallas as pl
 from jax.experimental.pallas import tpu as pltpu
+from jax.experimental.layout import Layout, with_layout_constraint
 from jax.sharding import PartitionSpec as P
 
 KERNEL = 4
@@ -11,6 +12,19 @@
 MESH = pl.DeviceIdType.MESH
 F32 = jnp.float32
 BF16 = jnp.bfloat16
+
+
+def coordinates():
+    replica = lax.axis_index("pair") * 2 + lax.axis_index("core")
+    return replica, lax.axis_index("fsdp"), lax.axis_index("tensor")
+
+
+def extents():
+    return lax.axis_size("pair") * 2, lax.axis_size("fsdp"), lax.axis_size("tensor")
+
+
+def device(replica, shard, place):
+    return (lax.div(replica, 2), lax.rem(replica, 2), shard, place)
 
 
 def dot(left, right):
@@ -395,16 +409,16 @@
     line_gain, line_head, stage, group_gain, group_conv,
     line_send, line_recv, group_send, group_recv,
 ):
-    dp, fsdp, tensor = (lax.axis_index(name) for name in ("dp", "fsdp", "tensor"))
+    dp, fsdp, tensor = coordinates()
     group = dp * fsdp_size + fsdp
     size = gain_out.shape[1]
 
     def line_peer(shift):
-        return (dp, fsdp, lax.rem(tensor + shift, line_size))
+        return device(dp, fsdp, lax.rem(tensor + shift, line_size))
 
     def group_peer(shift):
         peer = lax.rem(group + shift, group_size)
-        return peer, (lax.div(peer, fsdp_size), lax.rem(peer, fsdp_size), tensor)
+        return peer, device(lax.div(peer, fsdp_size), lax.rem(peer, fsdp_size), tensor)
 
     barrier = pltpu.get_barrier_semaphore()
     for shift in range(1, line_size):
@@ -469,8 +483,8 @@
 
 
 def reduce_small(gain, head, conv):
-    fsdp_size, line_size = lax.axis_size("fsdp"), lax.axis_size("tensor")
-    group_size = lax.axis_size("dp") * fsdp_size
+    replicas, fsdp_size, line_size = extents()
+    group_size = replicas * fsdp_size
     size = gain.shape[1] // group_size
     pad = max(size, head.shape[1])
     vmem = pl.BlockSpec(memory_space=pltpu.VMEM)
@@ -500,7 +514,104 @@
     )(gain, head, conv)
 
 
+def plan(count, parts, sums, rows, shared, unit):
+    latency, backlog, add, end = 1.5, 1.5, 0.15 + 0.8 / parts, 0.5 + 3.0 / parts
+    rank = {"spread": 0, "relay": 0, "finish": 1, "forward": 2, "inject": 3}
+    clock = [0.0] * count
+    free, come = {}, [{} for _ in range(count)]
+    todo = [set() for _ in range(count)]
+    done = [0] * count
+    at = [0] * count
+    tasks = [[[] for _ in range(len(shared) + 1)] for _ in range(count)]
+    own_finish = sums and not any(isinstance(step, tuple) for step in shared)
+    for place in range(count):
+        for part in range(parts):
+            for step in (1, -1):
+                behind = 0 <= place - step < count
+                for slot in range(count - 1) if sums else ():
+                    owner = count - 1 - slot if step > 0 else slot
+                    if (owner - place) * step > 0:
+                        todo[place].add(("forward" if behind else "inject", step, slot, part))
+                for distance in range(1, count) if rows else ():
+                    if 0 <= place - step * distance < count:
+                        todo[place].add(("relay", step, distance, part))
+            if rows and not sums:
+                todo[place].add(("spread", 0, 0, part))
+            if own_finish:
+                todo[place].add(("finish", 0, 0, part))
+
+    def ready(place, task):
+        kind, step, slot, part = task
+        if kind == "inject":
+            return max(0.0, free.get((place, step), 0.0) - backlog * unit)
+        if kind == "spread":
+            return max([0.0] + [free.get((place, way), 0.0) - backlog * unit for way in (1, -1)])
+        if kind == "forward":
+            return come[place].get(("sum", step, slot, part))
+        if kind == "relay":
+            return come[place].get(("row", step, slot, part))
+        if part != done[place]:
+            return None
+        times = [0.0]
+        for way in (1, -1):
+            if 0 <= place - way < count:
+                times.append(come[place].get(("sum", way, count - 1 - place if way > 0 else place, part)))
+        return None if None in times else max(times)
+
+    def send(place, step, key):
+        if 0 <= place + step < count:
+            free[place, step] = max(clock[place], free.get((place, step), 0.0)) + unit
+            come[place + step][key] = free[place, step] + latency
+
+    def choices(place):
+        found = [(ready(place, task), rank[task[0]], task[3], task[2], task[1], task) for task in todo[place]]
+        found = [(max(clock[place], entry[0]),) + entry[1:] for entry in found if entry[0] is not None]
+        if at[place] < len(shared):
+            step = shared[at[place]]
+            when = ready(place, ("finish", 0, 0, step[1])) if isinstance(step, tuple) else clock[place]
+            if when is not None:
+                found.append((max(when, clock[place]), 1 if isinstance(step, tuple) else 9, 0, 0, 0, step))
+        return min(found, key=lambda entry: entry[:5]) if found else None
+
+    while True:
+        best = None
+        for place in range(count):
+            choice = choices(place)
+            if choice is not None and (best is None or choice[0] < best[0][0]):
+                best = (choice, place)
+        if best is None:
+            return max(clock), tasks
+        choice, place = best
+        clock[place] = choice[0]
+        task = choice[5]
+        if isinstance(task, float):
+            clock[place] += task
+            at[place] += 1
+            continue
+        if len(task) == 2:
+            at[place] += 1
+        else:
+            todo[place].discard(task)
+            tasks[place][at[place]].append(task)
+        kind, step, slot, part = task if len(task) == 4 else ("finish", 0, 0, task[1])
+        if kind in ("inject", "forward"):
+            clock[place] += add if kind == "forward" else 0.02
+            send(place, step, ("sum", step, slot, part))
+        elif kind == "relay":
+            clock[place] += 0.05
+            if slot < count - 1:
+                send(place, step, ("row", step, slot + 1, part))
+        else:
+            if kind == "finish":
+                done[place] += 1
+                clock[place] += end
+            if rows:
+                for way in (1, -1):
+                    send(place, way, ("row", way, 1, part))
+
+
 PARTS = 4
+UNIT = 11.3
 
 
 def rms_scale(values):
@@ -515,31 +626,35 @@
 
 class Line:
 
-    def __init__(self, count, rows, sums, rows_out):
-        self.count = count
-        self.rows = rows
-        self.part = rows // PARTS
-        self.sums = sums
-        self.rows_out = rows_out
-        self.dp, self.fsdp, self.place = (lax.axis_index(name) for name in ("dp", "fsdp", "tensor"))
-
-    def device(self, step):
-        return (self.dp, self.fsdp, self.place + step)
-
-    def ahead(self, step):
-        return self.place < self.count - 1 if step > 0 else self.place > 0
-
-    def behind(self, step):
-        return self.ahead(-step)
-
-    def barrier(self):
+    def __init__(self, count, rows, scratch, shared, sums, spreads, parts=PARTS):
+        self.count, self.rows, self.parts = count, rows, parts
+        self.part = rows // parts
+        scratch = list(scratch)
+        self.sums, self.sends = {}, {}
+        if sums:
+            for step in (1, -1):
+                self.sums[step] = [scratch.pop(0) for _ in range(4)]
+            self.total_ref = scratch.pop(0)
+        if spreads:
+            for step in (1, -1):
+                self.sends[step] = [scratch.pop(0) for _ in range(2)]
+        self.replica, self.shard, self.place = coordinates()
+        self.tasks = plan(count, parts, sums, spreads, shared, UNIT / parts)[1]
+        self.started = [[] for _ in range(count)]
+        self.partial_ref = self.rows_ref = self.source_ref = self.finish = None
+
+    def greet(self, others=()):
         barrier = pltpu.get_barrier_semaphore()
         for step in (1, -1):
-            @pl.when(self.ahead(step))
+            @pl.when(self.place < self.count - 1 if step > 0 else self.place > 0)
             def _():
-                pl.semaphore_signal(barrier, inc=1, device_id=self.device(step), device_id_type=MESH)
+                pl.semaphore_signal(
+                    barrier, inc=1, device_id=device(self.replica, self.shard, self.place + step), device_id_type=MESH
+                )
+        for other in others:
+            pl.semaphore_signal(barrier, inc=1, device_id=other, device_id_type=MESH)
         ends = (self.place == 0).astype(jnp.int32) + (self.place == self.count - 1).astype(jnp.int32)
-        pl.semaphore_wait(barrier, 2 - ends)
+        pl.semaphore_wait(barrier, 2 - ends + len(others))
 
     def span(self, owner, part):
         return pl.ds(pl.multiple_of(owner * self.rows + part * self.part, self.part), self.part)
@@ -549,156 +664,141 @@
         return pltpu.make_async_remote_copy(
             src_ref=source, dst_ref=recv.at[slot, part],
             send_sem=send_sem.at[slot, part], recv_sem=recv_sem.at[slot, part],
-            device_id=self.device(step), device_id_type=MESH,
+            device_id=device(self.replica, self.shard, self.place + step), device_id_type=MESH,
         )
 
-    def owner_of(self, step, slot):
-        return self.count - 1 - slot if step > 0 else slot
-
-    def inject(self, partial_ref, part):
+    def row_copy(self, step, owner, distance, part, source=None):
+        send_sem, recv_sem = self.sends[step]
+        where = self.rows_ref.at[self.span(owner, part)]
+        return pltpu.make_async_remote_copy(
+            src_ref=where if source is None else source, dst_ref=where,
+            send_sem=send_sem.at[distance, part], recv_sem=recv_sem.at[distance, part],
+            device_id=device(self.replica, self.shard, self.place + step), device_id_type=MESH,
+        )
+
+    def emit(self, place, task):
+        kind, step, slot, part = task
+        if kind in ("inject", "forward"):
+            recv, send, _, _ = self.sums[step]
+            owner = self.count - 1 - slot if step > 0 else slot
+            source = self.partial_ref.at[self.span(owner, part)]
+            if kind == "forward":
+                self.sum_copy(source, step, slot, part).wait_recv()
+                mine = self.partial_ref[self.span(owner, part), :].astype(F32)
+                send[slot, part] = (mine + recv[slot, part].astype(F32)).astype(BF16)
+                source = send.at[slot, part]
+            copy = self.sum_copy(source, step, slot, part)
+            copy.start()
+        elif kind == "relay":
+            owner = place - step * slot
+            self.row_copy(step, owner, slot - 1, part).wait_recv()
+            if slot < self.count - 1 and 0 <= place + step < self.count:
+                self.row_copy(step, owner, slot, part).start()
+        elif kind == "spread":
+            self.spread_from(place, part)
+        else:
+            self.collect(part)
+            self.finish(part, pl.ds(part * self.part, self.part), None)
+
+    def spread_from(self, place, part):
         for step in (1, -1):
-            @pl.when(jnp.logical_not(self.behind(step)))
-            def _():
-                for slot in range(self.count - 1):
-                    owner = self.owner_of(step, slot)
-                    self.sum_copy(partial_ref.at[self.span(owner, part)], step, slot, part).start()
-
-    def passes(self, step, slot):
-        owner = self.owner_of(step, slot)
-        further = self.place < owner if step > 0 else self.place > owner
-        return jnp.logical_and(self.behind(step), further)
-
-    def forward(self, partial_ref, part):
-        for slot in range(self.count - 1):
-            for step in (1, -1):
-                recv, send, _, _ = self.sums[step]
-
-                @pl.when(self.passes(step, slot))
+            if 0 <= place + step < self.count:
+                source = None if self.source_ref is None else self.source_ref.at[pl.ds(part * self.part, self.part)]
+                self.row_copy(step, place, 0, part, source).start()
+
+    def run(self, index):
+        for place in range(self.count):
+            tasks = self.tasks[place][index]
+            if tasks:
+                @pl.when(self.place == place)
                 def _():
-                    self.sum_copy(send.at[slot, part], step, slot, part).wait_recv()
-                    mine = partial_ref[self.span(self.owner_of(step, slot), part), :].astype(F32)
-                    send[slot, part] = (mine + recv[slot, part].astype(F32)).astype(BF16)
-                    self.sum_copy(send.at[slot, part], step, slot, part).start()
-
-    def collect(self, partial_ref, total_ref, part):
-        total_ref[...] = partial_ref[self.span(self.place, part), :].astype(F32)
+                    for task in tasks:
+                        self.emit(place, task)
+
+    def run_at(self, base, step, count):
+        for index in range(count):
+            if any(tasks[base + index] for tasks in self.tasks):
+                @pl.when(step == index)
+                def _():
+                    self.run(base + index)
+
+    def collect(self, part):
+        self.total_ref[...] = self.partial_ref[self.span(self.place, part), :].astype(F32)
         for step in (1, -1):
             recv, send, _, _ = self.sums[step]
             slot = self.count - 1 - self.place if step > 0 else self.place
 
-            @pl.when(self.behind(step))
+            @pl.when(self.place > 0 if step > 0 else self.place < self.count - 1)
             def _():
                 self.sum_copy(send.at[0, part], step, slot, part).wait_recv()
-                total_ref[...] += recv[slot, part].astype(F32)
-
-    def drain_sums(self, partial_ref):
-        for part in range(PARTS):
-            for step in (1, -1):
-                _, send, _, _ = self.sums[step]
-                for slot in range(self.count - 1):
-                    owner = self.owner_of(step, slot)
-                    further = self.place < owner if step > 0 else self.place > owner
-
-                    @pl.when(further)
+                self.total_ref[...] += recv[slot, part].astype(F32)
+
+    def finish_all(self):
+        for part in range(self.parts):
+            self.run(part)
+            self.collect(part)
+            self.finish(part, pl.ds(part * self.part, self.part), self.span(self.place, part))
+            if self.sends:
+                for place in range(self.count):
+                    @pl.when(self.place == place)
                     def _():
-                        self.sum_copy(send.at[slot, part], step, slot, part).wait_send()
-
-    def row_copy(self, ref, step, owner, distance, part):
-        send_sem, recv_sem = self.rows_out[step]
-        where = ref.at[self.span(owner, part)]
-        return pltpu.make_async_remote_copy(
-            src_ref=where, dst_ref=where,
-            send_sem=send_sem.at[distance, part], recv_sem=recv_sem.at[distance, part],
-            device_id=self.device(step), device_id_type=MESH,
-        )
-
-    def spread(self, ref, part):
-        for step in (1, -1):
-            @pl.when(self.ahead(step))
+                        self.spread_from(place, part)
+        self.run(self.parts)
+        self.drain()
+
+    def drain(self):
+        for place in range(self.count):
+            @pl.when(self.place == place)
             def _():
-                self.row_copy(ref, step, self.place, 0, part).start()
-
-    def relay(self, ref, distance, part):
-        for step in (1, -1):
-            owner = self.place - step * distance
-            inside = owner >= 0 if step > 0 else owner < self.count
-
-            @pl.when(inside)
-            def _():
-                self.row_copy(ref, step, owner, distance - 1, part).wait_recv()
-
-                if distance < self.count - 1:
-                    @pl.when(self.ahead(step))
-                    def _():
-                        self.row_copy(ref, step, owner, distance, part).start()
-
-    def drain_rows(self, ref):
-        for part in range(PARTS):
-            for step in (1, -1):
-                for distance in range(self.count - 1):
-                    owner = self.place - step * distance
-                    inside = owner >= 0 if step > 0 else owner < self.count
-
-                    @pl.when(jnp.logical_and(inside, self.ahead(step)))
-                    def _():
-                        self.row_copy(ref, step, owner, distance, part).wait_send()
-
-
-def line_scratch(count, rows, features, spread):
+                for part in range(self.parts):
+                    for step in (1, -1):
+                        if self.sums:
+                            send = self.sums[step][1]
+                            for slot in range(self.count - 1):
+                                owner = self.count - 1 - slot if step > 0 else slot
+                                if (owner - place) * step > 0:
+                                    self.sum_copy(send.at[slot, part], step, slot, part).wait_send()
+                        if self.sends and 0 <= place + step < self.count:
+                            for distance in range(self.count - 1):
+                                owner = place - step * distance
+                                if 0 <= owner < self.count:
+                                    self.row_copy(step, owner, distance, part).wait_send()
+
+
+def line_scratch(count, rows, features, sums, spreads, parts=PARTS):
     dma = pltpu.SemaphoreType.DMA
-    slots = (count - 1, PARTS)
+    slots = (count - 1, parts)
     scratch = []
-    for _ in range(2):
-        scratch += [pltpu.VMEM(slots + (rows // PARTS, features), BF16)] * 2 + [dma(slots)] * 2
-    if spread:
+    if sums:
+        for _ in range(2):
+            scratch += [pltpu.VMEM(slots + (rows // parts, features), BF16)] * 2 + [dma(slots)] * 2
+        scratch.append(pltpu.VMEM((rows // parts, features), F32))
+    if spreads:
         scratch += [dma(slots)] * 4
-    return scratch + [pltpu.VMEM((rows // PARTS, features), F32)]
-
-
-def line_of(count, rows, scratch):
-    sums = {1: scratch[0:4], -1: scratch[4:8]}
-    rows_out = {1: scratch[8:10], -1: scratch[10:12]} if len(scratch) > 9 else None
-    return Line(count, rows, sums, rows_out), scratch[-1]
-
-
-def run_line(line, partial_ref, total_ref, finish, rows_ref):
-    line.barrier()
-    line.inject(partial_ref, 0)
-    line.inject(partial_ref, 1)
-    for turn in range(PARTS + (line.count - 1 if rows_ref is not None else 0)):
-        if turn < PARTS:
-            line.forward(partial_ref, turn)
-            line.collect(partial_ref, total_ref, turn)
-            finish(turn, pl.ds(turn * line.part, line.part), line.span(line.place, turn))
-            if rows_ref is not None:
-                line.spread(rows_ref, turn)
-            if turn + 2 < PARTS:
-                line.inject(partial_ref, turn + 2)
-        if rows_ref is not None:
-            for distance in range(1, line.count):
-                if 0 <= turn - distance < PARTS:
-                    line.relay(rows_ref, distance, turn - distance)
-    line.drain_sums(partial_ref)
-    if rows_ref is not None:
-        line.drain_rows(rows_ref)
+    return scratch
+
+
+FINISHES = [("finish", part) for part in range(PARTS)]
 
 
 def middle_kernel(count, partial_ref, input_ref, gain_ref, rows_ref, resid_ref, *scratch):
-    line, total_ref = line_of(count, input_ref.shape[0], scratch)
+    line = Line(count, input_ref.shape[0], scratch, FINISHES, True, True)
 
     def finish(part, local, place):
-        resid = input_ref[local, :].astype(F32) + total_ref[...]
+        resid = input_ref[local, :].astype(F32) + line.total_ref[...]
         resid_ref[local, :] = resid
         rows_ref[place, :] = (resid * rms_scale(resid) * gain_ref[...]).astype(BF16)
 
-    run_line(line, partial_ref, total_ref, finish, rows_ref)
+    line.partial_ref, line.rows_ref, line.finish = partial_ref, rows_ref, finish
+    line.greet()
+    line.finish_all()
 
 
 def turn_kernel(count, partial_ref, resid_ref, grad_ref, gain_ref, rows_ref, d_resid_ref, d_gain_ref, *scratch):
-    line, total_ref = line_of(count, resid_ref.shape[0], scratch)
+    line = Line(count, resid_ref.shape[0], scratch, FINISHES, True, True)
 
     def finish(part, local, place):
-        resid, total = resid_ref[local, :], total_ref[...]
+        resid, total = resid_ref[local, :], line.total_ref[...]
         scale = rms_scale(resid)
         sums = jnp.sum(total * resid * scale, axis=0, keepdims=True)
         d_gain_ref[...] = sums if part == 0 else d_gain_ref[...] + sums
@@ -706,23 +806,27 @@
         d_resid_ref[local, :] = d_resid
         rows_ref[place, :] = d_resid.astype(BF16)
 
-    run_line(line, partial_ref, total_ref, finish, rows_ref)
+    line.partial_ref, line.rows_ref, line.finish = partial_ref, rows_ref, finish
+    line.greet()
+    line.finish_all()
 
 
 def last_kernel(count, partial_ref, input_ref, d_resid_ref, gain_ref, d_input_ref, d_gain_ref, *scratch):
-    line, total_ref = line_of(count, input_ref.shape[0], scratch)
+    line = Line(count, input_ref.shape[0], scratch, FINISHES, True, False)
 
     def finish(part, local, place):
-        values, total = input_ref[local, :].astype(F32), total_ref[...]
+        values, total = input_ref[local, :].astype(F32), line.total_ref[...]
         scale = rms_scale(values)
         sums = jnp.sum(total * values * scale, axis=0, keepdims=True)
         d_gain_ref[...] = sums if part == 0 else d_gain_ref[...] + sums
         d_input_ref[local, :] = d_resid_ref[local, :] + rms_back(values, scale, gain_ref[...], total)
 
-    run_line(line, partial_ref, total_ref, finish, None)
-
-
-def line_call(kernel, name, ident, spread, out_shape, operands):
+    line.partial_ref, line.finish = partial_ref, finish
+    line.greet()
+    line.finish_all()
+
+
+def line_call(kernel, name, ident, spreads, out_shape, operands):
     count = lax.axis_size("tensor")
     partial_rows, features = operands[0].shape
     vmem = pl.BlockSpec(memory_space=pltpu.VMEM)
@@ -731,13 +835,372 @@
         out_shape=out_shape,
         in_specs=[vmem] * len(operands),
         out_specs=[vmem] * len(out_shape),
-        scratch_shapes=line_scratch(count, partial_rows // count, features, spread),
+        scratch_shapes=line_scratch(count, partial_rows // count, features, True, spreads),
         compiler_params=pltpu.CompilerParams(
             collective_id=ident, has_side_effects=True, vmem_limit_bytes=32 * 2**20
         ),
         cost_estimate=pl.CostEstimate(flops=10**9, bytes_accessed=60 * 2**20, transcendentals=0),
         name=name,
     )(*operands)
+
+
+def enter_kernel(
+    sizes, input_ref, gain_one_ref, gain_two_ref, beta_ref, gating_ref, query_ref, key_ref, value_ref, project_ref,
+    rows_ref, mix_ref, whole_project_ref, gains_ref,
+    all_rows, all_one, all_two, all_beta, local_sem, small_send, small_recv,
+    first_send, first_recv, second_send, second_recv, third_send, third_recv, *row_sems,
+):
+    replicas, shards, count = sizes
+    rows = input_ref.shape[0]
+    width = query_ref.shape[1]
+    heads = beta_ref.shape[0]
+    share = query_ref.shape[0]
+    sources = (gating_ref, query_ref, key_ref, value_ref, project_ref)
+    streams = len(sources)
+    pairs = replicas // 2
+    line = Line(count, rows, row_sems, [], False, True, parts=2)
+    line.rows_ref, line.source_ref = all_rows, input_ref
+    replica, shard, place = line.replica, line.shard, line.place
+    partner = replica + 1 - 2 * lax.rem(replica, 2)
+
+    def across(step):
+        return lax.rem(replica + 2 * step, replicas)
+
+    def shard_at(shift):
+        return lax.rem(shard + shift, shards)
+
+    def piece(ref, stream, row, col, part):
+        if stream < 4:
+            size = share // replicas
+            return ref.at[
+                pl.ds(pl.multiple_of(row + part * size, size), size),
+                pl.ds(col + stream * width if col is not None else 0, width),
+            ]
+        size = width // replicas
+        return ref.at[
+            pl.ds(pl.multiple_of(part * size, size), size),
+            pl.ds(pl.multiple_of(row, 128), share),
+        ]
+
+    def held(stream, owner, part):
+        ref = mix_ref if stream < 4 else whole_project_ref
+        return piece(ref, stream, owner * share, 0, part)
+
+    def own(stream, part):
+        ref = sources[stream]
+        if stream < 4:
+            return piece(ref, stream, 0, None, part)
+        return piece(ref, stream, 0, None, part)
+
+    def remote(source, target, send, recv, where):
+        return pltpu.make_async_remote_copy(
+            src_ref=source, dst_ref=target, send_sem=send, recv_sem=recv, device_id=where, device_id_type=MESH
+        )
+
+    def first(shift, stream, owner):
+        return remote(
+            own(stream, replica), held(stream, owner, replica),
+            first_send.at[shift - 1, stream], first_recv.at[shift - 1, stream],
+            device(replica, shard_at(shift), place),
+        )
+
+    def second(shift, step, stream, part):
+        where = held(stream, shard_at(shards - shift), part)
+        return remote(
+            where, where, second_send.at[shift - 1, step - 1, stream], second_recv.at[shift - 1, step - 1, stream],
+            device(across(step), shard, place),
+        )
+
+    def third(shift, step, stream, part):
+        where = held(stream, shard_at(shards - shift), part)
+        return remote(
+            where, where, third_send.at[shift - 1, step, stream], third_recv.at[shift - 1, step, stream],
+            device(partner, shard, place),
+        )
+
+    def spread(part):
+        for there in range(count):
+            @pl.when(place == there)
+            def _():
+                line.spread_from(there, part)
+
+    def relay(distance, part):
+        for there in range(count):
+            @pl.when(place == there)
+            def _():
+                for step in (1, -1):
+                    if 0 <= there - step * distance < count:
+                        line.emit(there, ("relay", step, distance, part))
+
+    features = share * shards
+    cols = pl.ds(pl.multiple_of(shard * share, 128), share)
+    smalls = ((gain_one_ref, all_one.at[:, cols]), (gain_two_ref, all_two.at[:, cols]), (beta_ref, all_beta.at[:, cols]))
+
+    def small(shift, index):
+        source, target = smalls[index]
+        return remote(
+            source, target, small_send.at[shift - 1, index], small_recv.at[shift - 1, index],
+            device(replica, shard_at(shift), place),
+        )
+
+    others = [device(replica, shard_at(shift), place) for shift in range(1, shards)]
+    others += [device(across(step), shard, place) for step in range(1, pairs)] + [device(partner, shard, place)]
+    line.greet(others)
+    for shift in range(1, shards):
+        for index in range(len(smalls)):
+            small(shift, index).start()
+    for part in range(2):
+        spread(part)
+    for stream in range(streams):
+        for shift in range(1, shards):
+            first(shift, stream, shard).start()
+    locals_ = [pltpu.make_async_copy(source, target, local_sem.at[index]) for index, (source, target) in enumerate(smalls)]
+    for stream in range(4):
+        locals_.append(pltpu.make_async_copy(
+            sources[stream],
+            mix_ref.at[pl.ds(pl.multiple_of(shard * share, share), share), pl.ds(stream * width, width)],
+            local_sem.at[3 + stream],
+        ))
+    locals_.append(pltpu.make_async_copy(project_ref, whole_project_ref.at[:, cols], local_sem.at[7]))
+    for copy in locals_:
+        copy.start()
+    for copy in locals_[:3]:
+        copy.wait()
+    for shift in range(1, shards):
+        for index in range(len(smalls)):
+            small(shift, index).wait()
+    gains_ref[...] = jnp.concatenate([all_one[...].astype(F32), all_two[...].astype(F32)], axis=0)
+    lanes = mix_ref.shape[1] - 4 * width
+    beta = jnp.concatenate([all_beta[...].astype(F32), jnp.zeros((lanes - heads, features), F32)], axis=0)
+    mix_ref[:, 4 * width :] = beta.T.astype(BF16)
+
+    def normalize(source, start, size):
+        values = source[pl.ds(start, size), :].astype(F32)
+        return (values * rms_scale(values) * gains_ref[0:1, :]).astype(BF16)
+
+    rows_ref[line.span(place, 0), :] = normalize(input_ref, 0, line.part)
+    rows_ref[line.span(place, 1), :] = normalize(input_ref, line.part, line.part)
+
+    for turn in range(max(streams + 2, 2 * (count - 1))):
+        if turn < streams:
+            for shift in range(1, shards):
+                first(shift, turn, shard_at(shards - shift)).wait_recv()
+                for step in range(1, pairs):
+                    second(shift, step, turn, replica).start()
+                third(shift, 0, turn, replica).start()
+        distance, part = turn // 2 + 1, turn % 2
+        if distance < count:
+            relay(distance, part)
+        if 0 <= turn - 1 < streams:
+            for shift in range(1, shards):
+                for step in range(1, pairs):
+                    came = across(pairs - step)
+                    second(shift, step, turn - 1, came).wait_recv()
+                    third(shift, step, turn - 1, came).start()
+        if distance < count:
+            for step in (1, -1):
+                owner = place - step * distance
+                inside = owner >= 0 if step > 0 else owner < count
+
+                @pl.when(inside)
+                def _():
+                    start = pl.multiple_of(owner * rows + part * line.part, line.part)
+                    rows_ref[line.span(owner, part), :] = normalize(all_rows, start, line.part)
+        if 0 <= turn - 2 < streams:
+            for shift in range(1, shards):
+                for step in range(pairs):
+                    third(shift, step, turn - 2, replica).wait_recv()
+    for copy in locals_[3:]:
+        copy.wait()
+    for stream in range(streams):
+        for shift in range(1, shards):
+            first(shift, stream, shard).wait_send()
+            for step in range(1, pairs):
+                second(shift, step, stream, replica).wait_send()
+            for step in range(pairs):
+                third(shift, step, stream, replica).wait_send()
+    line.drain()
+
+
+def enter(layer_input, first_gain, second_gain, w_beta, mixers, w_project):
+    replicas, shards, count = extents()
+    rows, features = layer_input.shape
+    width = mixers[0].shape[1]
+    share = mixers[0].shape[0]
+    heads = w_beta.shape[1]
+    pairs = replicas // 2
+    vmem = pl.BlockSpec(memory_space=pltpu.VMEM)
+    hbm = pl.BlockSpec(memory_space=pl.ANY)
+    dma = pltpu.SemaphoreType.DMA
+    far = max(shards - 1, 1)
+    out_shape = (
+        jax.ShapeDtypeStruct((count * rows, features), BF16),
+        jax.ShapeDtypeStruct((features, 4 * width + 128), BF16),
+        jax.ShapeDtypeStruct((width, features), BF16),
+        jax.ShapeDtypeStruct((2, features), F32),
+    )
+    return pl.pallas_call(
+        functools.partial(enter_kernel, (replicas, shards, count)),
+        out_shape=out_shape,
+        in_specs=[vmem] * 4 + [hbm] * 5,
+        out_specs=[vmem] * 4,
+        scratch_shapes=[
+            pltpu.VMEM((count * rows, features), BF16),
+            pltpu.VMEM((1, features), BF16),
+            pltpu.VMEM((1, features), BF16),
+            pltpu.VMEM((heads, features), BF16),
+            dma((8,)),
+            dma((far, 3)),
+            dma((far, 3)),
+            dma((far, 5)),
+            dma((far, 5)),
+            dma((far, max(pairs - 1, 1), 5)),
+            dma((far, max(pairs - 1, 1), 5)),
+            dma((far, pairs, 5)),
+            dma((far, pairs, 5)),
+        ]
+        + [dma((count - 1, 2))] * 4,
+        compiler_params=pltpu.CompilerParams(collective_id=5, has_side_effects=True, vmem_limit_bytes=40 * 2**20),
+        cost_estimate=pl.CostEstimate(flops=10**9, bytes_accessed=60 * 2**20, transcendentals=0),
+        name="enter",
+    )(layer_input, first_gain[None, :], second_gain[None, :], w_beta.T, *mixers, w_project)
+
+
+class Pair:
+
+    def __init__(self, features, owners, left_ref, right_ref, grad_refs, out_ref, scratch):
+        self.owners, self.left_ref, self.right_ref, self.grad_refs = owners, left_ref, right_ref, grad_refs
+        self.out_ref = out_ref
+        self.tiles, self.came, self.send_sem, self.recv_sem = scratch
+        self.core = lax.axis_index("core")
+        replica, shard, place = coordinates()
+        self.partner = device(replica + 1 - 2 * self.core, shard, place)
+        self.blocks, self.size = out_ref.shape[:2]
+        self.share = features // (2 * lax.axis_size("pair"))
+
+    def copy(self, block):
+        return pltpu.make_async_remote_copy(
+            src_ref=self.tiles.at[block], dst_ref=self.came.at[block], send_sem=self.send_sem.at[block],
+            recv_sem=self.recv_sem.at[block], device_id=self.partner, device_id_type=MESH,
+        )
+
+    def product(self, block, core):
+        steps = self.share // self.size
+        start = (lax.div(block, steps) * 2 + core) * self.share + lax.rem(block, steps) * self.size
+        cols = pl.ds(pl.multiple_of(start, self.size), self.size)
+        start = 0
+        for owner, grad_ref in zip(self.owners, self.grad_refs):
+            wide = grad_ref.shape[1]
+            values = dot_tn((self.left_ref if owner == 0 else self.right_ref)[:, cols], grad_ref[...])
+            yield slice(start, start + wide), values
+            start += wide
+
+    def theirs(self, block):
+        for span, values in self.product(block, 1 - self.core):
+            self.tiles[block, :, span] = values.astype(BF16)
+        self.copy(block).start()
+
+    def ours(self, block):
+        self.copy(block).wait_recv()
+        for span, values in self.product(block, self.core):
+            self.out_ref[block, :, span] = (values + self.came[block, :, span].astype(F32)).astype(BF16)
+
+    def drain(self):
+        for block in range(self.blocks):
+            self.copy(block).wait_send()
+
+
+def pair_shape(left, grads):
+    features = left.shape[1]
+    return features // (2 * CHUNK), CHUNK, sum(grad.shape[1] for grad in grads)
+
+
+def pair_scratch(shape):
+    dma = pltpu.SemaphoreType.DMA
+    return [pltpu.VMEM(shape, BF16), pltpu.VMEM(shape, BF16), dma(shape[:1]), dma(shape[:1])]
+
+
+def mix_grads_kernel(features, left_ref, right_ref, first_ref, second_ref, out_ref, *scratch):
+    pair = Pair(features, (0, 1), left_ref, right_ref, (first_ref, second_ref), out_ref, scratch)
+    barrier = pltpu.get_barrier_semaphore()
+    pl.semaphore_signal(barrier, inc=1, device_id=pair.partner, device_id_type=MESH)
+    pl.semaphore_wait(barrier, 1)
+    pl.loop(0, pair.blocks)(pair.theirs)
+    pl.loop(0, pair.blocks)(pair.ours)
+    pair.drain()
+
+
+def mix_grads(left, right, grads):
+    shape = pair_shape(left, grads)
+    vmem = pl.BlockSpec(memory_space=pltpu.VMEM)
+    out = pl.pallas_call(
+        functools.partial(mix_grads_kernel, left.shape[1]),
+        out_shape=jax.ShapeDtypeStruct(shape, BF16),
+        in_specs=[vmem] * 4,
+        out_specs=vmem,
+        scratch_shapes=pair_scratch(shape),
+        compiler_params=pltpu.CompilerParams(collective_id=7, has_side_effects=True, vmem_limit_bytes=40 * 2**20),
+        cost_estimate=pl.CostEstimate(
+            flops=2 * left.shape[0] * left.shape[1] * shape[2], bytes_accessed=30 * 2**20, transcendentals=0
+        ),
+        name="mix_grads",
+    )(left, right, *grads)
+    return out.reshape(shape[0] * shape[1], shape[2])
+
+
+BLOCK_TIME = 2.8
+
+
+def ffn_grads_kernel(
+    count, features, left_ref, right_ref, d_gate_ref, d_up_ref, hidden_ref, partial_ref, resid_ref,
+    out_ref, result_ref, *scratch,
+):
+    pair = Pair(features, (0, 0, 1), left_ref, right_ref, (d_gate_ref, d_up_ref, hidden_ref), out_ref, scratch[:4])
+    line = Line(count, resid_ref.shape[0], scratch[4:], [BLOCK_TIME] * (2 * pair.blocks), True, False)
+
+    def finish(part, local, place):
+        result_ref[local, :] = (resid_ref[local, :] + line.total_ref[...]).astype(BF16)
+
+    line.partial_ref, line.finish = partial_ref, finish
+    line.greet([pair.partner])
+
+    @pl.loop(0, pair.blocks)
+    def _(block):
+        line.run_at(0, block, pair.blocks)
+        pair.theirs(block)
+
+    @pl.loop(0, pair.blocks)
+    def _(block):
+        line.run_at(pair.blocks, block, pair.blocks)
+        pair.ours(block)
+
+    line.run(2 * pair.blocks)
+    line.drain()
+    pair.drain()
+
+
+def ffn_grads(left, right, grads, ffn_partial, resid):
+    count = lax.axis_size("tensor")
+    shape = pair_shape(left, grads)
+    vmem = pl.BlockSpec(memory_space=pltpu.VMEM)
+    sums, result = pl.pallas_call(
+        functools.partial(ffn_grads_kernel, count, left.shape[1]),
+        out_shape=(jax.ShapeDtypeStruct(shape, BF16), jax.ShapeDtypeStruct(resid.shape, BF16)),
+        in_specs=[vmem] * 7,
+        out_specs=[vmem] * 2,
+        scratch_shapes=pair_scratch(shape) + line_scratch(count, resid.shape[0], resid.shape[1], True, False),
+        compiler_params=pltpu.CompilerParams(collective_id=6, has_side_effects=True, vmem_limit_bytes=58 * 2**20),
+        cost_estimate=pl.CostEstimate(
+            flops=2 * left.shape[0] * left.shape[1] * shape[2], bytes_accessed=50 * 2**20, transcendentals=0
+        ),
+        name="ffn_grads",
+    )(left, right, *grads, ffn_partial, resid)
+    return sums.reshape(shape[0] * shape[1], shape[2]), result
+
+
+def group_scatter(sums):
+    shard = lax.psum_scatter(sums, ("pair", "fsdp"), scatter_dimension=0, tiled=True)
+    return with_layout_constraint(shard, Layout(major_to_minor=(0, 1))).astype(F32)
 
 
 def shifted(count, shift):
@@ -774,24 +1237,12 @@
     return whole
 
 
-def scatter_rows(partial_rows):
-    count = lax.axis_size("tensor")
-    mine = lax.axis_index("tensor")
-    height = partial_rows.shape[0] // count
-    total = lax.dynamic_slice_in_dim(partial_rows, mine * height, height, 0).astype(F32)
-    for shift in range(1, count):
-        target = lax.rem(mine + shift, count)
-        piece = lax.dynamic_slice_in_dim(partial_rows, target * height, height, 0)
-        total = total + lax.ppermute(piece, "tensor", shifted(count, shift)).astype(F32)
-    return total
-
-
-def gather_weights(pieces):
-    return lax.all_gather(jnp.concatenate(pieces, axis=1), ("fsdp", "dp"), axis=0, tiled=True)
-
-
-def scatter_grads(grads):
-    return lax.psum_scatter(grads, ("dp", "fsdp"), scatter_dimension=0, tiled=True).astype(F32)
+def gather_weights(pieces, axis):
+    return lax.all_gather(jnp.concatenate(pieces, axis=1), ("fsdp", "pair", "core"), axis=axis, tiled=True)
+
+
+def scatter_grads(grads, axis=0):
+    return lax.psum_scatter(grads, ("pair", "core", "fsdp"), scatter_dimension=axis, tiled=True).astype(F32)
 
 
 def body(
@@ -815,8 +1266,7 @@
     seq_lengths,
     output_grad,
 ):
-    replicas = lax.axis_size("dp")
-    replica = lax.axis_index("dp")
+    replicas, replica = extents()[0], coordinates()[0]
     width = w_query.shape[1]
     units = w_gate.shape[1]
     heads = w_beta.shape[1]
@@ -831,23 +1281,13 @@
     conv_k = conv_key.astype(F32)
     conv_v = conv_value.astype(F32)
     gain_head = head_gain.astype(F32)[None, :]
-    gains = lax.all_gather(jnp.stack([first_gain, second_gain]), "fsdp", axis=1, tiled=True).astype(F32)
+    rows_one, mix_full, project_full, gains = enter(
+        layer_input, first_gain, second_gain, w_beta, (w_gating, w_query, w_key, w_value), w_project
+    )
     gain_one, gain_two = gains[:1], gains[1:]
-    beta_piece = jnp.pad(piece(w_beta, 0), ((0, 0), (0, head_width - heads)))
-    mix_full = gather_weights(
-        [piece(w_gating, 0), piece(w_query, 0), piece(w_key, 0), piece(w_value, 0), beta_piece, piece(w_project, 1).T]
-    )
-    ffn_full = gather_weights(
-        [piece(w_gate, 0), piece(w_up, 0), piece(w_down, 1).T]
-    )
-    project_t = mix_full[:, 4 * width + head_width :]
-    mix_full = mix_full[:, : 4 * width + head_width]
-    gate_up = ffn_full[:, : 2 * units]
-    down_t = ffn_full[:, 2 * units :]
-
-    scale_one = rms_scale(input_float)
-    normed1 = (input_float * scale_one * gain_one).astype(BF16)
-    rows_one = gather_rows(normed1)
+    late, rows_one = lax.optimization_barrier(((w_gate, w_up, w_down), rows_one))
+    gate_up = gather_weights([piece(late[0], 0), piece(late[1], 0)], 0)
+    down = gather_weights([piece(late[2], 1)], 1)
     late_grad, rows_one = lax.optimization_barrier((output_grad, rows_one))
     came = send_rows(late_grad)
     raw = dot(rows_one, mix_full)
@@ -856,14 +1296,14 @@
     )
     gated, came = lax.optimization_barrier((gated, came))
     grad_rows = place_rows(output_grad, came)
-    attn_partial = dot_nt(gated, project_t).astype(BF16)
+    attn_partial = dot(gated, project_full).astype(BF16)
     whole_rows = jax.ShapeDtypeStruct(rows_one.shape, BF16)
     own_rows = jax.ShapeDtypeStruct(layer_input.shape, F32)
     gain_sums = jax.ShapeDtypeStruct((1, layer_input.shape[1]), F32)
     rows_two, resid = line_call(
         middle_kernel, "middle", 2, True, (whole_rows, own_rows), (attn_partial, layer_input, gain_two)
     )
-    d_hidden = dot(grad_rows, down_t)
+    d_hidden = dot_nt(grad_rows, down)
     both = dot(rows_two, gate_up)
     gate_val, up_val = both[:, :units], both[:, units:]
     gate_sig = jax.nn.sigmoid(gate_val)
@@ -872,30 +1312,23 @@
     d_gate = (d_hidden * up_val * gate_sig * (1.0 + gate_val * (1.0 - gate_sig))).astype(BF16)
     d_up = (d_hidden * silu_gate).astype(BF16)
     d_both = jnp.concatenate([d_gate, d_up], axis=1)
-    grad_down = dot_tn(grad_rows, hidden).astype(BF16)
-    down_shard = scatter_grads(grad_down)
-    grad_both = dot_tn(rows_two, d_both).astype(BF16)
-    both_shard = scatter_grads(grad_both)
-    d_partial, _, _ = lax.optimization_barrier(
-        (dot_nt(d_both, gate_up).astype(BF16), grad_down, grad_both)
-    )
+    ffn_partial = dot(hidden, down).astype(BF16)
+    ffn_sums, result = ffn_grads(rows_two, grad_rows, (d_gate, d_up, hidden), ffn_partial, resid)
+    ffn_shard = group_scatter(ffn_sums)
+    d_partial, _ = lax.optimization_barrier((dot_nt(d_both, gate_up).astype(BF16), ffn_sums))
     d_attn, d_resid, grad_second = line_call(
         turn_kernel, "turn", 3, True, (whole_rows, own_rows, gain_sums), (d_partial, resid, output_grad, gain_two)
     )
-    ffn_partial, d_attn, down_shard = lax.optimization_barrier((dot_nt(hidden, down_t).astype(BF16), d_attn, down_shard))
-    ffn_out = scatter_rows(ffn_partial)
-    result = (resid + ffn_out).astype(BF16)
-    d_gated = dot(d_attn, project_t)
-    grad_project = dot_tn(d_attn, gated).astype(BF16)
+    d_gated = dot_nt(d_attn, project_full)
     d_raw, d_conv, d_head = delta_backward(
         doc_starts, seq_lengths, raw, conv_q, conv_k, conv_v, gain_head, mixed, solve, update, state, d_gated
     )
-    grad_mix = dot_tn(rows_one, d_raw).astype(BF16)
-    mix_shard = scatter_grads(jnp.concatenate([grad_mix, grad_project], axis=1))
+    mix_sums, ffn_shard = lax.optimization_barrier(
+        (mix_grads(rows_one, d_attn, (d_raw, gated)), ffn_shard)
+    )
+    mix_shard = group_scatter(mix_sums)
     project_shard = mix_shard[:, 4 * width + head_width :]
-    mix_partial, result, both_shard = lax.optimization_barrier(
-        (dot_nt(d_raw, mix_full).astype(BF16), result, both_shard)
-    )
+    mix_partial = dot_nt(d_raw, mix_full).astype(BF16)
     input_grad, grad_first = line_call(
         last_kernel, "last", 4, False, (own_rows, gain_sums),
         (mix_partial, layer_input, d_resid, gain_one),
@@ -918,15 +1351,19 @@
         head_total[0],
         project_shard.T,
         gain_total[1],
-        both_shard[:, :units],
-        both_shard[:, units:],
-        down_shard.T,
+        ffn_shard[:, :units],
+        ffn_shard[:, units : 2 * units],
+        ffn_shard[:, 2 * units :].T,
     )
 
 
 def solution(mesh):
+    replicas, shards, count = (mesh.shape[name] for name in ("dp", "fsdp", "tensor"))
+    mesh = jax.sharding.Mesh(
+        mesh.devices.reshape(replicas // 2, 2, shards, count), ("pair", "core", "fsdp", "tensor")
+    )
     placed = (
-        P(("dp", "fsdp", "tensor"), None),
+        P(("pair", "core", "fsdp", "tensor"), None),
         P("fsdp"),
         P("fsdp", "tensor"),
         P("fsdp", "tensor"),
@@ -942,32 +1379,32 @@
         P("fsdp", "tensor"),
         P("fsdp", "tensor"),
         P("tensor", "fsdp"),
-        P(("dp", "fsdp"), None),
-        P(("dp", "fsdp")),
-        P(("dp", "fsdp", "tensor"), None),
+        P(("pair", "core", "fsdp"), None),
+        P(("pair", "core", "fsdp")),
+        P(("pair", "core", "fsdp", "tensor"), None),
     )
     return jax.shard_map(
         body,
         mesh=mesh,
         in_specs=placed,
         out_specs=(
-            P(("dp", "fsdp", "tensor"), None),
-            P(("dp", "fsdp", "tensor"), None),
-            P(("dp", "fsdp")),
-            P(("dp", "fsdp"), "tensor"),
-            P(("dp", "fsdp"), "tensor"),
-            P(("dp", "fsdp"), "tensor"),
-            P(("dp", "fsdp"), "tensor"),
-            P(("dp", "fsdp"), "tensor"),
+            P(("pair", "core", "fsdp", "tensor"), None),
+            P(("pair", "core", "fsdp", "tensor"), None),
+            P(("pair", "core", "fsdp")),
+            P(("pair", "core", "fsdp"), "tensor"),
+            P(("pair", "core", "fsdp"), "tensor"),
+            P(("pair", "core", "fsdp"), "tensor"),
+            P(("pair", "core", "fsdp"), "tensor"),
+            P(("pair", "core", "fsdp"), "tensor"),
             P(None, "tensor"),
             P(None, "tensor"),
             P(None, "tensor"),
             P(),
-            P("tensor", ("dp", "fsdp")),
-            P(("dp", "fsdp")),
-            P(("dp", "fsdp"), "tensor"),
-            P(("dp", "fsdp"), "tensor"),
-            P("tensor", ("dp", "fsdp")),
+            P("tensor", ("pair", "core", "fsdp")),
+            P(("pair", "core", "fsdp")),
+            P(("pair", "core", "fsdp"), "tensor"),
+            P(("pair", "core", "fsdp"), "tensor"),
+            P("tensor", ("pair", "core", "fsdp")),
         ),
         check_vma=False,
     )

time: 538 us -> 459 us (0.85)
  waiting for transfers between devices: 66.8 us -> 12.4 us
  Pallas kernels: 255 us -> 307 us
  matrix products: 87.5 us -> 58.8 us
  starting transfers between devices: 23.8 us -> 4.84 us
  local copies, waits for them, and re-layouts: 56.9 us -> 45.6 us
  other arithmetic: 16.6 us -> 6.74 us
  blocking collectives: 5.43 us -> 0 us
    pallas_call x0 -> x3, Pallas kernels: none -> 104 us  [the longest x1 47.2 us: ffn_grads(): pl.pallas_call(functools.partial(ffn_grads_kernel, count, left.shape[1]),...]
    pallas_call x3, Pallas kernels: 214 us -> 158 us  [line_call(): pl.pallas_call(functools.partial(kernel, count), out_shape=out_shape, in_...]
    ppermute x6 -> x0, waiting for transfers between devices: 47.6 us -> none  [the longest x3 27.7 us: gather_rows(): came = lax.ppermute(rows, 'tensor', shifted(count, shift))]
    dot_general x4 -> x0, matrix products: 25.5 us -> none  [dot_tn(): lax.dot_general(left, right, (((0,), (0,)), ((), ())), preferred_element_...]
    ppermute x6 -> x0, starting transfers between devices: 10.2 us -> none  [the longest x3 6.15 us: gather_rows(): came = lax.ppermute(rows, 'tensor', shifted(count, shift))]
    ppermute x3, starting transfers between devices: 13.2 us -> 4.68 us  [send_rows(): lax.ppermute(rows, 'tensor', shifted(count, shift))]
    ppermute x3, waiting for transfers between devices: 18.3 us -> 12.3 us  [send_rows(): lax.ppermute(rows, 'tensor', shifted(count, shift))]
    all_gather x1 -> x0, blocking collectives: 5.43 us -> none  [body(): lax.all_gather(jnp.stack([first_gain, second_gain]), 'fsdp', axis=1, tile...]
  transfers between devices with their start and end apart: 14 -> 7, of which waited for: 5 -> 1; matrix products, arithmetic and copies ran while one was open for 19% -> 13% of each run, Pallas kernels for 48% -> 47%
where the time goes in v3:
time: 459 us; the launch traced here: 450 us
  Pallas kernels  307 us (67%)
  matrix products  58.8 us (13%)
  local copies, waits for them, and re-layouts  45.6 us (10%)
  between operations  15.4 us (3%)
  waiting for transfers between devices  12.4 us (3%)
  other arithmetic  6.74 us (1%)
  starting transfers between devices  4.84 us (1%)
    pallas_call x3, Pallas kernels, line_call(): pl.pallas_call(functools.partial(kernel, count), out_shape=out_shape, in_...  158 us
    pallas_call x1, Pallas kernels, ffn_grads(): pl.pallas_call(functools.partial(ffn_grads_kernel, count, left.shape[1]),...  47.2 us
    pallas_call x1, Pallas kernels, enter(): pl.pallas_call(functools.partial(enter_kernel, (replicas, shards, count))...  45.6 us
    dot_general x4, matrix products, dot_nt(): lax.dot_general(left, right, (((1,), (1,)), ((), ())), preferred_element_...  30.2 us
    dot_general x4, matrix products, dot(): return jnp.dot(left, right, preferred_element_type=F32)  28.7 us
    unnamed x98, local copies, waits for them, and re-layouts  27 us
    pallas_call x1, Pallas kernels, delta_forward(): pl.pallas_call(forward_kernel, out_shape=(jax.ShapeDtypeStruct((rows, wid...  17.1 us
    pallas_call x1, Pallas kernels, delta_backward(): pl.pallas_call(backward_kernel, out_shape=(jax.ShapeDtypeStruct((rows, 4...  15.7 us
  transfers between devices with their start and end apart: 7, of which 1 were waited for; matrix products, arithmetic and copies ran while one was open for 13% of the time, Pallas kernels for 47%

profile of v3, /device:TPU:0, one launch (start us, length us, event | category | flops | bytes accessed | tf_op | source)
XLA Modules:
  0.0 450.4 jit_solution(14446906581591000216)
XLA Ops:
  8.8 1.2 copy-done.5
  10.0 1.2 copy-done.6
  11.2 1.2 copy-done.7
  12.5 1.2 copy-done.8
  13.7 1.2 copy-done.9
  14.9 1.0 copy-done.11
  16.6 45.6 %enter.1 = (bf16[512,2048]{1,0:T(8,128)(2,1)S(1)}, bf16[2048,2176]{1,0:T(8,128)(2,1)}, bf16[512,2048]{1,0:T(8,128)(2,1)S(1)}, f32[2,2048]{1,0:T(2,128)S(1)}) custom-call(bf16[128,2048]{1,0:T(8,128)(2,1)S(1)} %copy-done.11, bf16[1,1024]{1,0:T(2,128)(2,1)S(1)} %broadcast_in_dim.14.gain_one_ref, bf16[1,1024]{1,0:T(2,128)(2,1)S(1)} %broadcast_in_dim.15.gain_two_ref, ...), custom_call_target="tpu_custom_call" | custom-call | flops 1000000000 | bytes 62914560 | tf_op jit(solution)/shard_map/enter/pallas_call | solution.py:1042
  62.3 1.3 copy-done.15
  63.6 1.4 copy-done.17
  64.9 1.4 constant_dynamic-slice_fusion
  66.4 1.2 pad_maximum_fusion
  67.7 1.0 constant_dynamic-slice_fusion.2
  68.7 3.4 collective-permute-start.2
  72.2 1.2 collective-permute-start
  74.2 9.0 %fusion.9.raw_ref = f32[512,2176]{1,0:T(8,128)S(1)} fusion(bf16[512,2048]{1,0:T(8,128)(2,1)} %copy-done.15, bf16[2048,2176]{1,0:T(8,128)(2,1)} %get-tuple-element.57), kind=kOutput, calls=%fused_computation.29 | convolution fusion | flops 4563402752 | bytes 15466496 | tf_op jit(solution)/shard_map/dot_general | solution.py:31
  83.2 17.1 %delta_forward.1 = (bf16[512,512]{1,0:T(8,128)(2,1)S(1)}, f32[512,512]{1,0:T(8,128)S(1)}, bf16[8,256,256]{2,1,0:T(8,128)(2,1)S(1)}, bf16[512,512]{1,0:T(8,128)(2,1)S(1)}, bf16[4,128,128]{2,1,0:T(8,128)(2,1)S(1)}) custom-call(s32[1,4]{1,0:T(1,128)S(1)} %copy-done.20, s32[1]{0:T(128)S(6)} %copy.46.length_ref, f32[512,2176]{1,0:T(8,128)S(1)} %fusion.9.raw_ref, ...), custom_call_target="tpu_custom_call" | custom-call | flops 6442450944 | bytes 12582912 | tf_op jit(solution)/shard_map/delta_forward/pallas_call | solution.py:211
  100.3 1.0 copy-done.28
  101.3 1.0 copy-done.30
  103.1 1.6 broadcast_in_dim.18
  105.5 12.3 %collective-permute-done.1 = bf16[128,2048]{1,0:T(8,128)(2,1)} collective-permute-done((bf16[128,2048]{1,0:T(8,128)(2,1)S(1)}, bf16[128,2048]{1,0:T(8,128)(2,1)}, u32[]{:S(2)}, u32[]{:S(2)}) %collective-permute-start.1) | collective-permute-done | bytes 524320 | tf_op jit(solution)/shard_map/ppermute | solution.py:1225
  117.9 2.4 convolution_convert_fusion.1.partial_ref
  120.3 60.6 %middle.1 = (bf16[512,2048]{1,0:T(8,128)(2,1)S(1)}, f32[128,2048]{1,0:T(8,128)S(1)}) custom-call(bf16[512,2048]{1,0:T(8,128)(2,1)S(1)} %convolution_convert_fusion.1.partial_ref, bf16[128,2048]{1,0:T(8,128)(2,1)S(1)} %copy-done.12, f32[1,2048]{1,0:T(1,128)S(1)} %get-tuple-element.122.gain_ref), custom_call_target="tpu_custom_call" | custom-call | flops 1000000000 | bytes 62914560 | tf_op jit(solution)/shard_map/middle/pallas_call | solution.py:833
  181.9 1.3 copy-done.25
  183.2 1.9 constant_dynamic-update-slice_fusion.2
  185.0 1.9 constant_dynamic-update-slice_fusion.1
  186.9 1.9 constant_dynamic-update-slice_fusion.right_ref
  188.8 12.5 %fusion.10 = f32[512,2816]{1,0:T(8,128)} fusion(bf16[512,2048]{1,0:T(8,128)(2,1)} %copy-done.25, bf16[2048,2816]{1,0:T(8,128)(2,1)} %all-gather.5.cloned.1.call-done), kind=kOutput, calls=%fused_computation.30 | convolution fusion | flops 5905580032 | bytes 19398656 | tf_op jit(solution)/shard_map/dot_general | solution.py:31
  201.3 11.0 %multiply_convert_fusion.1 = (bf16[512,1408]{1,0:T(8,128)(2,1)}, bf16[512,1408]{1,0:T(8,128)(2,1)}, bf16[512,1408]{1,0:T(8,128)(2,1)S(1)}) fusion(f32[512,2816]{1,0:T(8,128)} %fusion.10, bf16[512,2048]{1,0:T(8,128)(2,1)} %constant_dynamic-update-slice_fusion.right_ref, bf16[1408,2048]{1,0:T(8,128)(2,1)} %all-gather.3.cloned.1.call-done), kind=kOutput, calls=%fused_computation.8 | convolution fusion | flops 2963603456 | bytes 17956864 | tf_op jit(solution)/shard_map/dot_general | solution.py:35
  212.3 4.7 %convolution_convert_fusion.2.partial_ref = bf16[512,2048]{1,0:T(8,128)(2,1)} fusion(bf16[512,1408]{1,0:T(8,128)(2,1)S(1)} %get-tuple-element.110.hidden_ref, bf16[1408,2048]{1,0:T(8,128)(2,1)S(1)} %copy-done.40), kind=kOutput, calls=%fused_computation.2 | convolution fusion | flops 2953838592 | bytes 9306112 | tf_op jit(solution)/shard_map/dot_general | solution.py:31
  217.0 47.2 %ffn_grads.1 = (bf16[4,256,4224]{2,1,0:T(8,128)(2,1)}, bf16[128,2048]{1,0:T(8,128)(2,1)}) custom-call(bf16[512,2048]{1,0:T(8,128)(2,1)} %copy-done.25, bf16[512,2048]{1,0:T(8,128)(2,1)} %constant_dynamic-update-slice_fusion.right_ref, bf16[512,1408]{1,0:T(8,128)(2,1)} %get-tuple-element.109.d_gate_ref, bf16[512,1408]{1,0:T(8,128)(2,1)} %get-tuple-element.108.d_up_ref, ...), custom_call_target="tpu_custom_call" | custom-call | flops 8858370048 | bytes 52428800 | tf_op jit(solution)/shard_map/ffn_grads/pallas_call | solution.py:1186
  264.3 1.3 copy-done.43
  265.5 9.5 %convolution_convert_fusion.partial_ref = bf16[512,2048]{1,0:T(8,128)(2,1)S(1)} fusion(bf16[2048,2816]{1,0:T(8,128)(2,1)} %all-gather.5.cloned.1.call-done, bf16[512,1408]{1,0:T(8,128)(2,1)S(1)} %copy-done.43, bf16[512,1408]{1,0:T(8,128)(2,1)} %get-tuple-element.109.d_gate_ref), kind=kOutput, calls=%fused_computation | convolution fusion | flops 5912395776 | bytes 16515072 | tf_op jit(solution)/shard_map/dot_general | solution.py:35
  275.1 58.2 %turn.1 = (bf16[512,2048]{1,0:T(8,128)(2,1)S(1)}, f32[128,2048]{1,0:T(8,128)S(1)}, f32[1,2048]{1,0:T(1,128)S(1)}) custom-call(bf16[512,2048]{1,0:T(8,128)(2,1)S(1)} %convolution_convert_fusion.partial_ref, f32[128,2048]{1,0:T(8,128)S(1)} %copy-done.22, bf16[128,2048]{1,0:T(8,128)(2,1)S(1)} %copy-done.10, f32[1,2048]{1,0:T(1,128)S(1)} %get-tuple-element.122.gain_ref), custom_call_target="tpu_custom_call" | custom-call | flops 1000000000 | bytes 62914560 | tf_op jit(solution)/shard_map/turn/pallas_call | solution.py:833
  333.4 1.3 fusion.11.grad_ref
  335.5 15.7 %delta_backward.1 = (bf16[512,2176]{1,0:T(8,128)(2,1)S(1)}, f32[4,1536]{1,0:T(4,128)S(1)}, f32[1,128]{1,0:T(1,128)S(1)}) custom-call(s32[1,4]{1,0:T(1,128)S(1)} %copy-done.20, s32[1]{0:T(128)S(6)} %copy.46.length_ref, f32[512,2176]{1,0:T(8,128)} %copy-done.26, f32[4,512]{1,0:T(4,128)S(1)} %convert_element_type.37.conv_q_ref, ...), custom_call_target="tpu_custom_call" | custom-call | flops 3221225472 | bytes 16777216 | tf_op jit(solution)/shard_map/delta_backward/pallas_call | solution.py:382
  351.2 11.1 %mix_grads.1 = bf16[4,256,2688]{2,1,0:T(8,128)(2,1)S(1)} custom-call(bf16[512,2048]{1,0:T(8,128)(2,1)S(1)} %copy-done.16, bf16[512,2048]{1,0:T(8,128)(2,1)S(1)} %get-tuple-element.78.right_ref, bf16[512,2176]{1,0:T(8,128)(2,1)S(1)} %get-tuple-element.79.first_ref, bf16[512,512]{1,0:T(8,128)(2,1)S(1)} %copy-done.33), custom_call_target="tpu_custom_call" | custom-call | flops 5637144576 | bytes 31457280 | tf_op jit(solution)/shard_map/mix_grads/pallas_call | solution.py:1136
  362.3 2.4 copy-done.2
  364.7 1.3 copy-done.27
  366.0 4.0 convert_element_type.47
  370.1 8.4 %convolution_convert_fusion.3.partial_ref = bf16[512,2048]{1,0:T(8,128)(2,1)S(1)} fusion(bf16[512,2176]{1,0:T(8,128)(2,1)} %copy-done.27, bf16[2048,2176]{1,0:T(8,128)(2,1)} %get-tuple-element.57), kind=kOutput, calls=%fused_computation.3 | convolution fusion | flops 4564451328 | bytes 13238272 | tf_op jit(solution)/shard_map/dot_general | solution.py:35
  378.5 39.6 %last.1 = (f32[128,2048]{1,0:T(8,128)S(1)}, f32[1,2048]{1,0:T(1,128)S(1)}) custom-call(bf16[512,2048]{1,0:T(8,128)(2,1)S(1)} %convolution_convert_fusion.3.partial_ref, bf16[128,2048]{1,0:T(8,128)(2,1)S(1)} %copy-done.13, f32[128,2048]{1,0:T(8,128)S(1)} %copy-done.24, f32[1,2048]{1,0:T(1,128)S(1)} %get-tuple-element.121.gain_ref), custom_call_target="tpu_custom_call" | custom-call | flops 1000000000 | bytes 62914560 | tf_op jit(solution)/shard_map/last/pallas_call | solution.py:833
  418.2 11.5 %reduce_small.1 = (f32[2,256]{1,0:T(2,128)S(1)}, f32[1,128]{1,0:T(1,128)S(1)}, f32[4,1536]{1,0:T(4,128)S(1)}) custom-call(f32[2,2048]{1,0:T(2,128)S(1)} %pad_maximum_fusion.1.gain_ref, f32[1,128]{1,0:T(1,128)S(1)} %get-tuple-element.84.head_ref, f32[4,1536]{1,0:T(4,128)S(1)} %get-tuple-element.85.conv_ref), custom_call_target="tpu_custom_call" | custom-call | tf_op jit(solution)/shard_map/reduce_small/pallas_call | solution.py:492
  430.9 1.9 slice_bitcast_fusion
  432.7 1.5 copy.38
  435.8 1.5 convert_element_type.48
  437.4 1.0 copy.37
  438.4 2.8 fusion.5
  442.0 1.0 copy.48
  (110 shorter events, 10.1 us)
Async XLA Ops:
  7.2 60.5 %copy-start = (bf16[1408,1024]{1,0:T(8,128)(2,1)S(1)}, bf16[1408,1024]{1,0:T(8,128)(2,1)}, u32[]{:S(2)}) copy-start(bf16[1408,1024]{1,0:T(8,128)(2,1)} %param.34) | copy-start | bytes 8650756
  7.2 181.6 %all-gather.5.cloned.1.call-start = ((), (), s32[]{:S(2)}) async-start(), calls=%async_computation.3 | async-start | bytes 12976128 | tf_op jit(solution)/shard_map/all_gather | solution.py:1241
  8.8 1.2 copy-start.5
  10.0 1.2 copy-start.6
  11.2 1.2 copy-start.7
  12.5 1.2 copy-start.8
  13.7 1.2 copy-start.9
  14.9 1.0 copy-start.11
  62.3 1.3 copy-start.15
  63.6 1.4 copy-start.17
  67.6 1.1 copy-start.10
  67.6 6.5 %copy-start.37 = (bf16[4,512]{1,0:T(4,128)(2,1)S(1)}, bf16[4,512]{1,0:T(4,128)(2,1)}, u32[]{:S(2)}) copy-start(bf16[4,512]{1,0:T(4,128)(2,1)} %param.26) | copy-start | bytes 12292
  67.6 6.5 %copy-start.38 = (bf16[4,512]{1,0:T(4,128)(2,1)S(1)}, bf16[4,512]{1,0:T(4,128)(2,1)}, u32[]{:S(2)}) copy-start(bf16[4,512]{1,0:T(4,128)(2,1)} %param.27) | copy-start | bytes 12292
  67.6 6.5 %copy-start.39 = (bf16[4,512]{1,0:T(4,128)(2,1)S(1)}, bf16[4,512]{1,0:T(4,128)(2,1)}, u32[]{:S(2)}) copy-start(bf16[4,512]{1,0:T(4,128)(2,1)} %param.28) | copy-start | bytes 12292
  67.6 6.6 %copy-start.41 = (bf16[128]{0:T(256)(128)(2,1)S(1)}, bf16[128]{0:T(256)(128)(2,1)}, u32[]{:S(2)}) copy-start(bf16[128]{0:T(256)(128)(2,1)} %param.29) | copy-start | bytes 772
  67.6 133.7 %all-gather.3.cloned.1.call-start = ((), (), s32[]{:S(2)}) async-start(), calls=%async_computation.2 | async-start | bytes 6488064 | tf_op jit(solution)/shard_map/all_gather | solution.py:1241
  68.7 297.4 %reduce-scatter.3.cloned.1.call-start = ((), (), s32[]{:S(2)}) async-start(), calls=%async_computation.4 | async-start | bytes 10813440 | tf_op jit(solution)/shard_map/reduce_scatter | solution.py:1202
  68.7 36.8 %collective-permute-start.2 = (bf16[128,2048]{1,0:T(8,128)(2,1)S(1)}, bf16[128,2048]{1,0:T(8,128)(2,1)}, u32[]{:S(2)}, u32[]{:S(2)}) collective-permute-start(bf16[128,2048]{1,0:T(8,128)(2,1)S(1)} %copy-done.10), channel_id=1, source_target_pairs={{0,3},{1,0},{2,1},{3,2},{4,7},{5,4},{6,5},{7,6},{8,11},{9,8},{10,9... | collective-permute-start | bytes 1572872 | tf_op jit(solution)/shard_map/ppermute | solution.py:1225
  72.2 45.7 %collective-permute-start.1 = (bf16[128,2048]{1,0:T(8,128)(2,1)S(1)}, bf16[128,2048]{1,0:T(8,128)(2,1)}, u32[]{:S(2)}, u32[]{:S(2)}) collective-permute-start(bf16[128,2048]{1,0:T(8,128)(2,1)S(1)} %copy-done.10), channel_id=1, source_target_pairs={{0,2},{1,3},{2,0},{3,1},{4,6},{5,7},{6,4},{7,5},{8,10},{9,11},{10,... | collective-permute-start | bytes 1572872 | tf_op jit(solution)/shard_map/ppermute | solution.py:1225
  72.2 45.7 %collective-permute-start = (bf16[128,2048]{1,0:T(8,128)(2,1)S(1)}, bf16[128,2048]{1,0:T(8,128)(2,1)}, u32[]{:S(2)}, u32[]{:S(2)}) collective-permute-start(bf16[128,2048]{1,0:T(8,128)(2,1)S(1)} %copy-done.10), channel_id=1, source_target_pairs={{0,1},{1,2},{2,3},{3,0},{4,5},{5,6},{6,7},{7,4},{8,9},{9,10},{10,1... | collective-permute-start | bytes 1572872 | tf_op jit(solution)/shard_map/ppermute | solution.py:1225
  74.2 9.0 %copy-start.20 = (s32[1,4]{1,0:T(1,128)S(1)}, s32[1,4]{1,0:T(1,128)}, u32[]{:S(2)}) copy-start(s32[1,4]{1,0:T(1,128)} %starts_ref.3) | copy-start | bytes 52
  83.2 17.1 %copy-start.26 = (f32[512,2176]{1,0:T(8,128)}, f32[512,2176]{1,0:T(8,128)S(1)}, u32[]{:S(2)}) copy-start(f32[512,2176]{1,0:T(8,128)S(1)} %fusion.9.raw_ref) | copy-start | bytes 13369348
  103.1 1.6 copy-start.32
  103.1 14.8 %copy-start.18 = (bf16[512,2048]{1,0:T(8,128)(2,1)S(1)}, bf16[512,2048]{1,0:T(8,128)(2,1)}, u32[]{:S(2)}) copy-start(bf16[512,2048]{1,0:T(8,128)(2,1)} %copy-done.17) | copy-start | bytes 6291460
  117.9 2.4 copy-start.12
  181.9 1.3 copy-start.25
  201.3 11.0 %copy-start.40 = (bf16[1408,2048]{1,0:T(8,128)(2,1)S(1)}, bf16[1408,2048]{1,0:T(8,128)(2,1)}, u32[]{:S(2)}) copy-start(bf16[1408,2048]{1,0:T(8,128)(2,1)} %all-gather.3.cloned.1.call-done) | copy-start | bytes 17301508
  212.2 4.7 %copy-start.42 = (bf16[512,1408]{1,0:T(8,128)(2,1)}, bf16[512,1408]{1,0:T(8,128)(2,1)S(1)}, u32[]{:S(2)}) copy-start(bf16[512,1408]{1,0:T(8,128)(2,1)S(1)} %get-tuple-element.110.hidden_ref) | copy-start | bytes 4325380
  264.2 1.4 copy-start.43
  264.2 170.1 %reduce-scatter.5.cloned.1.call-start = ((), (), s32[]{:S(2)}) async-start(), calls=%async_computation.5 | async-start | bytes 6881280 | tf_op jit(solution)/shard_map/reduce_scatter | solution.py:1202
  265.5 9.5 %copy-start.22 = (f32[128,2048]{1,0:T(8,128)S(1)}, f32[128,2048]{1,0:T(8,128)}, u32[]{:S(2)}) copy-start(f32[128,2048]{1,0:T(8,128)} %copy-done.21) | copy-start | bytes 3145732
  275.1 58.3 %copy-start.19 = (bf16[512,2048]{1,0:T(8,128)(2,1)S(1)}, bf16[512,2048]{1,0:T(8,128)(2,1)}, u32[]{:S(2)}) copy-start(bf16[512,2048]{1,0:T(8,128)(2,1)} %copy-done.17) | copy-start | bytes 6291460
  333.3 1.4 copy-start.23
  333.3 1.7 copy-start.29
  333.3 2.0 copy-start.31
  333.3 2.1 copy-start.35
  335.5 15.7 %copy-start.16 = (bf16[512,2048]{1,0:T(8,128)(2,1)S(1)}, bf16[512,2048]{1,0:T(8,128)(2,1)}, u32[]{:S(2)}) copy-start(bf16[512,2048]{1,0:T(8,128)(2,1)} %copy-done.15) | copy-start | bytes 6291460
  335.5 15.7 %copy-start.33 = (bf16[512,512]{1,0:T(8,128)(2,1)S(1)}, bf16[512,512]{1,0:T(8,128)(2,1)}, u32[]{:S(2)}) copy-start(bf16[512,512]{1,0:T(8,128)(2,1)} %copy-done.32) | copy-start | bytes 1572868
  362.3 2.4 copy-start.2
  364.7 1.3 copy-start.27
  370.0 60.8 %slice-start = ((s8[4325376]{0:T(1024)(128)(4,1)}), s8[4194304]{0:T(1024)(128)(4,1)S(1)}, s32[]{:S(2)}) async-start(s8[4325376]{0:T(1024)(128)(4,1)} %bitcast.31), calls=%async_computation.6 | async-start | bytes 8388608
  370.1 8.5 %copy-start.13 = (bf16[128,2048]{1,0:T(8,128)(2,1)S(1)}, bf16[128,2048]{1,0:T(8,128)(2,1)}, u32[]{:S(2)}) copy-start(bf16[128,2048]{1,0:T(8,128)(2,1)} %input_ref.5) | copy-start | bytes 1572868
  370.1 8.5 %copy-start.24 = (f32[128,2048]{1,0:T(8,128)S(1)}, f32[128,2048]{1,0:T(8,128)}, u32[]{:S(2)}) copy-start(f32[128,2048]{1,0:T(8,128)} %copy-done.23) | copy-start | bytes 3145732
  370.1 60.8 %slice-start.1 = ((s8[4325376]{0:T(1024)(128)(4,1)}), s8[131072]{0:T(1024)(128)(4,1)S(1)}, s32[]{:S(2)}) async-start(s8[4325376]{0:T(1024)(128)(4,1)} %bitcast.31), calls=%async_computation.7 | async-start | bytes 262144
  418.2 14.6 %copy-start.3 = (f32[128,2048]{1,0:T(8,128)}, f32[128,2048]{1,0:T(8,128)S(1)}, u32[]{:S(2)}) copy-start(f32[128,2048]{1,0:T(8,128)S(1)} %get-tuple-element.145) | copy-start | bytes 3145732
  438.4 2.8 copy-start.36
  438.4 3.6 copy-start.4
  438.4 5.0 %copy-start.1 = (bf16[1408,1024]{1,0:T(8,128)(2,1)S(1)}, bf16[1408,1024]{1,0:T(8,128)(2,1)}, u32[]{:S(2)}) copy-start(bf16[1408,1024]{1,0:T(8,128)(2,1)} %param.34) | copy-start | bytes 8650756
  (5 other events, 4.5 us)
Sparse Core Ops, SparseCore 0:
  67.7 67.0 all-gather.4
  137.2 44.3 all-gather.2
  264.3 86.7 reduce-scatter.2
  370.2 63.8 reduce-scatter.4

commit v4 on v3

--- a/solution.py
+++ b/solution.py
@@ -124,22 +124,44 @@
     return gate, act, scale
 
 
+TILE = 256
+PROJECT_TILE = 512
+ATTEND_TIMES = (1.2, 1.5, 0.9)
+
+
 def forward_kernel(
-    starts_ref, length_ref, raw_ref, conv_q_ref, conv_k_ref, conv_v_ref, gain_ref,
-    gated_ref, mixed_ref, solve_ref, update_ref, state_ref,
-    keep_ref, live_ref, carry_ref, strict_ref, incl_ref,
+    count, starts_ref, length_ref, rows_ref, mix_ref, project_ref, own_grad_ref, conv_q_ref, conv_k_ref, conv_v_ref, gain_ref,
+    raw_ref, gated_ref, mixed_ref, solve_ref, update_ref, state_ref, partial_ref, grad_rows_ref,
+    keep_ref, live_ref, carry_ref, strict_ref, incl_ref, *sems,
 ):
     rows, head_width = live_ref.shape
     width = gated_ref.shape[1]
     chunks = rows // CHUNK
+    heads = width // head_width
+    tiles, ends = 4 * width // TILE, project_ref.shape[1] // PROJECT_TILE
+    shared = [ATTEND_TIMES[0]] * tiles + [ATTEND_TIMES[1]] * (3 * heads) + [ATTEND_TIMES[2]] * ends
+    line = Line(count, rows // count, sems, shared, False, True, ATTEND_PARTS, ATTEND_LATENCY)
+    line.rows_ref, line.source_ref = grad_rows_ref, own_grad_ref
+    line.greet()
+    own = pl.ds(pl.multiple_of(line.place * line.rows, line.rows), line.rows)
+    grad_rows_ref[own, :] = own_grad_ref[...]
+
+    @pl.loop(0, tiles)
+    def _(tile):
+        line.run_at(0, tile, tiles)
+        cols = pl.ds(pl.multiple_of(tile * TILE, TILE), TILE)
+        raw_ref[:, cols] = dot(rows_ref[...], mix_ref[:, cols])
+
+    raw_ref[:, 4 * width :] = dot(rows_ref[...], mix_ref[:, 4 * width :])
     fill_masks(starts_ref, length_ref, keep_ref, live_ref, carry_ref)
     for chunk in range(chunks):
         strict, incl = pair_mask(starts_ref, chunk)
         strict_ref[chunk] = jnp.where(strict, 1.0, 0.0)
         incl_ref[chunk] = jnp.where(incl, 1.0, 0.0)
 
-    @pl.loop(0, width // head_width)
+    @pl.loop(0, heads)
     def _(head):
+        line.run_at(tiles, head, heads, 3)
         start = pl.multiple_of(head * head_width, head_width)
 
         def stream(index):
@@ -164,8 +186,11 @@
             pair = dot_nt(key_low[span], key_low[span])
             wide = jnp.concatenate([rate[span]] * (CHUNK // head_width), axis=1)
             system.append(pair * wide * strict_ref[chunk])
+        line.run_at(tiles + 1, head, heads, 3)
         memory = None
-        for chunk, solved in enumerate(invert(system)):
+        inverses = invert(system)
+        line.run_at(tiles + 2, head, heads, 3)
+        for chunk, solved in enumerate(inverses):
             span = slice(chunk * CHUNK, (chunk + 1) * CHUNK)
             solve_low = solved.astype(BF16)
             solve_ref[head * chunks + chunk] = solve_low
@@ -200,38 +225,52 @@
         gated = mixed * norm * gain_ref[...] * (gating * sigmoid(gating)) * live_ref[...]
         gated_ref[:, cols] = gated.astype(BF16)
 
-
-def delta_forward(starts, length, raw, conv_q, conv_k, conv_v, gain):
-    rows = raw.shape[0]
+    @pl.loop(0, ends)
+    def _(tile):
+        line.run_at(tiles + 3 * heads, tile, ends)
+        cols = pl.ds(pl.multiple_of(tile * PROJECT_TILE, PROJECT_TILE), PROJECT_TILE)
+        partial_ref[:, cols] = dot(gated_ref[...], project_ref[:, cols]).astype(BF16)
+
+    line.run(tiles + 3 * heads + ends)
+    line.drain()
+
+
+def attend(starts, length, rows_one, mix_full, project_full, own_grad, conv_q, conv_k, conv_v, gain):
+    rows, features = rows_one.shape
     head_width = gain.shape[-1]
     width = conv_q.shape[1]
     heads, chunks = width // head_width, rows // CHUNK
+    count = lax.axis_size("tensor")
     vmem = pl.BlockSpec(memory_space=pltpu.VMEM)
     smem = pl.BlockSpec(memory_space=pltpu.SMEM)
     return pl.pallas_call(
-        forward_kernel,
+        functools.partial(forward_kernel, count),
         out_shape=(
+            jax.ShapeDtypeStruct((rows, mix_full.shape[1]), F32),
             jax.ShapeDtypeStruct((rows, width), BF16),
             jax.ShapeDtypeStruct((rows, width), F32),
             jax.ShapeDtypeStruct((heads * chunks, CHUNK, CHUNK), BF16),
             jax.ShapeDtypeStruct((rows, width), BF16),
             jax.ShapeDtypeStruct((heads * (chunks - 1), head_width, head_width), BF16),
+            jax.ShapeDtypeStruct((rows, features), BF16),
+            jax.ShapeDtypeStruct((rows, features), BF16),
         ),
-        in_specs=[smem, smem] + [vmem] * 5,
-        out_specs=[vmem] * 5,
+        in_specs=[smem, smem] + [vmem] * 8,
+        out_specs=[vmem] * 8,
         scratch_shapes=[
             pltpu.VMEM((KERNEL - 1, rows, head_width), F32),
             pltpu.VMEM((rows, head_width), F32),
             pltpu.VMEM((chunks - 1, rows, head_width), F32),
             pltpu.VMEM((chunks, CHUNK, CHUNK), F32),
             pltpu.VMEM((chunks, CHUNK, CHUNK), F32),
-        ],
-        compiler_params=pltpu.CompilerParams(vmem_limit_bytes=40 * 1024 * 1024),
+        ]
+        + line_scratch(count, rows // count, features, False, True, ATTEND_PARTS),
+        compiler_params=pltpu.CompilerParams(collective_id=8, has_side_effects=True, vmem_limit_bytes=48 * 2**20),
         cost_estimate=pl.CostEstimate(
-            flops=2 * 24 * heads * chunks * CHUNK**3, bytes_accessed=12 * 2**20, transcendentals=0
+            flops=2 * 24 * heads * chunks * CHUNK**3, bytes_accessed=40 * 2**20, transcendentals=0
         ),
-        name="delta_forward",
-    )(starts, length, raw, conv_q, conv_k, conv_v, gain)
+        name="attend",
+    )(starts, length, rows_one, mix_full, project_full, own_grad, conv_q, conv_k, conv_v, gain)
 
 
 def backward_kernel(
@@ -514,8 +553,8 @@
     )(gain, head, conv)
 
 
-def plan(count, parts, sums, rows, shared, unit):
-    latency, backlog, add, end = 1.5, 1.5, 0.15 + 0.8 / parts, 0.5 + 3.0 / parts
+def plan(count, parts, sums, rows, shared, unit, latency=1.5):
+    backlog, add, end = 1.5, 0.15 + 0.8 / parts, 0.5 + 3.0 / parts
     rank = {"spread": 0, "relay": 0, "finish": 1, "forward": 2, "inject": 3}
     clock = [0.0] * count
     free, come = {}, [{} for _ in range(count)]
@@ -611,6 +650,9 @@
 
 
 PARTS = 4
+TURN_PARTS = 4
+ATTEND_PARTS = 4
+ATTEND_LATENCY, FFN_LATENCY = 1.5, 1.5
 UNIT = 11.3
 
 
@@ -626,7 +668,7 @@
 
 class Line:
 
-    def __init__(self, count, rows, scratch, shared, sums, spreads, parts=PARTS):
+    def __init__(self, count, rows, scratch, shared, sums, spreads, parts=PARTS, latency=1.5):
         self.count, self.rows, self.parts = count, rows, parts
         self.part = rows // parts
         scratch = list(scratch)
@@ -639,7 +681,7 @@
             for step in (1, -1):
                 self.sends[step] = [scratch.pop(0) for _ in range(2)]
         self.replica, self.shard, self.place = coordinates()
-        self.tasks = plan(count, parts, sums, spreads, shared, UNIT / parts)[1]
+        self.tasks = plan(count, parts, sums, spreads, shared, UNIT / parts, latency)[1]
         self.started = [[] for _ in range(count)]
         self.partial_ref = self.rows_ref = self.source_ref = self.finish = None
 
@@ -715,12 +757,12 @@
                     for task in tasks:
                         self.emit(place, task)
 
-    def run_at(self, base, step, count):
+    def run_at(self, base, step, count, stride=1):
         for index in range(count):
-            if any(tasks[base + index] for tasks in self.tasks):
+            if any(tasks[base + stride * index] for tasks in self.tasks):
                 @pl.when(step == index)
                 def _():
-                    self.run(base + index)
+                    self.run(base + stride * index)
 
     def collect(self, part):
         self.total_ref[...] = self.partial_ref[self.span(self.place, part), :].astype(F32)
@@ -778,11 +820,12 @@
     return scratch
 
 
-FINISHES = [("finish", part) for part in range(PARTS)]
+def finishes(parts):
+    return [("finish", part) for part in range(parts)]
 
 
 def middle_kernel(count, partial_ref, input_ref, gain_ref, rows_ref, resid_ref, *scratch):
-    line = Line(count, input_ref.shape[0], scratch, FINISHES, True, True)
+    line = Line(count, input_ref.shape[0], scratch, finishes(TURN_PARTS), True, True, TURN_PARTS)
 
     def finish(part, local, place):
         resid = input_ref[local, :].astype(F32) + line.total_ref[...]
@@ -795,7 +838,7 @@
 
 
 def turn_kernel(count, partial_ref, resid_ref, grad_ref, gain_ref, rows_ref, d_resid_ref, d_gain_ref, *scratch):
-    line = Line(count, resid_ref.shape[0], scratch, FINISHES, True, True)
+    line = Line(count, resid_ref.shape[0], scratch, finishes(TURN_PARTS), True, True, TURN_PARTS)
 
     def finish(part, local, place):
         resid, total = resid_ref[local, :], line.total_ref[...]
@@ -812,7 +855,7 @@
 
 
 def last_kernel(count, partial_ref, input_ref, d_resid_ref, gain_ref, d_input_ref, d_gain_ref, *scratch):
-    line = Line(count, input_ref.shape[0], scratch, FINISHES, True, False)
+    line = Line(count, input_ref.shape[0], scratch, finishes(PARTS), True, False)
 
     def finish(part, local, place):
         values, total = input_ref[local, :].astype(F32), line.total_ref[...]
@@ -835,7 +878,9 @@
         out_shape=out_shape,
         in_specs=[vmem] * len(operands),
         out_specs=[vmem] * len(out_shape),
-        scratch_shapes=line_scratch(count, partial_rows // count, features, True, spreads),
+        scratch_shapes=line_scratch(
+            count, partial_rows // count, features, True, spreads, TURN_PARTS if spreads else PARTS
+        ),
         compiler_params=pltpu.CompilerParams(
             collective_id=ident, has_side_effects=True, vmem_limit_bytes=32 * 2**20
         ),
@@ -1030,7 +1075,7 @@
     heads = w_beta.shape[1]
     pairs = replicas // 2
     vmem = pl.BlockSpec(memory_space=pltpu.VMEM)
-    hbm = pl.BlockSpec(memory_space=pl.ANY)
+    hbm = pl.BlockSpec(memory_space=pltpu.HBM)
     dma = pltpu.SemaphoreType.DMA
     far = max(shards - 1, 1)
     out_shape = (
@@ -1071,7 +1116,7 @@
     def __init__(self, features, owners, left_ref, right_ref, grad_refs, out_ref, scratch):
         self.owners, self.left_ref, self.right_ref, self.grad_refs = owners, left_ref, right_ref, grad_refs
         self.out_ref = out_ref
-        self.tiles, self.came, self.send_sem, self.recv_sem = scratch
+        self.tiles, self.came, self.send_sem, self.recv_sem, self.out_sem = scratch
         self.core = lax.axis_index("core")
         replica, shard, place = coordinates()
         self.partner = device(replica + 1 - 2 * self.core, shard, place)
@@ -1100,14 +1145,18 @@
             self.tiles[block, :, span] = values.astype(BF16)
         self.copy(block).start()
 
+    def store(self, block):
+        return pltpu.make_async_copy(self.tiles.at[block], self.out_ref.at[block], self.out_sem.at[block])
+
     def ours(self, block):
-        self.copy(block).wait_recv()
+        self.copy(block).wait()
         for span, values in self.product(block, self.core):
-            self.out_ref[block, :, span] = (values + self.came[block, :, span].astype(F32)).astype(BF16)
+            self.tiles[block, :, span] = (values + self.came[block, :, span].astype(F32)).astype(BF16)
+        self.store(block).start()
 
     def drain(self):
         for block in range(self.blocks):
-            self.copy(block).wait_send()
+            self.store(block).wait()
 
 
 def pair_shape(left, grads):
@@ -1117,7 +1166,7 @@
 
 def pair_scratch(shape):
     dma = pltpu.SemaphoreType.DMA
-    return [pltpu.VMEM(shape, BF16), pltpu.VMEM(shape, BF16), dma(shape[:1]), dma(shape[:1])]
+    return [pltpu.VMEM(shape, BF16), pltpu.VMEM(shape, BF16)] + [dma(shape[:1])] * 3
 
 
 def mix_grads_kernel(features, left_ref, right_ref, first_ref, second_ref, out_ref, *scratch):
@@ -1137,7 +1186,7 @@
         functools.partial(mix_grads_kernel, left.shape[1]),
         out_shape=jax.ShapeDtypeStruct(shape, BF16),
         in_specs=[vmem] * 4,
-        out_specs=vmem,
+        out_specs=pl.BlockSpec(memory_space=pltpu.HBM),
         scratch_shapes=pair_scratch(shape),
         compiler_params=pltpu.CompilerParams(collective_id=7, has_side_effects=True, vmem_limit_bytes=40 * 2**20),
         cost_estimate=pl.CostEstimate(
@@ -1148,15 +1197,18 @@
     return out.reshape(shape[0] * shape[1], shape[2])
 
 
-BLOCK_TIME = 2.8
+BLOCK_TIME, TILE_TIME = 2.8, 1.3
 
 
 def ffn_grads_kernel(
-    count, features, left_ref, right_ref, d_gate_ref, d_up_ref, hidden_ref, partial_ref, resid_ref,
-    out_ref, result_ref, *scratch,
+    count, features, left_ref, right_ref, d_gate_ref, d_up_ref, hidden_ref, partial_ref, resid_ref, gate_up_ref,
+    out_ref, result_ref, d_partial_ref, *scratch,
 ):
-    pair = Pair(features, (0, 0, 1), left_ref, right_ref, (d_gate_ref, d_up_ref, hidden_ref), out_ref, scratch[:4])
-    line = Line(count, resid_ref.shape[0], scratch[4:], [BLOCK_TIME] * (2 * pair.blocks), True, False)
+    pair = Pair(features, (0, 0, 1), left_ref, right_ref, (d_gate_ref, d_up_ref, hidden_ref), out_ref, scratch[:5])
+    tiles = features // TILE
+    units = d_gate_ref.shape[1]
+    shared = [BLOCK_TIME] * (2 * pair.blocks) + [TILE_TIME] * tiles
+    line = Line(count, resid_ref.shape[0], scratch[5:], shared, True, False, latency=FFN_LATENCY)
 
     def finish(part, local, place):
         result_ref[local, :] = (resid_ref[local, :] + line.total_ref[...]).astype(BF16)
@@ -1174,67 +1226,40 @@
         line.run_at(pair.blocks, block, pair.blocks)
         pair.ours(block)
 
-    line.run(2 * pair.blocks)
+    @pl.loop(0, tiles)
+    def _(tile):
+        line.run_at(2 * pair.blocks, tile, tiles)
+        cols = pl.ds(pl.multiple_of(tile * TILE, TILE), TILE)
+        values = dot_nt(d_gate_ref[...], gate_up_ref[cols, :units]) + dot_nt(d_up_ref[...], gate_up_ref[cols, units:])
+        d_partial_ref[:, cols] = values.astype(BF16)
+
+    line.run(2 * pair.blocks + tiles)
     line.drain()
     pair.drain()
 
 
-def ffn_grads(left, right, grads, ffn_partial, resid):
+def ffn_grads(left, right, grads, ffn_partial, resid, gate_up):
     count = lax.axis_size("tensor")
     shape = pair_shape(left, grads)
     vmem = pl.BlockSpec(memory_space=pltpu.VMEM)
-    sums, result = pl.pallas_call(
+    sums, result, d_partial = pl.pallas_call(
         functools.partial(ffn_grads_kernel, count, left.shape[1]),
-        out_shape=(jax.ShapeDtypeStruct(shape, BF16), jax.ShapeDtypeStruct(resid.shape, BF16)),
-        in_specs=[vmem] * 7,
-        out_specs=[vmem] * 2,
+        out_shape=(jax.ShapeDtypeStruct(shape, BF16), jax.ShapeDtypeStruct(resid.shape, BF16), jax.ShapeDtypeStruct(left.shape, BF16)),
+        in_specs=[vmem] * 8,
+        out_specs=[pl.BlockSpec(memory_space=pltpu.HBM), vmem, vmem],
         scratch_shapes=pair_scratch(shape) + line_scratch(count, resid.shape[0], resid.shape[1], True, False),
         compiler_params=pltpu.CompilerParams(collective_id=6, has_side_effects=True, vmem_limit_bytes=58 * 2**20),
         cost_estimate=pl.CostEstimate(
             flops=2 * left.shape[0] * left.shape[1] * shape[2], bytes_accessed=50 * 2**20, transcendentals=0
         ),
         name="ffn_grads",
-    )(left, right, *grads, ffn_partial, resid)
-    return sums.reshape(shape[0] * shape[1], shape[2]), result
+    )(left, right, *grads, ffn_partial, resid, gate_up)
+    return sums.reshape(shape[0] * shape[1], shape[2]), result, d_partial
 
 
 def group_scatter(sums):
     shard = lax.psum_scatter(sums, ("pair", "fsdp"), scatter_dimension=0, tiled=True)
     return with_layout_constraint(shard, Layout(major_to_minor=(0, 1))).astype(F32)
-
-
-def shifted(count, shift):
-    return [(index, (index + shift) % count) for index in range(count)]
-
-
-def gather_rows(rows):
-    count = lax.axis_size("tensor")
-    mine = lax.axis_index("tensor")
-    height = rows.shape[0]
-    whole = jnp.zeros((count * height, rows.shape[1]), rows.dtype)
-    whole = lax.dynamic_update_slice_in_dim(whole, rows, mine * height, 0)
-    for shift in range(1, count):
-        came = lax.ppermute(rows, "tensor", shifted(count, shift))
-        source = lax.rem(mine + count - shift, count)
-        whole = lax.dynamic_update_slice_in_dim(whole, came, source * height, 0)
-    return whole
-
-
-def send_rows(rows):
-    count = lax.axis_size("tensor")
-    return [lax.ppermute(rows, "tensor", shifted(count, shift)) for shift in range(1, count)]
-
-
-def place_rows(rows, came):
-    count = lax.axis_size("tensor")
-    mine = lax.axis_index("tensor")
-    height = rows.shape[0]
-    whole = jnp.zeros((count * height, rows.shape[1]), rows.dtype)
-    whole = lax.dynamic_update_slice_in_dim(whole, rows, mine * height, 0)
-    for shift in range(1, count):
-        source = lax.rem(mine + count - shift, count)
-        whole = lax.dynamic_update_slice_in_dim(whole, came[shift - 1], source * height, 0)
-    return whole
 
 
 def gather_weights(pieces, axis):
@@ -1288,15 +1313,9 @@
     late, rows_one = lax.optimization_barrier(((w_gate, w_up, w_down), rows_one))
     gate_up = gather_weights([piece(late[0], 0), piece(late[1], 0)], 0)
     down = gather_weights([piece(late[2], 1)], 1)
-    late_grad, rows_one = lax.optimization_barrier((output_grad, rows_one))
-    came = send_rows(late_grad)
-    raw = dot(rows_one, mix_full)
-    gated, mixed, solve, update, state = delta_forward(
-        doc_starts, seq_lengths, raw, conv_q, conv_k, conv_v, gain_head
+    raw, gated, mixed, solve, update, state, attn_partial, grad_rows = attend(
+        doc_starts, seq_lengths, rows_one, mix_full, project_full, output_grad, conv_q, conv_k, conv_v, gain_head
     )
-    gated, came = lax.optimization_barrier((gated, came))
-    grad_rows = place_rows(output_grad, came)
-    attn_partial = dot(gated, project_full).astype(BF16)
     whole_rows = jax.ShapeDtypeStruct(rows_one.shape, BF16)
     own_rows = jax.ShapeDtypeStruct(layer_input.shape, F32)
     gain_sums = jax.ShapeDtypeStruct((1, layer_input.shape[1]), F32)
@@ -1311,11 +1330,9 @@
     hidden = (silu_gate * up_val).astype(BF16)
     d_gate = (d_hidden * up_val * gate_sig * (1.0 + gate_val * (1.0 - gate_sig))).astype(BF16)
     d_up = (d_hidden * silu_gate).astype(BF16)
-    d_both = jnp.concatenate([d_gate, d_up], axis=1)
     ffn_partial = dot(hidden, down).astype(BF16)
-    ffn_sums, result = ffn_grads(rows_two, grad_rows, (d_gate, d_up, hidden), ffn_partial, resid)
+    ffn_sums, result, d_partial = ffn_grads(rows_two, grad_rows, (d_gate, d_up, hidden), ffn_partial, resid, gate_up)
     ffn_shard = group_scatter(ffn_sums)
-    d_partial, _ = lax.optimization_barrier((dot_nt(d_both, gate_up).astype(BF16), ffn_sums))
     d_attn, d_resid, grad_second = line_call(
         turn_kernel, "turn", 3, True, (whole_rows, own_rows, gain_sums), (d_partial, resid, output_grad, gain_two)
     )

time: 459 us -> 446 us (0.972)
  Pallas kernels: 307 us -> 338 us
  matrix products: 58.8 us -> 36.4 us
  waiting for transfers between devices: 12.4 us -> 0.79 us
  local copies, waits for them, and re-layouts: 45.6 us -> 39.4 us
  starting transfers between devices: 4.84 us -> 0.16 us
    pallas_call x1, Pallas kernels: 17.1 us -> 46.8 us  [attend(): pl.pallas_call(functools.partial(forward_kernel, count), out_shape=(jax.S...]
    ppermute x3 -> x0, waiting for transfers between devices: 12.3 us -> none  [send_rows(): lax.ppermute(rows, 'tensor', shifted(count, shift))]
    dot_general x4 -> x2, matrix products: 28.7 us -> 17.3 us  [dot(): return jnp.dot(left, right, preferred_element_type=F32)]
    dot_general x4 -> x3, matrix products: 30.2 us -> 19.1 us  [dot_nt(): lax.dot_general(left, right, (((1,), (1,)), ((), ())), preferred_element_...]
    dynamic_update_slice x4 -> x0, local copies, waits for them, and re-layouts: 6.46 us -> none  [the longest x3 5.63 us: place_rows(): lax.dynamic_update_slice_in_dim(whole, came[shift - 1], source * height, 0)]
    ppermute x3 -> x0, starting transfers between devices: 4.68 us -> none  [send_rows(): lax.ppermute(rows, 'tensor', shifted(count, shift))]
  transfers between devices with their start and end apart: 7 -> 4, of which waited for: 1 -> 1; matrix products, arithmetic and copies ran while one was open for 13% -> 6% of each run, Pallas kernels for 47% -> 55%
where the time goes in v4:
time: 446 us; the launch traced here: 437 us
  Pallas kernels  338 us (76%)
  local copies, waits for them, and re-layouts  39.4 us (9%)
  matrix products  36.4 us (8%)
  between operations  15.4 us (3%)
  other arithmetic  6.74 us (2%)
    pallas_call x3, Pallas kernels, line_call(): pl.pallas_call(functools.partial(kernel, count), out_shape=out_shape, in_...  158 us
    pallas_call x1, Pallas kernels, ffn_grads(): pl.pallas_call(functools.partial(ffn_grads_kernel, count, left.shape[1]),...  50 us
    pallas_call x1, Pallas kernels, attend(): pl.pallas_call(functools.partial(forward_kernel, count), out_shape=(jax.S...  46.8 us
    pallas_call x1, Pallas kernels, enter(): pl.pallas_call(functools.partial(enter_kernel, (replicas, shards, count))...  45.6 us
    unnamed x98, local copies, waits for them, and re-layouts  28.8 us
    dot_general x3, matrix products, dot_nt(): lax.dot_general(left, right, (((1,), (1,)), ((), ())), preferred_element_...  19.1 us
    dot_general x2, matrix products, dot(): return jnp.dot(left, right, preferred_element_type=F32)  17.3 us
    pallas_call x1, Pallas kernels, delta_backward(): pl.pallas_call(backward_kernel, out_shape=(jax.ShapeDtypeStruct((rows, 4...  15.4 us
  transfers between devices with their start and end apart: 4, of which 1 were waited for; matrix products, arithmetic and copies ran while one was open for 6% of the time, Pallas kernels for 55%

profile of v4, /device:TPU:0, one launch (start us, length us, event | category | flops | bytes accessed | tf_op | source)
XLA Modules:
  0.0 436.7 jit_solution(8962724534671097077)
XLA Ops:
  7.3 0.8 broadcast_in_dim.11.gain_one_ref
  8.1 0.7 broadcast_in_dim.12.gain_two_ref
  8.8 1.2 copy-done.5
  10.0 1.2 copy-done.6
  11.2 1.2 copy-done.7
  12.5 1.2 copy-done.8
  13.7 1.2 copy-done.9
  14.9 1.0 copy-done.10
  16.0 0.7 copy-done.12
  16.6 45.6 %enter.1 = (bf16[512,2048]{1,0:T(8,128)(2,1)S(1)}, bf16[2048,2176]{1,0:T(8,128)(2,1)}, bf16[512,2048]{1,0:T(8,128)(2,1)S(1)}, f32[2,2048]{1,0:T(2,128)S(1)}) custom-call(bf16[128,2048]{1,0:T(8,128)(2,1)S(1)} %copy-done.10, bf16[1,1024]{1,0:T(2,128)(2,1)S(1)} %broadcast_in_dim.11.gain_one_ref, bf16[1,1024]{1,0:T(2,128)(2,1)S(1)} %broadcast_in_dim.12.gain_two_ref, ...), custom_call_target="tpu_custom_call" | custom-call | flops 1000000000 | bytes 62914560 | tf_op jit(solution)/shard_map/enter/pallas_call | solution.py:1087
  62.3 1.3 copy-done.13
  63.6 1.3 copy-done.15
  64.9 1.4 constant_dynamic-slice_fusion
  66.4 1.2 pad_maximum_fusion
  67.7 1.0 constant_dynamic-slice_fusion.2
  69.5 1.0 copy-done.17
  70.5 46.8 %attend.1 = (f32[512,2176]{1,0:T(8,128)}, bf16[512,512]{1,0:T(8,128)(2,1)S(1)}, f32[512,512]{1,0:T(8,128)S(1)}, bf16[8,256,256]{2,1,0:T(8,128)(2,1)S(1)}, bf16[5...) custom-call(s32[1,4]{1,0:T(1,128)S(1)} %copy-done.18, ...), custom_call_target="tpu_custom_call" | custom-call | flops 6442450944 | bytes 41943040 | tf_op jit(solution)/shard_map/attend/pallas_call | solution.py:246
  117.3 1.0 copy-done.26
  118.3 1.0 copy-done.28
  119.3 0.8 copy-done.30
  120.1 0.8 copy-done.34
  120.9 59.8 %middle.1 = (bf16[512,2048]{1,0:T(8,128)(2,1)S(1)}, f32[128,2048]{1,0:T(8,128)S(1)}) custom-call(bf16[512,2048]{1,0:T(8,128)(2,1)S(1)} %get-tuple-element.55.partial_ref, bf16[128,2048]{1,0:T(8,128)(2,1)S(1)} %copy-done.11, f32[1,2048]{1,0:T(1,128)S(1)} %get-tuple-element.116.gain_ref), custom_call_target="tpu_custom_call" | custom-call | flops 1000000000 | bytes 62914560 | tf_op jit(solution)/shard_map/middle/pallas_call | solution.py:876
  180.7 1.0 copy-done.22
  181.7 1.3 copy-done.24
  183.0 12.6 %fusion.5 = f32[512,2816]{1,0:T(8,128)} fusion(bf16[512,2048]{1,0:T(8,128)(2,1)} %copy-done.24, bf16[2048,2816]{1,0:T(8,128)(2,1)} %all-gather.5.cloned.1.call-done.gate_up_ref), kind=kOutput, calls=%fused_computation.19 | convolution fusion | flops 5905580032 | bytes 19398656 | tf_op jit(solution)/shard_map/dot_general | solution.py:31
  195.6 9.4 %multiply_convert_fusion.1 = (bf16[512,1408]{1,0:T(8,128)(2,1)}, bf16[512,1408]{1,0:T(8,128)(2,1)}, bf16[512,1408]{1,0:T(8,128)(2,1)S(1)}) fusion(f32[512,2816]{1,0:T(8,128)} %fusion.5, bf16[512,2048]{1,0:T(8,128)(2,1)S(1)} %copy-done.42, bf16[1408,2048]{1,0:T(8,128)(2,1)} %all-gather.3.cloned.1.call-done), kind=kOutput, calls=%fused_computation.3 | convolution fusion | flops 2963603456 | bytes 17956864 | tf_op jit(solution)/shard_map/dot_general | solution.py:35
  205.0 4.7 %convolution_convert_fusion.partial_ref = bf16[512,2048]{1,0:T(8,128)(2,1)} fusion(bf16[512,1408]{1,0:T(8,128)(2,1)S(1)} %get-tuple-element.104.hidden_ref, bf16[1408,2048]{1,0:T(8,128)(2,1)S(1)} %copy-done.40), kind=kOutput, calls=%fused_computation | convolution fusion | flops 2953838592 | bytes 9306112 | tf_op jit(solution)/shard_map/dot_general | solution.py:31
  209.7 50.0 %ffn_grads.1 = (bf16[4,256,4224]{2,1,0:T(8,128)(2,1)}, bf16[128,2048]{1,0:T(8,128)(2,1)}, bf16[512,2048]{1,0:T(8,128)(2,1)}) custom-call(bf16[512,2048]{1,0:T(8,128)(2,1)} %copy-done.24, bf16[512,2048]{1,0:T(8,128)(2,1)} %get-tuple-element.58.right_ref, bf16[512,1408]{1,0:T(8,128)(2,1)} %get-tuple-element.103.d_gate_ref, ...), custom_call_target="tpu_custom_call" | custom-call | flops 8858370048 | bytes 52428800 | tf_op jit(solution)/shard_map/ffn_grads/pallas_call | solution.py:1245
  259.8 1.5 copy-done.19
  261.3 1.2 copy-done.23
  262.5 57.8 %turn.1 = (bf16[512,2048]{1,0:T(8,128)(2,1)S(1)}, f32[128,2048]{1,0:T(8,128)S(1)}, f32[1,2048]{1,0:T(1,128)S(1)}) custom-call(bf16[512,2048]{1,0:T(8,128)(2,1)S(1)} %copy-done.19, f32[128,2048]{1,0:T(8,128)S(1)} %copy-done.23, bf16[128,2048]{1,0:T(8,128)(2,1)S(1)} %copy-done.17, f32[1,2048]{1,0:T(1,128)S(1)} %get-tuple-element.116.gain_ref), custom_call_target="tpu_custom_call" | custom-call | flops 1000000000 | bytes 62914560 | tf_op jit(solution)/shard_map/turn/pallas_call | solution.py:876
  320.4 1.3 fusion.6.grad_ref
  322.4 15.4 %delta_backward.1 = (bf16[512,2176]{1,0:T(8,128)(2,1)S(1)}, f32[4,1536]{1,0:T(4,128)S(1)}, f32[1,128]{1,0:T(1,128)S(1)}) custom-call(s32[1,4]{1,0:T(1,128)S(1)} %copy-done.18, s32[1]{0:T(128)S(6)} %copy.42.length_ref, f32[512,2176]{1,0:T(8,128)} %get-tuple-element.64.raw_ref, f32[4,512]{1,0:T(4,128)S(1)} %convert_element_type.31.conv_q_ref, ...), custom_call_target="tpu_custom_call" | custom-call | flops 3221225472 | bytes 16777216 | tf_op jit(solution)/shard_map/delta_backward/pallas_call | solution.py:421
  337.9 11.3 %mix_grads.1 = bf16[4,256,2688]{2,1,0:T(8,128)(2,1)S(1)} custom-call(bf16[512,2048]{1,0:T(8,128)(2,1)S(1)} %copy-done.14, bf16[512,2048]{1,0:T(8,128)(2,1)S(1)} %get-tuple-element.70.right_ref, bf16[512,2176]{1,0:T(8,128)(2,1)S(1)} %get-tuple-element.71.first_ref, bf16[512,512]{1,0:T(8,128)(2,1)S(1)} %copy-done.35), custom_call_target="tpu_custom_call" | custom-call | flops 5637144576 | bytes 31457280 | tf_op jit(solution)/shard_map/mix_grads/pallas_call | solution.py:1185
  349.2 2.4 copy-done.2
  351.6 4.0 convert_element_type.39
  355.7 8.4 %convolution_convert_fusion.1.partial_ref = bf16[512,2048]{1,0:T(8,128)(2,1)S(1)} fusion(bf16[512,2176]{1,0:T(8,128)(2,1)} %copy-done.25, bf16[2048,2176]{1,0:T(8,128)(2,1)} %get-tuple-element.53.mix_ref), kind=kOutput, calls=%fused_computation.1 | convolution fusion | flops 4564451328 | bytes 13238272 | tf_op jit(solution)/shard_map/dot_general | solution.py:35
  364.1 40.0 %last.1 = (f32[128,2048]{1,0:T(8,128)S(1)}, f32[1,2048]{1,0:T(1,128)S(1)}) custom-call(bf16[512,2048]{1,0:T(8,128)(2,1)S(1)} %convolution_convert_fusion.1.partial_ref, bf16[128,2048]{1,0:T(8,128)(2,1)S(1)} %copy-done.11, f32[128,2048]{1,0:T(8,128)S(1)} %copy-done.21, f32[1,2048]{1,0:T(1,128)S(1)} %get-tuple-element.115.gain_ref), custom_call_target="tpu_custom_call" | custom-call | flops 1000000000 | bytes 62914560 | tf_op jit(solution)/shard_map/last/pallas_call | solution.py:876
  404.2 11.1 %reduce_small.1 = (f32[2,256]{1,0:T(2,128)S(1)}, f32[1,128]{1,0:T(1,128)S(1)}, f32[4,1536]{1,0:T(4,128)S(1)}) custom-call(f32[2,2048]{1,0:T(2,128)S(1)} %pad_maximum_fusion.1.gain_ref, f32[1,128]{1,0:T(1,128)S(1)} %get-tuple-element.76.head_ref, f32[4,1536]{1,0:T(4,128)S(1)} %get-tuple-element.77.conv_ref), custom_call_target="tpu_custom_call" | custom-call | tf_op jit(solution)/shard_map/reduce_small/pallas_call | solution.py:531
  416.5 1.9 slice_bitcast_fusion
  418.3 1.5 copy.38
  419.9 0.7 reduce-scatter.5.cloned.1.call-done
  420.6 0.8 slice.78
  422.1 1.5 convert_element_type.40
  423.7 1.0 copy.37
  424.7 2.7 fusion.1
  427.5 0.8 copy.43
  428.3 1.0 copy.44
  (96 shorter events, 3.6 us)
Async XLA Ops:
  7.2 60.5 %copy-start = (bf16[1408,1024]{1,0:T(8,128)(2,1)S(1)}, bf16[1408,1024]{1,0:T(8,128)(2,1)}, u32[]{:S(2)}) copy-start(bf16[1408,1024]{1,0:T(8,128)(2,1)} %param.34) | copy-start | bytes 8650756
  7.2 175.8 %all-gather.5.cloned.1.call-start = ((), (), s32[]{:S(2)}) async-start(), calls=%async_computation.3 | async-start | bytes 12976128 | tf_op jit(solution)/shard_map/all_gather | solution.py:1266
  8.8 1.2 copy-start.5
  10.0 1.2 copy-start.6
  11.2 1.2 copy-start.7
  12.5 1.2 copy-start.8
  13.7 1.2 copy-start.9
  14.9 1.0 copy-start.10
  62.3 1.3 copy-start.13
  63.6 1.3 copy-start.15
  66.3 3.0 copy-start.37
  66.4 3.0 copy-start.38
  66.4 3.1 copy-start.39
  66.4 3.1 copy-start.41
  66.4 3.1 copy-start.18
  67.6 127.9 %all-gather.3.cloned.1.call-start = ((), (), s32[]{:S(2)}) async-start(), calls=%async_computation.2 | async-start | bytes 6488064 | tf_op jit(solution)/shard_map/all_gather | solution.py:1266
  68.7 283.0 %reduce-scatter.3.cloned.1.call-start = ((), (), s32[]{:S(2)}) async-start(), calls=%async_computation.4 | async-start | bytes 10813440 | tf_op jit(solution)/shard_map/reduce_scatter | solution.py:1261
  69.5 1.0 copy-start.17
  70.5 50.4 %copy-start.11 = (bf16[128,2048]{1,0:T(8,128)(2,1)S(1)}, bf16[128,2048]{1,0:T(8,128)(2,1)}, u32[]{:S(2)}) copy-start(bf16[128,2048]{1,0:T(8,128)(2,1)} %input_ref.5) | copy-start | bytes 1572868
  117.3 1.0 copy-start.26
  118.3 1.0 copy-start.28
  119.3 0.8 copy-start.30
  120.9 74.7 %copy-start.32 = (bf16[4,128,128]{2,1,0:T(8,128)(2,1)}, bf16[4,128,128]{2,1,0:T(8,128)(2,1)S(1)}, u32[]{:S(2)}) copy-start(bf16[4,128,128]{2,1,0:T(8,128)(2,1)S(1)} %get-tuple-element.68.state_ref) | copy-start | bytes 393220
  180.7 1.0 copy-start.22
  181.7 1.3 copy-start.24
  183.0 12.6 %copy-start.42 = (bf16[512,2048]{1,0:T(8,128)(2,1)S(1)}, bf16[512,2048]{1,0:T(8,128)(2,1)}, u32[]{:S(2)}) copy-start(bf16[512,2048]{1,0:T(8,128)(2,1)} %get-tuple-element.58.right_ref) | copy-start | bytes 6291460
  195.6 9.4 %copy-start.40 = (bf16[1408,2048]{1,0:T(8,128)(2,1)S(1)}, bf16[1408,2048]{1,0:T(8,128)(2,1)}, u32[]{:S(2)}) copy-start(bf16[1408,2048]{1,0:T(8,128)(2,1)} %all-gather.3.cloned.1.call-done) | copy-start | bytes 17301508
  204.9 4.8 %copy-start.43 = (bf16[512,1408]{1,0:T(8,128)(2,1)}, bf16[512,1408]{1,0:T(8,128)(2,1)S(1)}, u32[]{:S(2)}) copy-start(bf16[512,1408]{1,0:T(8,128)(2,1)S(1)} %get-tuple-element.104.hidden_ref) | copy-start | bytes 4325380
  259.7 1.6 copy-start.19
  259.7 160.9 %reduce-scatter.5.cloned.1.call-start = ((), (), s32[]{:S(2)}) async-start(), calls=%async_computation.5 | async-start | bytes 6881280 | tf_op jit(solution)/shard_map/reduce_scatter | solution.py:1261
  259.8 60.6 %copy-start.16 = (bf16[512,2048]{1,0:T(8,128)(2,1)S(1)}, bf16[512,2048]{1,0:T(8,128)(2,1)}, u32[]{:S(2)}) copy-start(bf16[512,2048]{1,0:T(8,128)(2,1)} %copy-done.15) | copy-start | bytes 6291460
  261.3 1.2 copy-start.23
  320.4 1.4 copy-start.20
  320.4 1.6 copy-start.27
  320.4 1.9 copy-start.29
  320.4 2.0 copy-start.31
  320.4 2.0 copy-start.33
  322.4 15.4 %copy-start.14 = (bf16[512,2048]{1,0:T(8,128)(2,1)S(1)}, bf16[512,2048]{1,0:T(8,128)(2,1)}, u32[]{:S(2)}) copy-start(bf16[512,2048]{1,0:T(8,128)(2,1)} %copy-done.13) | copy-start | bytes 6291460
  322.4 15.5 %copy-start.35 = (bf16[512,512]{1,0:T(8,128)(2,1)S(1)}, bf16[512,512]{1,0:T(8,128)(2,1)}, u32[]{:S(2)}) copy-start(bf16[512,512]{1,0:T(8,128)(2,1)} %copy-done.34) | copy-start | bytes 1572868
  337.9 11.3 %copy-start.25 = (bf16[512,2176]{1,0:T(8,128)(2,1)}, bf16[512,2176]{1,0:T(8,128)(2,1)S(1)}, u32[]{:S(2)}) copy-start(bf16[512,2176]{1,0:T(8,128)(2,1)S(1)} %get-tuple-element.71.first_ref) | copy-start | bytes 6684676
  349.2 2.4 copy-start.2
  355.6 60.8 %slice-start = ((s8[4325376]{0:T(1024)(128)(4,1)}), s8[4194304]{0:T(1024)(128)(4,1)S(1)}, s32[]{:S(2)}) async-start(s8[4325376]{0:T(1024)(128)(4,1)} %bitcast.26), calls=%async_computation.6 | async-start | bytes 8388608
  355.7 8.5 %copy-start.21 = (f32[128,2048]{1,0:T(8,128)S(1)}, f32[128,2048]{1,0:T(8,128)}, u32[]{:S(2)}) copy-start(f32[128,2048]{1,0:T(8,128)} %copy-done.20) | copy-start | bytes 3145732
  355.7 60.8 %slice-start.1 = ((s8[4325376]{0:T(1024)(128)(4,1)}), s8[131072]{0:T(1024)(128)(4,1)S(1)}, s32[]{:S(2)}) async-start(s8[4325376]{0:T(1024)(128)(4,1)} %bitcast.26), calls=%async_computation.7 | async-start | bytes 262144
  404.1 14.2 %copy-start.3 = (f32[128,2048]{1,0:T(8,128)}, f32[128,2048]{1,0:T(8,128)S(1)}, u32[]{:S(2)}) copy-start(f32[128,2048]{1,0:T(8,128)S(1)} %get-tuple-element.139) | copy-start | bytes 3145732
  423.7 6.0 %copy-start.1 = (bf16[1408,1024]{1,0:T(8,128)(2,1)S(1)}, bf16[1408,1024]{1,0:T(8,128)(2,1)}, u32[]{:S(2)}) copy-start(bf16[1408,1024]{1,0:T(8,128)(2,1)} %param.34) | copy-start | bytes 8650756
  424.7 2.7 copy-start.36
  424.7 3.5 copy-start.4
  (2 other events, 1.5 us)
Sparse Core Ops, SparseCore 0:
  67.7 67.0 all-gather.4
  137.3 44.3 all-gather.2
  259.9 85.7 reduce-scatter.2
  355.8 64.7 reduce-scatter.4

commit v5 on v4

--- a/solution.py
+++ b/solution.py
@@ -129,150 +129,6 @@
 ATTEND_TIMES = (1.2, 1.5, 0.9)
 
 
-def forward_kernel(
-    count, starts_ref, length_ref, rows_ref, mix_ref, project_ref, own_grad_ref, conv_q_ref, conv_k_ref, conv_v_ref, gain_ref,
-    raw_ref, gated_ref, mixed_ref, solve_ref, update_ref, state_ref, partial_ref, grad_rows_ref,
-    keep_ref, live_ref, carry_ref, strict_ref, incl_ref, *sems,
-):
-    rows, head_width = live_ref.shape
-    width = gated_ref.shape[1]
-    chunks = rows // CHUNK
-    heads = width // head_width
-    tiles, ends = 4 * width // TILE, project_ref.shape[1] // PROJECT_TILE
-    shared = [ATTEND_TIMES[0]] * tiles + [ATTEND_TIMES[1]] * (3 * heads) + [ATTEND_TIMES[2]] * ends
-    line = Line(count, rows // count, sems, shared, False, True, ATTEND_PARTS, ATTEND_LATENCY)
-    line.rows_ref, line.source_ref = grad_rows_ref, own_grad_ref
-    line.greet()
-    own = pl.ds(pl.multiple_of(line.place * line.rows, line.rows), line.rows)
-    grad_rows_ref[own, :] = own_grad_ref[...]
-
-    @pl.loop(0, tiles)
-    def _(tile):
-        line.run_at(0, tile, tiles)
-        cols = pl.ds(pl.multiple_of(tile * TILE, TILE), TILE)
-        raw_ref[:, cols] = dot(rows_ref[...], mix_ref[:, cols])
-
-    raw_ref[:, 4 * width :] = dot(rows_ref[...], mix_ref[:, 4 * width :])
-    fill_masks(starts_ref, length_ref, keep_ref, live_ref, carry_ref)
-    for chunk in range(chunks):
-        strict, incl = pair_mask(starts_ref, chunk)
-        strict_ref[chunk] = jnp.where(strict, 1.0, 0.0)
-        incl_ref[chunk] = jnp.where(incl, 1.0, 0.0)
-
-    @pl.loop(0, heads)
-    def _(head):
-        line.run_at(tiles, head, heads, 3)
-        start = pl.multiple_of(head * head_width, head_width)
-
-        def stream(index):
-            return raw_ref[:, pl.ds(pl.multiple_of(index * width + start, head_width), head_width)]
-
-        cols = pl.ds(start, head_width)
-        conv, _ = convolve(stream(Q), conv_q_ref[:, cols], keep_ref)
-        _, act, scale = unit_rows(conv)
-        query = (act * scale).astype(BF16)
-        conv, _ = convolve(stream(K), conv_k_ref[:, cols], keep_ref)
-        _, act, scale = unit_rows(conv)
-        keyed = act * scale
-        key_low = keyed.astype(BF16)
-        conv, _ = convolve(stream(V), conv_v_ref[:, cols], keep_ref)
-        valued = conv * sigmoid(conv)
-        rate = sigmoid(column(raw_ref[:, 4 * width :], head)) * live_ref[...]
-        scaled_value = (valued * rate).astype(BF16)
-        scaled_key = keyed * rate
-        system = []
-        for chunk in range(chunks):
-            span = slice(chunk * CHUNK, (chunk + 1) * CHUNK)
-            pair = dot_nt(key_low[span], key_low[span])
-            wide = jnp.concatenate([rate[span]] * (CHUNK // head_width), axis=1)
-            system.append(pair * wide * strict_ref[chunk])
-        line.run_at(tiles + 1, head, heads, 3)
-        memory = None
-        inverses = invert(system)
-        line.run_at(tiles + 2, head, heads, 3)
-        for chunk, solved in enumerate(inverses):
-            span = slice(chunk * CHUNK, (chunk + 1) * CHUNK)
-            solve_low = solved.astype(BF16)
-            solve_ref[head * chunks + chunk] = solve_low
-            score = dot_nt(query[span], key_low[span]) * incl_ref[chunk]
-            if chunk == 0:
-                update = dot(solve_low, scaled_value[span])
-                update_low = update.astype(BF16)
-                mixed = dot(score.astype(BF16), update_low)
-            else:
-                carry = carry_ref[chunk - 1][span]
-                right = jnp.concatenate(
-                    [scaled_value[span], (scaled_key[span] * carry).astype(BF16)], axis=1
-                )
-                both = dot(solve_low, right)
-                memory_low = memory.astype(BF16)
-                state_ref[head * (chunks - 1) + chunk - 1] = memory_low
-                update = both[:, :head_width] - dot(both[:, head_width:].astype(BF16), memory_low)
-                update_low = update.astype(BF16)
-                mixed = carry * dot(query[span], memory_low) + dot(score.astype(BF16), update_low)
-            update_ref[span, cols] = update_low
-            mixed_ref[span, cols] = mixed
-            if chunk + 1 < chunks:
-                last = (keyed[span] * carry_ref[chunk][span]).astype(BF16)
-                fresh = dot_tn(last, update_low)
-                if memory is None:
-                    memory = fresh
-                else:
-                    memory = memory * carry_ref[chunk - 1][span][CHUNK - 1 :] + fresh
-        mixed = mixed_ref[:, cols]
-        norm = lax.rsqrt(lane_sum(mixed * mixed) * (1.0 / head_width) + 1e-05)
-        gating = stream(G)
-        gated = mixed * norm * gain_ref[...] * (gating * sigmoid(gating)) * live_ref[...]
-        gated_ref[:, cols] = gated.astype(BF16)
-
-    @pl.loop(0, ends)
-    def _(tile):
-        line.run_at(tiles + 3 * heads, tile, ends)
-        cols = pl.ds(pl.multiple_of(tile * PROJECT_TILE, PROJECT_TILE), PROJECT_TILE)
-        partial_ref[:, cols] = dot(gated_ref[...], project_ref[:, cols]).astype(BF16)
-
-    line.run(tiles + 3 * heads + ends)
-    line.drain()
-
-
-def attend(starts, length, rows_one, mix_full, project_full, own_grad, conv_q, conv_k, conv_v, gain):
-    rows, features = rows_one.shape
-    head_width = gain.shape[-1]
-    width = conv_q.shape[1]
-    heads, chunks = width // head_width, rows // CHUNK
-    count = lax.axis_size("tensor")
-    vmem = pl.BlockSpec(memory_space=pltpu.VMEM)
-    smem = pl.BlockSpec(memory_space=pltpu.SMEM)
-    return pl.pallas_call(
-        functools.partial(forward_kernel, count),
-        out_shape=(
-            jax.ShapeDtypeStruct((rows, mix_full.shape[1]), F32),
-            jax.ShapeDtypeStruct((rows, width), BF16),
-            jax.ShapeDtypeStruct((rows, width), F32),
-            jax.ShapeDtypeStruct((heads * chunks, CHUNK, CHUNK), BF16),
-            jax.ShapeDtypeStruct((rows, width), BF16),
-            jax.ShapeDtypeStruct((heads * (chunks - 1), head_width, head_width), BF16),
-            jax.ShapeDtypeStruct((rows, features), BF16),
-            jax.ShapeDtypeStruct((rows, features), BF16),
-        ),
-        in_specs=[smem, smem] + [vmem] * 8,
-        out_specs=[vmem] * 8,
-        scratch_shapes=[
-            pltpu.VMEM((KERNEL - 1, rows, head_width), F32),
-            pltpu.VMEM((rows, head_width), F32),
-            pltpu.VMEM((chunks - 1, rows, head_width), F32),
-            pltpu.VMEM((chunks, CHUNK, CHUNK), F32),
-            pltpu.VMEM((chunks, CHUNK, CHUNK), F32),
-        ]
-        + line_scratch(count, rows // count, features, False, True, ATTEND_PARTS),
-        compiler_params=pltpu.CompilerParams(collective_id=8, has_side_effects=True, vmem_limit_bytes=48 * 2**20),
-        cost_estimate=pl.CostEstimate(
-            flops=2 * 24 * heads * chunks * CHUNK**3, bytes_accessed=40 * 2**20, transcendentals=0
-        ),
-        name="attend",
-    )(starts, length, rows_one, mix_full, project_full, own_grad, conv_q, conv_k, conv_v, gain)
-
-
 def backward_kernel(
     starts_ref, length_ref, raw_ref, conv_q_ref, conv_k_ref, conv_v_ref, gain_ref,
     mixed_ref, solve_ref, update_ref, state_ref, grad_ref,
@@ -313,15 +169,15 @@
         d_mixed = norm * (d_normal - normal * (lane_sum(d_normal * normal) * (1.0 / head_width)))
         d_mixed_low = d_mixed.astype(BF16)
 
-        conv_q, parts_q = convolve(raw_ref[:, place(Q)], conv_q_ref[:, cols], keep_ref)
+        conv_q, parts_q = convolve(raw_ref[:, place(Q)], conv_q_ref[:, cols].astype(F32), keep_ref)
         gate_q, act_q, scale_q = unit_rows(conv_q)
         unit_q = act_q * scale_q
         query = unit_q.astype(BF16)
-        conv_k, parts_k = convolve(raw_ref[:, place(K)], conv_k_ref[:, cols], keep_ref)
+        conv_k, parts_k = convolve(raw_ref[:, place(K)], conv_k_ref[:, cols].astype(F32), keep_ref)
         gate_k, act_k, scale_k = unit_rows(conv_k)
         keyed = act_k * scale_k
         key_low = keyed.astype(BF16)
-        conv_v, parts_v = convolve(raw_ref[:, place(V)], conv_v_ref[:, cols], keep_ref)
+        conv_v, parts_v = convolve(raw_ref[:, place(V)], conv_v_ref[:, cols].astype(F32), keep_ref)
         gate_v = sigmoid(conv_v)
         valued = conv_v * gate_v
         sig = sigmoid(column(raw_ref[:, 4 * width :], head))
@@ -405,10 +261,10 @@
             d_act = scale * (d_unit - unit * lane_sum(d_unit * unit))
             return d_act * gate * (1.0 + conv - act)
 
-        conv_back(Q, unit_back(d_query_ref[...], unit_q, scale_q, conv_q, act_q, gate_q), parts_q, conv_q_ref[:, cols])
-        conv_back(K, unit_back(d_key_ref[...], keyed, scale_k, conv_k, act_k, gate_k), parts_k, conv_k_ref[:, cols])
+        conv_back(Q, unit_back(d_query_ref[...], unit_q, scale_q, conv_q, act_q, gate_q), parts_q, conv_q_ref[:, cols].astype(F32))
+        conv_back(K, unit_back(d_key_ref[...], keyed, scale_k, conv_k, act_k, gate_k), parts_k, conv_k_ref[:, cols].astype(F32))
         d_conv_v = d_value_ref[...] * gate_v * (1.0 + conv_v - valued)
-        conv_back(V, d_conv_v, parts_v, conv_v_ref[:, cols])
+        conv_back(V, d_conv_v, parts_v, conv_v_ref[:, cols].astype(F32))
 
 
 def delta_backward(starts, length, raw, conv_q, conv_k, conv_v, gain, mixed, solve, update, state, grad):
@@ -435,7 +291,7 @@
             pltpu.VMEM((chunks, CHUNK, CHUNK), F32),
         ]
         + [pltpu.VMEM((rows, head_width), F32)] * 4,
-        compiler_params=pltpu.CompilerParams(vmem_limit_bytes=48 * 1024 * 1024),
+        compiler_params=pltpu.CompilerParams(vmem_limit_bytes=18 * 2**20),
         cost_estimate=pl.CostEstimate(
             flops=2 * 12 * heads * chunks * CHUNK**3, bytes_accessed=16 * 2**20, transcendentals=0
         ),
@@ -548,7 +404,7 @@
             dma((group_size - 1, 2)),
             dma((group_size - 1, 2)),
         ],
-        compiler_params=pltpu.CompilerParams(collective_id=1, has_side_effects=True, vmem_limit_bytes=16 * 2**20),
+        compiler_params=pltpu.CompilerParams(collective_id=1, has_side_effects=True, vmem_limit_bytes=8 * 2**20),
         name="reduce_small",
     )(gain, head, conv)
 
@@ -650,6 +506,8 @@
 
 
 PARTS = 4
+LANES = 512
+FFN_MEMORY = 52 * 2**20
 TURN_PARTS = 4
 ATTEND_PARTS = 4
 ATTEND_LATENCY, FFN_LATENCY = 1.5, 1.5
@@ -726,8 +584,13 @@
             source = self.partial_ref.at[self.span(owner, part)]
             if kind == "forward":
                 self.sum_copy(source, step, slot, part).wait_recv()
-                mine = self.partial_ref[self.span(owner, part), :].astype(F32)
-                send[slot, part] = (mine + recv[slot, part].astype(F32)).astype(BF16)
+
+                @pl.loop(0, self.partial_ref.shape[1] // LANES)
+                def _(step_index):
+                    cols = pl.ds(pl.multiple_of(step_index * LANES, LANES), LANES)
+                    mine = self.partial_ref[self.span(owner, part), cols].astype(F32)
+                    send[slot, part, :, cols] = (mine + recv[slot, part, :, cols].astype(F32)).astype(BF16)
+
                 source = send.at[slot, part]
             copy = self.sum_copy(source, step, slot, part)
             copy.start()
@@ -765,26 +628,40 @@
                     self.run(base + stride * index)
 
     def collect(self, part):
-        self.total_ref[...] = self.partial_ref[self.span(self.place, part), :].astype(F32)
+        places = []
         for step in (1, -1):
             recv, send, _, _ = self.sums[step]
             slot = self.count - 1 - self.place if step > 0 else self.place
-
-            @pl.when(self.place > 0 if step > 0 else self.place < self.count - 1)
+            has = self.place > 0 if step > 0 else self.place < self.count - 1
+
+            @pl.when(has)
             def _():
                 self.sum_copy(send.at[0, part], step, slot, part).wait_recv()
-                self.total_ref[...] += recv[slot, part].astype(F32)
+
+            places.append((recv, slot, has))
+
+        @pl.loop(0, self.partial_ref.shape[1] // LANES)
+        def _(index):
+            cols = pl.ds(pl.multiple_of(index * LANES, LANES), LANES)
+            self.total_ref[:, cols] = self.partial_ref[self.span(self.place, part), cols].astype(F32)
+            for recv, slot, has in places:
+                @pl.when(has)
+                def _():
+                    self.total_ref[:, cols] += recv[slot, part, :, cols].astype(F32)
 
     def finish_all(self):
-        for part in range(self.parts):
-            self.run(part)
+        @pl.loop(0, self.parts)
+        def _(part):
+            self.run_at(0, part, self.parts)
             self.collect(part)
-            self.finish(part, pl.ds(part * self.part, self.part), self.span(self.place, part))
+            local = pl.ds(pl.multiple_of(part * self.part, self.part), self.part)
+            self.finish(part, local, self.span(self.place, part))
             if self.sends:
                 for place in range(self.count):
                     @pl.when(self.place == place)
                     def _():
                         self.spread_from(place, part)
+
         self.run(self.parts)
         self.drain()
 
@@ -844,11 +721,12 @@
         resid, total = resid_ref[local, :], line.total_ref[...]
         scale = rms_scale(resid)
         sums = jnp.sum(total * resid * scale, axis=0, keepdims=True)
-        d_gain_ref[...] = sums if part == 0 else d_gain_ref[...] + sums
+        d_gain_ref[...] += sums
         d_resid = grad_ref[local, :].astype(F32) + rms_back(resid, scale, gain_ref[...], total)
         d_resid_ref[local, :] = d_resid
         rows_ref[place, :] = d_resid.astype(BF16)
 
+    d_gain_ref[...] = jnp.zeros_like(d_gain_ref)
     line.partial_ref, line.rows_ref, line.finish = partial_ref, rows_ref, finish
     line.greet()
     line.finish_all()
@@ -861,9 +739,10 @@
         values, total = input_ref[local, :].astype(F32), line.total_ref[...]
         scale = rms_scale(values)
         sums = jnp.sum(total * values * scale, axis=0, keepdims=True)
-        d_gain_ref[...] = sums if part == 0 else d_gain_ref[...] + sums
+        d_gain_ref[...] += sums
         d_input_ref[local, :] = d_resid_ref[local, :] + rms_back(values, scale, gain_ref[...], total)
 
+    d_gain_ref[...] = jnp.zeros_like(d_gain_ref)
     line.partial_ref, line.finish = partial_ref, finish
     line.greet()
     line.finish_all()
@@ -882,17 +761,22 @@
             count, partial_rows // count, features, True, spreads, TURN_PARTS if spreads else PARTS
         ),
         compiler_params=pltpu.CompilerParams(
-            collective_id=ident, has_side_effects=True, vmem_limit_bytes=32 * 2**20
+            collective_id=ident, has_side_effects=True, vmem_limit_bytes=16 * 2**20
         ),
         cost_estimate=pl.CostEstimate(flops=10**9, bytes_accessed=60 * 2**20, transcendentals=0),
         name=name,
     )(*operands)
 
 
-def enter_kernel(
-    sizes, input_ref, gain_one_ref, gain_two_ref, beta_ref, gating_ref, query_ref, key_ref, value_ref, project_ref,
-    rows_ref, mix_ref, whole_project_ref, gains_ref,
-    all_rows, all_one, all_two, all_beta, local_sem, small_send, small_recv,
+def begin_kernel(
+    sizes, starts_ref, length_ref, input_ref, own_gains_ref, beta_ref, own_grad_ref,
+    conv_q_ref, conv_k_ref, conv_v_ref, gain_ref,
+    gating_ref, query_ref, key_ref, value_ref, project_ref, gate_ref, up_ref,
+    gains_ref, partial_ref, grad_rows_ref, rows_ref, mix_ref, whole_project_ref, gate_up_ref,
+    raw_ref, gated_ref, mixed_ref, solve_ref, update_ref, state_ref,
+    all_rows, normed, mix_all, project_all, ffn_all, raw_all, gated_all, mixed_all, solve_all, update_all, state_all,
+    keep_ref, live_ref, carry_ref, strict_ref, incl_ref,
+    all_gains, all_beta, local_sem, store_sem, small_send, small_recv,
     first_send, first_recv, second_send, second_recv, third_send, third_recv, *row_sems,
 ):
     replicas, shards, count = sizes
@@ -900,10 +784,16 @@
     width = query_ref.shape[1]
     heads = beta_ref.shape[0]
     share = query_ref.shape[0]
-    sources = (gating_ref, query_ref, key_ref, value_ref, project_ref)
-    streams = len(sources)
+    units = gate_ref.shape[1]
+    half = share // 2
+    streams = [(ref, mix_all, False, 0, share, index * width) for index, ref in enumerate((gating_ref, query_ref, key_ref, value_ref))]
+    streams.append((project_ref, project_all, True, 0, width, 0))
+    for first_row in (0, half):
+        for index, ref in enumerate((gate_ref, up_ref)):
+            streams.append((ref, ffn_all, False, first_row, half, index * units))
+    count_streams = len(streams)
     pairs = replicas // 2
-    line = Line(count, rows, row_sems, [], False, True, parts=2)
+    line = Line(count, rows, row_sems[:4], [], False, True, parts=2)
     line.rows_ref, line.source_ref = all_rows, input_ref
     replica, shard, place = line.replica, line.shard, line.place
     partner = replica + 1 - 2 * lax.rem(replica, 2)
@@ -914,28 +804,20 @@
     def shard_at(shift):
         return lax.rem(shard + shift, shards)
 
-    def piece(ref, stream, row, col, part):
-        if stream < 4:
-            size = share // replicas
-            return ref.at[
-                pl.ds(pl.multiple_of(row + part * size, size), size),
-                pl.ds(col + stream * width if col is not None else 0, width),
+    def held(stream, owner, part):
+        ref, whole, spread_cols, first_row, height, col = streams[stream]
+        size = height // replicas
+        if spread_cols:
+            return whole.at[
+                pl.ds(pl.multiple_of(part * size, size), size), pl.ds(pl.multiple_of(owner * share, 128), share)
             ]
-        size = width // replicas
-        return ref.at[
-            pl.ds(pl.multiple_of(part * size, size), size),
-            pl.ds(pl.multiple_of(row, 128), share),
-        ]
-
-    def held(stream, owner, part):
-        ref = mix_ref if stream < 4 else whole_project_ref
-        return piece(ref, stream, owner * share, 0, part)
+        start = owner * share + first_row + part * size
+        return whole.at[pl.ds(pl.multiple_of(start, size), size), pl.ds(col, ref.shape[1])]
 
     def own(stream, part):
-        ref = sources[stream]
-        if stream < 4:
-            return piece(ref, stream, 0, None, part)
-        return piece(ref, stream, 0, None, part)
+        ref, _, spread_cols, first_row, height, _ = streams[stream]
+        size = height // replicas
+        return ref.at[pl.ds(pl.multiple_of(first_row + part * size, size), size), :]
 
     def remote(source, target, send, recv, where):
         return pltpu.make_async_remote_copy(
@@ -979,7 +861,7 @@
 
     features = share * shards
     cols = pl.ds(pl.multiple_of(shard * share, 128), share)
-    smalls = ((gain_one_ref, all_one.at[:, cols]), (gain_two_ref, all_two.at[:, cols]), (beta_ref, all_beta.at[:, cols]))
+    smalls = ((own_gains_ref, all_gains.at[:, cols]), (beta_ref, all_beta.at[:, cols]))
 
     def small(shift, index):
         source, target = smalls[index]
@@ -996,38 +878,41 @@
             small(shift, index).start()
     for part in range(2):
         spread(part)
-    for stream in range(streams):
+    for stream in range(count_streams):
         for shift in range(1, shards):
             first(shift, stream, shard).start()
     locals_ = [pltpu.make_async_copy(source, target, local_sem.at[index]) for index, (source, target) in enumerate(smalls)]
-    for stream in range(4):
+    own_rows = pl.ds(pl.multiple_of(shard * share, share), share)
+    for index, ref in enumerate((gating_ref, query_ref, key_ref, value_ref)):
         locals_.append(pltpu.make_async_copy(
-            sources[stream],
-            mix_ref.at[pl.ds(pl.multiple_of(shard * share, share), share), pl.ds(stream * width, width)],
-            local_sem.at[3 + stream],
+            ref, mix_all.at[own_rows, pl.ds(index * width, width)], local_sem.at[2 + index],
         ))
-    locals_.append(pltpu.make_async_copy(project_ref, whole_project_ref.at[:, cols], local_sem.at[7]))
+    locals_.append(pltpu.make_async_copy(project_ref, project_all.at[:, cols], local_sem.at[6]))
+    for index, ref in enumerate((gate_ref, up_ref)):
+        locals_.append(pltpu.make_async_copy(
+            ref, ffn_all.at[own_rows, pl.ds(index * units, units)], local_sem.at[7 + index],
+        ))
     for copy in locals_:
         copy.start()
-    for copy in locals_[:3]:
+    for copy in locals_[:2]:
         copy.wait()
     for shift in range(1, shards):
         for index in range(len(smalls)):
             small(shift, index).wait()
-    gains_ref[...] = jnp.concatenate([all_one[...].astype(F32), all_two[...].astype(F32)], axis=0)
-    lanes = mix_ref.shape[1] - 4 * width
+    gains_ref[...] = all_gains[...].astype(F32)
+    lanes = mix_all.shape[1] - 4 * width
     beta = jnp.concatenate([all_beta[...].astype(F32), jnp.zeros((lanes - heads, features), F32)], axis=0)
-    mix_ref[:, 4 * width :] = beta.T.astype(BF16)
+    mix_all[:, 4 * width :] = beta.T.astype(BF16)
 
     def normalize(source, start, size):
         values = source[pl.ds(start, size), :].astype(F32)
         return (values * rms_scale(values) * gains_ref[0:1, :]).astype(BF16)
 
-    rows_ref[line.span(place, 0), :] = normalize(input_ref, 0, line.part)
-    rows_ref[line.span(place, 1), :] = normalize(input_ref, line.part, line.part)
-
-    for turn in range(max(streams + 2, 2 * (count - 1))):
-        if turn < streams:
+    normed[line.span(place, 0), :] = normalize(input_ref, 0, line.part)
+    normed[line.span(place, 1), :] = normalize(input_ref, line.part, line.part)
+
+    def serve(turn):
+        if turn < count_streams:
             for shift in range(1, shards):
                 first(shift, turn, shard_at(shards - shift)).wait_recv()
                 for step in range(1, pairs):
@@ -1036,7 +921,7 @@
         distance, part = turn // 2 + 1, turn % 2
         if distance < count:
             relay(distance, part)
-        if 0 <= turn - 1 < streams:
+        if 0 <= turn - 1 < count_streams:
             for shift in range(1, shards):
                 for step in range(1, pairs):
                     came = across(pairs - step)
@@ -1050,65 +935,226 @@
                 @pl.when(inside)
                 def _():
                     start = pl.multiple_of(owner * rows + part * line.part, line.part)
-                    rows_ref[line.span(owner, part), :] = normalize(all_rows, start, line.part)
-        if 0 <= turn - 2 < streams:
+                    normed[line.span(owner, part), :] = normalize(all_rows, start, line.part)
+        if 0 <= turn - 2 < count_streams:
             for shift in range(1, shards):
                 for step in range(pairs):
                     third(shift, step, turn - 2, replica).wait_recv()
-    for copy in locals_[3:]:
+    ready = max(6, 2 * (count - 1))
+    for turn in range(ready):
+        serve(turn)
+    for copy in locals_[2:]:
         copy.wait()
-    for stream in range(streams):
+
+    rows, head_width = live_ref.shape
+    chunks = rows // CHUNK
+    heads = width // head_width
+    tiles, ends = 4 * width // TILE, features // PROJECT_TILE
+    shared = [ATTEND_TIMES[0]] * tiles + [ATTEND_TIMES[1]] * (3 * heads) + [ATTEND_TIMES[2]] * ends
+    first_line, line = line, Line(count, rows // count, row_sems[4:], shared, False, True, ATTEND_PARTS, ATTEND_LATENCY)
+    line.rows_ref, line.source_ref = grad_rows_ref, own_grad_ref
+    grad_rows_ref[pl.ds(pl.multiple_of(place * line.rows, line.rows), line.rows), :] = own_grad_ref[...]
+    stores = [(normed, rows_ref), (mix_all, mix_ref), (ffn_all.at[own_rows], gate_up_ref.at[own_rows])]
+
+    def store(index):
+        return pltpu.make_async_copy(*stores[index], store_sem.at[index])
+
+    for index in range(len(stores)):
+        store(index).start()
+
+    @pl.loop(0, tiles)
+    def _(tile):
+        line.run_at(0, tile, tiles)
+
+        @pl.when(tile == tiles // 2)
+        def _():
+            serve(ready)
+
+        cols = pl.ds(pl.multiple_of(tile * TILE, TILE), TILE)
+        raw_all[:, cols] = dot(normed[...], mix_all[:, cols])
+
+    raw_all[:, 4 * width :] = dot(normed[...], mix_all[:, 4 * width :])
+    stores.append((raw_all, raw_ref))
+    store(len(stores) - 1).start()
+    serve(ready + 1)
+    fill_masks(starts_ref, length_ref, keep_ref, live_ref, carry_ref)
+    for chunk in range(chunks):
+        strict, incl = pair_mask(starts_ref, chunk)
+        strict_ref[chunk] = jnp.where(strict, 1.0, 0.0)
+        incl_ref[chunk] = jnp.where(incl, 1.0, 0.0)
+
+    @pl.loop(0, heads)
+    def _(head):
+        line.run_at(tiles, head, heads, 3)
+        start = pl.multiple_of(head * head_width, head_width)
+
+        def stream(index):
+            return raw_all[:, pl.ds(pl.multiple_of(index * width + start, head_width), head_width)]
+
+        cols = pl.ds(start, head_width)
+        conv, _ = convolve(stream(Q), conv_q_ref[:, cols].astype(F32), keep_ref)
+        _, act, scale = unit_rows(conv)
+        query = (act * scale).astype(BF16)
+        conv, _ = convolve(stream(K), conv_k_ref[:, cols].astype(F32), keep_ref)
+        _, act, scale = unit_rows(conv)
+        keyed = act * scale
+        key_low = keyed.astype(BF16)
+        conv, _ = convolve(stream(V), conv_v_ref[:, cols].astype(F32), keep_ref)
+        valued = conv * sigmoid(conv)
+        rate = sigmoid(column(raw_all[:, 4 * width :], head)) * live_ref[...]
+        scaled_value = (valued * rate).astype(BF16)
+        scaled_key = keyed * rate
+        system = []
+        for chunk in range(chunks):
+            span = slice(chunk * CHUNK, (chunk + 1) * CHUNK)
+            pair = dot_nt(key_low[span], key_low[span])
+            wide = jnp.concatenate([rate[span]] * (CHUNK // head_width), axis=1)
+            system.append(pair * wide * strict_ref[chunk])
+        line.run_at(tiles + 1, head, heads, 3)
+        memory = None
+        inverses = invert(system)
+        line.run_at(tiles + 2, head, heads, 3)
+        for chunk, solved in enumerate(inverses):
+            span = slice(chunk * CHUNK, (chunk + 1) * CHUNK)
+            solve_low = solved.astype(BF16)
+            solve_all[head * chunks + chunk] = solve_low
+            score = dot_nt(query[span], key_low[span]) * incl_ref[chunk]
+            if chunk == 0:
+                update = dot(solve_low, scaled_value[span])
+                update_low = update.astype(BF16)
+                mixed = dot(score.astype(BF16), update_low)
+            else:
+                carry = carry_ref[chunk - 1][span]
+                right = jnp.concatenate(
+                    [scaled_value[span], (scaled_key[span] * carry).astype(BF16)], axis=1
+                )
+                both = dot(solve_low, right)
+                memory_low = memory.astype(BF16)
+                state_all[head * (chunks - 1) + chunk - 1] = memory_low
+                update = both[:, :head_width] - dot(both[:, head_width:].astype(BF16), memory_low)
+                update_low = update.astype(BF16)
+                mixed = carry * dot(query[span], memory_low) + dot(score.astype(BF16), update_low)
+            update_all[span, cols] = update_low
+            mixed_all[span, cols] = mixed
+            if chunk + 1 < chunks:
+                last = (keyed[span] * carry_ref[chunk][span]).astype(BF16)
+                fresh = dot_tn(last, update_low)
+                if memory is None:
+                    memory = fresh
+                else:
+                    memory = memory * carry_ref[chunk - 1][span][CHUNK - 1 :] + fresh
+        mixed = mixed_all[:, cols]
+        norm = lax.rsqrt(lane_sum(mixed * mixed) * (1.0 / head_width) + 1e-05)
+        gating = stream(G)
+        gated = mixed * norm * gain_ref[...] * (gating * sigmoid(gating)) * live_ref[...]
+        gated_all[:, cols] = gated.astype(BF16)
+        for index in range(1, heads, 2):
+            @pl.when(head == index)
+            def _():
+                serve(ready + 2 + index // 2)
+
+    stores += [
+        (project_all, whole_project_ref), (gated_all, gated_ref), (mixed_all, mixed_ref), (solve_all, solve_ref),
+        (update_all, update_ref), (state_all, state_ref),
+    ]
+    for shift in range(1, shards):
+        there = pl.ds(pl.multiple_of(shard_at(shift) * share, half), half)
+        stores.append((ffn_all.at[there], gate_up_ref.at[there]))
+    for index in range(3 + 1, len(stores)):
+        store(index).start()
+
+    @pl.loop(0, ends)
+    def _(tile):
+        line.run_at(tiles + 3 * heads, tile, ends)
+        cols = pl.ds(pl.multiple_of(tile * PROJECT_TILE, PROJECT_TILE), PROJECT_TILE)
+        partial_ref[:, cols] = dot(gated_all[...], project_all[:, cols]).astype(BF16)
+
+    line.run(tiles + 3 * heads + ends)
+    line.drain()
+    for turn in range(ready + 2 + heads // 2, count_streams + 2):
+        serve(turn)
+    for shift in range(1, shards):
+        there = pl.ds(pl.multiple_of(shard_at(shift) * share + half, half), half)
+        stores.append((ffn_all.at[there], gate_up_ref.at[there]))
+        store(len(stores) - 1).start()
+    for index in range(len(stores)):
+        store(index).wait()
+
+    for stream in range(count_streams):
         for shift in range(1, shards):
             first(shift, stream, shard).wait_send()
             for step in range(1, pairs):
                 second(shift, step, stream, replica).wait_send()
             for step in range(pairs):
                 third(shift, step, stream, replica).wait_send()
-    line.drain()
-
-
-def enter(layer_input, first_gain, second_gain, w_beta, mixers, w_project):
+    first_line.drain()
+
+
+def begin(starts, length, layer_input, first_gain, second_gain, w_beta, output_grad, convs, gain, mixers, w_project, ffn):
     replicas, shards, count = extents()
     rows, features = layer_input.shape
-    width = mixers[0].shape[1]
-    share = mixers[0].shape[0]
-    heads = w_beta.shape[1]
-    pairs = replicas // 2
+    share, width = mixers[0].shape
+    heads_here = w_beta.shape[1]
+    head_width = gain.shape[-1]
+    seq_rows = count * rows
+    heads, chunks = width // head_width, seq_rows // CHUNK
+    pairs, far = replicas // 2, max(shards - 1, 1)
+    streams = 9
+    wide = 4 * width + head_width
+    hbm_out = [
+        ((seq_rows, features), BF16),
+        ((features, wide), BF16),
+        ((width, features), BF16),
+        ((features, 2 * ffn[0].shape[1]), BF16),
+        ((seq_rows, wide), F32),
+        ((seq_rows, width), BF16),
+        ((seq_rows, width), F32),
+        ((heads * chunks, CHUNK, CHUNK), BF16),
+        ((seq_rows, width), BF16),
+        ((heads * (chunks - 1), head_width, head_width), BF16),
+    ]
+    vmem_out = [((2, features), F32), ((seq_rows, features), BF16), ((seq_rows, features), BF16)]
     vmem = pl.BlockSpec(memory_space=pltpu.VMEM)
     hbm = pl.BlockSpec(memory_space=pltpu.HBM)
+    smem = pl.BlockSpec(memory_space=pltpu.SMEM)
     dma = pltpu.SemaphoreType.DMA
-    far = max(shards - 1, 1)
-    out_shape = (
-        jax.ShapeDtypeStruct((count * rows, features), BF16),
-        jax.ShapeDtypeStruct((features, 4 * width + 128), BF16),
-        jax.ShapeDtypeStruct((width, features), BF16),
-        jax.ShapeDtypeStruct((2, features), F32),
+    weights = [pltpu.with_memory_space_constraint(weight, pltpu.HBM) for weight in (*mixers, w_project, *ffn)]
+    return pl.pallas_call(
+        functools.partial(begin_kernel, (replicas, shards, count)),
+        out_shape=[jax.ShapeDtypeStruct(*entry) for entry in vmem_out] + [pltpu.HBM(*entry) for entry in hbm_out],
+        in_specs=[smem] * 2 + [vmem] * 8 + [hbm] * 7,
+        out_specs=[vmem] * 3 + [hbm] * len(hbm_out),
+        scratch_shapes=[pltpu.VMEM((seq_rows, features), BF16)]
+        + [pltpu.VMEM(*entry) for entry in hbm_out]
+        + [
+            pltpu.VMEM((KERNEL - 1, seq_rows, head_width), F32),
+            pltpu.VMEM((seq_rows, head_width), F32),
+            pltpu.VMEM((chunks - 1, seq_rows, head_width), F32),
+            pltpu.VMEM((chunks, CHUNK, CHUNK), F32),
+            pltpu.VMEM((chunks, CHUNK, CHUNK), F32),
+            pltpu.VMEM((2, features), BF16),
+            pltpu.VMEM((heads_here, features), BF16),
+            dma((9,)),
+            dma((10 + 2 * far,)),
+            dma((far, 2)),
+            dma((far, 2)),
+            dma((far, streams)),
+            dma((far, streams)),
+            dma((far, max(pairs - 1, 1), streams)),
+            dma((far, max(pairs - 1, 1), streams)),
+            dma((far, pairs, streams)),
+            dma((far, pairs, streams)),
+        ]
+        + line_scratch(count, rows, features, False, True, 2)
+        + line_scratch(count, rows, features, False, True, ATTEND_PARTS),
+        compiler_params=pltpu.CompilerParams(collective_id=5, has_side_effects=True, vmem_limit_bytes=56 * 2**20),
+        cost_estimate=pl.CostEstimate(
+            flops=2 * 36 * heads * chunks * CHUNK**3, bytes_accessed=60 * 2**20, transcendentals=0
+        ),
+        name="begin",
+    )(
+        starts, length, layer_input, jnp.stack([first_gain, second_gain]), w_beta.T, output_grad, *convs, gain, *weights
     )
-    return pl.pallas_call(
-        functools.partial(enter_kernel, (replicas, shards, count)),
-        out_shape=out_shape,
-        in_specs=[vmem] * 4 + [hbm] * 5,
-        out_specs=[vmem] * 4,
-        scratch_shapes=[
-            pltpu.VMEM((count * rows, features), BF16),
-            pltpu.VMEM((1, features), BF16),
-            pltpu.VMEM((1, features), BF16),
-            pltpu.VMEM((heads, features), BF16),
-            dma((8,)),
-            dma((far, 3)),
-            dma((far, 3)),
-            dma((far, 5)),
-            dma((far, 5)),
-            dma((far, max(pairs - 1, 1), 5)),
-            dma((far, max(pairs - 1, 1), 5)),
-            dma((far, pairs, 5)),
-            dma((far, pairs, 5)),
-        ]
-        + [dma((count - 1, 2))] * 4,
-        compiler_params=pltpu.CompilerParams(collective_id=5, has_side_effects=True, vmem_limit_bytes=40 * 2**20),
-        cost_estimate=pl.CostEstimate(flops=10**9, bytes_accessed=60 * 2**20, transcendentals=0),
-        name="enter",
-    )(layer_input, first_gain[None, :], second_gain[None, :], w_beta.T, *mixers, w_project)
 
 
 class Pair:
@@ -1184,11 +1230,11 @@
     vmem = pl.BlockSpec(memory_space=pltpu.VMEM)
     out = pl.pallas_call(
         functools.partial(mix_grads_kernel, left.shape[1]),
-        out_shape=jax.ShapeDtypeStruct(shape, BF16),
+        out_shape=pltpu.HBM(shape, BF16),
         in_specs=[vmem] * 4,
         out_specs=pl.BlockSpec(memory_space=pltpu.HBM),
         scratch_shapes=pair_scratch(shape),
-        compiler_params=pltpu.CompilerParams(collective_id=7, has_side_effects=True, vmem_limit_bytes=40 * 2**20),
+        compiler_params=pltpu.CompilerParams(collective_id=7, has_side_effects=True, vmem_limit_bytes=24 * 2**20),
         cost_estimate=pl.CostEstimate(
             flops=2 * left.shape[0] * left.shape[1] * shape[2], bytes_accessed=30 * 2**20, transcendentals=0
         ),
@@ -1204,6 +1250,9 @@
     count, features, left_ref, right_ref, d_gate_ref, d_up_ref, hidden_ref, partial_ref, resid_ref, gate_up_ref,
     out_ref, result_ref, d_partial_ref, *scratch,
 ):
+    *scratch, weights, weights_sem = scratch
+    load = pltpu.make_async_copy(gate_up_ref, weights, weights_sem)
+    load.start()
     pair = Pair(features, (0, 0, 1), left_ref, right_ref, (d_gate_ref, d_up_ref, hidden_ref), out_ref, scratch[:5])
     tiles = features // TILE
     units = d_gate_ref.shape[1]
@@ -1226,11 +1275,13 @@
         line.run_at(pair.blocks, block, pair.blocks)
         pair.ours(block)
 
+    load.wait()
+
     @pl.loop(0, tiles)
     def _(tile):
         line.run_at(2 * pair.blocks, tile, tiles)
         cols = pl.ds(pl.multiple_of(tile * TILE, TILE), TILE)
-        values = dot_nt(d_gate_ref[...], gate_up_ref[cols, :units]) + dot_nt(d_up_ref[...], gate_up_ref[cols, units:])
+        values = dot_nt(d_gate_ref[...], weights[cols, :units]) + dot_nt(d_up_ref[...], weights[cols, units:])
         d_partial_ref[:, cols] = values.astype(BF16)
 
     line.run(2 * pair.blocks + tiles)
@@ -1245,15 +1296,17 @@
     sums, result, d_partial = pl.pallas_call(
         functools.partial(ffn_grads_kernel, count, left.shape[1]),
         out_shape=(jax.ShapeDtypeStruct(shape, BF16), jax.ShapeDtypeStruct(resid.shape, BF16), jax.ShapeDtypeStruct(left.shape, BF16)),
-        in_specs=[vmem] * 8,
+        in_specs=[vmem] * 7 + [pl.BlockSpec(memory_space=pltpu.HBM)],
         out_specs=[pl.BlockSpec(memory_space=pltpu.HBM), vmem, vmem],
-        scratch_shapes=pair_scratch(shape) + line_scratch(count, resid.shape[0], resid.shape[1], True, False),
-        compiler_params=pltpu.CompilerParams(collective_id=6, has_side_effects=True, vmem_limit_bytes=58 * 2**20),
+        scratch_shapes=pair_scratch(shape)
+        + line_scratch(count, resid.shape[0], resid.shape[1], True, False)
+        + [pltpu.VMEM(gate_up.shape, BF16), pltpu.SemaphoreType.DMA],
+        compiler_params=pltpu.CompilerParams(collective_id=6, has_side_effects=True, vmem_limit_bytes=FFN_MEMORY),
         cost_estimate=pl.CostEstimate(
             flops=2 * left.shape[0] * left.shape[1] * shape[2], bytes_accessed=50 * 2**20, transcendentals=0
         ),
         name="ffn_grads",
-    )(left, right, *grads, ffn_partial, resid, gate_up)
+    )(left, right, *grads, ffn_partial, resid, pltpu.with_memory_space_constraint(gate_up, pltpu.HBM))
     return sums.reshape(shape[0] * shape[1], shape[2]), result, d_partial
 
 
@@ -1302,20 +1355,18 @@
         return lax.dynamic_slice_in_dim(weight, replica * size, size, axis)
 
     input_float = layer_input.astype(F32)
-    conv_q = conv_query.astype(F32)
-    conv_k = conv_key.astype(F32)
-    conv_v = conv_value.astype(F32)
+    conv_q, conv_k, conv_v = conv_query, conv_key, conv_value
     gain_head = head_gain.astype(F32)[None, :]
-    rows_one, mix_full, project_full, gains = enter(
-        layer_input, first_gain, second_gain, w_beta, (w_gating, w_query, w_key, w_value), w_project
+    (
+        gains, attn_partial, grad_rows, rows_one, mix_full, project_full, gate_up,
+        raw, gated, mixed, solve, update, state,
+    ) = begin(
+        doc_starts, seq_lengths, layer_input, first_gain, second_gain, w_beta, output_grad, (conv_q, conv_k, conv_v),
+        gain_head, (w_gating, w_query, w_key, w_value), w_project, (w_gate, w_up),
     )
     gain_one, gain_two = gains[:1], gains[1:]
-    late, rows_one = lax.optimization_barrier(((w_gate, w_up, w_down), rows_one))
-    gate_up = gather_weights([piece(late[0], 0), piece(late[1], 0)], 0)
-    down = gather_weights([piece(late[2], 1)], 1)
-    raw, gated, mixed, solve, update, state, attn_partial, grad_rows = attend(
-        doc_starts, seq_lengths, rows_one, mix_full, project_full, output_grad, conv_q, conv_k, conv_v, gain_head
-    )
+    late, attn_partial = lax.optimization_barrier((w_down, attn_partial))
+    down = gather_weights([piece(late, 1)], 1)
     whole_rows = jax.ShapeDtypeStruct(rows_one.shape, BF16)
     own_rows = jax.ShapeDtypeStruct(layer_input.shape, F32)
     gain_sums = jax.ShapeDtypeStruct((1, layer_input.shape[1]), F32)

time: 446 us -> 414 us (0.928); the launches traced: 437 us -> 413 us
  local copies, waits for them, and re-layouts: 39.4 us -> 26.4 us
  Pallas kernels: 338 us -> 328 us
    unnamed x98 -> x72, local copies, waits for them, and re-layouts: 28.8 us -> 15.8 us
    pallas_call x2 -> x1, Pallas kernels: 92.4 us -> 87.5 us  [begin(): pl.pallas_call(functools.partial(begin_kernel, (replicas, shards, count))...]
  transfers between devices with their start and end apart: 4 -> 3, of which waited for: 1 -> 0; matrix products, arithmetic and copies ran while one was open for 6% -> 7% of each run, Pallas kernels for 55% -> 47%
where the time goes in v5:
time: 414 us; the launch traced here: 413 us
  Pallas kernels  328 us (79%)
  matrix products  36.8 us (9%)
  local copies, waits for them, and re-layouts  26.4 us (6%)
  between operations  15 us (4%)
  other arithmetic  7.28 us (2%)
    pallas_call x3, Pallas kernels, line_call(): pl.pallas_call(functools.partial(kernel, count), out_shape=out_shape, in_...  157 us
    pallas_call x1, Pallas kernels, begin(): pl.pallas_call(functools.partial(begin_kernel, (replicas, shards, count))...  87.5 us
    pallas_call x1, Pallas kernels, ffn_grads(): pl.pallas_call(functools.partial(ffn_grads_kernel, count, left.shape[1]),...  46.2 us
    dot_general x3, matrix products, dot_nt(): lax.dot_general(left, right, (((1,), (1,)), ((), ())), preferred_element_...  20.8 us
    dot_general x2, matrix products, dot(): return jnp.dot(left, right, preferred_element_type=F32)  16 us
    unnamed x72, local copies, waits for them, and re-layouts  15.8 us
    pallas_call x1, Pallas kernels, delta_backward(): pl.pallas_call(backward_kernel, out_shape=(jax.ShapeDtypeStruct((rows, 4...  13.6 us
    pallas_call x1, Pallas kernels, mix_grads(): pl.pallas_call(functools.partial(mix_grads_kernel, left.shape[1]), out_sh...  12.2 us
  transfers between devices with their start and end apart: 3, of which 0 were waited for; matrix products, arithmetic and copies ran while one was open for 7% of the time, Pallas kernels for 47%

profile of v5, /device:TPU:0, one launch (start us, length us, event | category | flops | bytes accessed | tf_op | source)
XLA Modules:
  0.0 413.5 jit_solution(9311969396071665621)
XLA Ops:
  7.2 0.0 all-gather.2.cloned.1.call-start
  8.1 1.2 bitcast_convert_fusion.gain_ref
  9.2 0.7 stack.9
  9.9 0.7 stack.10
  10.6 0.6 pad_maximum_fusion.1.own_gains_ref
  11.2 87.5 %begin.1 = (f32[2,2048]{1,0:T(2,128)}, bf16[512,2048]{1,0:T(8,128)(2,1)}, bf16[512,2048]{1,0:T(8,128)(2,1)}, bf16[512,2048]{1,0:T(8,128)(2,1)}, bf16[2048,2176]{...) custom-call(s32[1,4]{1,0:T(1,128)} %starts_ref.3, ...), custom_call_target="tpu_custom_call" | custom-call | flops 9663676416 | bytes 62914560 | tf_op jit(solution)/shard_map/begin/pallas_call | solution.py:1122
  98.7 1.0 constant_dynamic-slice_fusion
  99.7 0.0 all-gather.2.cloned.1.call-update
  99.7 0.0 reduce-scatter.3.cloned.1.call-start
  99.8 0.8 fusion.3
  100.6 1.6 copy-done.17
  102.2 58.8 %middle.1 = (bf16[512,2048]{1,0:T(8,128)(2,1)S(1)}, f32[128,2048]{1,0:T(8,128)S(1)}) custom-call(bf16[512,2048]{1,0:T(8,128)(2,1)S(1)} %copy-done.17, bf16[128,2048]{1,0:T(8,128)(2,1)S(1)} %copy-done.5, f32[1,2048]{1,0:T(1,128)S(1)} %get-tuple-element.114.gain_ref), custom_call_target="tpu_custom_call" | custom-call | flops 1000000000 | bytes 62914560 | tf_op jit(solution)/shard_map/middle/pallas_call | solution.py:755
  161.1 1.3 copy-done.18
  162.3 11.3 %fusion.5 = f32[512,2816]{1,0:T(8,128)} fusion(bf16[512,2048]{1,0:T(8,128)(2,1)S(1)} %get-tuple-element.53.left_ref, bf16[2048,2816]{1,0:T(8,128)(2,1)} %get-tuple-element.56.gate_up_ref), kind=kOutput, calls=%fused_computation.17 | convolution fusion | flops 5905580032 | bytes 19398656 | tf_op jit(solution)/shard_map/dot_general | solution.py:31
  173.6 9.3 %multiply_convert_fusion.1 = (bf16[512,1408]{1,0:T(8,128)(2,1)}, bf16[512,1408]{1,0:T(8,128)(2,1)}, bf16[512,1408]{1,0:T(8,128)(2,1)S(1)}) fusion(f32[512,2816]{1,0:T(8,128)} %fusion.5, bf16[512,2048]{1,0:T(8,128)(2,1)S(1)} %copy-done.27, bf16[1408,2048]{1,0:T(8,128)(2,1)} %all-gather.2.cloned.1.call-done), kind=kOutput, calls=%fused_computation.3 | convolution fusion | flops 2963603456 | bytes 17956864 | tf_op jit(solution)/shard_map/dot_general | solution.py:35
  182.9 4.7 %convolution_convert_fusion.partial_ref = bf16[512,2048]{1,0:T(8,128)(2,1)} fusion(bf16[512,1408]{1,0:T(8,128)(2,1)S(1)} %get-tuple-element.102.hidden_ref, bf16[1408,2048]{1,0:T(8,128)(2,1)S(1)} %copy-done.26), kind=kOutput, calls=%fused_computation | convolution fusion | flops 2953838592 | bytes 9306112 | tf_op jit(solution)/shard_map/dot_general | solution.py:31
  187.7 46.2 %ffn_grads.1 = (bf16[4,256,4224]{2,1,0:T(8,128)(2,1)}, bf16[128,2048]{1,0:T(8,128)(2,1)S(1)}, bf16[512,2048]{1,0:T(8,128)(2,1)}) custom-call(bf16[512,2048]{1,0:T(8,128)(2,1)} %copy-done.18, bf16[512,2048]{1,0:T(8,128)(2,1)} %get-tuple-element.54.right_ref, bf16[512,1408]{1,0:T(8,128)(2,1)} %get-tuple-element.101.d_gate_ref, ...), custom_call_target="tpu_custom_call" | custom-call | flops 8858370048 | bytes 52428800 | tf_op jit(solution)/shard_map/ffn_grads/pallas_call | solution.py:1296
  233.8 0.0 reduce-scatter.3.cloned.1.call-update
  233.9 0.0 reduce-scatter.5.cloned.1.call-start
  233.9 0.9 copy-done.4
  234.9 0.7 copy-done.11
  235.6 1.2 copy-done.15
  236.8 57.9 %turn.1 = (bf16[512,2048]{1,0:T(8,128)(2,1)S(1)}, f32[128,2048]{1,0:T(8,128)S(1)}, f32[1,2048]{1,0:T(1,128)S(1)}) custom-call(bf16[512,2048]{1,0:T(8,128)(2,1)S(1)} %copy-done.11, f32[128,2048]{1,0:T(8,128)S(1)} %copy-done.15, bf16[128,2048]{1,0:T(8,128)(2,1)S(1)} %copy-done.4, f32[1,2048]{1,0:T(1,128)S(1)} %get-tuple-element.114.gain_ref), custom_call_target="tpu_custom_call" | custom-call | flops 1000000000 | bytes 62914560 | tf_op jit(solution)/shard_map/turn/pallas_call | solution.py:755
  294.7 1.0 copy-done.12
  295.7 3.0 fusion.6.grad_ref
  298.9 13.6 %delta_backward.1 = (bf16[512,2176]{1,0:T(8,128)(2,1)S(1)}, f32[4,1536]{1,0:T(4,128)S(1)}, f32[1,128]{1,0:T(1,128)S(1)}) custom-call(s32[1,4]{1,0:T(1,128)S(1)} %copy-done.10, s32[1]{0:T(128)S(6)} %copy.42.length_ref, f32[512,2176]{1,0:T(8,128)S(1)} %bitcast.25, bf16[4,512]{1,0:T(4,128)(2,1)S(1)} %copy-done.7, bf16[4,512]{1,0:T(4,128)(2,1)S(1)} %copy-done.8, ...), custom_call_target="tpu_custom_call" | custom-call | flops 3221225472 | bytes 16777216 | tf_op jit(solution)/shard_map/delta_backward/pallas_call | solution.py:277
  312.5 1.3 copy-done.19
  313.8 12.2 %mix_grads.1 = bf16[4,256,2688]{2,1,0:T(8,128)(2,1)} custom-call(bf16[512,2048]{1,0:T(8,128)(2,1)S(1)} %copy-done.23, bf16[512,2048]{1,0:T(8,128)(2,1)S(1)} %get-tuple-element.65.right_ref, bf16[512,2176]{1,0:T(8,128)(2,1)S(1)} %get-tuple-element.67.first_ref, bf16[512,512]{1,0:T(8,128)(2,1)S(1)} %copy-done.25), custom_call_target="tpu_custom_call" | custom-call | flops 5637144576 | bytes 31457280 | tf_op jit(solution)/shard_map/mix_grads/pallas_call | solution.py:1231
  326.0 0.0 reduce-scatter.3.cloned.1.call-done
  326.0 4.0 convert_element_type.27
  330.0 0.0 reduce-scatter.5.cloned.1.call-update
  330.1 8.4 %convolution_convert_fusion.1.partial_ref = bf16[512,2048]{1,0:T(8,128)(2,1)S(1)} fusion(bf16[512,2176]{1,0:T(8,128)(2,1)} %copy-done.19, bf16[2048,2176]{1,0:T(8,128)(2,1)} %get-tuple-element.68), kind=kOutput, calls=%fused_computation.1 | convolution fusion | flops 4564451328 | bytes 13238272 | tf_op jit(solution)/shard_map/dot_general | solution.py:35
  338.5 40.3 %last.1 = (f32[128,2048]{1,0:T(8,128)S(1)}, f32[1,2048]{1,0:T(1,128)S(1)}) custom-call(bf16[512,2048]{1,0:T(8,128)(2,1)S(1)} %convolution_convert_fusion.1.partial_ref, bf16[128,2048]{1,0:T(8,128)(2,1)S(1)} %copy-done.6, f32[128,2048]{1,0:T(8,128)S(1)} %copy-done.13, f32[1,2048]{1,0:T(1,128)S(1)} %get-tuple-element.113.gain_ref), custom_call_target="tpu_custom_call" | custom-call | flops 1000000000 | bytes 62914560 | tf_op jit(solution)/shard_map/last/pallas_call | solution.py:755
  378.8 1.0 copy-done.2
  379.8 11.5 %reduce_small.1 = (f32[2,256]{1,0:T(2,128)S(1)}, f32[1,128]{1,0:T(1,128)S(1)}, f32[4,1536]{1,0:T(4,128)S(1)}) custom-call(f32[2,2048]{1,0:T(2,128)S(1)} %pad_maximum_fusion.gain_ref, f32[1,128]{1,0:T(1,128)S(1)} %get-tuple-element.73.head_ref, f32[4,1536]{1,0:T(4,128)S(1)} %get-tuple-element.74.conv_ref), custom_call_target="tpu_custom_call" | custom-call | tf_op jit(solution)/shard_map/reduce_small/pallas_call | solution.py:387
  391.3 0.6 fusion.4
  391.9 0.6 fusion.2
  392.5 1.9 slice_bitcast_fusion
  394.3 1.5 copy.38
  395.9 0.8 slice.78
  396.7 0.7 copy.36
  397.4 1.5 convert_element_type.28
  398.9 0.9 slice_bitcast_fusion.1
  399.8 2.2 copy.37
  402.0 2.7 fusion.1
  404.7 0.8 copy.43
  405.5 1.0 copy.44
  406.4 0.5 copy.45
  (63 shorter events, 0.2 us)
Async XLA Ops:
  7.2 91.5 %copy-start = (bf16[1408,1024]{1,0:T(8,128)(2,1)S(1)}, bf16[1408,1024]{1,0:T(8,128)(2,1)}, u32[]{:S(2)}) copy-start(bf16[1408,1024]{1,0:T(8,128)(2,1)} %param.34) | copy-start | bytes 8650756
  7.2 166.4 %all-gather.2.cloned.1.call-start = ((), (), s32[]{:S(2)}) async-start(), calls=%async_computation.2 | async-start | bytes 6488064 | tf_op jit(solution)/shard_map/all_gather | solution.py:1319
  11.2 89.4 %copy-start.5 = (bf16[128,2048]{1,0:T(8,128)(2,1)S(1)}, bf16[128,2048]{1,0:T(8,128)(2,1)}, u32[]{:S(2)}) copy-start(bf16[128,2048]{1,0:T(8,128)(2,1)} %input_ref.5) | copy-start | bytes 1572868
  99.7 226.3 %reduce-scatter.3.cloned.1.call-start = ((), (), s32[]{:S(2)}) async-start(), calls=%async_computation.3 | async-start | bytes 10813440 | tf_op jit(solution)/shard_map/reduce_scatter | solution.py:1314
  100.6 1.6 copy-start.17
  161.0 1.3 copy-start.18
  161.0 26.6 %copy-start.14 = (f32[128,2048]{1,0:T(8,128)}, f32[128,2048]{1,0:T(8,128)S(1)}, u32[]{:S(2)}) copy-start(f32[128,2048]{1,0:T(8,128)S(1)} %get-tuple-element.57.resid_ref) | copy-start | bytes 3145732
  162.3 11.3 %copy-start.27 = (bf16[512,2048]{1,0:T(8,128)(2,1)S(1)}, bf16[512,2048]{1,0:T(8,128)(2,1)}, u32[]{:S(2)}) copy-start(bf16[512,2048]{1,0:T(8,128)(2,1)} %get-tuple-element.54.right_ref) | copy-start | bytes 6291460
  173.6 9.3 %copy-start.26 = (bf16[1408,2048]{1,0:T(8,128)(2,1)S(1)}, bf16[1408,2048]{1,0:T(8,128)(2,1)}, u32[]{:S(2)}) copy-start(bf16[1408,2048]{1,0:T(8,128)(2,1)} %all-gather.2.cloned.1.call-done) | copy-start | bytes 17301508
  182.9 4.7 %copy-start.28 = (bf16[512,1408]{1,0:T(8,128)(2,1)}, bf16[512,1408]{1,0:T(8,128)(2,1)S(1)}, u32[]{:S(2)}) copy-start(bf16[512,1408]{1,0:T(8,128)(2,1)S(1)} %get-tuple-element.102.hidden_ref) | copy-start | bytes 4325380
  233.8 1.0 copy-start.4
  233.8 1.8 copy-start.11
  233.9 162.0 %reduce-scatter.5.cloned.1.call-start = ((), (), s32[]{:S(2)}) async-start(), calls=%async_computation.4 | async-start | bytes 6881280 | tf_op jit(solution)/shard_map/reduce_scatter | solution.py:1314
  235.6 1.2 copy-start.15
  236.8 62.0 %slice-start = ((s8[4456448]{0:T(1024)(128)(4,1)}), s8[4194304]{0:T(1024)(128)(4,1)S(1)}, s32[]{:S(2)}) async-start(s8[4456448]{0:T(1024)(128)(4,1)} %bitcast.24), calls=%async_computation.5 | async-start | bytes 8388608
  294.7 1.0 copy-start.12
  295.7 3.1 copy-start.7
  295.7 3.1 copy-start.8
  295.7 3.1 copy-start.9
  295.7 3.1 copy-start.10
  295.7 3.1 copy-start.16
  295.7 3.1 slice-start.1
  295.7 3.1 copy-start.20
  295.7 3.1 copy-start.21
  295.7 3.1 copy-start.22
  295.7 3.1 copy-start.24
  298.9 14.9 %copy-start.23 = (bf16[512,2048]{1,0:T(8,128)(2,1)S(1)}, bf16[512,2048]{1,0:T(8,128)(2,1)}, u32[]{:S(2)}) copy-start(bf16[512,2048]{1,0:T(8,128)(2,1)} %get-tuple-element.76.left_ref) | copy-start | bytes 6291460
  298.9 14.9 %copy-start.25 = (bf16[512,512]{1,0:T(8,128)(2,1)S(1)}, bf16[512,512]{1,0:T(8,128)(2,1)}, u32[]{:S(2)}) copy-start(bf16[512,512]{1,0:T(8,128)(2,1)} %get-tuple-element.77.second_ref) | copy-start | bytes 1572868
  312.5 1.3 copy-start.19
  330.0 62.5 %slice-start.2 = ((s8[4325376]{0:T(1024)(128)(4,1)}), s8[4194304]{0:T(1024)(128)(4,1)S(1)}, s32[]{:S(2)}) async-start(s8[4325376]{0:T(1024)(128)(4,1)} %bitcast.26), calls=%async_computation.7 | async-start | bytes 8388608
  330.0 8.5 %copy-start.6 = (bf16[128,2048]{1,0:T(8,128)(2,1)S(1)}, bf16[128,2048]{1,0:T(8,128)(2,1)}, u32[]{:S(2)}) copy-start(bf16[128,2048]{1,0:T(8,128)(2,1)} %input_ref.5) | copy-start | bytes 1572868
  330.0 8.5 %copy-start.13 = (f32[128,2048]{1,0:T(8,128)S(1)}, f32[128,2048]{1,0:T(8,128)}, u32[]{:S(2)}) copy-start(f32[128,2048]{1,0:T(8,128)} %copy-done.12) | copy-start | bytes 3145732
  330.0 62.4 %slice-start.3 = ((s8[4325376]{0:T(1024)(128)(4,1)}), s8[131072]{0:T(1024)(128)(4,1)S(1)}, s32[]{:S(2)}) async-start(s8[4325376]{0:T(1024)(128)(4,1)} %bitcast.26), calls=%async_computation.8 | async-start | bytes 262144
  378.8 1.0 copy-start.2
  399.8 7.2 %copy-start.1 = (bf16[1408,1024]{1,0:T(8,128)(2,1)S(1)}, bf16[1408,1024]{1,0:T(8,128)(2,1)}, u32[]{:S(2)}) copy-start(bf16[1408,1024]{1,0:T(8,128)(2,1)} %param.34) | copy-start | bytes 8650756
  402.0 3.5 copy-start.3
Sparse Core Ops, SparseCore 0:
  99.8 43.1 all-gather.1
  234.0 86.4 reduce-scatter.2
  330.1 65.5 reduce-scatter.4

commit v6 on v5

--- a/solution.py
+++ b/solution.py
@@ -3,7 +3,6 @@
 from jax import lax
 from jax.experimental import pallas as pl
 from jax.experimental.pallas import tpu as pltpu
-from jax.experimental.layout import Layout, with_layout_constraint
 from jax.sharding import PartitionSpec as P
 
 KERNEL = 4
@@ -1311,8 +1310,28 @@
 
 
 def group_scatter(sums):
-    shard = lax.psum_scatter(sums, ("pair", "fsdp"), scatter_dimension=0, tiled=True)
-    return with_layout_constraint(shard, Layout(major_to_minor=(0, 1))).astype(F32)
+    return lax.psum_scatter(sums, ("pair", "fsdp"), scatter_dimension=0, tiled=True)
+
+
+def widen_kernel(parts, shard_ref, *out_refs):
+    for (start, stop, flip), out_ref in zip(parts, out_refs):
+        values = shard_ref[:, start:stop].astype(F32)
+        out_ref[...] = values.T if flip else values
+
+
+def widen(shard, parts, name):
+    rows = shard.shape[0]
+    shapes = [(stop - start, rows) if flip else (rows, stop - start) for start, stop, flip in parts]
+    vmem = pl.BlockSpec(memory_space=pltpu.VMEM)
+    return pl.pallas_call(
+        functools.partial(widen_kernel, parts),
+        out_shape=[jax.ShapeDtypeStruct(shape, F32) for shape in shapes],
+        in_specs=[vmem],
+        out_specs=[vmem] * len(parts),
+        compiler_params=pltpu.CompilerParams(vmem_limit_bytes=16 * 2**20),
+        cost_estimate=pl.CostEstimate(flops=10**6, bytes_accessed=8 * 2**20, transcendentals=0),
+        name=name,
+    )(shard)
 
 
 def gather_weights(pieces, axis):
@@ -1395,7 +1414,17 @@
         (mix_grads(rows_one, d_attn, (d_raw, gated)), ffn_shard)
     )
     mix_shard = group_scatter(mix_sums)
-    project_shard = mix_shard[:, 4 * width + head_width :]
+    beta_start = 4 * width
+    project_start = beta_start + head_width
+    grad_gating, grad_query, grad_key, grad_value, grad_beta, grad_project = widen(
+        mix_shard,
+        [(index * width, (index + 1) * width, False) for index in range(4)]
+        + [(beta_start, beta_start + heads, False), (project_start, project_start + width, True)],
+        "widen_mix",
+    )
+    grad_gate, grad_up, grad_down = widen(
+        ffn_shard, [(0, units, False), (units, 2 * units, False), (2 * units, 3 * units, True)], "widen_ffn"
+    )
     mix_partial = dot_nt(d_raw, mix_full).astype(BF16)
     input_grad, grad_first = line_call(
         last_kernel, "last", 4, False, (own_rows, gain_sums),
@@ -1408,20 +1437,20 @@
         result,
         input_grad,
         gain_total[0],
-        mix_shard[:, width : 2 * width],
-        mix_shard[:, 2 * width : 3 * width],
-        mix_shard[:, 3 * width : 4 * width],
-        mix_shard[:, :width],
-        mix_shard[:, 4 * width : 4 * width + heads],
+        grad_query,
+        grad_key,
+        grad_value,
+        grad_gating,
+        grad_beta,
         conv_totals[:, :width],
         conv_totals[:, width : 2 * width],
         conv_totals[:, 2 * width :],
         head_total[0],
-        project_shard.T,
+        grad_project,
         gain_total[1],
-        ffn_shard[:, :units],
-        ffn_shard[:, units : 2 * units],
-        ffn_shard[:, 2 * units :].T,
+        grad_gate,
+        grad_up,
+        grad_down,
     )
 
 

time: 414 us -> 406 us (0.981)
  local copies, waits for them, and re-layouts: 26.4 us -> 18.7 us
  other arithmetic: 7.28 us -> 1.82 us
    convert_element_type x2 -> x0, other arithmetic: 5.47 us -> none  [group_scatter(): with_layout_constraint(shard, Layout(major_to_minor=(0, 1))).astype(F32)]
    unnamed x72 -> x70, local copies, waits for them, and re-layouts: 15.8 us -> 14.4 us
  transfers between devices with their start and end apart: 3 -> 3, of which waited for: 0 -> 1; matrix products, arithmetic and copies ran while one was open for 7% -> 6% of each run, Pallas kernels for 47% -> 48%
where the time goes in v6:
time: 406 us; the launch traced here: 405 us
  Pallas kernels  332 us (82%)
  matrix products  36.8 us (9%)
  local copies, waits for them, and re-layouts  18.7 us (5%)
  between operations  15 us (4%)
    pallas_call x3, Pallas kernels, line_call(): pl.pallas_call(functools.partial(kernel, count), out_shape=out_shape, in_...  157 us
    pallas_call x1, Pallas kernels, begin(): pl.pallas_call(functools.partial(begin_kernel, (replicas, shards, count))...  87.5 us
    pallas_call x1, Pallas kernels, ffn_grads(): pl.pallas_call(functools.partial(ffn_grads_kernel, count, left.shape[1]),...  46.2 us
    dot_general x3, matrix products, dot_nt(): lax.dot_general(left, right, (((1,), (1,)), ((), ())), preferred_element_...  20.8 us
    dot_general x2, matrix products, dot(): return jnp.dot(left, right, preferred_element_type=F32)  16 us
    unnamed x70, local copies, waits for them, and re-layouts  14.4 us
    pallas_call x1, Pallas kernels, delta_backward(): pl.pallas_call(backward_kernel, out_shape=(jax.ShapeDtypeStruct((rows, 4...  13.6 us
    pallas_call x1, Pallas kernels, mix_grads(): pl.pallas_call(functools.partial(mix_grads_kernel, left.shape[1]), out_sh...  12.2 us
  transfers between devices with their start and end apart: 3, of which 1 were waited for; matrix products, arithmetic and copies ran while one was open for 6% of the time, Pallas kernels for 48%

profile of v6, /device:TPU:0, one launch (start us, length us, event | category | flops | bytes accessed | tf_op | source)
XLA Modules:
  0.0 405.2 jit_solution(2271836539667663975)
XLA Ops:
  7.2 0.0 copy-start
  7.2 0.0 all-gather.2.cloned.1.call-start
  8.1 1.2 bitcast_convert_fusion.gain_ref
  9.2 0.7 stack.9
  9.9 0.7 stack.10
  10.6 0.6 pad_maximum_fusion.1.own_gains_ref
  11.2 87.5 %begin.1 = (f32[2,2048]{1,0:T(2,128)}, bf16[512,2048]{1,0:T(8,128)(2,1)}, bf16[512,2048]{1,0:T(8,128)(2,1)}, bf16[512,2048]{1,0:T(8,128)(2,1)}, bf16[2048,2176]{...) custom-call(s32[1,4]{1,0:T(1,128)} %starts_ref.3, ...), custom_call_target="tpu_custom_call" | custom-call | flops 9663676416 | bytes 62914560 | tf_op jit(solution)/shard_map/begin/pallas_call | solution.py:1121
  98.7 1.0 constant_dynamic-slice_fusion
  99.7 0.0 all-gather.2.cloned.1.call-update
  99.7 0.0 reduce-scatter.3.cloned.1.call-start
  99.8 0.8 fusion.2
  100.6 1.6 copy-done.19
  102.2 58.9 %middle.1 = (bf16[512,2048]{1,0:T(8,128)(2,1)S(1)}, f32[128,2048]{1,0:T(8,128)S(1)}) custom-call(bf16[512,2048]{1,0:T(8,128)(2,1)S(1)} %copy-done.19, bf16[128,2048]{1,0:T(8,128)(2,1)S(1)} %copy-done.6, f32[1,2048]{1,0:T(1,128)S(1)} %get-tuple-element.125.gain_ref), custom_call_target="tpu_custom_call" | custom-call | flops 1000000000 | bytes 62914560 | tf_op jit(solution)/shard_map/middle/pallas_call | solution.py:754
  161.0 0.0 copy-start.15
  161.0 1.0 copy-done.15
  162.0 1.3 copy-done.20
  163.3 11.3 %fusion.4 = f32[512,2816]{1,0:T(8,128)} fusion(bf16[512,2048]{1,0:T(8,128)(2,1)S(1)} %get-tuple-element.62.left_ref, bf16[2048,2816]{1,0:T(8,128)(2,1)} %get-tuple-element.65.gate_up_ref), kind=kOutput, calls=%fused_computation.14 | convolution fusion | flops 5905580032 | bytes 19398656 | tf_op jit(solution)/shard_map/dot_general | solution.py:30
  174.6 9.4 %multiply_convert_fusion.1 = (bf16[512,1408]{1,0:T(8,128)(2,1)}, bf16[512,1408]{1,0:T(8,128)(2,1)}, bf16[512,1408]{1,0:T(8,128)(2,1)S(1)}) fusion(f32[512,2816]{1,0:T(8,128)} %fusion.4, bf16[512,2048]{1,0:T(8,128)(2,1)S(1)} %copy-done.29, bf16[1408,2048]{1,0:T(8,128)(2,1)} %all-gather.2.cloned.1.call-done), kind=kOutput, calls=%fused_computation.3 | convolution fusion | flops 2963603456 | bytes 17956864 | tf_op jit(solution)/shard_map/dot_general | solution.py:34
  184.0 0.0 copy-start.16
  184.0 4.7 %convolution_convert_fusion.partial_ref = bf16[512,2048]{1,0:T(8,128)(2,1)} fusion(bf16[512,1408]{1,0:T(8,128)(2,1)S(1)} %get-tuple-element.120.hidden_ref, bf16[1408,2048]{1,0:T(8,128)(2,1)S(1)} %copy-done.28), kind=kOutput, calls=%fused_computation | convolution fusion | flops 2953838592 | bytes 9306112 | tf_op jit(solution)/shard_map/dot_general | solution.py:30
  188.7 46.2 %ffn_grads.1 = (bf16[4,256,4224]{2,1,0:T(8,128)(2,1)}, bf16[128,2048]{1,0:T(8,128)(2,1)S(1)}, bf16[512,2048]{1,0:T(8,128)(2,1)}) custom-call(bf16[512,2048]{1,0:T(8,128)(2,1)} %copy-done.20, bf16[512,2048]{1,0:T(8,128)(2,1)} %get-tuple-element.63.right_ref, bf16[512,1408]{1,0:T(8,128)(2,1)} %get-tuple-element.119.d_gate_ref, ...), custom_call_target="tpu_custom_call" | custom-call | flops 8858370048 | bytes 52428800 | tf_op jit(solution)/shard_map/ffn_grads/pallas_call | solution.py:1295
  234.9 0.0 copy-start.5
  235.0 0.0 reduce-scatter.3.cloned.1.call-update
  235.0 0.0 reduce-scatter.5.cloned.1.call-start
  235.0 0.9 copy-done.5
  236.0 0.7 copy-done.12
  236.7 1.2 copy-done.17
  237.9 57.9 %turn.1 = (bf16[512,2048]{1,0:T(8,128)(2,1)S(1)}, f32[128,2048]{1,0:T(8,128)S(1)}, f32[1,2048]{1,0:T(1,128)S(1)}) custom-call(bf16[512,2048]{1,0:T(8,128)(2,1)S(1)} %copy-done.12, f32[128,2048]{1,0:T(8,128)S(1)} %copy-done.17, bf16[128,2048]{1,0:T(8,128)(2,1)S(1)} %copy-done.5, f32[1,2048]{1,0:T(1,128)S(1)} %get-tuple-element.125.gain_ref), custom_call_target="tpu_custom_call" | custom-call | flops 1000000000 | bytes 62914560 | tf_op jit(solution)/shard_map/turn/pallas_call | solution.py:754
  295.8 1.0 copy-done.13
  296.9 3.0 fusion.5.grad_ref
  300.0 13.6 %delta_backward.1 = (bf16[512,2176]{1,0:T(8,128)(2,1)S(1)}, f32[4,1536]{1,0:T(4,128)S(1)}, f32[1,128]{1,0:T(1,128)S(1)}) custom-call(s32[1,4]{1,0:T(1,128)S(1)} %copy-done.11, s32[1]{0:T(128)S(6)} %copy.40.length_ref, f32[512,2176]{1,0:T(8,128)S(1)} %bitcast.21, bf16[4,512]{1,0:T(4,128)(2,1)S(1)} %copy-done.8, bf16[4,512]{1,0:T(4,128)(2,1)S(1)} %copy-done.9, ...), custom_call_target="tpu_custom_call" | custom-call | flops 3221225472 | bytes 16777216 | tf_op jit(solution)/shard_map/delta_backward/pallas_call | solution.py:276
  313.6 12.2 %mix_grads.1 = bf16[4,256,2688]{2,1,0:T(8,128)(2,1)} custom-call(bf16[512,2048]{1,0:T(8,128)(2,1)S(1)} %copy-done.25, bf16[512,2048]{1,0:T(8,128)(2,1)S(1)} %get-tuple-element.74.right_ref, bf16[512,2176]{1,0:T(8,128)(2,1)S(1)} %get-tuple-element.76.first_ref, bf16[512,512]{1,0:T(8,128)(2,1)S(1)} %copy-done.27), custom_call_target="tpu_custom_call" | custom-call | flops 5637144576 | bytes 31457280 | tf_op jit(solution)/shard_map/mix_grads/pallas_call | solution.py:1230
  325.8 0.0 reduce-scatter.3.cloned.1.call-done.shard_ref
  325.8 0.0 reduce-scatter.5.cloned.1.call-update
  325.9 8.4 %convolution_convert_fusion.1.partial_ref = bf16[512,2048]{1,0:T(8,128)(2,1)S(1)} fusion(bf16[512,2176]{1,0:T(8,128)(2,1)} %copy-done.21, bf16[2048,2176]{1,0:T(8,128)(2,1)} %get-tuple-element.77), kind=kOutput, calls=%fused_computation.1 | convolution fusion | flops 4564451328 | bytes 13238272 | tf_op jit(solution)/shard_map/dot_general | solution.py:34
  334.3 40.0 %last.1 = (f32[128,2048]{1,0:T(8,128)S(1)}, f32[1,2048]{1,0:T(1,128)S(1)}) custom-call(bf16[512,2048]{1,0:T(8,128)(2,1)S(1)} %convolution_convert_fusion.1.partial_ref, bf16[128,2048]{1,0:T(8,128)(2,1)S(1)} %copy-done.7, f32[128,2048]{1,0:T(8,128)S(1)} %copy-done.14, f32[1,2048]{1,0:T(1,128)S(1)} %get-tuple-element.124.gain_ref), custom_call_target="tpu_custom_call" | custom-call | flops 1000000000 | bytes 62914560 | tf_op jit(solution)/shard_map/last/pallas_call | solution.py:754
  374.3 1.0 copy-done.4
  375.4 11.4 %reduce_small.1 = (f32[2,256]{1,0:T(2,128)S(1)}, f32[1,128]{1,0:T(1,128)S(1)}, f32[4,1536]{1,0:T(4,128)S(1)}) custom-call(f32[2,2048]{1,0:T(2,128)S(1)} %pad_maximum_fusion.gain_ref, f32[1,128]{1,0:T(1,128)S(1)} %get-tuple-element.82.head_ref, f32[4,1536]{1,0:T(4,128)S(1)} %get-tuple-element.83.conv_ref), custom_call_target="tpu_custom_call" | custom-call | tf_op jit(solution)/shard_map/reduce_small/pallas_call | solution.py:386
  386.8 0.6 fusion.3
  387.4 0.6 fusion.1
  388.0 2.4 widen_ffn.1
  390.4 1.1 reduce-scatter.5.cloned.1.call-done.shard_ref
  391.5 1.3 copy-done.3
  392.8 1.6 widen_mix.1
  394.4 0.7 copy.36
  395.1 0.8 copy.41
  395.9 2.3 copy.42
  398.2 0.5 copy.43
  (56 shorter events, 0.1 us)
Async XLA Ops:
  7.2 91.5 %copy-start = (bf16[1408,1024]{1,0:T(8,128)(2,1)S(1)}, bf16[1408,1024]{1,0:T(8,128)(2,1)}, u32[]{:S(2)}) copy-start(bf16[1408,1024]{1,0:T(8,128)(2,1)} %param.34) | copy-start | bytes 8650756
  7.2 167.4 %all-gather.2.cloned.1.call-start = ((), (), s32[]{:S(2)}) async-start(), calls=%async_computation.2 | async-start | bytes 6488064 | tf_op jit(solution)/shard_map/all_gather | solution.py:1338
  11.2 89.3 %copy-start.6 = (bf16[128,2048]{1,0:T(8,128)(2,1)S(1)}, bf16[128,2048]{1,0:T(8,128)(2,1)}, u32[]{:S(2)}) copy-start(bf16[128,2048]{1,0:T(8,128)(2,1)} %input_ref.5) | copy-start | bytes 1572868
  99.7 226.1 %reduce-scatter.3.cloned.1.call-start = ((), (), s32[]{:S(2)}) async-start(), calls=%async_computation.3 | async-start | bytes 10813440 | tf_op jit(solution)/shard_map/reduce_scatter | solution.py:1313
  100.6 1.6 copy-start.19
  161.0 1.0 copy-start.15
  162.0 1.3 copy-start.20
  163.3 11.3 %copy-start.29 = (bf16[512,2048]{1,0:T(8,128)(2,1)S(1)}, bf16[512,2048]{1,0:T(8,128)(2,1)}, u32[]{:S(2)}) copy-start(bf16[512,2048]{1,0:T(8,128)(2,1)} %get-tuple-element.63.right_ref) | copy-start | bytes 6291460
  174.6 9.4 %copy-start.28 = (bf16[1408,2048]{1,0:T(8,128)(2,1)S(1)}, bf16[1408,2048]{1,0:T(8,128)(2,1)}, u32[]{:S(2)}) copy-start(bf16[1408,2048]{1,0:T(8,128)(2,1)} %all-gather.2.cloned.1.call-done) | copy-start | bytes 17301508
  184.0 4.7 %copy-start.30 = (bf16[512,1408]{1,0:T(8,128)(2,1)}, bf16[512,1408]{1,0:T(8,128)(2,1)S(1)}, u32[]{:S(2)}) copy-start(bf16[512,1408]{1,0:T(8,128)(2,1)S(1)} %get-tuple-element.120.hidden_ref) | copy-start | bytes 4325380
  184.0 4.7 %copy-start.16 = (f32[128,2048]{1,0:T(8,128)S(1)}, f32[128,2048]{1,0:T(8,128)}, u32[]{:S(2)}) copy-start(f32[128,2048]{1,0:T(8,128)} %copy-done.15) | copy-start | bytes 3145732
  234.9 1.0 copy-start.5
  234.9 1.8 copy-start.12
  235.0 156.5 %reduce-scatter.5.cloned.1.call-start = ((), (), s32[]{:S(2)}) async-start(), calls=%async_computation.4 | async-start | bytes 6881280 | tf_op jit(solution)/shard_map/reduce_scatter | solution.py:1313
  236.7 1.2 copy-start.17
  237.9 62.0 %slice-start = ((s8[4456448]{0:T(1024)(128)(4,1)}), s8[4194304]{0:T(1024)(128)(4,1)S(1)}, s32[]{:S(2)}) async-start(s8[4456448]{0:T(1024)(128)(4,1)} %bitcast.20), calls=%async_computation.5 | async-start | bytes 8388608
  295.8 1.0 copy-start.13
  296.8 3.1 copy-start.8
  296.8 3.1 copy-start.9
  296.8 3.1 copy-start.10
  296.8 3.1 copy-start.11
  296.8 3.1 copy-start.18
  296.8 3.1 slice-start.1
  296.8 3.1 copy-start.22
  296.8 3.1 copy-start.23
  296.8 3.1 copy-start.24
  296.8 3.1 copy-start.26
  300.0 13.6 %copy-start.25 = (bf16[512,2048]{1,0:T(8,128)(2,1)S(1)}, bf16[512,2048]{1,0:T(8,128)(2,1)}, u32[]{:S(2)}) copy-start(bf16[512,2048]{1,0:T(8,128)(2,1)} %get-tuple-element.85.left_ref) | copy-start | bytes 6291460
  300.0 13.6 %copy-start.27 = (bf16[512,512]{1,0:T(8,128)(2,1)S(1)}, bf16[512,512]{1,0:T(8,128)(2,1)}, u32[]{:S(2)}) copy-start(bf16[512,512]{1,0:T(8,128)(2,1)} %get-tuple-element.86.second_ref) | copy-start | bytes 1572868
  313.6 12.2 %copy-start.21 = (bf16[512,2176]{1,0:T(8,128)(2,1)}, bf16[512,2176]{1,0:T(8,128)(2,1)S(1)}, u32[]{:S(2)}) copy-start(bf16[512,2176]{1,0:T(8,128)(2,1)S(1)} %get-tuple-element.76.first_ref) | copy-start | bytes 6684676
  325.9 8.4 %copy-start.7 = (bf16[128,2048]{1,0:T(8,128)(2,1)S(1)}, bf16[128,2048]{1,0:T(8,128)(2,1)}, u32[]{:S(2)}) copy-start(bf16[128,2048]{1,0:T(8,128)(2,1)} %input_ref.5) | copy-start | bytes 1572868
  325.9 8.4 %copy-start.14 = (f32[128,2048]{1,0:T(8,128)S(1)}, f32[128,2048]{1,0:T(8,128)}, u32[]{:S(2)}) copy-start(f32[128,2048]{1,0:T(8,128)} %copy-done.13) | copy-start | bytes 3145732
  334.3 53.7 %copy-start.2 = (bf16[256,4224]{1,0:T(8,128)(2,1)S(1)}, bf16[256,4224]{1,0:T(8,128)(2,1)}, u32[]{:S(2)}) copy-start(bf16[256,4224]{1,0:T(8,128)(2,1)} %reduce-scatter.3.cloned.1.call-done.shard_ref) | copy-start | bytes 6488068
  374.3 1.0 copy-start.4
  388.0 10.7 %copy-start.1 = (bf16[1408,1024]{1,0:T(8,128)(2,1)S(1)}, bf16[1408,1024]{1,0:T(8,128)(2,1)}, u32[]{:S(2)}) copy-start(bf16[1408,1024]{1,0:T(8,128)(2,1)} %param.34) | copy-start | bytes 8650756
  391.5 1.3 copy-start.3
Sparse Core Ops, SparseCore 0:
  99.8 43.1 all-gather.1
  235.1 86.3 reduce-scatter.2
  326.0 65.4 reduce-scatter.4

commit v7 on v6

--- a/solution.py
+++ b/solution.py
@@ -1156,6 +1156,15 @@
     )
 
 
+def fetched(far_refs, scratch):
+    count = len(far_refs)
+    near, sems, rest = scratch[:count], scratch[count], scratch[count + 1 :]
+    loads = [pltpu.make_async_copy(far, ref, sems.at[index]) for index, (far, ref) in enumerate(zip(far_refs, near))]
+    for load in loads:
+        load.start()
+    return near, rest, loads
+
+
 class Pair:
 
     def __init__(self, features, owners, left_ref, right_ref, grad_refs, out_ref, scratch):
@@ -1246,12 +1255,13 @@
 
 
 def ffn_grads_kernel(
-    count, features, left_ref, right_ref, d_gate_ref, d_up_ref, hidden_ref, partial_ref, resid_ref, gate_up_ref,
+    count, features, partial_ref, gate_up_ref, left_far, right_far, d_gate_far, d_up_far, hidden_far, resid_far,
     out_ref, result_ref, d_partial_ref, *scratch,
 ):
     *scratch, weights, weights_sem = scratch
-    load = pltpu.make_async_copy(gate_up_ref, weights, weights_sem)
-    load.start()
+    near, scratch, loads = fetched((left_far, right_far, d_gate_far, d_up_far, hidden_far, resid_far), scratch)
+    left_ref, right_ref, d_gate_ref, d_up_ref, hidden_ref, resid_ref = near
+    weights_load = pltpu.make_async_copy(gate_up_ref, weights, weights_sem)
     pair = Pair(features, (0, 0, 1), left_ref, right_ref, (d_gate_ref, d_up_ref, hidden_ref), out_ref, scratch[:5])
     tiles = features // TILE
     units = d_gate_ref.shape[1]
@@ -1267,6 +1277,13 @@
     @pl.loop(0, pair.blocks)
     def _(block):
         line.run_at(0, block, pair.blocks)
+
+        @pl.when(block == 0)
+        def _():
+            for load in loads:
+                load.wait()
+            weights_load.start()
+
         pair.theirs(block)
 
     @pl.loop(0, pair.blocks)
@@ -1274,7 +1291,7 @@
         line.run_at(pair.blocks, block, pair.blocks)
         pair.ours(block)
 
-    load.wait()
+    weights_load.wait()
 
     @pl.loop(0, tiles)
     def _(tile):
@@ -1290,14 +1307,17 @@
 
 def ffn_grads(left, right, grads, ffn_partial, resid, gate_up):
     count = lax.axis_size("tensor")
+    far = (left, right, *grads, resid)
     shape = pair_shape(left, grads)
     vmem = pl.BlockSpec(memory_space=pltpu.VMEM)
     sums, result, d_partial = pl.pallas_call(
         functools.partial(ffn_grads_kernel, count, left.shape[1]),
         out_shape=(jax.ShapeDtypeStruct(shape, BF16), jax.ShapeDtypeStruct(resid.shape, BF16), jax.ShapeDtypeStruct(left.shape, BF16)),
-        in_specs=[vmem] * 7 + [pl.BlockSpec(memory_space=pltpu.HBM)],
+        in_specs=[vmem] + [pl.BlockSpec(memory_space=pltpu.HBM)] * (1 + len(far)),
         out_specs=[pl.BlockSpec(memory_space=pltpu.HBM), vmem, vmem],
-        scratch_shapes=pair_scratch(shape)
+        scratch_shapes=[pltpu.VMEM(operand.shape, operand.dtype) for operand in far]
+        + [pltpu.SemaphoreType.DMA((len(far),))]
+        + pair_scratch(shape)
         + line_scratch(count, resid.shape[0], resid.shape[1], True, False)
         + [pltpu.VMEM(gate_up.shape, BF16), pltpu.SemaphoreType.DMA],
         compiler_params=pltpu.CompilerParams(collective_id=6, has_side_effects=True, vmem_limit_bytes=FFN_MEMORY),
@@ -1305,7 +1325,7 @@
             flops=2 * left.shape[0] * left.shape[1] * shape[2], bytes_accessed=50 * 2**20, transcendentals=0
         ),
         name="ffn_grads",
-    )(left, right, *grads, ffn_partial, resid, pltpu.with_memory_space_constraint(gate_up, pltpu.HBM))
+    )(ffn_partial, *[pltpu.with_memory_space_constraint(operand, pltpu.HBM) for operand in (gate_up, *far)])
     return sums.reshape(shape[0] * shape[1], shape[2]), result, d_partial
 
 

time: 406 us -> 403 us (level)
    unnamed x70 -> x68, local copies, waits for them, and re-layouts: 14.4 us -> 14.4 us
  transfers between devices with their start and end apart: 3 -> 3, of which waited for: 1 -> 1; matrix products, arithmetic and copies ran while one was open for 6% -> 6% of each run, Pallas kernels for 48% -> 49%
where the time goes in v7:
time: 403 us
  Pallas kernels  329 us (82%)
  matrix products  36.8 us (9%)
  local copies, waits for them, and re-layouts  18.7 us (5%)
  between operations  15 us (4%)
    pallas_call x3, Pallas kernels, line_call(): pl.pallas_call(functools.partial(kernel, count), out_shape=out_shape, in_...  157 us
    pallas_call x1, Pallas kernels, begin(): pl.pallas_call(functools.partial(begin_kernel, (replicas, shards, count))...  87.5 us
    pallas_call x1, Pallas kernels, ffn_grads(): pl.pallas_call(functools.partial(ffn_grads_kernel, count, left.shape[1]),...  43.8 us
    dot_general x3, matrix products, dot_nt(): lax.dot_general(left, right, (((1,), (1,)), ((), ())), preferred_element_...  20.8 us
    dot_general x2, matrix products, dot(): return jnp.dot(left, right, preferred_element_type=F32)  16 us
    unnamed x68, local copies, waits for them, and re-layouts  14.4 us
    pallas_call x1, Pallas kernels, delta_backward(): pl.pallas_call(backward_kernel, out_shape=(jax.ShapeDtypeStruct((rows, 4...  13.6 us
    pallas_call x1, Pallas kernels, mix_grads(): pl.pallas_call(functools.partial(mix_grads_kernel, left.shape[1]), out_sh...  12.2 us
  transfers between devices with their start and end apart: 3, of which 1 were waited for; matrix products, arithmetic and copies ran while one was open for 6% of the time, Pallas kernels for 49%

profile of v7, /device:TPU:0, one launch (start us, length us, event | category | flops | bytes accessed | tf_op | source)
XLA Modules:
  0.0 402.7 jit_solution(14172620657800685577)
XLA Ops:
  7.2 0.0 copy-start
  7.2 0.0 all-gather.2.cloned.1.call-start
  8.1 1.2 bitcast_convert_fusion.gain_ref
  9.2 0.7 stack.9
  9.9 0.7 stack.10
  10.6 0.6 pad_maximum_fusion.1.own_gains_ref
  11.2 87.5 %begin.1 = (f32[2,2048]{1,0:T(2,128)}, bf16[512,2048]{1,0:T(8,128)(2,1)}, bf16[512,2048]{1,0:T(8,128)(2,1)}, bf16[512,2048]{1,0:T(8,128)(2,1)}, bf16[2048,2176]{...) custom-call(s32[1,4]{1,0:T(1,128)} %starts_ref.3, ...), custom_call_target="tpu_custom_call" | custom-call | flops 9663676416 | bytes 62914560 | tf_op jit(solution)/shard_map/begin/pallas_call | solution.py:1121
  98.7 1.0 constant_dynamic-slice_fusion
  99.7 0.0 all-gather.2.cloned.1.call-update
  99.7 0.0 reduce-scatter.3.cloned.1.call-start
  99.8 0.8 fusion.2
  100.6 1.6 copy-done.18
  102.2 58.9 %middle.1 = (bf16[512,2048]{1,0:T(8,128)(2,1)S(1)}, f32[128,2048]{1,0:T(8,128)S(1)}) custom-call(bf16[512,2048]{1,0:T(8,128)(2,1)S(1)} %copy-done.18, bf16[128,2048]{1,0:T(8,128)(2,1)S(1)} %copy-done.6, f32[1,2048]{1,0:T(1,128)S(1)} %get-tuple-element.125.gain_ref), custom_call_target="tpu_custom_call" | custom-call | flops 1000000000 | bytes 62914560 | tf_op jit(solution)/shard_map/middle/pallas_call | solution.py:754
  161.1 0.0 copy-start.15
  161.1 1.0 copy-done.15
  162.0 1.3 copy-done.19
  163.3 11.3 %fusion.4 = f32[512,2816]{1,0:T(8,128)} fusion(bf16[512,2048]{1,0:T(8,128)(2,1)S(1)} %get-tuple-element.62.left_far, bf16[2048,2816]{1,0:T(8,128)(2,1)} %get-tuple-element.63.gate_up_ref), kind=kOutput, calls=%fused_computation.14 | convolution fusion | flops 5905580032 | bytes 19398656 | tf_op jit(solution)/shard_map/dot_general | solution.py:30
  174.7 9.3 %multiply_convert_fusion = (bf16[512,1408]{1,0:T(8,128)(2,1)}, bf16[512,1408]{1,0:T(8,128)(2,1)}, bf16[512,1408]{1,0:T(8,128)(2,1)S(1)}) fusion(f32[512,2816]{1,0:T(8,128)} %fusion.4, bf16[512,2048]{1,0:T(8,128)(2,1)S(1)} %copy-done.28, bf16[1408,2048]{1,0:T(8,128)(2,1)} %all-gather.2.cloned.1.call-done), kind=kOutput, calls=%fused_computation.2 | convolution fusion | flops 2963603456 | bytes 17956864 | tf_op jit(solution)/shard_map/dot_general | solution.py:34
  184.0 4.7 %convolution_convert_fusion.partial_ref = bf16[512,2048]{1,0:T(8,128)(2,1)} fusion(bf16[512,1408]{1,0:T(8,128)(2,1)S(1)} %get-tuple-element.120.hidden_far, bf16[1408,2048]{1,0:T(8,128)(2,1)S(1)} %copy-done.27), kind=kOutput, calls=%fused_computation | convolution fusion | flops 2953838592 | bytes 9306112 | tf_op jit(solution)/shard_map/dot_general | solution.py:30
  188.7 43.8 %ffn_grads.1 = (bf16[4,256,4224]{2,1,0:T(8,128)(2,1)}, bf16[128,2048]{1,0:T(8,128)(2,1)S(1)}, bf16[512,2048]{1,0:T(8,128)(2,1)}) custom-call(bf16[512,2048]{1,0:T(8,128)(2,1)} %convolution_convert_fusion.partial_ref, bf16[2048,2816]{1,0:T(8,128)(2,1)} %get-tuple-element.63.gate_up_ref, bf16[512,2048]{1,0:T(8,128)(2,1)} %copy-done.19, ...), custom_call_target="tpu_custom_call" | custom-call | flops 8858370048 | bytes 52428800 | tf_op jit(solution)/shard_map/ffn_grads/pallas_call | solution.py:1313
  232.5 0.0 copy-start.5
  232.5 0.0 reduce-scatter.3.cloned.1.call-update
  232.5 0.0 reduce-scatter.5.cloned.1.call-start
  232.6 0.9 copy-done.5
  233.5 0.7 copy-done.12
  234.2 1.2 copy-done.16
  235.5 57.9 %turn.1 = (bf16[512,2048]{1,0:T(8,128)(2,1)S(1)}, f32[128,2048]{1,0:T(8,128)S(1)}, f32[1,2048]{1,0:T(1,128)S(1)}) custom-call(bf16[512,2048]{1,0:T(8,128)(2,1)S(1)} %copy-done.12, f32[128,2048]{1,0:T(8,128)S(1)} %copy-done.16, bf16[128,2048]{1,0:T(8,128)(2,1)S(1)} %copy-done.5, f32[1,2048]{1,0:T(1,128)S(1)} %get-tuple-element.125.gain_ref), custom_call_target="tpu_custom_call" | custom-call | flops 1000000000 | bytes 62914560 | tf_op jit(solution)/shard_map/turn/pallas_call | solution.py:754
  293.4 1.0 copy-done.13
  294.3 0.0 copy-start.17
  294.4 3.0 fusion.5.grad_ref
  297.6 13.6 %delta_backward.1 = (bf16[512,2176]{1,0:T(8,128)(2,1)S(1)}, f32[4,1536]{1,0:T(4,128)S(1)}, f32[1,128]{1,0:T(1,128)S(1)}) custom-call(s32[1,4]{1,0:T(1,128)S(1)} %copy-done.11, s32[1]{0:T(128)S(6)} %copy.40.length_ref, f32[512,2176]{1,0:T(8,128)S(1)} %bitcast.21, bf16[4,512]{1,0:T(4,128)(2,1)S(1)} %copy-done.8, bf16[4,512]{1,0:T(4,128)(2,1)S(1)} %copy-done.9, ...), custom_call_target="tpu_custom_call" | custom-call | flops 3221225472 | bytes 16777216 | tf_op jit(solution)/shard_map/delta_backward/pallas_call | solution.py:276
  311.1 12.2 %mix_grads.1 = bf16[4,256,2688]{2,1,0:T(8,128)(2,1)} custom-call(bf16[512,2048]{1,0:T(8,128)(2,1)S(1)} %copy-done.24, bf16[512,2048]{1,0:T(8,128)(2,1)S(1)} %get-tuple-element.74.right_ref, bf16[512,2176]{1,0:T(8,128)(2,1)S(1)} %get-tuple-element.76.first_ref, bf16[512,512]{1,0:T(8,128)(2,1)S(1)} %copy-done.26), custom_call_target="tpu_custom_call" | custom-call | flops 5637144576 | bytes 31457280 | tf_op jit(solution)/shard_map/mix_grads/pallas_call | solution.py:1239
  323.4 0.0 reduce-scatter.3.cloned.1.call-done.shard_ref
  323.4 0.0 reduce-scatter.5.cloned.1.call-update
  323.4 8.4 %convolution_convert_fusion.1.partial_ref = bf16[512,2048]{1,0:T(8,128)(2,1)S(1)} fusion(bf16[512,2176]{1,0:T(8,128)(2,1)} %copy-done.20, bf16[2048,2176]{1,0:T(8,128)(2,1)} %get-tuple-element.77), kind=kOutput, calls=%fused_computation.1 | convolution fusion | flops 4564451328 | bytes 13238272 | tf_op jit(solution)/shard_map/dot_general | solution.py:34
  331.9 40.0 %last.1 = (f32[128,2048]{1,0:T(8,128)S(1)}, f32[1,2048]{1,0:T(1,128)S(1)}) custom-call(bf16[512,2048]{1,0:T(8,128)(2,1)S(1)} %convolution_convert_fusion.1.partial_ref, bf16[128,2048]{1,0:T(8,128)(2,1)S(1)} %copy-done.7, f32[128,2048]{1,0:T(8,128)S(1)} %copy-done.14, f32[1,2048]{1,0:T(1,128)S(1)} %get-tuple-element.124.gain_ref), custom_call_target="tpu_custom_call" | custom-call | flops 1000000000 | bytes 62914560 | tf_op jit(solution)/shard_map/last/pallas_call | solution.py:754
  371.9 1.0 copy-done.4
  372.9 11.4 %reduce_small.1 = (f32[2,256]{1,0:T(2,128)S(1)}, f32[1,128]{1,0:T(1,128)S(1)}, f32[4,1536]{1,0:T(4,128)S(1)}) custom-call(f32[2,2048]{1,0:T(2,128)S(1)} %pad_maximum_fusion.gain_ref, f32[1,128]{1,0:T(1,128)S(1)} %get-tuple-element.82.head_ref, f32[4,1536]{1,0:T(4,128)S(1)} %get-tuple-element.83.conv_ref), custom_call_target="tpu_custom_call" | custom-call | tf_op jit(solution)/shard_map/reduce_small/pallas_call | solution.py:386
  384.4 0.6 fusion.3
  384.9 0.6 fusion.1
  385.6 2.4 widen_ffn.1
  388.0 1.0 reduce-scatter.5.cloned.1.call-done.shard_ref
  389.0 1.3 copy-done.3
  390.3 1.6 widen_mix.1
  391.9 0.7 copy.36
  392.6 0.8 copy.41
  393.4 2.3 copy.42
  395.7 0.5 copy.43
  (54 shorter events, 0.1 us)
Async XLA Ops:
  7.2 91.5 %copy-start = (bf16[1408,1024]{1,0:T(8,128)(2,1)S(1)}, bf16[1408,1024]{1,0:T(8,128)(2,1)}, u32[]{:S(2)}) copy-start(bf16[1408,1024]{1,0:T(8,128)(2,1)} %param.34) | copy-start | bytes 8650756
  7.2 167.5 %all-gather.2.cloned.1.call-start = ((), (), s32[]{:S(2)}) async-start(), calls=%async_computation.2 | async-start | bytes 6488064 | tf_op jit(solution)/shard_map/all_gather | solution.py:1358
  11.2 89.4 %copy-start.6 = (bf16[128,2048]{1,0:T(8,128)(2,1)S(1)}, bf16[128,2048]{1,0:T(8,128)(2,1)}, u32[]{:S(2)}) copy-start(bf16[128,2048]{1,0:T(8,128)(2,1)} %input_ref.5) | copy-start | bytes 1572868
  99.7 223.7 %reduce-scatter.3.cloned.1.call-start = ((), (), s32[]{:S(2)}) async-start(), calls=%async_computation.3 | async-start | bytes 10813440 | tf_op jit(solution)/shard_map/reduce_scatter | solution.py:1333
  100.6 1.6 copy-start.18
  161.1 1.0 copy-start.15
  162.0 1.3 copy-start.19
  163.3 11.3 %copy-start.28 = (bf16[512,2048]{1,0:T(8,128)(2,1)S(1)}, bf16[512,2048]{1,0:T(8,128)(2,1)}, u32[]{:S(2)}) copy-start(bf16[512,2048]{1,0:T(8,128)(2,1)} %get-tuple-element.65.right_far) | copy-start | bytes 6291460
  174.7 9.3 %copy-start.27 = (bf16[1408,2048]{1,0:T(8,128)(2,1)S(1)}, bf16[1408,2048]{1,0:T(8,128)(2,1)}, u32[]{:S(2)}) copy-start(bf16[1408,2048]{1,0:T(8,128)(2,1)} %all-gather.2.cloned.1.call-done) | copy-start | bytes 17301508
  184.0 4.7 %copy-start.29 = (bf16[512,1408]{1,0:T(8,128)(2,1)}, bf16[512,1408]{1,0:T(8,128)(2,1)S(1)}, u32[]{:S(2)}) copy-start(bf16[512,1408]{1,0:T(8,128)(2,1)S(1)} %get-tuple-element.120.hidden_far) | copy-start | bytes 4325380
  232.5 1.0 copy-start.5
  232.5 1.8 copy-start.12
  232.5 156.5 %reduce-scatter.5.cloned.1.call-start = ((), (), s32[]{:S(2)}) async-start(), calls=%async_computation.4 | async-start | bytes 6881280 | tf_op jit(solution)/shard_map/reduce_scatter | solution.py:1333
  234.2 1.2 copy-start.16
  235.5 62.0 %slice-start = ((s8[4456448]{0:T(1024)(128)(4,1)}), s8[4194304]{0:T(1024)(128)(4,1)S(1)}, s32[]{:S(2)}) async-start(s8[4456448]{0:T(1024)(128)(4,1)} %bitcast.20), calls=%async_computation.5 | async-start | bytes 8388608
  293.3 1.0 copy-start.13
  294.3 3.1 copy-start.8
  294.3 3.1 copy-start.9
  294.3 3.1 copy-start.10
  294.3 3.1 copy-start.11
  294.3 3.1 copy-start.17
  294.3 3.1 slice-start.1
  294.3 3.1 copy-start.21
  294.4 3.1 copy-start.22
  294.4 3.1 copy-start.23
  294.4 3.1 copy-start.25
  297.5 13.6 %copy-start.24 = (bf16[512,2048]{1,0:T(8,128)(2,1)S(1)}, bf16[512,2048]{1,0:T(8,128)(2,1)}, u32[]{:S(2)}) copy-start(bf16[512,2048]{1,0:T(8,128)(2,1)} %get-tuple-element.85.left_ref) | copy-start | bytes 6291460
  297.5 13.6 %copy-start.26 = (bf16[512,512]{1,0:T(8,128)(2,1)S(1)}, bf16[512,512]{1,0:T(8,128)(2,1)}, u32[]{:S(2)}) copy-start(bf16[512,512]{1,0:T(8,128)(2,1)} %get-tuple-element.86.second_ref) | copy-start | bytes 1572868
  311.1 12.2 %copy-start.20 = (bf16[512,2176]{1,0:T(8,128)(2,1)}, bf16[512,2176]{1,0:T(8,128)(2,1)S(1)}, u32[]{:S(2)}) copy-start(bf16[512,2176]{1,0:T(8,128)(2,1)S(1)} %get-tuple-element.76.first_ref) | copy-start | bytes 6684676
  323.4 8.4 %copy-start.7 = (bf16[128,2048]{1,0:T(8,128)(2,1)S(1)}, bf16[128,2048]{1,0:T(8,128)(2,1)}, u32[]{:S(2)}) copy-start(bf16[128,2048]{1,0:T(8,128)(2,1)} %input_ref.5) | copy-start | bytes 1572868
  323.4 8.4 %copy-start.14 = (f32[128,2048]{1,0:T(8,128)S(1)}, f32[128,2048]{1,0:T(8,128)}, u32[]{:S(2)}) copy-start(f32[128,2048]{1,0:T(8,128)} %copy-done.13) | copy-start | bytes 3145732
  331.8 53.7 %copy-start.2 = (bf16[256,4224]{1,0:T(8,128)(2,1)S(1)}, bf16[256,4224]{1,0:T(8,128)(2,1)}, u32[]{:S(2)}) copy-start(bf16[256,4224]{1,0:T(8,128)(2,1)} %reduce-scatter.3.cloned.1.call-done.shard_ref) | copy-start | bytes 6488068
  371.9 1.0 copy-start.4
  385.6 10.7 %copy-start.1 = (bf16[1408,1024]{1,0:T(8,128)(2,1)S(1)}, bf16[1408,1024]{1,0:T(8,128)(2,1)}, u32[]{:S(2)}) copy-start(bf16[1408,1024]{1,0:T(8,128)(2,1)} %param.34) | copy-start | bytes 8650756
  389.0 1.3 copy-start.3
Sparse Core Ops, SparseCore 0:
  99.8 43.1 all-gather.1
  232.6 86.2 reduce-scatter.2
  323.5 65.4 reduce-scatter.4

commit v8 on v7

--- a/solution.py
+++ b/solution.py
@@ -506,7 +506,7 @@
 
 PARTS = 4
 LANES = 512
-FFN_MEMORY = 52 * 2**20
+FFN_MEMORY = 50 * 2**20
 TURN_PARTS = 4
 ATTEND_PARTS = 4
 ATTEND_LATENCY, FFN_LATENCY = 1.5, 1.5

time: 403 us -> 403 us (level)
    unnamed x68 -> x64, local copies, waits for them, and re-layouts: 14.4 us -> 13.7 us
where the time goes in v8:
time: 403 us; the launch traced here: 402 us
  Pallas kernels  328 us (81%)
  matrix products  38.2 us (9%)
  local copies, waits for them, and re-layouts  18 us (4%)
  between operations  15 us (4%)
    pallas_call x3, Pallas kernels, line_call(): pl.pallas_call(functools.partial(kernel, count), out_shape=out_shape, in_...  157 us
    pallas_call x1, Pallas kernels, begin(): pl.pallas_call(functools.partial(begin_kernel, (replicas, shards, count))...  87.5 us
    pallas_call x1, Pallas kernels, ffn_grads(): pl.pallas_call(functools.partial(ffn_grads_kernel, count, left.shape[1]),...  42.4 us
    dot_general x3, matrix products, dot_nt(): lax.dot_general(left, right, (((1,), (1,)), ((), ())), preferred_element_...  22.4 us
    dot_general x2, matrix products, dot(): return jnp.dot(left, right, preferred_element_type=F32)  15.8 us
    unnamed x64, local copies, waits for them, and re-layouts  13.7 us
    pallas_call x1, Pallas kernels, delta_backward(): pl.pallas_call(backward_kernel, out_shape=(jax.ShapeDtypeStruct((rows, 4...  13.6 us
    pallas_call x1, Pallas kernels, mix_grads(): pl.pallas_call(functools.partial(mix_grads_kernel, left.shape[1]), out_sh...  12.2 us
  transfers between devices with their start and end apart: 3, of which 1 were waited for; matrix products, arithmetic and copies ran while one was open for 6% of the time, Pallas kernels for 49%

profile of v8, /device:TPU:0, one launch (start us, length us, event | category | flops | bytes accessed | tf_op | source)
XLA Modules:
  0.0 402.5 jit_solution(3168482281919116585)
XLA Ops:
  7.2 0.0 copy-start
  7.2 0.0 all-gather.2.cloned.1.call-start
  8.1 1.2 bitcast_convert_fusion.gain_ref
  9.2 0.7 stack.9
  9.9 0.7 stack.10
  10.6 0.6 pad_maximum_fusion.1.own_gains_ref
  11.2 87.5 %begin.1 = (f32[2,2048]{1,0:T(2,128)}, bf16[512,2048]{1,0:T(8,128)(2,1)}, bf16[512,2048]{1,0:T(8,128)(2,1)}, bf16[512,2048]{1,0:T(8,128)(2,1)}, bf16[2048,2176]{...) custom-call(s32[1,4]{1,0:T(1,128)} %starts_ref.3, ...), custom_call_target="tpu_custom_call" | custom-call | flops 9663676416 | bytes 62914560 | tf_op jit(solution)/shard_map/begin/pallas_call | solution.py:1121
  98.7 1.0 constant_dynamic-slice_fusion
  99.7 0.0 all-gather.2.cloned.1.call-update
  99.7 0.0 reduce-scatter.3.cloned.1.call-start
  99.8 0.8 fusion.2
  100.6 1.6 copy-done.17
  102.2 58.9 %middle.1 = (bf16[512,2048]{1,0:T(8,128)(2,1)S(1)}, f32[128,2048]{1,0:T(8,128)S(1)}) custom-call(bf16[512,2048]{1,0:T(8,128)(2,1)S(1)} %copy-done.17, bf16[128,2048]{1,0:T(8,128)(2,1)S(1)} %copy-done.6, f32[1,2048]{1,0:T(1,128)S(1)} %get-tuple-element.125.gain_ref), custom_call_target="tpu_custom_call" | custom-call | flops 1000000000 | bytes 62914560 | tf_op jit(solution)/shard_map/middle/pallas_call | solution.py:754
  161.1 0.0 copy-start.14
  161.1 1.0 copy-done.14
  162.0 1.3 copy-done.18
  163.3 11.1 %fusion.4 = f32[512,2816]{1,0:T(8,128)} fusion(bf16[512,2048]{1,0:T(8,128)(2,1)S(1)} %get-tuple-element.62.left_far, bf16[2048,2816]{1,0:T(8,128)(2,1)} %get-tuple-element.63.gate_up_ref), kind=kOutput, calls=%fused_computation.14 | convolution fusion | flops 5905580032 | bytes 19398656 | tf_op jit(solution)/shard_map/dot_general | solution.py:30
  174.4 11.0 %multiply_convert_fusion = (bf16[512,1408]{1,0:T(8,128)(2,1)}, bf16[512,1408]{1,0:T(8,128)(2,1)}, bf16[512,1408]{1,0:T(8,128)(2,1)S(1)}) fusion(f32[512,2816]{1,0:T(8,128)} %fusion.4, bf16[512,2048]{1,0:T(8,128)(2,1)} %get-tuple-element.65.right_far, bf16[1408,2048]{1,0:T(8,128)(2,1)} %all-gather.2.cloned.1.call-done), kind=kOutput, calls=%fused_computation.2 | convolution fusion | flops 2963603456 | bytes 17956864 | tf_op jit(solution)/shard_map/dot_general | solution.py:34
  185.4 4.7 %convolution_convert_fusion.partial_ref = bf16[512,2048]{1,0:T(8,128)(2,1)} fusion(bf16[512,1408]{1,0:T(8,128)(2,1)S(1)} %get-tuple-element.120.hidden_far, bf16[1408,2048]{1,0:T(8,128)(2,1)S(1)} %copy-done.26), kind=kOutput, calls=%fused_computation | convolution fusion | flops 2953838592 | bytes 9306112 | tf_op jit(solution)/shard_map/dot_general | solution.py:30
  190.1 42.4 %ffn_grads.1 = (bf16[4,256,4224]{2,1,0:T(8,128)(2,1)}, bf16[128,2048]{1,0:T(8,128)(2,1)S(1)}, bf16[512,2048]{1,0:T(8,128)(2,1)S(1)}) custom-call(bf16[512,2048]{1,0:T(8,128)(2,1)} %convolution_convert_fusion.partial_ref, bf16[2048,2816]{1,0:T(8,128)(2,1)} %get-tuple-element.63.gate_up_ref, bf16[512,2048]{1,0:T(8,128)(2,1)} %copy-done.18, ...), custom_call_target="tpu_custom_call" | custom-call | flops 8858370048 | bytes 52428800 | tf_op jit(solution)/shard_map/ffn_grads/pallas_call | solution.py:1313
  232.5 0.0 reduce-scatter.3.cloned.1.call-update
  232.5 0.0 reduce-scatter.5.cloned.1.call-start
  232.6 1.0 copy-done.5
  233.5 1.2 copy-done.15
  234.7 57.9 %turn.1 = (bf16[512,2048]{1,0:T(8,128)(2,1)S(1)}, f32[128,2048]{1,0:T(8,128)S(1)}, f32[1,2048]{1,0:T(1,128)S(1)}) custom-call(bf16[512,2048]{1,0:T(8,128)(2,1)S(1)} %get-tuple-element.73.partial_ref, f32[128,2048]{1,0:T(8,128)S(1)} %copy-done.15, bf16[128,2048]{1,0:T(8,128)(2,1)S(1)} %copy-done.5, f32[1,2048]{1,0:T(1,128)S(1)} %get-tuple-element.125.gain_ref), custom_call_target="tpu_custom_call" | custom-call | flops 1000000000 | bytes 62914560 | tf_op jit(solution)/shard_map/turn/pallas_call | solution.py:754
  292.6 1.0 copy-done.12
  293.6 0.0 copy-start.16
  293.7 3.0 fusion.5.grad_ref
  296.8 13.6 %delta_backward.1 = (bf16[512,2176]{1,0:T(8,128)(2,1)S(1)}, f32[4,1536]{1,0:T(4,128)S(1)}, f32[1,128]{1,0:T(1,128)S(1)}) custom-call(s32[1,4]{1,0:T(1,128)S(1)} %copy-done.11, s32[1]{0:T(128)S(6)} %copy.40.length_ref, f32[512,2176]{1,0:T(8,128)S(1)} %bitcast.21, bf16[4,512]{1,0:T(4,128)(2,1)S(1)} %copy-done.8, bf16[4,512]{1,0:T(4,128)(2,1)S(1)} %copy-done.9, ...), custom_call_target="tpu_custom_call" | custom-call | flops 3221225472 | bytes 16777216 | tf_op jit(solution)/shard_map/delta_backward/pallas_call | solution.py:276
  310.5 12.2 %mix_grads.1 = bf16[4,256,2688]{2,1,0:T(8,128)(2,1)} custom-call(bf16[512,2048]{1,0:T(8,128)(2,1)S(1)} %copy-done.23, bf16[512,2048]{1,0:T(8,128)(2,1)S(1)} %get-tuple-element.74.right_ref, bf16[512,2176]{1,0:T(8,128)(2,1)S(1)} %get-tuple-element.76.first_ref, bf16[512,512]{1,0:T(8,128)(2,1)S(1)} %copy-done.25), custom_call_target="tpu_custom_call" | custom-call | flops 5637144576 | bytes 31457280 | tf_op jit(solution)/shard_map/mix_grads/pallas_call | solution.py:1239
  322.7 0.0 reduce-scatter.3.cloned.1.call-done.shard_ref
  322.7 0.0 reduce-scatter.5.cloned.1.call-update
  322.7 0.0 copy-start.7
  322.7 0.0 copy-start.13
  322.8 8.4 %convolution_convert_fusion.1.partial_ref = bf16[512,2048]{1,0:T(8,128)(2,1)S(1)} fusion(bf16[512,2176]{1,0:T(8,128)(2,1)} %copy-done.19, bf16[2048,2176]{1,0:T(8,128)(2,1)} %get-tuple-element.77), kind=kOutput, calls=%fused_computation.1 | convolution fusion | flops 4564451328 | bytes 13238272 | tf_op jit(solution)/shard_map/dot_general | solution.py:34
  331.2 40.4 %last.1 = (f32[128,2048]{1,0:T(8,128)S(1)}, f32[1,2048]{1,0:T(1,128)S(1)}) custom-call(bf16[512,2048]{1,0:T(8,128)(2,1)S(1)} %convolution_convert_fusion.1.partial_ref, bf16[128,2048]{1,0:T(8,128)(2,1)S(1)} %copy-done.7, f32[128,2048]{1,0:T(8,128)S(1)} %copy-done.13, f32[1,2048]{1,0:T(1,128)S(1)} %get-tuple-element.124.gain_ref), custom_call_target="tpu_custom_call" | custom-call | flops 1000000000 | bytes 62914560 | tf_op jit(solution)/shard_map/last/pallas_call | solution.py:754
  371.6 1.0 copy-done.4
  372.6 11.4 %reduce_small.1 = (f32[2,256]{1,0:T(2,128)S(1)}, f32[1,128]{1,0:T(1,128)S(1)}, f32[4,1536]{1,0:T(4,128)S(1)}) custom-call(f32[2,2048]{1,0:T(2,128)S(1)} %pad_maximum_fusion.gain_ref, f32[1,128]{1,0:T(1,128)S(1)} %get-tuple-element.82.head_ref, f32[4,1536]{1,0:T(4,128)S(1)} %get-tuple-element.83.conv_ref), custom_call_target="tpu_custom_call" | custom-call | tf_op jit(solution)/shard_map/reduce_small/pallas_call | solution.py:386
  384.0 0.6 fusion.3
  384.6 0.6 fusion.1
  385.2 2.4 widen_ffn.1
  387.6 1.1 reduce-scatter.5.cloned.1.call-done.shard_ref
  388.7 1.3 copy-done.3
  390.1 1.6 widen_mix.1
  391.7 0.7 copy.36
  392.3 0.8 copy.41
  393.1 2.3 copy.42
  395.4 0.5 copy.43
  (50 shorter events, 0.1 us)
Async XLA Ops:
  7.2 91.5 %copy-start = (bf16[1408,1024]{1,0:T(8,128)(2,1)S(1)}, bf16[1408,1024]{1,0:T(8,128)(2,1)}, u32[]{:S(2)}) copy-start(bf16[1408,1024]{1,0:T(8,128)(2,1)} %param.34) | copy-start | bytes 8650756
  7.2 167.2 %all-gather.2.cloned.1.call-start = ((), (), s32[]{:S(2)}) async-start(), calls=%async_computation.2 | async-start | bytes 6488064 | tf_op jit(solution)/shard_map/all_gather | solution.py:1358
  11.2 89.4 %copy-start.6 = (bf16[128,2048]{1,0:T(8,128)(2,1)S(1)}, bf16[128,2048]{1,0:T(8,128)(2,1)}, u32[]{:S(2)}) copy-start(bf16[128,2048]{1,0:T(8,128)(2,1)} %input_ref.5) | copy-start | bytes 1572868
  99.7 223.0 %reduce-scatter.3.cloned.1.call-start = ((), (), s32[]{:S(2)}) async-start(), calls=%async_computation.3 | async-start | bytes 10813440 | tf_op jit(solution)/shard_map/reduce_scatter | solution.py:1333
  100.6 1.6 copy-start.17
  161.1 1.0 copy-start.14
  162.0 1.3 copy-start.18
  174.4 11.0 %copy-start.26 = (bf16[1408,2048]{1,0:T(8,128)(2,1)S(1)}, bf16[1408,2048]{1,0:T(8,128)(2,1)}, u32[]{:S(2)}) copy-start(bf16[1408,2048]{1,0:T(8,128)(2,1)} %all-gather.2.cloned.1.call-done) | copy-start | bytes 17301508
  185.4 4.7 %copy-start.27 = (bf16[512,1408]{1,0:T(8,128)(2,1)}, bf16[512,1408]{1,0:T(8,128)(2,1)S(1)}, u32[]{:S(2)}) copy-start(bf16[512,1408]{1,0:T(8,128)(2,1)S(1)} %get-tuple-element.120.hidden_far) | copy-start | bytes 4325380
  232.5 1.0 copy-start.5
  232.5 156.2 %reduce-scatter.5.cloned.1.call-start = ((), (), s32[]{:S(2)}) async-start(), calls=%async_computation.4 | async-start | bytes 6881280 | tf_op jit(solution)/shard_map/reduce_scatter | solution.py:1333
  233.5 1.2 copy-start.15
  234.7 61.9 %slice-start = ((s8[4456448]{0:T(1024)(128)(4,1)}), s8[4194304]{0:T(1024)(128)(4,1)S(1)}, s32[]{:S(2)}) async-start(s8[4456448]{0:T(1024)(128)(4,1)} %bitcast.20), calls=%async_computation.5 | async-start | bytes 8388608
  292.6 1.0 copy-start.12
  293.6 3.1 copy-start.8
  293.6 3.1 copy-start.9
  293.6 3.1 copy-start.10
  293.6 3.1 copy-start.11
  293.6 3.1 copy-start.16
  293.6 3.1 slice-start.1
  293.6 3.1 copy-start.20
  293.6 3.1 copy-start.21
  293.6 3.1 copy-start.22
  293.7 3.1 copy-start.24
  296.8 13.6 %copy-start.23 = (bf16[512,2048]{1,0:T(8,128)(2,1)S(1)}, bf16[512,2048]{1,0:T(8,128)(2,1)}, u32[]{:S(2)}) copy-start(bf16[512,2048]{1,0:T(8,128)(2,1)} %get-tuple-element.85.left_ref) | copy-start | bytes 6291460
  296.8 13.6 %copy-start.25 = (bf16[512,512]{1,0:T(8,128)(2,1)S(1)}, bf16[512,512]{1,0:T(8,128)(2,1)}, u32[]{:S(2)}) copy-start(bf16[512,512]{1,0:T(8,128)(2,1)} %get-tuple-element.86.second_ref) | copy-start | bytes 1572868
  310.4 12.2 %copy-start.19 = (bf16[512,2176]{1,0:T(8,128)(2,1)}, bf16[512,2176]{1,0:T(8,128)(2,1)S(1)}, u32[]{:S(2)}) copy-start(bf16[512,2176]{1,0:T(8,128)(2,1)S(1)} %get-tuple-element.76.first_ref) | copy-start | bytes 6684676
  322.7 8.4 %copy-start.7 = (bf16[128,2048]{1,0:T(8,128)(2,1)S(1)}, bf16[128,2048]{1,0:T(8,128)(2,1)}, u32[]{:S(2)}) copy-start(bf16[128,2048]{1,0:T(8,128)(2,1)} %input_ref.5) | copy-start | bytes 1572868
  322.7 8.4 %copy-start.13 = (f32[128,2048]{1,0:T(8,128)S(1)}, f32[128,2048]{1,0:T(8,128)}, u32[]{:S(2)}) copy-start(f32[128,2048]{1,0:T(8,128)} %copy-done.12) | copy-start | bytes 3145732
  331.2 54.0 %copy-start.2 = (bf16[256,4224]{1,0:T(8,128)(2,1)S(1)}, bf16[256,4224]{1,0:T(8,128)(2,1)}, u32[]{:S(2)}) copy-start(bf16[256,4224]{1,0:T(8,128)(2,1)} %reduce-scatter.3.cloned.1.call-done.shard_ref) | copy-start | bytes 6488068
  371.6 1.0 copy-start.4
  385.2 10.8 %copy-start.1 = (bf16[1408,1024]{1,0:T(8,128)(2,1)S(1)}, bf16[1408,1024]{1,0:T(8,128)(2,1)}, u32[]{:S(2)}) copy-start(bf16[1408,1024]{1,0:T(8,128)(2,1)} %param.34) | copy-start | bytes 8650756
  388.7 1.3 copy-start.3
Sparse Core Ops, SparseCore 0:
  99.8 43.1 all-gather.1
  232.6 86.3 reduce-scatter.2
  322.9 65.8 reduce-scatter.4
